TPU v7x, 128 devices: a whole 4x4x4 slice. The times are simulated.
128 devices in a mesh: rows: 8 (over z, core), cols: 16 (over y, x).
Axes of the slice: x: 4, y: 4, z: 4, core: 2. Of those that a mesh axis runs over, the one named last changes fastest.
Arguments:
- pivot_rhs: float32 [4, 4096, 1024], P(None, 'cols'), may hold values from -6 to 6
- bound_sol: bfloat16 [16384, 1024], P('rows'), may hold values from -6 to 6
- border_tiles: bfloat16 [16384, 4, 4096], P('rows', None, 'cols'), may hold values from -0.046875 to 0.046875
- lower_tiles: bfloat16 [6, 4096, 4096], P(None, 'rows', 'cols'), may hold values from -0.09375 to 0.09375
- inverse_diag: bfloat16 [4, 4096, 4096], P(None, 'cols', 'rows'), may hold values from -0.09375 to 0.09375
- owner_map: int32 [128, 128, 1], P(('rows', 'cols')), may hold values from 0 to 127; in each aligned block of 128 rows (0 to 127, 128 to 255, ..., all dimensions but the last counted through in order) at most 2 rows name the same one
Outputs:
- child_rows: float32 [32768, 1024], P(('rows', 'cols'))
Inputs may be any that keep to these rules, and one draw needn't show every extreme that they name: `owner_map`: among the rows of one device (one index of the first dimension), no owner is named more than 2 times, a bound that some block reaches; every owner is named somewhere.
All inputs are finite; a program needn't handle non-finite values.
Results may differ from a plain program's by a relative error of at most 0.008.
Values may be sent and summed in bfloat16 or wider, within the bound.
No kernel may reach another device: no remote copies, remote signals or barrier semaphores. Data moves between devices by JAX's collectives and lax.ppermute only.
A program may use at most 64 MiB of HBM per device.

v0:
```python
import jax
import jax.numpy as jnp
from jax import lax
from jax.sharding import PartitionSpec as P


def pair_slot(later, earlier):
    return later * (later - 1) // 2 + earlier


def pack_rows(rows_here, owners, devices, most):
    onehot = (owners[:, None] == jnp.arange(devices, dtype=jnp.int32)[None, :]).astype(jnp.int32)
    ranks = jnp.cumsum(onehot, axis=0) - onehot
    slots = jnp.sum(ranks * onehot, axis=1)
    target = owners * most + slots
    select = (jnp.arange(devices * most, dtype=jnp.int32)[:, None] == target[None, :]).astype(
        jnp.float32
    )
    return jnp.dot(
        select, rows_here, precision=lax.Precision.HIGHEST, preferred_element_type=jnp.float32
    )


def tile_term(tile, vectors):
    return lax.dot_general(
        tile, vectors, (((0,), (0,)), ((), ())), preferred_element_type=jnp.float32
    )


def local(pivot_rhs, bound_sol, border_tiles, lower_tiles, inverse_diag, owner_map):
    devices = lax.axis_size("rows") * lax.axis_size("cols")
    blocks = pivot_rhs.shape[0]
    width_here = pivot_rhs.shape[1]
    sources = pivot_rhs.shape[2]
    rows_dev = owner_map.shape[1]
    most = max(2, 2 * rows_dev // devices)
    border_part = lax.dot_general(
        border_tiles, bound_sol, (((0,), (0,)), ((), ())), preferred_element_type=jnp.float32
    )
    pending = []
    border_full = lax.psum(border_part, "rows")
    for k in range(blocks):
        pending.append(jnp.zeros((width_here, sources), jnp.float32))
    rounded = [None] * blocks
    own_rows = [None] * blocks
    for k in reversed(range(blocks)):
        local_sum = pending[k]
        for j in range(k + 1, blocks):
            local_sum = local_sum + tile_term(lower_tiles[pair_slot(j, k)], rounded[j])
        summed = lax.psum(local_sum, "rows")
        summed = summed + border_full[k]
        residual = (pivot_rhs[k] - summed).astype(jnp.bfloat16)
        inverse_here = inverse_diag[k]
        solved_here = lax.psum_scatter(
            tile_term(inverse_here, residual), "cols", scatter_dimension=0, tiled=True
        )
        own_rows[k] = solved_here
        if k > 0:
            rounded[k] = lax.all_gather(
                solved_here.astype(jnp.bfloat16), "cols", axis=0, tiled=True
            )
    rows_here = jnp.concatenate(own_rows, axis=0)
    owners = owner_map[0, :, 0]
    buffer = pack_rows(rows_here, owners, devices, most).reshape(devices, most, sources)
    received = lax.all_to_all(buffer, ("rows", "cols"), split_axis=0, concat_axis=0, tiled=True)
    return received.reshape(devices * most, sources)


def solution(mesh):
    placed = (
        P(None, "cols", None),
        P("rows", None),
        P("rows", None, "cols"),
        P(None, "rows", "cols"),
        P(None, "cols", "rows"),
        P(("rows", "cols"), None, None),
    )
    return jax.shard_map(
        local, mesh=mesh, in_specs=placed, out_specs=P(("rows", "cols"), None), check_vma=False
    )
```

profile of v0, /device:TPU:1, one launch (start us, length us, event | category | flops | bytes accessed | tf_op | source)
XLA Modules:
  0.0 773.4 jit_solution(16388644528442897463)
XLA Ops:
  6.5 10.0 %fusion = f32[4,256,1024]{2,1,0:T(8,128)} fusion(bf16[2048,1024]{1,0:T(8,128)(2,1)} %param.7, bf16[2048,4,256]{2,1,0:T(4,128)(2,1)} %param.8), kind=kOutput, calls=%fused_computation | convolution fusion | flops 4294967296 | bytes 12582912 | tf_op jit(solution)/shard_map/dot_general | solution.py:37
  16.6 74.5 %all-reduce.5.cloned.1.call-done = f32[4,256,1024]{2,1,0:T(8,128)} async-done(((f32[4,256,1024]{2,1,0:T(8,128)}), f32[4,256,1024]{2,1,0:T(8,128)}) %all-reduce.5.cloned.1.call-update) | async-done | bytes 4194320 | tf_op jit(solution)/shard_map/psum | solution.py:41
  91.2 2.1 convolution_bitcast_fusion.3
  93.2 1.8 copy.28
  95.1 74.3 %reduce-scatter.13.cloned.1.call-done = f32[32,1024]{1,0:T(8,128)} async-done(((f32[512,1024]{1,0:T(8,128)}), f32[32,1024]{1,0:T(8,128)}) %reduce-scatter.13.cloned.1.call-update) | async-done | bytes 131088 | tf_op jit(solution)/shard_map/reduce_scatter | solution.py:54
  169.5 1.5 convert_element_type.31
  171.1 42.9 %all-gather.4.cloned.1.call-done = bf16[512,1024]{1,0:T(8,128)(2,1)} async-done(((bf16[32,1024]{1,0:T(8,128)(2,1)}), bf16[512,1024]{1,0:T(8,128)(2,1)}) %all-gather.4.cloned.1.call-update) | async-done | bytes 1048592 | tf_op jit(solution)/shard_map/all_gather | solution.py:59
  214.0 2.7 convolution_bitcast_fusion.4
  216.8 61.5 %all-reduce.7.cloned.1.call-done = f32[256,1024]{1,0:T(8,128)} async-done(((f32[256,1024]{1,0:T(8,128)}), f32[256,1024]{1,0:T(8,128)}) %all-reduce.7.cloned.1.call-update) | async-done | bytes 1048592 | tf_op jit(solution)/shard_map/psum | solution.py:50
  278.3 2.5 convolution_bitcast_fusion.2
  280.8 1.8 copy.30
  282.7 73.8 %reduce-scatter.15.cloned.1.call-done = f32[32,1024]{1,0:T(8,128)} async-done(((f32[512,1024]{1,0:T(8,128)}), f32[32,1024]{1,0:T(8,128)}) %reduce-scatter.15.cloned.1.call-update) | async-done | bytes 131088 | tf_op jit(solution)/shard_map/reduce_scatter | solution.py:54
  356.5 1.5 convert_element_type.33
  358.1 42.5 %all-gather.6.cloned.1.call-done = bf16[512,1024]{1,0:T(8,128)(2,1)} async-done(((bf16[32,1024]{1,0:T(8,128)(2,1)}), bf16[512,1024]{1,0:T(8,128)(2,1)}) %all-gather.6.cloned.1.call-update) | async-done | bytes 1048592 | tf_op jit(solution)/shard_map/all_gather | solution.py:59
  400.6 1.7 fusion.35
  402.4 2.4 fusion.4
  404.9 61.5 %all-reduce.9.cloned.1.call-done = f32[256,1024]{1,0:T(8,128)} async-done(((f32[256,1024]{1,0:T(8,128)}), f32[256,1024]{1,0:T(8,128)}) %all-reduce.9.cloned.1.call-update) | async-done | bytes 1048592 | tf_op jit(solution)/shard_map/psum | solution.py:50
  466.4 2.5 convolution_bitcast_fusion.1
  468.8 1.8 copy.32
  470.8 73.8 %reduce-scatter.17.cloned.1.call-done = f32[32,1024]{1,0:T(8,128)} async-done(((f32[512,1024]{1,0:T(8,128)}), f32[32,1024]{1,0:T(8,128)}) %reduce-scatter.17.cloned.1.call-update) | async-done | bytes 131088 | tf_op jit(solution)/shard_map/reduce_scatter | solution.py:54
  544.6 1.5 convert_element_type.35
  546.2 42.9 %all-gather.8.cloned.1.call-done = bf16[512,1024]{1,0:T(8,128)(2,1)} async-done(((bf16[32,1024]{1,0:T(8,128)(2,1)}), bf16[512,1024]{1,0:T(8,128)(2,1)}) %all-gather.8.cloned.1.call-update) | async-done | bytes 1048592 | tf_op jit(solution)/shard_map/all_gather | solution.py:59
  589.1 1.7 fusion.31
  590.8 1.4 convolution_add_fusion.1
  592.3 2.4 fusion.3
  595.0 61.3 %all-reduce.11.cloned.1.call-done = f32[256,1024]{1,0:T(8,128)} async-done(((f32[256,1024]{1,0:T(8,128)}), f32[256,1024]{1,0:T(8,128)}) %all-reduce.11.cloned.1.call-update) | async-done | bytes 1048592 | tf_op jit(solution)/shard_map/psum | solution.py:50
  656.3 2.5 convolution_bitcast_fusion
  658.8 1.9 copy.34
  661.8 72.8 %reduce-scatter.19.cloned.1.call-done = f32[32,1024]{1,0:T(8,128)} async-done(((f32[512,1024]{1,0:T(8,128)}), f32[32,1024]{1,0:T(8,128)}) %reduce-scatter.19.cloned.1.call-update) | async-done | bytes 131088
  734.6 1.1 copy.35
  737.3 27.9 %all_to_all.5 = f32[128,2,1024]{2,1,0:T(2,128)S(1)} all-to-all(f32[128,2,1024]{2,1,0:T(2,128)S(1)} %reshape.16), channel_id=1, replica_groups=mesh['rows'=8,'cols'=16] {'rows','cols'}, dimensions={0} | all-to-all | bytes 2097152 | tf_op jit(solution)/shard_map/all_to_all | solution.py:65
  765.2 1.7 reshape.17
  (43 shorter events, 3.4 us)
Async XLA Ops:
  6.5 84.6 %all-reduce.5.cloned.1.call-start = ((), (), s32[]{:S(2)}) async-start(), calls=%async_computation.5 | async-start | bytes 8388608 | tf_op jit(solution)/shard_map/psum | solution.py:41
  16.6 152.9 %reduce-scatter.13.cloned.1.call-start = ((), (), s32[]{:S(2)}) async-start(), calls=%async_computation.12 | async-start | bytes 2228224 | tf_op jit(solution)/shard_map/reduce_scatter | solution.py:54
  95.1 118.9 %all-gather.4.cloned.1.call-start = ((), (), s32[]{:S(2)}) async-start(), calls=%async_computation.6 | async-start | bytes 1114112 | tf_op jit(solution)/shard_map/all_gather | solution.py:59
  171.0 107.3 %all-reduce.7.cloned.1.call-start = ((), (), s32[]{:S(2)}) async-start(), calls=%async_computation.7 | async-start | bytes 2097152 | tf_op jit(solution)/shard_map/psum | solution.py:50
  216.7 139.7 %reduce-scatter.15.cloned.1.call-start = ((), (), s32[]{:S(2)}) async-start(), calls=%async_computation.13 | async-start | bytes 2228224 | tf_op jit(solution)/shard_map/reduce_scatter | solution.py:54
  280.8 121.6 %copy-start = (bf16[512,1024]{1,0:T(8,128)(2,1)S(1)}, bf16[512,1024]{1,0:T(8,128)(2,1)}, u32[]{:S(2)}) copy-start(bf16[512,1024]{1,0:T(8,128)(2,1)} %all-gather.4.cloned.1.call-done) | copy-start | bytes 3145732
  282.6 118.0 %all-gather.6.cloned.1.call-start = ((), (), s32[]{:S(2)}) async-start(), calls=%async_computation.8 | async-start | bytes 1114112 | tf_op jit(solution)/shard_map/all_gather | solution.py:59
  358.0 108.3 %all-reduce.9.cloned.1.call-start = ((), (), s32[]{:S(2)}) async-start(), calls=%async_computation.9 | async-start | bytes 2097152 | tf_op jit(solution)/shard_map/psum | solution.py:50
  404.8 139.7 %reduce-scatter.17.cloned.1.call-start = ((), (), s32[]{:S(2)}) async-start(), calls=%async_computation.14 | async-start | bytes 2228224 | tf_op jit(solution)/shard_map/reduce_scatter | solution.py:54
  470.7 120.1 %copy-start.1 = (bf16[512,1024]{1,0:T(8,128)(2,1)S(1)}, bf16[512,1024]{1,0:T(8,128)(2,1)}, u32[]{:S(2)}) copy-start(bf16[512,1024]{1,0:T(8,128)(2,1)} %all-gather.6.cloned.1.call-done) | copy-start | bytes 3145732
  470.7 118.4 %all-gather.8.cloned.1.call-start = ((), (), s32[]{:S(2)}) async-start(), calls=%async_computation.10 | async-start | bytes 1114112 | tf_op jit(solution)/shard_map/all_gather | solution.py:59
  546.1 110.1 %all-reduce.11.cloned.1.call-start = ((), (), s32[]{:S(2)}) async-start(), calls=%async_computation.11 | async-start | bytes 2097152 | tf_op jit(solution)/shard_map/psum | solution.py:50
  594.7 139.9 %reduce-scatter.19.cloned.1.call-start = ((), (), s32[]{:S(2)}) async-start(), calls=%async_computation.15 | async-start | bytes 2228224
  658.8 1.9 copy-start.5
  658.8 2.4 copy-start.2
  658.8 2.6 copy-start.3
  658.8 2.8 copy-start.4
Sparse Core Ops, SparseCore 0:
  16.7 74.4 all-reduce.4
  95.2 74.1 reduce-scatter.12
  171.8 42.1 all-gather.3
  216.9 61.3 all-reduce.6
  282.8 73.6 reduce-scatter.14
  358.5 42.1 all-gather.5
  404.9 61.3 all-reduce.8
  470.8 73.6 reduce-scatter.16
  546.9 42.0 all-gather.7
  594.8 61.3 all-reduce.10
  660.8 73.7 reduce-scatter.18
where the time goes:
time: 774 us; the launch traced here: 773 us
  waiting for transfers between devices  682 us (88%)
  matrix products  33 us (4%)
  blocking collectives  27.9 us (4%)
  between operations  13.4 us (2%)
  local copies, waits for them, and re-layouts  11.4 us (1%)
    reduce_scatter x3, waiting for transfers between devices, local(): lax.psum_scatter(tile_term(inverse_here, residual), 'cols', scatter_dimen...  222 us
    psum x3, waiting for transfers between devices, local(): summed = lax.psum(local_sum, 'rows')  184 us
    all_gather x3, waiting for transfers between devices, local(): lax.all_gather(solved_here.astype(jnp.bfloat16), 'cols', axis=0, tiled=True)  128 us
    psum x1, waiting for transfers between devices, local(): border_full = lax.psum(border_part, 'rows')  74.5 us
    unnamed x12, waiting for transfers between devices  73 us
    all_to_all x1, blocking collectives, local(): lax.all_to_all(buffer, ('rows', 'cols'), split_axis=0, concat_axis=0, til...  27.9 us
    dot_general x10, matrix products, tile_term(): lax.dot_general(tile, vectors, (((0,), (0,)), ((), ())), preferred_elemen...  22 us
  transfers between devices with their start and end apart: 11, of which 11 were waited for; matrix products, arithmetic and copies ran while one was open for 0% of the time, Pallas kernels for 0%

commit v1 on v0

v1 whole, which is shorter than its diff:
```python
import jax
import jax.numpy as jnp
from jax import lax
from jax.experimental import pallas as pl
from jax.experimental.pallas import tpu as pltpu
from jax.sharding import Mesh, PartitionSpec as P

BF16 = jnp.bfloat16
F32 = jnp.float32
VMEM_LIMIT = 48 * 1024 * 1024


def pair_slot(later, earlier):
    return later * (later - 1) // 2 + earlier


def shift(value, axis, by):
    return lax.ppermute(value, axis, [(i, (i + by) % 4) for i in range(4)])


def swap(value):
    return lax.ppermute(value, "core", [(0, 1), (1, 0)])


def spread(value, axis):
    far = shift(value, axis, 2)
    right = shift(value, axis, 1)
    left = shift(value, axis, 3)
    return (value, right, far, left)


def deal(pieces, axis):
    far = shift(pieces[2], axis, 2)
    right = shift(pieces[1], axis, 1)
    left = shift(pieces[3], axis, 3)
    return (pieces[0], right, far, left)


def add_up(refs):
    total = refs[0][...].astype(F32)
    for ref in refs[1:]:
        total = total + ref[...].astype(F32)
    return total


def params(**extra):
    return pltpu.CompilerParams(vmem_limit_bytes=VMEM_LIMIT, **extra)


def cost(flops, moved):
    return pl.CostEstimate(flops=flops, bytes_accessed=moved, transcendentals=0)


def whole(shape):
    return pl.BlockSpec(shape, lambda *_: (0,) * len(shape))


SCALARS = pl.BlockSpec(memory_space=pltpu.SMEM)


def first_kernel(place, v0, v1, v2, v3, mine, other, o0, o1, o2, o3, turned):
    core, x = place[0], place[2]
    turned[...] = add_up((v0, v1, v2, v3)).T.astype(BF16)
    here = pl.ds(pl.multiple_of(core * 512, 512), 512)
    there = pl.ds(pl.multiple_of((1 - core) * 512, 512), 512)
    for step, out in enumerate((o0, o1, o2, o3)):
        rows = pl.ds(pl.multiple_of(lax.rem(x + step, 4) * 128, 128), 128)
        left = turned[rows, :]
        out[:, here] = jnp.dot(left, mine[...], preferred_element_type=F32).astype(BF16)
        out[:, there] = jnp.dot(left, other[...], preferred_element_type=F32).astype(BF16)


def first_product(place, pieces, mine, other):
    shape = jax.ShapeDtypeStruct((128, 1024), BF16)
    return pl.pallas_call(
        first_kernel,
        out_shape=(shape,) * 4,
        in_specs=[SCALARS] + [pl.BlockSpec(memory_space=pltpu.VMEM)] * 6,
        out_specs=(pl.BlockSpec(memory_space=pltpu.VMEM),) * 4,
        scratch_shapes=[pltpu.VMEM((512, 256), BF16)],
        compiler_params=params(),
        cost_estimate=cost(2 * 512 * 256 * 1024, 3 << 20),
        name="first_product",
    )(place, *pieces, mine, other)


def turn_kernel(place, v0, v1, v2, v3, out):
    x = place[2]
    for step, ref in enumerate((v0, v1, v2, v3)):
        lanes = pl.ds(pl.multiple_of(lax.rem(x + 4 - step, 4) * 256, 256), 256)
        for k in range(3):
            out[k, :, lanes] = ref[k].astype(F32).T


def turn(place, pieces):
    return pl.pallas_call(
        turn_kernel,
        out_shape=jax.ShapeDtypeStruct((3, 128, 1024), F32),
        in_specs=[SCALARS] + [pl.BlockSpec(memory_space=pltpu.VMEM)] * 4,
        out_specs=pl.BlockSpec(memory_space=pltpu.VMEM),
        compiler_params=params(),
        cost_estimate=cost(3 * 128 * 1024, 3 << 20),
        name="turn",
    )(place, *pieces)


def lower_step(base, pieces, tiles, at, dtype):
    count = len(pieces)

    def kernel(*refs):
        parts = refs[:count]
        base_ref, tile, out, kept, vec = refs[count:]

        @pl.when(pl.program_id(0) == 0)
        def _():
            vec[...] = add_up(parts).astype(BF16)
            kept[...] = vec[...]

        total = base_ref[...].astype(F32)
        total = total - jnp.dot(vec[:, :512], tile[0, 0], preferred_element_type=F32)
        total = total - jnp.dot(vec[:, 512:], tile[1, 0], preferred_element_type=F32)
        out[...] = total.astype(dtype)

    return pl.pallas_call(
        kernel,
        grid=(4,),
        out_shape=(
            jax.ShapeDtypeStruct((128, 1024), dtype),
            jax.ShapeDtypeStruct((128, 1024), BF16),
        ),
        in_specs=[whole((128, 1024))] * count
        + [
            pl.BlockSpec((128, 256), lambda i: (0, i)),
            pl.BlockSpec((2, 1, 512, 256), lambda i: (0, i, at, 0)),
        ],
        out_specs=(pl.BlockSpec((128, 256), lambda i: (0, i)), whole((128, 1024))),
        scratch_shapes=[pltpu.VMEM((128, 1024), BF16)],
        compiler_params=params(),
        cost_estimate=cost(2 * 128 * 1024 * 1024, 4 << 20),
        name="lower_step",
    )(*pieces, base, tiles)


def diag_step(pieces, tiles, at):
    def kernel(v0, v1, v2, v3, tile, out, vec):
        @pl.when(pl.program_id(0) == 0)
        def _():
            vec[...] = add_up((v0, v1, v2, v3)).astype(BF16)

        total = jnp.dot(vec[:, :256], tile[0, 0], preferred_element_type=F32)
        for x in range(1, 4):
            total = total + jnp.dot(
                vec[:, x * 256 : (x + 1) * 256], tile[0, x], preferred_element_type=F32
            )
        out[...] = total.astype(BF16)

    return pl.pallas_call(
        kernel,
        grid=(4,),
        out_shape=jax.ShapeDtypeStruct((128, 1024), BF16),
        in_specs=[whole((128, 1024))] * 4
        + [pl.BlockSpec((1, 4, 256, 256), lambda i: (i // 2, 0, 2 * at + i % 2, 0))],
        out_specs=pl.BlockSpec((128, 256), lambda i: (0, i)),
        scratch_shapes=[pltpu.VMEM((128, 1024), BF16)],
        compiler_params=params(),
        cost_estimate=cost(2 * 128 * 1024 * 1024, 4 << 20),
        name="diag_step",
    )(*pieces, tiles)


def last_step(place, pieces, tiles, at):
    def kernel(place_ref, v0, v1, v2, v3, tile, o0, o1, o2, o3, vec, full):
        step = pl.program_id(0)

        @pl.when(step == 0)
        def _():
            vec[...] = add_up((v0, v1, v2, v3)).astype(BF16)

        total = jnp.dot(vec[:, :256], tile[0, 0], preferred_element_type=F32)
        for x in range(1, 4):
            total = total + jnp.dot(
                vec[:, x * 256 : (x + 1) * 256], tile[0, x], preferred_element_type=F32
            )
        full[:, pl.ds(pl.multiple_of(step * 256, 256), 256)] = total.astype(BF16)

        @pl.when(step == 3)
        def _():
            y = place_ref[1]
            for by, out in enumerate((o0, o1, o2, o3)):
                start = lax.rem(y + by, 4) * 128
                out[:, :128] = full[:, pl.ds(pl.multiple_of(start, 128), 128)]
                out[:, 128:] = full[:, pl.ds(pl.multiple_of(start + 512, 128), 128)]

    return pl.pallas_call(
        kernel,
        grid=(4,),
        out_shape=(jax.ShapeDtypeStruct((128, 256), BF16),) * 4,
        in_specs=[SCALARS]
        + [whole((128, 1024))] * 4
        + [pl.BlockSpec((1, 4, 256, 256), lambda i: (i // 2, 0, 2 * at + i % 2, 0))],
        out_specs=(whole((128, 256)),) * 4,
        scratch_shapes=[pltpu.VMEM((128, 1024), BF16), pltpu.VMEM((128, 1024), BF16)],
        compiler_params=params(),
        cost_estimate=cost(2 * 128 * 1024 * 1024, 4 << 20),
        name="last_step",
    )(place, *pieces, tiles)


def chosen(target, block):
    slots = lax.broadcasted_iota(jnp.int32, (256, 256), 0) + block * 256
    return jnp.where(slots == target, 1.0, 0.0).astype(BF16)


def picked(target, block, rows):
    return lax.dot_general(
        chosen(target, block), rows, (((1,), (1,)), ((), ())), preferred_element_type=F32
    )


def pack_known(place, target, known):
    def kernel(place_ref, target_ref, x1, x2, x3, out):
        block = pl.program_id(0)
        start = pl.multiple_of(place_ref[1] * 128, 128)
        again = pl.multiple_of(place_ref[1] * 128 + 512, 128)
        total = jnp.zeros((256, 128), F32)
        for k, ref in ((1, x1), (2, x2), (3, x3)):
            rows = jnp.concatenate([ref[:, pl.ds(start, 128)], ref[:, pl.ds(again, 128)]], axis=1)
            total = total + picked(target_ref[k], block, rows)
        out[...] = total.astype(BF16)

    return pl.pallas_call(
        kernel,
        grid=(8,),
        out_shape=jax.ShapeDtypeStruct((2048, 128), BF16),
        in_specs=[SCALARS, whole((4, 1, 256))] + [whole((128, 1024))] * 3,
        out_specs=pl.BlockSpec((256, 128), lambda i: (i, 0)),
        compiler_params=params(),
        cost_estimate=cost(2 * 2048 * 768 * 128, 2 << 20),
        name="pack_known",
    )(place, target, *known)


def pack_last(target, pieces, base):
    def kernel(target_ref, v0, v1, v2, v3, base_ref, out, rows):
        block = pl.program_id(0)

        @pl.when(block == 0)
        def _():
            rows[...] = add_up((v0, v1, v2, v3)).astype(BF16)

        total = base_ref[...].astype(F32) + picked(target_ref[0], block, rows[...])
        out[...] = total.astype(BF16)

    return pl.pallas_call(
        kernel,
        grid=(8,),
        out_shape=jax.ShapeDtypeStruct((2048, 128), BF16),
        in_specs=[whole((4, 1, 256))]
        + [whole((128, 256))] * 4
        + [pl.BlockSpec((256, 128), lambda i: (i, 0))],
        out_specs=pl.BlockSpec((256, 128), lambda i: (i, 0)),
        scratch_shapes=[pltpu.VMEM((128, 256), BF16)],
        compiler_params=params(),
        cost_estimate=cost(2 * 2048 * 256 * 128, 2 << 20),
        name="pack_last",
    )(target, *pieces, base)


def unpack(received):
    def kernel(got, out):
        for core in range(2):
            for y in range(4):
                for x in range(4):
                    tile = got[0, core, y, x].astype(F32)
                    lanes = pl.ds((core * 4 + x) * 128, 128)
                    for half in range(2):
                        out[pl.ds(half * 32 + y * 8, 8), lanes] = tile[half * 8 : half * 8 + 8]

    return pl.pallas_call(
        kernel,
        grid=(4,),
        out_shape=jax.ShapeDtypeStruct((256, 1024), F32),
        in_specs=[pl.BlockSpec((1, 2, 4, 4, 16, 128), lambda i: (i, 0, 0, 0, 0, 0))],
        out_specs=pl.BlockSpec((64, 1024), lambda i: (i, 0)),
        compiler_params=params(),
        cost_estimate=cost(256 * 1024, 2 << 20),
        name="unpack",
    )(received.reshape(4, 2, 4, 4, 16, 128))


def slots_of(owners, core, x):
    pair = swap(owners)
    both = jnp.where(core == 0, jnp.stack([owners, pair]), jnp.stack([pair, owners]))
    around = [both] + [shift(both, "x", -by) for by in (1, 2, 3)]
    twice = jnp.stack(around + around)
    ordered = lax.dynamic_slice_in_dim(twice, lax.rem(4 - x, 4), 4, axis=0)
    named = ordered.transpose(1, 0, 2).reshape(8, 128)
    same = named[:, :, None] == named[:, None, :]
    earlier = jnp.arange(128)[None, :, None] > jnp.arange(128)[None, None, :]
    ranks = jnp.sum((same & earlier).astype(jnp.int32), axis=2)
    target = named * 16 + jnp.arange(8, dtype=jnp.int32)[:, None] * 2 + ranks
    return target.reshape(8, 4, 32).transpose(1, 0, 2).reshape(4, 1, 256)


def halves(tile):
    return [tile[:, :256], tile[:, 256:]]


def gathered(parts):
    rows = sum(part.shape[0] for part in parts)
    joined = jnp.concatenate(parts, axis=0) if len(parts) > 1 else parts[0]
    return lax.all_gather(joined, ("core", "x"), axis=0, tiled=False).reshape(2, 4, rows, 256)


def local(pivot_rhs, bound_sol, border_tiles, lower_tiles, inverse_diag, owner_map):
    z, core, y, x = (lax.axis_index(name) for name in ("z", "core", "y", "x"))
    place = jnp.stack([core, y, x, z]).astype(jnp.int32)
    lead = jnp.where((z == 0) & (core == 0), 1.0, 0.0).astype(F32)

    def lower(j, k):
        return lower_tiles[pair_slot(j, k)]

    early = gathered([lower(3, 2)] + halves(inverse_diag[2]))
    middle = gathered([lower(3, 1), lower(2, 1)] + halves(inverse_diag[1]))
    late = gathered([lower(3, 0), lower(2, 0), lower(1, 0)])
    end = gathered(halves(inverse_diag[0]))
    other_diag = swap(inverse_diag[3])

    def border(tiles):
        return lax.dot_general(
            tiles, bound_sol, (((0,), (0,)), ((), ())), preferred_element_type=F32
        )

    def paired(part):
        axis = part.ndim - 1
        away = lax.dynamic_slice_in_dim(part, (1 - core) * 512, 512, axis=axis)
        home = lax.dynamic_slice_in_dim(part, core * 512, 512, axis=axis)
        return (home.astype(F32) + swap(away).astype(F32)).astype(BF16)

    top = (lead * pivot_rhs[3] - border(border_tiles[:, 3, :])).astype(BF16)
    products = first_product(place, spread(paired(top), "z"), inverse_diag[3], other_diag)

    rest = paired((lead * pivot_rhs[:3] - border(border_tiles[:, :3, :])).astype(BF16))
    cut = [
        lax.dynamic_slice_in_dim(rest, lax.rem(x + by, 4) * 128, 128, axis=2) for by in range(4)
    ]
    base = turn(place, deal(cut, "x"))
    target = slots_of(owner_map[0, :, 0], core, x)

    over_x = deal(products, "x")
    partial = sum(piece.astype(F32) for piece in over_x).astype(BF16)
    pieces = spread(partial, "y")
    residual, x3 = lower_step(base[2], pieces, early, 0, BF16)
    over_z = spread(residual, "z")
    base1, _ = lower_step(base[1], (x3,), middle, 0, F32)
    pieces = spread(diag_step(over_z, early, 1), "y")
    residual, x2 = lower_step(base1, pieces, middle, 1, BF16)
    over_z = spread(residual, "z")
    base0, _ = lower_step(base[0], (x3,), late, 0, F32)
    pieces = spread(diag_step(over_z, middle, 2), "y")
    base0, _ = lower_step(base0, (x2,), late, 1, F32)
    residual, x1 = lower_step(base0, pieces, late, 2, BF16)
    over_z = spread(residual, "z")
    packed = pack_known(place, target, (x1, x2, x3))
    rows = deal(last_step(place, over_z, end, 0), "y")
    packed = pack_last(target, rows, packed).reshape(128, 16, 128)
    received = lax.all_to_all(
        packed, ("z", "core", "y", "x"), split_axis=0, concat_axis=0, tiled=True
    )
    return unpack(received)


def solution(mesh):
    fine = Mesh(mesh.devices.reshape(4, 2, 4, 4), ("z", "core", "y", "x"))
    rows, cols = ("z", "core"), ("y", "x")
    placed = (
        P(None, cols, None),
        P(rows, None),
        P(rows, None, cols),
        P(None, rows, cols),
        P(None, cols, rows),
        P(rows + cols, None, None),
    )
    return jax.shard_map(
        local, mesh=fine, in_specs=placed, out_specs=P(rows + cols, None), check_vma=False
    )
```

time: 774 us -> 218 us (0.28)
  waiting for transfers between devices: 682 us -> 55.5 us
  starting transfers between devices: 0.6 us -> 62.7 us
  Pallas kernels: 0 us -> 35.3 us
  matrix products: 33 us -> 11.7 us
    psum x4 -> x0, waiting for transfers between devices: 259 us -> none  [the longest x3 184 us: local(): summed = lax.psum(local_sum, 'rows')]
    reduce_scatter x3 -> x0, waiting for transfers between devices: 222 us -> none  [local(): lax.psum_scatter(tile_term(inverse_here, residual), 'cols', scatter_dimen...]
    all_gather x3 -> x4, waiting for transfers between devices: 128 us -> 15.4 us  [gathered(): lax.all_gather(joined, ('core', 'x'), axis=0, tiled=False)]
    unnamed x12 -> x4, waiting for transfers between devices: 73 us -> 0.07 us
    ppermute x0 -> x37, starting transfers between devices: none -> 62.5 us  [the longest x33 53.2 us: shift(): return lax.ppermute(value, axis, [(i, (i + by) % 4) for i in range(4)])]
    ppermute x0 -> x37, waiting for transfers between devices: none -> 40 us  [the longest x33 40 us: shift(): return lax.ppermute(value, axis, [(i, (i + by) % 4) for i in range(4)])]
    pallas_call x0 -> x14, Pallas kernels: none -> 35.3 us  [the longest x6 20.8 us: lower_step(): pl.pallas_call(kernel, grid=(4,), out_shape=(jax.ShapeDtypeStruct((128, 1...]
    dot_general x12 -> x2, matrix products: 33 us -> 11.7 us  [border(): lax.dot_general(tiles, bound_sol, (((0,), (0,)), ((), ())), preferred_ele...]
  transfers between devices with their start and end apart: 11 -> 41, of which waited for: 11 -> 12; matrix products, arithmetic and copies ran while one was open for 0% -> 10% of each run, Pallas kernels for 0% -> 14%
where the time goes in v1:
time: 218 us; the launch traced here: 217 us
  starting transfers between devices  62.7 us (29%)
  waiting for transfers between devices  55.5 us (25%)
  Pallas kernels  35.3 us (16%)
  blocking collectives  22.6 us (10%)
  between operations  13.5 us (6%)
  matrix products  11.7 us (5%)
  local copies, waits for them, and re-layouts  11.3 us (5%)
  other arithmetic  4.57 us (2%)
    ppermute x33, starting transfers between devices, shift(): return lax.ppermute(value, axis, [(i, (i + by) % 4) for i in range(4)])  53.2 us
    ppermute x33, waiting for transfers between devices, shift(): return lax.ppermute(value, axis, [(i, (i + by) % 4) for i in range(4)])  40 us
    all_to_all x1, blocking collectives, local(): lax.all_to_all(packed, ('z', 'core', 'y', 'x'), split_axis=0, concat_axis...  22.6 us
    pallas_call x6, Pallas kernels, lower_step(): pl.pallas_call(kernel, grid=(4,), out_shape=(jax.ShapeDtypeStruct((128, 1...  20.8 us
    all_gather x4, waiting for transfers between devices, gathered(): lax.all_gather(joined, ('core', 'x'), axis=0, tiled=False)  15.4 us
    dot_general x2, matrix products, border(): lax.dot_general(tiles, bound_sol, (((0,), (0,)), ((), ())), preferred_ele...  11.7 us
    ppermute x4, starting transfers between devices, swap(): return lax.ppermute(value, 'core', [(0, 1), (1, 0)])  9.3 us
    pallas_call x2, Pallas kernels, diag_step(): pl.pallas_call(kernel, grid=(4,), out_shape=jax.ShapeDtypeStruct((128, 10...  4.49 us
  transfers between devices with their start and end apart: 41, of which 12 were waited for; matrix products, arithmetic and copies ran while one was open for 10% of the time, Pallas kernels for 14%

profile of v1, /device:TPU:1, one launch (start us, length us, event | category | flops | bytes accessed | tf_op | source)
XLA Modules:
  0.0 217.1 jit_solution(14152338850512411901)
XLA Ops:
  12.7 4.2 %slice.71 = bf16[2048,1,256]{2,1,0:T(2,128)(2,1)S(1)} slice(bf16[2048,4,256]{2,1,0:T(4,128)(2,1)} %param.8), slice={[0:2048], [3:4], [0:256]} | slice | bytes 2097152 | tf_op jit(solution)/shard_map/slice | solution.py:340
  17.0 3.8 %fusion.7 = bf16[256,1024]{1,0:T(8,128)(2,1)S(1)} fusion(bf16[2048,1024]{1,0:T(8,128)(2,1)} %param.7, bf16[2048,1,256]{2,1,0:T(2,128)(2,1)S(1)} %slice.71, f32[4,256,1024]{2,1,0:T(8,128)} %param.6, f32[]{:T(128)S(6)} %select_n.51), kind=kOutput, calls=%fused_computation.6 | convolution fusion | flops 1074528256 | bytes 6815748 | tf_op jit(solution)/shard_map/dot_general | solution.py:330
  23.9 7.9 %subtract_convert_fusion = bf16[3,256,1024]{2,1,0:T(8,128)(2,1)S(1)} fusion(f32[4,256,1024]{2,1,0:T(8,128)} %param.6, bf16[2048,1024]{1,0:T(8,128)(2,1)} %param.7, bf16[2048,3,256]{2,1,0:T(4,128)(2,1)} %bitcast.85, f32[]{:T(128)S(6)} %select_n.51), kind=kOutput, calls=%fused_computation.3 | convolution fusion | flops 3223584768 | bytes 12058628 | tf_op jit(solution)/shard_map/dot_general | solution.py:330
  34.9 3.3 %collective-permute-start.6 = (bf16[256,512]{1,0:T(8,128)(2,1)S(1)}, bf16[256,512]{1,0:T(8,128)(2,1)S(1)}, u32[]{:S(2)}, u32[]{:S(2)}) collective-permute-start(bf16[256,512]{1,0:T(8,128)(2,1)S(1)} %add_convert_fusion.2.v0), channel_id=1, source_target_pairs={{0,64},{32,96},{64,0},{96,32},{1,65},{33,97},{65,1},{97,33},{2,66}... | collective-permute-start | bytes 786440 | tf_op jit(solution)/shard_map/ppermute | solution.py:18
  38.9 4.4 %collective-permute-done.5.v1 = bf16[256,512]{1,0:T(8,128)(2,1)S(1)} collective-permute-done((bf16[256,512]{1,0:T(8,128)(2,1)S(1)}, bf16[256,512]{1,0:T(8,128)(2,1)S(1)}, u32[]{:S(2)}, u32[]{:S(2)}) %collective-permute-start.5) | collective-permute-done | bytes 262176 | tf_op jit(solution)/shard_map/ppermute | solution.py:18
  43.3 6.4 %collective-permute-done.6.v2 = bf16[256,512]{1,0:T(8,128)(2,1)S(1)} collective-permute-done((bf16[256,512]{1,0:T(8,128)(2,1)S(1)}, bf16[256,512]{1,0:T(8,128)(2,1)S(1)}, u32[]{:S(2)}, u32[]{:S(2)}) %collective-permute-start.6) | collective-permute-done | bytes 262176 | tf_op jit(solution)/shard_map/ppermute | solution.py:18
  50.9 2.7 %collective-permute-start.11 = (bf16[128,1024]{1,0:T(8,128)(2,1)S(1)}, bf16[128,1024]{1,0:T(8,128)(2,1)S(1)}, u32[]{:S(2)}, u32[]{:S(2)}) collective-permute-start(bf16[128,1024]{1,0:T(8,128)(2,1)S(1)} %get-tuple-element.25), channel_id=1, source_target_pairs={{0,3},{1,0},{2,1},{3,2},{4,7},{5,4},{6,5},{7,6},{8,11},{9,8},{10,9... | collective-permute-start | bytes 786440 | tf_op jit(solution)/shard_map/ppermute | solution.py:18
  58.9 4.4 %collective-permute-start.18 = (bf16[3,256,128]{2,1,0:T(8,128)(2,1)S(1)}, bf16[3,256,128]{2,1,0:T(8,128)(2,1)S(1)}, u32[]{:S(2)}, u32[]{:S(2)}) collective-permute-start(bf16[3,256,128]{2,1,0:T(8,128)(2,1)S(1)} %get-tuple-element.54), channel_id=1, source_target_pairs={{0,3},{1,0},{2,1},{3,2},{4,7},{5,4},{6,5},{7,6},{8,11},{9,8},{10,9... | collective-permute-start | bytes 589832 | tf_op jit(solution)/shard_map/ppermute | solution.py:18
  63.3 11.1 %collective-permute-done.9 = bf16[128,1024]{1,0:T(8,128)(2,1)S(1)} collective-permute-done((bf16[128,1024]{1,0:T(8,128)(2,1)S(1)}, bf16[128,1024]{1,0:T(8,128)(2,1)S(1)}, u32[]{:S(2)}, u32[]{:S(2)}) %collective-permute-start.9) | collective-permute-done | bytes 262176 | tf_op jit(solution)/shard_map/ppermute | solution.py:18
  75.9 2.6 %collective-permute-start.13 = (bf16[128,1024]{1,0:T(8,128)(2,1)S(1)}, bf16[128,1024]{1,0:T(8,128)(2,1)S(1)}, u32[]{:S(2)}, u32[]{:S(2)}) collective-permute-start(bf16[128,1024]{1,0:T(8,128)(2,1)S(1)} %add_convert_fusion.1.refs_0_), channel_id=1, source_target_pairs={{0,8},{4,12},{8,0},{12,4},{1,9},{5,13},{9,1},{13,5},{2,10},{6,14},... | collective-permute-start | bytes 786440 | tf_op jit(solution)/shard_map/ppermute | solution.py:18
  78.6 4.8 %collective-permute-done.16.v1 = bf16[3,256,128]{2,1,0:T(8,128)(2,1)S(1)} collective-permute-done((bf16[3,256,128]{2,1,0:T(8,128)(2,1)S(1)}, bf16[3,256,128]{2,1,0:T(8,128)(2,1)S(1)}, u32[]{:S(2)}, u32[]{:S(2)}) %collective-permute-start.16) | collective-permute-done | bytes 196640 | tf_op jit(solution)/shard_map/ppermute | solution.py:18
  83.4 2.6 %collective-permute-start.14 = (bf16[128,1024]{1,0:T(8,128)(2,1)S(1)}, bf16[128,1024]{1,0:T(8,128)(2,1)S(1)}, u32[]{:S(2)}, u32[]{:S(2)}) collective-permute-start(bf16[128,1024]{1,0:T(8,128)(2,1)S(1)} %add_convert_fusion.1.refs_0_), channel_id=1, source_target_pairs={{0,12},{4,0},{8,4},{12,8},{1,13},{5,1},{9,5},{13,9},{2,14},{6,2},{... | collective-permute-start | bytes 786440 | tf_op jit(solution)/shard_map/ppermute | solution.py:18
  86.1 3.3 %collective-permute-done.17.v2 = bf16[3,256,128]{2,1,0:T(8,128)(2,1)S(1)} collective-permute-done((bf16[3,256,128]{2,1,0:T(8,128)(2,1)S(1)}, bf16[3,256,128]{2,1,0:T(8,128)(2,1)S(1)}, u32[]{:S(2)}, u32[]{:S(2)}) %collective-permute-start.17) | collective-permute-done | bytes 196640 | tf_op jit(solution)/shard_map/ppermute | solution.py:18
  90.3 3.3 %lower_step.6 = (bf16[128,1024]{1,0:T(8,128)(2,1)S(1)}, bf16[128,1024]{1,0:T(8,128)(2,1)S(1)}) custom-call(bf16[128,1024]{1,0:T(8,128)(2,1)S(1)} %add_convert_fusion.1.refs_0_, bf16[128,1024]{1,0:T(8,128)(2,1)S(1)} %collective-permute-done.12.refs_1_, bf16[128,1024]{1,0:T(8,128)(2,1)S(1)} %collective-permute-done.13.refs_2_, ...), custom_call_target="tpu_custom_call" | custom-call | flops 268435456 | bytes 4194304 | tf_op jit(solution)/shard_map/lower_step/pallas_call | solution.py:124
  93.7 2.6 %collective-permute-start.19 = (bf16[128,1024]{1,0:T(8,128)(2,1)S(1)}, bf16[128,1024]{1,0:T(8,128)(2,1)S(1)}, u32[]{:S(2)}, u32[]{:S(2)}) collective-permute-start(bf16[128,1024]{1,0:T(8,128)(2,1)S(1)} %get-tuple-element.26.v0), channel_id=1, source_target_pairs={{0,32},{32,64},{64,96},{96,0},{1,33},{33,65},{65,97},{97,1},{2,34}... | collective-permute-start | bytes 786440 | tf_op jit(solution)/shard_map/ppermute | solution.py:18
  96.2 3.2 %collective-permute-start.20 = (bf16[128,1024]{1,0:T(8,128)(2,1)S(1)}, bf16[128,1024]{1,0:T(8,128)(2,1)S(1)}, u32[]{:S(2)}, u32[]{:S(2)}) collective-permute-start(bf16[128,1024]{1,0:T(8,128)(2,1)S(1)} %get-tuple-element.26.v0), channel_id=1, source_target_pairs={{0,64},{32,96},{64,0},{96,32},{1,65},{33,97},{65,1},{97,33},{2,66}... | collective-permute-start | bytes 786440 | tf_op jit(solution)/shard_map/ppermute | solution.py:18
  99.4 3.0 %collective-permute-done.19.v1 = bf16[128,1024]{1,0:T(8,128)(2,1)S(1)} collective-permute-done((bf16[128,1024]{1,0:T(8,128)(2,1)S(1)}, bf16[128,1024]{1,0:T(8,128)(2,1)S(1)}, u32[]{:S(2)}, u32[]{:S(2)}) %collective-permute-start.19) | collective-permute-done | bytes 262176 | tf_op jit(solution)/shard_map/ppermute | solution.py:18
  102.4 4.5 %collective-permute-done.20.v2 = bf16[128,1024]{1,0:T(8,128)(2,1)S(1)} collective-permute-done((bf16[128,1024]{1,0:T(8,128)(2,1)S(1)}, bf16[128,1024]{1,0:T(8,128)(2,1)S(1)}, u32[]{:S(2)}, u32[]{:S(2)}) %collective-permute-start.20) | collective-permute-done | bytes 262176 | tf_op jit(solution)/shard_map/ppermute | solution.py:18
  109.8 2.8 %collective-permute-start.23 = (bf16[128,1024]{1,0:T(8,128)(2,1)S(1)}, bf16[128,1024]{1,0:T(8,128)(2,1)S(1)}, u32[]{:S(2)}, u32[]{:S(2)}) collective-permute-start(bf16[128,1024]{1,0:T(8,128)(2,1)S(1)} %diag_step.2.refs_0_), channel_id=1, source_target_pairs={{0,8},{4,12},{8,0},{12,4},{1,9},{5,13},{9,1},{13,5},{2,10},{6,14},... | collective-permute-start | bytes 786440 | tf_op jit(solution)/shard_map/ppermute | solution.py:18
  113.7 3.7 %lower_step.7 = (f32[128,1024]{1,0:T(8,128)S(1)}, bf16[128,1024]{1,0:T(8,128)(2,1)}) custom-call(bf16[128,1024]{1,0:T(8,128)(2,1)S(1)} %get-tuple-element.27.refs_0_.x3, f32[128,1024]{1,0:T(8,128)S(1)} %get-tuple-element.48.refs_1_, bf16[2,4,1536,256]{3,2,1,0:T(8,128)(2,1)} %bitcast.82), custom_call_target="tpu_custom_call" | custom-call | flops 268435456 | bytes 4194304 | tf_op jit(solution)/shard_map/lower_step/pallas_call | solution.py:124
  119.3 3.2 %lower_step.8 = (bf16[128,1024]{1,0:T(8,128)(2,1)S(1)}, bf16[128,1024]{1,0:T(8,128)(2,1)S(1)}) custom-call(bf16[128,1024]{1,0:T(8,128)(2,1)S(1)} %diag_step.2.refs_0_, bf16[128,1024]{1,0:T(8,128)(2,1)S(1)} %collective-permute-done.22.refs_1_, bf16[128,1024]{1,0:T(8,128)(2,1)S(1)} %collective-permute-done.23.refs_2_, ...), custom_call_target="tpu_custom_call" | custom-call | flops 268435456 | bytes 4194304 | tf_op jit(solution)/shard_map/lower_step/pallas_call | solution.py:124
  125.3 7.4 %collective-permute-start = (s32[128]{0:T(128)S(1)}, s32[128]{0:T(128)S(1)}, u32[]{:S(2)}, u32[]{:S(2)}) collective-permute-start(s32[128]{0:T(128)S(1)} %bitcast.93), channel_id=1, source_target_pairs={{0,16},{16,0},{1,17},{17,1},{2,18},{18,2},{3,19},{19,3},{4,20},{20... | collective-permute-start | bytes 1544 | tf_op jit(solution)/shard_map/ppermute | solution.py:22
  132.8 3.1 %diag_step.3.refs_0_ = bf16[128,1024]{1,0:T(8,128)(2,1)S(1)} custom-call(bf16[128,1024]{1,0:T(8,128)(2,1)S(1)} %get-tuple-element.29.v0, bf16[128,1024]{1,0:T(8,128)(2,1)S(1)} %collective-permute-done.25.v1, bf16[128,1024]{1,0:T(8,128)(2,1)S(1)} %collective-permute-done.26.v2, bf16[128,1024]{1,0:T(8,128)(2,1)S(1)} %collective-permute-done.27.v3, ...), custom_call_target="tpu_custom_call" | custom-call | flops 268435456 | bytes 4194304 | tf_op jit(solution)/shard_map/diag_step/pallas_call | solution.py:157
  141.4 4.9 %all-gather.13.cloned.1.call-done = bf16[12288,256]{1,0:T(8,128)(2,1)} async-done(((bf16[1536,256]{1,0:T(8,128)(2,1)}), bf16[12288,256]{1,0:T(8,128)(2,1)}) %all-gather.13.cloned.1.call-update) | async-done | bytes 6291472 | tf_op jit(solution)/shard_map/all_gather | solution.py:312
  146.3 3.7 %lower_step.9 = (f32[128,1024]{1,0:T(8,128)S(1)}, bf16[128,1024]{1,0:T(8,128)(2,1)}) custom-call(bf16[128,1024]{1,0:T(8,128)(2,1)S(1)} %get-tuple-element.27.refs_0_.x3, f32[128,1024]{1,0:T(8,128)S(1)} %get-tuple-element.47.refs_1_, bf16[2,4,1536,256]{3,2,1,0:T(8,128)(2,1)} %bitcast.79), custom_call_target="tpu_custom_call" | custom-call | flops 268435456 | bytes 4194304 | tf_op jit(solution)/shard_map/lower_step/pallas_call | solution.py:124
  150.0 3.7 %lower_step.10 = (f32[128,1024]{1,0:T(8,128)S(1)}, bf16[128,1024]{1,0:T(8,128)(2,1)}) custom-call(bf16[128,1024]{1,0:T(8,128)(2,1)S(1)} %get-tuple-element.30.refs_0_.x2, f32[128,1024]{1,0:T(8,128)S(1)} %get-tuple-element.31.refs_1_, bf16[2,4,1536,256]{3,2,1,0:T(8,128)(2,1)} %bitcast.80), custom_call_target="tpu_custom_call" | custom-call | flops 268435456 | bytes 4194304 | tf_op jit(solution)/shard_map/lower_step/pallas_call | solution.py:124
  153.9 3.2 %lower_step.11 = (bf16[128,1024]{1,0:T(8,128)(2,1)S(1)}, bf16[128,1024]{1,0:T(8,128)(2,1)S(1)}) custom-call(bf16[128,1024]{1,0:T(8,128)(2,1)S(1)} %diag_step.3.refs_0_, bf16[128,1024]{1,0:T(8,128)(2,1)S(1)} %collective-permute-done.28.refs_1_, bf16[128,1024]{1,0:T(8,128)(2,1)S(1)} %collective-permute-done.29.refs_2_, ...), custom_call_target="tpu_custom_call" | custom-call | flops 268435456 | bytes 4194304 | tf_op jit(solution)/shard_map/lower_step/pallas_call | solution.py:124
  158.5 2.6 %collective-permute-start.32 = (bf16[128,1024]{1,0:T(8,128)(2,1)S(1)}, bf16[128,1024]{1,0:T(8,128)(2,1)S(1)}, u32[]{:S(2)}, u32[]{:S(2)}) collective-permute-start(bf16[128,1024]{1,0:T(8,128)(2,1)S(1)} %get-tuple-element.33.v0), channel_id=1, source_target_pairs={{0,64},{32,96},{64,0},{96,32},{1,65},{33,97},{65,1},{97,33},{2,66}... | collective-permute-start | bytes 786440 | tf_op jit(solution)/shard_map/ppermute | solution.py:18
  162.7 10.5 %all-gather.15.cloned.1.call-done = bf16[4096,256]{1,0:T(8,128)(2,1)} async-done(((bf16[512,256]{1,0:T(8,128)(2,1)}), bf16[4096,256]{1,0:T(8,128)(2,1)}) %all-gather.15.cloned.1.call-update) | async-done | bytes 2097168 | tf_op jit(solution)/shard_map/all_gather | solution.py:312
  178.0 2.5 %collective-permute-start.35 = (bf16[128,256]{1,0:T(8,128)(2,1)S(1)}, bf16[128,256]{1,0:T(8,128)(2,1)S(1)}, u32[]{:S(2)}, u32[]{:S(2)}) collective-permute-start(bf16[128,256]{1,0:T(8,128)(2,1)S(1)} %get-tuple-element.36), channel_id=1, source_target_pairs={{0,8},{4,12},{8,0},{12,4},{1,9},{5,13},{9,1},{13,5},{2,10},{6,14},... | collective-permute-start | bytes 196616 | tf_op jit(solution)/shard_map/ppermute | solution.py:18
  181.8 3.0 %pack_known.1.base_ref = bf16[2048,128]{1,0:T(8,128)(2,1)S(1)} custom-call(s32[4]{0:T(128)S(1)} %pad_add_fusion.place.place_ref, s32[4,1,256]{2,1,0:T(1,128)S(1)} %reshape.115.target_ref, bf16[128,1024]{1,0:T(8,128)(2,1)S(1)} %get-tuple-element.38.x1, bf16[128,1024]{1,0:T(8,128)(2,1)S(1)} %get-tuple-element.30.refs_0_.x2, ...), custom_call_target="tpu_custom_call" | custom-call | flops 402653184 | bytes 2097152 | tf_op jit(solution)/shard_map/pack_known/pallas_call | solution.py:231
  186.4 22.6 %all_to_all.5 = bf16[128,16,128]{2,1,0:T(8,128)(2,1)S(1)} all-to-all(bf16[128,16,128]{2,1,0:T(8,128)(2,1)S(1)} %bitcast.78), channel_id=1, replica_groups=mesh['z'=4,'core'=2,'y'=4,'x'=4] {'z','core','y','x'}, dimensions={0} | all-to-all | bytes 1048576 | tf_op jit(solution)/shard_map/all_to_all | solution.py:367
  (116 shorter events, 48.7 us)
Async XLA Ops:
  6.5 83.8 %all-gather.9.cloned.1.call-start = ((), (), s32[]{:S(2)}) async-start(), calls=%async_computation.1 | async-start | bytes 4718592 | tf_op jit(solution)/shard_map/all_gather | solution.py:312
  9.6 104.0 %all-gather.11.cloned.1.call-start = ((), (), s32[]{:S(2)}) async-start(), calls=%async_computation.2 | async-start | bytes 7077888 | tf_op jit(solution)/shard_map/all_gather | solution.py:312
  11.7 134.6 %all-gather.13.cloned.1.call-start = ((), (), s32[]{:S(2)}) async-start(), calls=%async_computation.3 | async-start | bytes 7077888 | tf_op jit(solution)/shard_map/all_gather | solution.py:312
  12.7 160.5 %all-gather.15.cloned.1.call-start = ((), (), s32[]{:S(2)}) async-start(), calls=%async_computation.4 | async-start | bytes 2359296 | tf_op jit(solution)/shard_map/all_gather | solution.py:312
  21.6 11.5 %collective-permute-start.4 = (bf16[256,512]{1,0:T(8,128)(2,1)S(1)}, bf16[256,512]{1,0:T(8,128)(2,1)S(1)}, u32[]{:S(2)}, u32[]{:S(2)}) collective-permute-start(bf16[256,512]{1,0:T(8,128)(2,1)S(1)} %constant_dynamic-slice_fusion.5), channel_id=1, source_target_pairs={{0,16},{16,0},{1,17},{17,1},{2,18},{18,2},{3,19},{19,3},{4,20},{20... | collective-permute-start | bytes 786440 | tf_op jit(solution)/shard_map/ppermute | solution.py:22
  31.9 22.7 %collective-permute-start.15 = (bf16[3,256,512]{2,1,0:T(8,128)(2,1)S(1)}, bf16[3,256,512]{2,1,0:T(8,128)(2,1)S(1)}, u32[]{:S(2)}, u32[]{:S(2)}) collective-permute-start(bf16[3,256,512]{2,1,0:T(8,128)(2,1)S(1)} %constant_dynamic-slice_fusion.4), channel_id=1, source_target_pairs={{0,16},{16,0},{1,17},{17,1},{2,18},{18,2},{3,19},{19,3},{4,20},{20... | collective-permute-start | bytes 2359304 | tf_op jit(solution)/shard_map/ppermute | solution.py:22
  33.2 10.2 %collective-permute-start.5 = (bf16[256,512]{1,0:T(8,128)(2,1)S(1)}, bf16[256,512]{1,0:T(8,128)(2,1)S(1)}, u32[]{:S(2)}, u32[]{:S(2)}) collective-permute-start(bf16[256,512]{1,0:T(8,128)(2,1)S(1)} %add_convert_fusion.2.v0), channel_id=1, source_target_pairs={{0,32},{32,64},{64,96},{96,0},{1,33},{33,65},{65,97},{97,1},{2,34}... | collective-permute-start | bytes 786440 | tf_op jit(solution)/shard_map/ppermute | solution.py:18
  34.9 14.8 %collective-permute-start.6 = (bf16[256,512]{1,0:T(8,128)(2,1)S(1)}, bf16[256,512]{1,0:T(8,128)(2,1)S(1)}, u32[]{:S(2)}, u32[]{:S(2)}) collective-permute-start(bf16[256,512]{1,0:T(8,128)(2,1)S(1)} %add_convert_fusion.2.v0), channel_id=1, source_target_pairs={{0,64},{32,96},{64,0},{96,32},{1,65},{33,97},{65,1},{97,33},{2,66}... | collective-permute-start | bytes 786440 | tf_op jit(solution)/shard_map/ppermute | solution.py:18
  38.2 11.5 %collective-permute-start.7 = (bf16[256,512]{1,0:T(8,128)(2,1)S(1)}, bf16[256,512]{1,0:T(8,128)(2,1)S(1)}, u32[]{:S(2)}, u32[]{:S(2)}) collective-permute-start(bf16[256,512]{1,0:T(8,128)(2,1)S(1)} %add_convert_fusion.2.v0), channel_id=1, source_target_pairs={{0,96},{32,0},{64,32},{96,64},{1,97},{33,1},{65,33},{97,65},{2,98}... | collective-permute-start | bytes 786440 | tf_op jit(solution)/shard_map/ppermute | solution.py:18
  53.5 9.8 %collective-permute-start.10 = (bf16[128,1024]{1,0:T(8,128)(2,1)S(1)}, bf16[128,1024]{1,0:T(8,128)(2,1)S(1)}, u32[]{:S(2)}, u32[]{:S(2)}) collective-permute-start(bf16[128,1024]{1,0:T(8,128)(2,1)S(1)} %get-tuple-element.24), channel_id=1, source_target_pairs={{0,2},{1,3},{2,0},{3,1},{4,6},{5,7},{6,4},{7,5},{8,10},{9,11},{10,... | collective-permute-start | bytes 786440 | tf_op jit(solution)/shard_map/ppermute | solution.py:18
  54.0 20.4 %collective-permute-start.9 = (bf16[128,1024]{1,0:T(8,128)(2,1)S(1)}, bf16[128,1024]{1,0:T(8,128)(2,1)S(1)}, u32[]{:S(2)}, u32[]{:S(2)}) collective-permute-start(bf16[128,1024]{1,0:T(8,128)(2,1)S(1)} %get-tuple-element.23), channel_id=1, source_target_pairs={{0,1},{1,2},{2,3},{3,0},{4,5},{5,6},{6,7},{7,4},{8,9},{9,10},{10,1... | collective-permute-start | bytes 786440 | tf_op jit(solution)/shard_map/ppermute | solution.py:18
  55.1 28.3 %collective-permute-start.16 = (bf16[3,256,128]{2,1,0:T(8,128)(2,1)S(1)}, bf16[3,256,128]{2,1,0:T(8,128)(2,1)S(1)}, u32[]{:S(2)}, u32[]{:S(2)}) collective-permute-start(bf16[3,256,128]{2,1,0:T(8,128)(2,1)S(1)} %get-tuple-element.56), channel_id=1, source_target_pairs={{0,1},{1,2},{2,3},{3,0},{4,5},{5,6},{6,7},{7,4},{8,9},{9,10},{10,1... | collective-permute-start | bytes 589832 | tf_op jit(solution)/shard_map/ppermute | solution.py:18
  56.7 32.6 %collective-permute-start.17 = (bf16[3,256,128]{2,1,0:T(8,128)(2,1)S(1)}, bf16[3,256,128]{2,1,0:T(8,128)(2,1)S(1)}, u32[]{:S(2)}, u32[]{:S(2)}) collective-permute-start(bf16[3,256,128]{2,1,0:T(8,128)(2,1)S(1)} %get-tuple-element.55), channel_id=1, source_target_pairs={{0,2},{1,3},{2,0},{3,1},{4,6},{5,7},{6,4},{7,5},{8,10},{9,11},{10,... | collective-permute-start | bytes 589832 | tf_op jit(solution)/shard_map/ppermute | solution.py:18
  58.9 30.4 %collective-permute-start.18 = (bf16[3,256,128]{2,1,0:T(8,128)(2,1)S(1)}, bf16[3,256,128]{2,1,0:T(8,128)(2,1)S(1)}, u32[]{:S(2)}, u32[]{:S(2)}) collective-permute-start(bf16[3,256,128]{2,1,0:T(8,128)(2,1)S(1)} %get-tuple-element.54), channel_id=1, source_target_pairs={{0,3},{1,0},{2,1},{3,2},{4,7},{5,4},{6,5},{7,6},{8,11},{9,8},{10,9... | collective-permute-start | bytes 589832 | tf_op jit(solution)/shard_map/ppermute | solution.py:18
  74.6 15.7 %collective-permute-start.12 = (bf16[128,1024]{1,0:T(8,128)(2,1)S(1)}, bf16[128,1024]{1,0:T(8,128)(2,1)S(1)}, u32[]{:S(2)}, u32[]{:S(2)}) collective-permute-start(bf16[128,1024]{1,0:T(8,128)(2,1)S(1)} %add_convert_fusion.1.refs_0_), channel_id=1, source_target_pairs={{0,4},{4,8},{8,12},{12,0},{1,5},{5,9},{9,13},{13,1},{2,6},{6,10},{... | collective-permute-start | bytes 786440 | tf_op jit(solution)/shard_map/ppermute | solution.py:18
  75.9 14.3 %collective-permute-start.13 = (bf16[128,1024]{1,0:T(8,128)(2,1)S(1)}, bf16[128,1024]{1,0:T(8,128)(2,1)S(1)}, u32[]{:S(2)}, u32[]{:S(2)}) collective-permute-start(bf16[128,1024]{1,0:T(8,128)(2,1)S(1)} %add_convert_fusion.1.refs_0_), channel_id=1, source_target_pairs={{0,8},{4,12},{8,0},{12,4},{1,9},{5,13},{9,1},{13,5},{2,10},{6,14},... | collective-permute-start | bytes 786440 | tf_op jit(solution)/shard_map/ppermute | solution.py:18
  93.7 8.7 %collective-permute-start.19 = (bf16[128,1024]{1,0:T(8,128)(2,1)S(1)}, bf16[128,1024]{1,0:T(8,128)(2,1)S(1)}, u32[]{:S(2)}, u32[]{:S(2)}) collective-permute-start(bf16[128,1024]{1,0:T(8,128)(2,1)S(1)} %get-tuple-element.26.v0), channel_id=1, source_target_pairs={{0,32},{32,64},{64,96},{96,0},{1,33},{33,65},{65,97},{97,1},{2,34}... | collective-permute-start | bytes 786440 | tf_op jit(solution)/shard_map/ppermute | solution.py:18
  96.2 10.6 %collective-permute-start.20 = (bf16[128,1024]{1,0:T(8,128)(2,1)S(1)}, bf16[128,1024]{1,0:T(8,128)(2,1)S(1)}, u32[]{:S(2)}, u32[]{:S(2)}) collective-permute-start(bf16[128,1024]{1,0:T(8,128)(2,1)S(1)} %get-tuple-element.26.v0), channel_id=1, source_target_pairs={{0,64},{32,96},{64,0},{96,32},{1,65},{33,97},{65,1},{97,33},{2,66}... | collective-permute-start | bytes 786440 | tf_op jit(solution)/shard_map/ppermute | solution.py:18
  108.3 9.1 %collective-permute-start.22 = (bf16[128,1024]{1,0:T(8,128)(2,1)S(1)}, bf16[128,1024]{1,0:T(8,128)(2,1)S(1)}, u32[]{:S(2)}, u32[]{:S(2)}) collective-permute-start(bf16[128,1024]{1,0:T(8,128)(2,1)S(1)} %diag_step.2.refs_0_), channel_id=1, source_target_pairs={{0,4},{4,8},{8,12},{12,0},{1,5},{5,9},{9,13},{13,1},{2,6},{6,10},{... | collective-permute-start | bytes 786440 | tf_op jit(solution)/shard_map/ppermute | solution.py:18
  109.8 9.5 %collective-permute-start.23 = (bf16[128,1024]{1,0:T(8,128)(2,1)S(1)}, bf16[128,1024]{1,0:T(8,128)(2,1)S(1)}, u32[]{:S(2)}, u32[]{:S(2)}) collective-permute-start(bf16[128,1024]{1,0:T(8,128)(2,1)S(1)} %diag_step.2.refs_0_), channel_id=1, source_target_pairs={{0,8},{4,12},{8,0},{12,4},{1,9},{5,13},{9,1},{13,5},{2,10},{6,14},... | collective-permute-start | bytes 786440 | tf_op jit(solution)/shard_map/ppermute | solution.py:18
  122.5 10.2 %collective-permute-start.25 = (bf16[128,1024]{1,0:T(8,128)(2,1)S(1)}, bf16[128,1024]{1,0:T(8,128)(2,1)S(1)}, u32[]{:S(2)}, u32[]{:S(2)}) collective-permute-start(bf16[128,1024]{1,0:T(8,128)(2,1)S(1)} %get-tuple-element.29.v0), channel_id=1, source_target_pairs={{0,32},{32,64},{64,96},{96,0},{1,33},{33,65},{65,97},{97,1},{2,34}... | collective-permute-start | bytes 786440 | tf_op jit(solution)/shard_map/ppermute | solution.py:18
  122.6 10.1 %collective-permute-start.26 = (bf16[128,1024]{1,0:T(8,128)(2,1)S(1)}, bf16[128,1024]{1,0:T(8,128)(2,1)S(1)}, u32[]{:S(2)}, u32[]{:S(2)}) collective-permute-start(bf16[128,1024]{1,0:T(8,128)(2,1)S(1)} %get-tuple-element.29.v0), channel_id=1, source_target_pairs={{0,64},{32,96},{64,0},{96,32},{1,65},{33,97},{65,1},{97,33},{2,66}... | collective-permute-start | bytes 786440 | tf_op jit(solution)/shard_map/ppermute | solution.py:18
  125.3 15.4 %collective-permute-start = (s32[128]{0:T(128)S(1)}, s32[128]{0:T(128)S(1)}, u32[]{:S(2)}, u32[]{:S(2)}) collective-permute-start(s32[128]{0:T(128)S(1)} %bitcast.93), channel_id=1, source_target_pairs={{0,16},{16,0},{1,17},{17,1},{2,18},{18,2},{3,19},{19,3},{4,20},{20... | collective-permute-start | bytes 1544 | tf_op jit(solution)/shard_map/ppermute | solution.py:22
  135.9 17.7 %collective-permute-start.28 = (bf16[128,1024]{1,0:T(8,128)(2,1)S(1)}, bf16[128,1024]{1,0:T(8,128)(2,1)S(1)}, u32[]{:S(2)}, u32[]{:S(2)}) collective-permute-start(bf16[128,1024]{1,0:T(8,128)(2,1)S(1)} %diag_step.3.refs_0_), channel_id=1, source_target_pairs={{0,4},{4,8},{8,12},{12,0},{1,5},{5,9},{9,13},{13,1},{2,6},{6,10},{... | collective-permute-start | bytes 786440 | tf_op jit(solution)/shard_map/ppermute | solution.py:18
  137.3 16.7 %collective-permute-start.29 = (bf16[128,1024]{1,0:T(8,128)(2,1)S(1)}, bf16[128,1024]{1,0:T(8,128)(2,1)S(1)}, u32[]{:S(2)}, u32[]{:S(2)}) collective-permute-start(bf16[128,1024]{1,0:T(8,128)(2,1)S(1)} %diag_step.3.refs_0_), channel_id=1, source_target_pairs={{0,8},{4,12},{8,0},{12,4},{1,9},{5,13},{9,1},{13,5},{2,10},{6,14},... | collective-permute-start | bytes 786440 | tf_op jit(solution)/shard_map/ppermute | solution.py:18
  139.1 14.8 %collective-permute-start.30 = (bf16[128,1024]{1,0:T(8,128)(2,1)S(1)}, bf16[128,1024]{1,0:T(8,128)(2,1)S(1)}, u32[]{:S(2)}, u32[]{:S(2)}) collective-permute-start(bf16[128,1024]{1,0:T(8,128)(2,1)S(1)} %diag_step.3.refs_0_), channel_id=1, source_target_pairs={{0,12},{4,0},{8,4},{12,8},{1,13},{5,1},{9,5},{13,9},{2,14},{6,2},{... | collective-permute-start | bytes 786440 | tf_op jit(solution)/shard_map/ppermute | solution.py:18
  140.6 20.4 %collective-permute-start.1 = (s32[2,128]{1,0:T(2,128)S(1)}, s32[2,128]{1,0:T(2,128)S(1)}, u32[]{:S(2)}, u32[]{:S(2)}) collective-permute-start(s32[2,128]{1,0:T(2,128)S(1)} %add_select_fusion), channel_id=1, source_target_pairs={{0,3},{1,0},{2,1},{3,2},{4,7},{5,4},{6,5},{7,6},{8,11},{9,8},{10,9... | collective-permute-start | bytes 3080 | tf_op jit(solution)/shard_map/ppermute | solution.py:18
  140.7 21.4 %collective-permute-start.2 = (s32[2,128]{1,0:T(2,128)S(1)}, s32[2,128]{1,0:T(2,128)S(1)}, u32[]{:S(2)}, u32[]{:S(2)}) collective-permute-start(s32[2,128]{1,0:T(2,128)S(1)} %add_select_fusion), channel_id=1, source_target_pairs={{0,2},{1,3},{2,0},{3,1},{4,6},{5,7},{6,4},{7,5},{8,10},{9,11},{10,... | collective-permute-start | bytes 3080 | tf_op jit(solution)/shard_map/ppermute | solution.py:18
  153.6 8.5 %collective-permute-start.3 = (s32[2,128]{1,0:T(2,128)S(1)}, s32[2,128]{1,0:T(2,128)S(1)}, u32[]{:S(2)}, u32[]{:S(2)}) collective-permute-start(s32[2,128]{1,0:T(2,128)S(1)} %add_select_fusion), channel_id=1, source_target_pairs={{0,1},{1,2},{2,3},{3,0},{4,5},{5,6},{6,7},{7,4},{8,9},{9,10},{10,1... | collective-permute-start | bytes 3080 | tf_op jit(solution)/shard_map/ppermute | solution.py:18
  157.1 16.1 %collective-permute-start.31 = (bf16[128,1024]{1,0:T(8,128)(2,1)S(1)}, bf16[128,1024]{1,0:T(8,128)(2,1)S(1)}, u32[]{:S(2)}, u32[]{:S(2)}) collective-permute-start(bf16[128,1024]{1,0:T(8,128)(2,1)S(1)} %get-tuple-element.33.v0), channel_id=1, source_target_pairs={{0,32},{32,64},{64,96},{96,0},{1,33},{33,65},{65,97},{97,1},{2,34}... | collective-permute-start | bytes 786440 | tf_op jit(solution)/shard_map/ppermute | solution.py:18
  158.5 14.7 %collective-permute-start.32 = (bf16[128,1024]{1,0:T(8,128)(2,1)S(1)}, bf16[128,1024]{1,0:T(8,128)(2,1)S(1)}, u32[]{:S(2)}, u32[]{:S(2)}) collective-permute-start(bf16[128,1024]{1,0:T(8,128)(2,1)S(1)} %get-tuple-element.33.v0), channel_id=1, source_target_pairs={{0,64},{32,96},{64,0},{96,32},{1,65},{33,97},{65,1},{97,33},{2,66}... | collective-permute-start | bytes 786440 | tf_op jit(solution)/shard_map/ppermute | solution.py:18
  161.1 12.1 %collective-permute-start.33 = (bf16[128,1024]{1,0:T(8,128)(2,1)S(1)}, bf16[128,1024]{1,0:T(8,128)(2,1)S(1)}, u32[]{:S(2)}, u32[]{:S(2)}) collective-permute-start(bf16[128,1024]{1,0:T(8,128)(2,1)S(1)} %get-tuple-element.33.v0), channel_id=1, source_target_pairs={{0,96},{32,0},{64,32},{96,64},{1,97},{33,1},{65,33},{97,65},{2,98}... | collective-permute-start | bytes 786440 | tf_op jit(solution)/shard_map/ppermute | solution.py:18
  (17 other events, 115.5 us)
Sparse Core Ops, SparseCore 0:
  9.8 35.6 all-gather.8
  47.2 57.3 all-gather.10
  106.3 39.9 all-gather.12
  147.9 25.2 all-gather.14

commit v2 on v1

v2 whole, which is shorter than its diff:
```python
import jax
import jax.numpy as jnp
from jax import lax
from jax.experimental import pallas as pl
from jax.experimental.pallas import tpu as pltpu
from jax.sharding import Mesh, PartitionSpec as P

BF16 = jnp.bfloat16
F32 = jnp.float32
VMEM_LIMIT = 48 * 1024 * 1024


def pair_slot(later, earlier):
    return later * (later - 1) // 2 + earlier


def shift(value, axis, by):
    return lax.ppermute(value, axis, [(i, (i + by) % 4) for i in range(4)])


def swap(value):
    return lax.ppermute(value, "core", [(0, 1), (1, 0)])


def spread(value, axis):
    far = shift(value, axis, 2)
    right = shift(value, axis, 1)
    left = shift(value, axis, 3)
    return (value, right, far, left)


def deal(pieces, axis):
    far = shift(pieces[2], axis, 2)
    right = shift(pieces[1], axis, 1)
    left = shift(pieces[3], axis, 3)
    return (pieces[0], right, far, left)


def add_up(refs):
    total = refs[0][...].astype(F32)
    for ref in refs[1:]:
        total = total + ref[...].astype(F32)
    return total


def params(**extra):
    return pltpu.CompilerParams(vmem_limit_bytes=VMEM_LIMIT, **extra)


def cost(flops, moved):
    return pl.CostEstimate(flops=flops, bytes_accessed=moved, transcendentals=0)


def whole(shape):
    return pl.BlockSpec(shape, lambda *_: (0,) * len(shape))


SCALARS = pl.BlockSpec(memory_space=pltpu.SMEM)
VMEM = pl.BlockSpec(memory_space=pltpu.VMEM)


def turn(place, pieces, dtype):
    blocks = pieces[0].shape[0]

    def kernel(place_ref, v0, v1, v2, v3, out):
        for step, ref in enumerate((v0, v1, v2, v3)):
            start = lax.rem(place_ref[2] + 4 - step, 4) * 256
            lanes = pl.ds(pl.multiple_of(start, 256), 256)
            for k in range(blocks):
                out[k, :, lanes] = ref[k].astype(F32).T.astype(dtype)

    return pl.pallas_call(
        kernel,
        out_shape=jax.ShapeDtypeStruct((blocks, 128, 1024), dtype),
        in_specs=[SCALARS] + [VMEM] * 4,
        out_specs=VMEM,
        compiler_params=params(),
        cost_estimate=cost(blocks * 128 * 1024, blocks << 20),
        name="turn",
    )(place, *pieces)


def lower_step(base, pieces, tiles, at, dtype):
    count = len(pieces)

    def kernel(*refs):
        parts = refs[:count]
        base_ref, tiles_ref, out, kept, tile, sems = refs[count:]
        copies = [
            pltpu.make_async_copy(
                tiles_ref.at[:, i, pl.ds(at * 512, 512), :], tile.at[:, i], sems.at[i]
            )
            for i in range(4)
        ]
        for copy in copies:
            copy.start()
        kept[...] = add_up(parts).astype(BF16)
        for i, copy in enumerate(copies):
            lanes = slice(i * 256, (i + 1) * 256)
            copy.wait()
            total = base_ref[:, lanes].astype(F32)
            total = total - jnp.dot(kept[:, :512], tile[0, i], preferred_element_type=F32)
            total = total - jnp.dot(kept[:, 512:], tile[1, i], preferred_element_type=F32)
            out[:, lanes] = total.astype(dtype)

    return pl.pallas_call(
        kernel,
        out_shape=(
            jax.ShapeDtypeStruct((128, 1024), dtype),
            jax.ShapeDtypeStruct((128, 1024), BF16),
        ),
        in_specs=[VMEM] * count + [VMEM, pl.BlockSpec(memory_space=pltpu.HBM)],
        out_specs=(VMEM, VMEM),
        scratch_shapes=[
            pltpu.VMEM((2, 4, 512, 256), BF16),
            pltpu.SemaphoreType.DMA((4,)),
        ],
        compiler_params=params(),
        cost_estimate=cost(2 * 128 * 1024 * 1024, 4 << 20),
        name="lower_step",
    )(*pieces, base, tiles)


def times_diag(place_ref, vec, tiles, out):
    core, x = place_ref[0], place_ref[2]
    for side, group in ((core, tiles[:4]), (1 - core, tiles[4:])):
        total = None
        for step, tile in enumerate(group):
            start = lax.rem(x + 4 - step, 4) * 256
            left = vec[:, pl.ds(pl.multiple_of(start, 256), 256)]
            term = jnp.dot(left, tile[...], preferred_element_type=F32)
            total = term if total is None else total + term
        out[:, pl.ds(pl.multiple_of(side * 512, 512), 512)] = total.astype(BF16)


def diag_step(place, pieces, tiles):
    def kernel(place_ref, *refs):
        out, vec = refs[12:]
        vec[...] = add_up(refs[:4]).astype(BF16)
        times_diag(place_ref, vec, refs[4:12], out)

    return pl.pallas_call(
        kernel,
        out_shape=jax.ShapeDtypeStruct((128, 1024), BF16),
        in_specs=[SCALARS] + [VMEM] * 12,
        out_specs=VMEM,
        scratch_shapes=[pltpu.VMEM((128, 1024), BF16)],
        compiler_params=params(),
        cost_estimate=cost(2 * 128 * 1024 * 1024, 4 << 20),
        name="diag_step",
    )(place, *pieces, *tiles)


def last_step(place, pieces, tiles):
    def kernel(place_ref, *refs):
        vec, full = refs[16:]
        vec[...] = add_up(refs[:4]).astype(BF16)
        times_diag(place_ref, vec, refs[4:12], full)
        for by, out in enumerate(refs[12:16]):
            start = lax.rem(place_ref[1] + by, 4) * 128
            out[:, :128] = full[:, pl.ds(pl.multiple_of(start, 128), 128)]
            out[:, 128:] = full[:, pl.ds(pl.multiple_of(start + 512, 128), 128)]

    return pl.pallas_call(
        kernel,
        out_shape=(jax.ShapeDtypeStruct((128, 256), BF16),) * 4,
        in_specs=[SCALARS] + [VMEM] * 12,
        out_specs=(VMEM,) * 4,
        scratch_shapes=[pltpu.VMEM((128, 1024), BF16), pltpu.VMEM((128, 1024), BF16)],
        compiler_params=params(),
        cost_estimate=cost(2 * 128 * 1024 * 1024, 4 << 20),
        name="last_step",
    )(place, *pieces, *tiles)


def chosen(target, block):
    slots = lax.broadcasted_iota(jnp.int32, (256, 256), 0) + block * 256
    return jnp.where(slots == target, 1.0, 0.0).astype(BF16)


def picked(select, rows):
    return lax.dot_general(
        select, rows, (((1,), (1,)), ((), ())), preferred_element_type=F32
    )


def pack_known(place, target, known):
    def kernel(place_ref, target_ref, x1, x2, x3, out, still):
        block = pl.program_id(0)
        start = pl.multiple_of(place_ref[1] * 128, 128)
        again = pl.multiple_of(place_ref[1] * 128 + 512, 128)
        total = jnp.zeros((256, 128), F32)
        for k, ref in ((1, x1), (2, x2), (3, x3)):
            rows = jnp.concatenate([ref[:, pl.ds(start, 128)], ref[:, pl.ds(again, 128)]], axis=1)
            total = total + picked(chosen(target_ref[k], block), rows)
        out[...] = total.astype(BF16)
        still[...] = chosen(target_ref[0], block)

    return pl.pallas_call(
        kernel,
        grid=(8,),
        out_shape=(
            jax.ShapeDtypeStruct((2048, 128), BF16),
            jax.ShapeDtypeStruct((2048, 256), BF16),
        ),
        in_specs=[SCALARS, whole((4, 1, 256))] + [whole((128, 1024))] * 3,
        out_specs=(
            pl.BlockSpec((256, 128), lambda i: (i, 0)),
            pl.BlockSpec((256, 256), lambda i: (i, 0)),
        ),
        compiler_params=params(),
        cost_estimate=cost(2 * 2048 * 768 * 128, 2 << 20),
        name="pack_known",
    )(place, target, *known)


def pack_last(still, pieces, base):
    def kernel(still_ref, v0, v1, v2, v3, base_ref, out):
        rows = add_up((v0, v1, v2, v3)).astype(BF16)
        out[...] = (base_ref[...].astype(F32) + picked(still_ref[...], rows)).astype(BF16)

    return pl.pallas_call(
        kernel,
        out_shape=jax.ShapeDtypeStruct((2048, 128), BF16),
        in_specs=[VMEM] * 6,
        out_specs=VMEM,
        compiler_params=params(),
        cost_estimate=cost(2 * 2048 * 256 * 128, 2 << 20),
        name="pack_last",
    )(still, *pieces, base)


def unpack(received):
    def kernel(got, out):
        for core in range(2):
            for y in range(4):
                for x in range(4):
                    tile = got[0, core, y, x].astype(F32)
                    lanes = pl.ds((core * 4 + x) * 128, 128)
                    for half in range(2):
                        out[pl.ds(half * 32 + y * 8, 8), lanes] = tile[half * 8 : half * 8 + 8]

    return pl.pallas_call(
        kernel,
        grid=(4,),
        out_shape=jax.ShapeDtypeStruct((256, 1024), F32),
        in_specs=[pl.BlockSpec((1, 2, 4, 4, 16, 128), lambda i: (i, 0, 0, 0, 0, 0))],
        out_specs=pl.BlockSpec((64, 1024), lambda i: (i, 0)),
        compiler_params=params(),
        cost_estimate=cost(256 * 1024, 2 << 20),
        name="unpack",
    )(received.reshape(4, 2, 4, 4, 16, 128))


def slots_of(owners, core, x):
    pair = swap(owners)
    both = jnp.where(core == 0, jnp.stack([owners, pair]), jnp.stack([pair, owners]))
    around = [both] + [shift(both, "x", -by) for by in (1, 2, 3)]
    twice = jnp.stack(around + around)
    ordered = lax.dynamic_slice_in_dim(twice, lax.rem(4 - x, 4), 4, axis=0)
    named = ordered.transpose(1, 0, 2).reshape(8, 128)
    same = named[:, :, None] == named[:, None, :]
    earlier = jnp.arange(128)[None, :, None] > jnp.arange(128)[None, None, :]
    ranks = jnp.sum((same & earlier).astype(jnp.int32), axis=2)
    target = named * 16 + jnp.arange(8, dtype=jnp.int32)[:, None] * 2 + ranks
    return target.reshape(8, 4, 32).transpose(1, 0, 2).reshape(4, 1, 256)


def gathered(parts):
    rows = sum(part.shape[0] for part in parts)
    joined = jnp.concatenate(parts, axis=0) if len(parts) > 1 else parts[0]
    return lax.all_gather(joined, ("core", "x"), axis=0, tiled=False).reshape(2, 4, rows, 256)


def after(value, event):
    return value + (event[0, 0] * 0).astype(value.dtype)


def collected(tile):
    around = spread(tile, "x")
    return around + tuple(swap(piece) for piece in around)


def local(pivot_rhs, bound_sol, border_tiles, lower_tiles, inverse_diag, owner_map):
    z, core, y, x = (lax.axis_index(name) for name in ("z", "core", "y", "x"))
    place = jnp.stack([core, y, x, z]).astype(jnp.int32)
    lead = jnp.where((z == 0) & (core == 0), 1.0, 0.0).astype(F32)

    def lower(j, k):
        return lower_tiles[pair_slot(j, k)]

    early = gathered([lower(3, 2)])
    middle = gathered([lower(3, 1), lower(2, 1)])
    late = gathered([lower(3, 0), lower(2, 0), lower(1, 0)])

    flat = lax.optimization_barrier(border_tiles.reshape(border_tiles.shape[0], -1))

    def border(tiles):
        return lax.dot_general(
            tiles, bound_sol, (((0,), (0,)), ((), ())), preferred_element_type=F32
        )

    def paired(part):
        axis = part.ndim - 1
        away = lax.dynamic_slice_in_dim(part, (1 - core) * 512, 512, axis=axis)
        home = lax.dynamic_slice_in_dim(part, core * 512, 512, axis=axis)
        return (home + swap(away)).astype(BF16)

    def dealt(part):
        cut = [
            lax.dynamic_slice_in_dim(part, lax.rem(x + by, 4) * 128, 128, axis=2)
            for by in range(4)
        ]
        return deal(cut, "x")

    top = lead * pivot_rhs[3] - border(flat[:, 768:])
    top = paired(top[None])
    tiles3 = collected(after(inverse_diag[3], top[0]))
    residual = turn(place, dealt(top), BF16)[0]
    over_z = spread(residual, "z")
    rest = border(after(flat[:, :768], residual)).reshape(3, 256, 1024)
    base = turn(place, dealt(paired(lead * pivot_rhs[:3] - rest)), F32)
    pieces = spread(diag_step(place, over_z, tiles3), "y")
    tiles2 = collected(after(inverse_diag[2], pieces[0]))
    residual, x3 = lower_step(base[2], pieces, early, 0, BF16)
    over_z = spread(residual, "z")
    target = slots_of(owner_map[0, :, 0], core, x)
    pieces = spread(diag_step(place, over_z, tiles2), "y")
    base1, _ = lower_step(base[1], (x3,), middle, 0, F32)
    tiles1 = collected(after(inverse_diag[1], pieces[0]))
    residual, x2 = lower_step(base1, pieces, middle, 1, BF16)
    over_z = spread(residual, "z")
    pieces = spread(diag_step(place, over_z, tiles1), "y")
    base0, _ = lower_step(base[0], (x3,), late, 0, F32)
    base0, _ = lower_step(base0, (x2,), late, 1, F32)
    tiles0 = collected(after(inverse_diag[0], pieces[0]))
    residual, x1 = lower_step(base0, pieces, late, 2, BF16)
    over_z = spread(residual, "z")
    packed, still = pack_known(place, target, (x1, x2, x3))
    rows = deal(last_step(place, over_z, tiles0), "y")
    packed = pack_last(still, rows, packed).reshape(128, 16, 128)
    received = lax.all_to_all(
        packed, ("z", "core", "y", "x"), split_axis=0, concat_axis=0, tiled=True
    )
    return unpack(received)


def solution(mesh):
    fine = Mesh(mesh.devices.reshape(4, 2, 4, 4), ("z", "core", "y", "x"))
    rows, cols = ("z", "core"), ("y", "x")
    placed = (
        P(None, cols, None),
        P(rows, None),
        P(rows, None, cols),
        P(None, rows, cols),
        P(None, cols, rows),
        P(rows + cols, None, None),
    )
    return jax.shard_map(
        local, mesh=fine, in_specs=placed, out_specs=P(rows + cols, None), check_vma=False
    )
```

time: 218 us -> 288 us (1.32)
  starting transfers between devices: 62.7 us -> 105 us
  waiting for transfers between devices: 55.5 us -> 84.6 us
  Pallas kernels: 35.3 us -> 25.2 us
  local copies, waits for them, and re-layouts: 11.3 us -> 17.1 us
  between operations: 13.5 us -> 16.9 us
    ppermute x33 -> x45, waiting for transfers between devices: 40 us -> 82.1 us  [shift(): return lax.ppermute(value, axis, [(i, (i + by) % 4) for i in range(4)])]
    ppermute x4 -> x19, starting transfers between devices: 9.3 us -> 48.4 us  [swap(): return lax.ppermute(value, 'core', [(0, 1), (1, 0)])]
    all_gather x4 -> x3, waiting for transfers between devices: 15.4 us -> 0.02 us  [gathered(): lax.all_gather(joined, ('core', 'x'), axis=0, tiled=False)]
    pallas_call x13 -> x14, Pallas kernels: 33.7 us -> 23.7 us  [the longest x6 12.9 us: lower_step(): pl.pallas_call(kernel, out_shape=(jax.ShapeDtypeStruct((128, 1024), dtype...]
    unnamed x16 -> x23, local copies, waits for them, and re-layouts: 3.25 us -> 11.4 us
    ppermute x33 -> x45, starting transfers between devices: 53.2 us -> 56 us  [shift(): return lax.ppermute(value, axis, [(i, (i + by) % 4) for i in range(4)])]
  transfers between devices with their start and end apart: 41 -> 67, of which waited for: 12 -> 22; matrix products, arithmetic and copies ran while one was open for 10% -> 9% of each run, Pallas kernels for 14% -> 7%
where the time goes in v2:
time: 288 us; the launch traced here: 287 us
  starting transfers between devices  105 us (36%)
  waiting for transfers between devices  84.6 us (29%)
  Pallas kernels  25.2 us (9%)
  blocking collectives  22.8 us (8%)
  local copies, waits for them, and re-layouts  17.1 us (6%)
  between operations  16.9 us (6%)
  matrix products  10.5 us (4%)
  other arithmetic  5.72 us (2%)
    ppermute x45, waiting for transfers between devices, shift(): return lax.ppermute(value, axis, [(i, (i + by) % 4) for i in range(4)])  82.1 us
    ppermute x45, starting transfers between devices, shift(): return lax.ppermute(value, axis, [(i, (i + by) % 4) for i in range(4)])  56 us
    ppermute x19, starting transfers between devices, swap(): return lax.ppermute(value, 'core', [(0, 1), (1, 0)])  48.4 us
    all_to_all x1, blocking collectives, local(): lax.all_to_all(packed, ('z', 'core', 'y', 'x'), split_axis=0, concat_axis...  22.8 us
    pallas_call x6, Pallas kernels, lower_step(): pl.pallas_call(kernel, out_shape=(jax.ShapeDtypeStruct((128, 1024), dtype...  12.9 us
    unnamed x23, local copies, waits for them, and re-layouts  11.4 us
    dot_general x2, matrix products, border(): lax.dot_general(tiles, bound_sol, (((0,), (0,)), ((), ())), preferred_ele...  10.5 us
  transfers between devices with their start and end apart: 67, of which 22 were waited for; matrix products, arithmetic and copies ran while one was open for 9% of the time, Pallas kernels for 7%

profile of v2, /device:TPU:1, one launch (start us, length us, event | category | flops | bytes accessed | tf_op | source)
XLA Modules:
  0.0 287.4 jit_solution(18323329529485047810)
XLA Ops:
  10.7 5.2 %copy.25 = bf16[256,8,4,256]{3,1,2,0:T(8,128)(2,1)} copy(bf16[256,8,4,256]{3,2,1,0:T(4,128)(2,1)} %bitcast.92) | data formatting | bytes 8388608
  15.9 4.1 %convolution_subtract_fusion = f32[256,1024]{1,0:T(8,128)S(1)} fusion(bf16[2048,1024]{1,0:T(8,128)(2,1)} %param.7, bf16[2048,1024]{1,0:T(8,128)(2,1)} %bitcast.93, f32[4,256,1024]{2,1,0:T(8,128)} %param.6, f32[]{:T(128)S(6)} %select_n.55), kind=kOutput, calls=%fused_computation.5 | convolution fusion | flops 1074266112 | bytes 7340036 | tf_op jit(solution)/shard_map/dot_general | solution.py:299
  29.6 4.0 %collective-permute-done.6.v2 = bf16[1,256,128]{2,1,0:T(8,128)(2,1)S(1)} collective-permute-done((bf16[1,256,128]{2,1,0:T(8,128)(2,1)S(1)}, bf16[1,256,128]{2,1,0:T(8,128)(2,1)S(1)}, u32[]{:S(2)}, u32[]{:S(2)}) %collective-permute-start.6) | collective-permute-done | bytes 65568 | tf_op jit(solution)/shard_map/ppermute | solution.py:18
  35.5 6.4 %fusion = f32[768,1024]{1,0:T(8,128)S(1)} fusion(bf16[2048,1024]{1,0:T(8,128)(2,1)} %param.7, bf16[2048,1024]{1,0:T(8,128)(2,1)} %bitcast.94, bf16[]{:T(256)} %bitcast.31), kind=kOutput, calls=%fused_computation.1 | convolution fusion | flops 3222798336 | bytes 10486272 | tf_op jit(solution)/shard_map/dot_general | solution.py:299
  45.7 2.7 collective-permute-start.12
  50.8 4.0 %collective-permute-done.11.refs_5_ = bf16[256,512]{1,0:T(8,128)(2,1)S(1)} collective-permute-done((bf16[256,512]{1,0:T(8,128)(2,1)S(1)}, bf16[256,512]{1,0:T(8,128)(2,1)S(1)}, u32[]{:S(2)}, u32[]{:S(2)}) %collective-permute-start.11) | collective-permute-done | bytes 262176 | tf_op jit(solution)/shard_map/ppermute | solution.py:18
  56.5 8.0 %collective-permute-done.12.refs_6_ = bf16[256,512]{1,0:T(8,128)(2,1)S(1)} collective-permute-done((bf16[256,512]{1,0:T(8,128)(2,1)S(1)}, bf16[256,512]{1,0:T(8,128)(2,1)S(1)}, u32[]{:S(2)}, u32[]{:S(2)}) %collective-permute-start.12) | collective-permute-done | bytes 262176 | tf_op jit(solution)/shard_map/ppermute | solution.py:18
  64.4 5.0 %collective-permute-start.9 = (bf16[128,1024]{1,0:T(8,128)(2,1)S(1)}, bf16[128,1024]{1,0:T(8,128)(2,1)S(1)}, u32[]{:S(2)}, u32[]{:S(2)}) collective-permute-start(bf16[128,1024]{1,0:T(8,128)(2,1)S(1)} %bitcast.86), channel_id=1, source_target_pairs={{0,64},{32,96},{64,0},{96,32},{1,65},{33,97},{65,1},{97,33},{2,66}... | collective-permute-start | bytes 786440 | tf_op jit(solution)/shard_map/ppermute | solution.py:18
  70.9 2.7 collective-permute-start.15
  76.7 5.1 %collective-permute-done.10.refs_3_ = bf16[128,1024]{1,0:T(8,128)(2,1)S(1)} collective-permute-done((bf16[128,1024]{1,0:T(8,128)(2,1)S(1)}, bf16[128,1024]{1,0:T(8,128)(2,1)S(1)}, u32[]{:S(2)}, u32[]{:S(2)}) %collective-permute-start.10) | collective-permute-done | bytes 262176 | tf_op jit(solution)/shard_map/ppermute | solution.py:18
  84.1 2.7 collective-permute-start.19
  88.9 3.8 %collective-permute-start.23 = (bf16[3,256,128]{2,1,0:T(8,128)(2,1)S(1)}, bf16[3,256,128]{2,1,0:T(8,128)(2,1)S(1)}, u32[]{:S(2)}, u32[]{:S(2)}) collective-permute-start(bf16[3,256,128]{2,1,0:T(8,128)(2,1)S(1)} %get-tuple-element.47), channel_id=1, source_target_pairs={{0,2},{1,3},{2,0},{3,1},{4,6},{5,7},{6,4},{7,5},{8,10},{9,11},{10,... | collective-permute-start | bytes 589832 | tf_op jit(solution)/shard_map/ppermute | solution.py:18
  94.5 13.3 %collective-permute-done.23.v2 = bf16[3,256,128]{2,1,0:T(8,128)(2,1)S(1)} collective-permute-done((bf16[3,256,128]{2,1,0:T(8,128)(2,1)S(1)}, bf16[3,256,128]{2,1,0:T(8,128)(2,1)S(1)}, u32[]{:S(2)}, u32[]{:S(2)}) %collective-permute-start.23) | collective-permute-done | bytes 196640 | tf_op jit(solution)/shard_map/ppermute | solution.py:18
  107.7 3.5 %collective-permute-start.29 = (bf16[256,512]{1,0:T(8,128)(2,1)S(1)}, bf16[256,512]{1,0:T(8,128)(2,1)}, u32[]{:S(2)}, u32[]{:S(2)}) collective-permute-start(bf16[256,512]{1,0:T(8,128)(2,1)S(1)} %add_bitcast_fusion.2.refs_4_), channel_id=1, source_target_pairs={{0,2},{1,3},{2,0},{3,1},{4,6},{5,7},{6,4},{7,5},{8,10},{9,11},{10,... | collective-permute-start | bytes 786440 | tf_op jit(solution)/shard_map/ppermute | solution.py:18
  112.1 9.4 %collective-permute-start.31 = (bf16[256,512]{1,0:T(8,128)(2,1)S(1)}, bf16[256,512]{1,0:T(8,128)(2,1)}, u32[]{:S(2)}, u32[]{:S(2)}) collective-permute-start(bf16[256,512]{1,0:T(8,128)(2,1)S(1)} %add_bitcast_fusion.2.refs_4_), channel_id=1, source_target_pairs={{0,16},{16,0},{1,17},{17,1},{2,18},{18,2},{3,19},{19,3},{4,20},{20... | collective-permute-start | bytes 786440 | tf_op jit(solution)/shard_map/ppermute | solution.py:22
  121.7 8.8 %collective-permute-start.33 = (bf16[256,512]{1,0:T(8,128)(2,1)}, bf16[256,512]{1,0:T(8,128)(2,1)}, u32[]{:S(2)}, u32[]{:S(2)}) collective-permute-start(bf16[256,512]{1,0:T(8,128)(2,1)} %collective-permute-done.29.refs_6_), channel_id=1, source_target_pairs={{0,16},{16,0},{1,17},{17,1},{2,18},{18,2},{3,19},{19,3},{4,20},{20... | collective-permute-start | bytes 786440 | tf_op jit(solution)/shard_map/ppermute | solution.py:22
  130.5 8.1 %collective-permute-start.34 = (bf16[256,512]{1,0:T(8,128)(2,1)}, bf16[256,512]{1,0:T(8,128)(2,1)}, u32[]{:S(2)}, u32[]{:S(2)}) collective-permute-start(bf16[256,512]{1,0:T(8,128)(2,1)} %collective-permute-done.30.refs_7_), channel_id=1, source_target_pairs={{0,16},{16,0},{1,17},{17,1},{2,18},{18,2},{3,19},{19,3},{4,20},{20... | collective-permute-start | bytes 786440 | tf_op jit(solution)/shard_map/ppermute | solution.py:22
  144.4 6.8 %collective-permute-done.25.refs_1_ = bf16[128,1024]{1,0:T(8,128)(2,1)S(1)} collective-permute-done((bf16[128,1024]{1,0:T(8,128)(2,1)S(1)}, bf16[128,1024]{1,0:T(8,128)(2,1)S(1)}, u32[]{:S(2)}, u32[]{:S(2)}) %collective-permute-start.25) | collective-permute-done | bytes 262176 | tf_op jit(solution)/shard_map/ppermute | solution.py:18
  151.2 4.8 %collective-permute-done.26.refs_2_ = bf16[128,1024]{1,0:T(8,128)(2,1)S(1)} collective-permute-done((bf16[128,1024]{1,0:T(8,128)(2,1)S(1)}, bf16[128,1024]{1,0:T(8,128)(2,1)S(1)}, u32[]{:S(2)}, u32[]{:S(2)}) %collective-permute-start.26) | collective-permute-done | bytes 262176 | tf_op jit(solution)/shard_map/ppermute | solution.py:18
  167.4 4.0 %collective-permute-done.36.refs_2_ = bf16[128,1024]{1,0:T(8,128)(2,1)S(1)} collective-permute-done((bf16[128,1024]{1,0:T(8,128)(2,1)S(1)}, bf16[128,1024]{1,0:T(8,128)(2,1)S(1)}, u32[]{:S(2)}, u32[]{:S(2)}) %collective-permute-start.36) | collective-permute-done | bytes 262176 | tf_op jit(solution)/shard_map/ppermute | solution.py:18
  172.1 2.8 collective-permute-start.44
  175.0 3.5 %collective-permute-start.45 = (bf16[256,512]{1,0:T(8,128)(2,1)S(1)}, bf16[256,512]{1,0:T(8,128)(2,1)S(1)}, u32[]{:S(2)}, u32[]{:S(2)}) collective-permute-start(bf16[256,512]{1,0:T(8,128)(2,1)S(1)} %collective-permute-done.41.refs_5_), channel_id=1, source_target_pairs={{0,16},{16,0},{1,17},{17,1},{2,18},{18,2},{3,19},{19,3},{4,20},{20... | collective-permute-start | bytes 786440 | tf_op jit(solution)/shard_map/ppermute | solution.py:22
  183.9 3.0 %lower_step.8 = (bf16[128,1024]{1,0:T(8,128)(2,1)S(1)}, bf16[128,1024]{1,0:T(8,128)(2,1)S(1)}) custom-call(bf16[128,1024]{1,0:T(8,128)(2,1)S(1)} %diag_step.4.refs_0_, bf16[128,1024]{1,0:T(8,128)(2,1)S(1)} %copy-done.3, bf16[128,1024]{1,0:T(8,128)(2,1)S(1)} %copy-done.5, bf16[128,1024]{1,0:T(8,128)(2,1)} %collective-permute-done.37.refs_3_, ...), custom_call_target="tpu_custom_call" | custom-call | flops 268435456 | bytes 4194304 | tf_op jit(solution)/shard_map/lower_step/pallas_call | solution.py:106
  187.6 3.1 %collective-permute-start.39 = (bf16[128,1024]{1,0:T(8,128)(2,1)S(1)}, bf16[128,1024]{1,0:T(8,128)(2,1)S(1)}, u32[]{:S(2)}, u32[]{:S(2)}) collective-permute-start(bf16[128,1024]{1,0:T(8,128)(2,1)S(1)} %get-tuple-element.23.refs_0_), channel_id=1, source_target_pairs={{0,64},{32,96},{64,0},{96,32},{1,65},{33,97},{65,1},{97,33},{2,66}... | collective-permute-start | bytes 786440 | tf_op jit(solution)/shard_map/ppermute | solution.py:18
  190.7 5.3 %collective-permute-done.38.refs_1_ = bf16[128,1024]{1,0:T(8,128)(2,1)S(1)} collective-permute-done((bf16[128,1024]{1,0:T(8,128)(2,1)S(1)}, bf16[128,1024]{1,0:T(8,128)(2,1)S(1)}, u32[]{:S(2)}, u32[]{:S(2)}) %collective-permute-start.38) | collective-permute-done | bytes 262176 | tf_op jit(solution)/shard_map/ppermute | solution.py:18
  196.0 6.7 %collective-permute-done.39.refs_2_ = bf16[128,1024]{1,0:T(8,128)(2,1)S(1)} collective-permute-done((bf16[128,1024]{1,0:T(8,128)(2,1)S(1)}, bf16[128,1024]{1,0:T(8,128)(2,1)S(1)}, u32[]{:S(2)}, u32[]{:S(2)}) %collective-permute-start.39) | collective-permute-done | bytes 262176 | tf_op jit(solution)/shard_map/ppermute | solution.py:18
  210.6 2.9 collective-permute-start.1
  232.3 3.1 %collective-permute-start.52 = (bf16[128,1024]{1,0:T(8,128)(2,1)S(1)}, bf16[128,1024]{1,0:T(8,128)(2,1)S(1)}, u32[]{:S(2)}, u32[]{:S(2)}) collective-permute-start(bf16[128,1024]{1,0:T(8,128)(2,1)S(1)} %get-tuple-element.29.refs_0_), channel_id=1, source_target_pairs={{0,64},{32,96},{64,0},{96,32},{1,65},{33,97},{65,1},{97,33},{2,66}... | collective-permute-start | bytes 786440 | tf_op jit(solution)/shard_map/ppermute | solution.py:18
  236.1 5.4 %collective-permute-done.51.refs_1_ = bf16[128,1024]{1,0:T(8,128)(2,1)S(1)} collective-permute-done((bf16[128,1024]{1,0:T(8,128)(2,1)S(1)}, bf16[128,1024]{1,0:T(8,128)(2,1)S(1)}, u32[]{:S(2)}, u32[]{:S(2)}) %collective-permute-start.51) | collective-permute-done | bytes 262176 | tf_op jit(solution)/shard_map/ppermute | solution.py:18
  241.5 6.0 %collective-permute-done.52.refs_2_ = bf16[128,1024]{1,0:T(8,128)(2,1)S(1)} collective-permute-done((bf16[128,1024]{1,0:T(8,128)(2,1)S(1)}, bf16[128,1024]{1,0:T(8,128)(2,1)S(1)}, u32[]{:S(2)}, u32[]{:S(2)}) %collective-permute-start.52) | collective-permute-done | bytes 262176 | tf_op jit(solution)/shard_map/ppermute | solution.py:18
  253.1 3.0 %pack_known.1 = (bf16[2048,128]{1,0:T(8,128)(2,1)S(1)}, bf16[2048,256]{1,0:T(8,128)(2,1)S(1)}) custom-call(s32[4]{0:T(128)S(1)} %pad_add_fusion.place_ref, s32[4,1,256]{2,1,0:T(1,128)S(1)} %reshape.138.target_ref, bf16[128,1024]{1,0:T(8,128)(2,1)S(1)} %copy-done.7, bf16[128,1024]{1,0:T(8,128)(2,1)S(1)} %get-tuple-element.24.refs_0_.x2, ...), custom_call_target="tpu_custom_call" | custom-call | flops 402653184 | bytes 2097152 | tf_op jit(solution)/shard_map/pack_known/pallas_call | solution.py:199
  256.6 22.8 %all_to_all.5 = bf16[128,16,128]{2,1,0:T(8,128)(2,1)S(1)} all-to-all(bf16[128,16,128]{2,1,0:T(8,128)(2,1)S(1)} %bitcast.83), channel_id=1, replica_groups=mesh['z'=4,'core'=2,'y'=4,'x'=4] {'z','core','y','x'}, dimensions={0} | all-to-all | bytes 1048576 | tf_op jit(solution)/shard_map/all_to_all | solution.py:342
  (179 shorter events, 90.5 us)
Async XLA Ops:
  6.5 132.2 %all-gather.6.cloned.1.call-start = ((), (), s32[]{:S(2)}) async-start(), calls=%async_computation.1 | async-start | bytes 2359296 | tf_op jit(solution)/shard_map/all_gather | solution.py:272
  8.7 169.8 %all-gather.8.cloned.1.call-start = ((), (), s32[]{:S(2)}) async-start(), calls=%async_computation.2 | async-start | bytes 4718592 | tf_op jit(solution)/shard_map/all_gather | solution.py:272
  9.7 211.3 %all-gather.10.cloned.1.call-start = ((), (), s32[]{:S(2)}) async-start(), calls=%async_computation.3 | async-start | bytes 7077888 | tf_op jit(solution)/shard_map/all_gather | solution.py:272
  43.1 45.0 %collective-permute-start.21 = (f32[3,256,512]{2,1,0:T(8,128)S(1)}, f32[3,256,512]{2,1,0:T(8,128)S(1)}, u32[]{:S(2)}, u32[]{:S(2)}) collective-permute-start(f32[3,256,512]{2,1,0:T(8,128)S(1)} %constant_dynamic-slice_fusion.4), channel_id=1, source_target_pairs={{0,16},{16,0},{1,17},{17,1},{2,18},{18,2},{3,19},{19,3},{4,20},{20... | collective-permute-start | bytes 4718600 | tf_op jit(solution)/shard_map/ppermute | solution.py:22
  45.7 18.7 %collective-permute-start.12 = (bf16[256,512]{1,0:T(8,128)(2,1)S(1)}, bf16[256,512]{1,0:T(8,128)(2,1)S(1)}, u32[]{:S(2)}, u32[]{:S(2)}) collective-permute-start(bf16[256,512]{1,0:T(8,128)(2,1)S(1)} %add_bitcast_fusion.3.refs_4_), channel_id=1, source_target_pairs={{0,2},{1,3},{2,0},{3,1},{4,6},{5,7},{6,4},{7,5},{8,10},{9,11},{10,... | collective-permute-start | bytes 786440 | tf_op jit(solution)/shard_map/ppermute | solution.py:18
  48.4 21.0 %collective-permute-start.13 = (bf16[256,512]{1,0:T(8,128)(2,1)S(1)}, bf16[256,512]{1,0:T(8,128)(2,1)S(1)}, u32[]{:S(2)}, u32[]{:S(2)}) collective-permute-start(bf16[256,512]{1,0:T(8,128)(2,1)S(1)} %add_bitcast_fusion.3.refs_4_), channel_id=1, source_target_pairs={{0,3},{1,0},{2,1},{3,2},{4,7},{5,4},{6,5},{7,6},{8,11},{9,8},{10,9... | collective-permute-start | bytes 786440 | tf_op jit(solution)/shard_map/ppermute | solution.py:18
  50.0 20.9 %collective-permute-start.14 = (bf16[256,512]{1,0:T(8,128)(2,1)S(1)}, bf16[256,512]{1,0:T(8,128)(2,1)S(1)}, u32[]{:S(2)}, u32[]{:S(2)}) collective-permute-start(bf16[256,512]{1,0:T(8,128)(2,1)S(1)} %add_bitcast_fusion.3.refs_4_), channel_id=1, source_target_pairs={{0,16},{16,0},{1,17},{17,1},{2,18},{18,2},{3,19},{19,3},{4,20},{20... | collective-permute-start | bytes 786440 | tf_op jit(solution)/shard_map/ppermute | solution.py:22
  54.8 18.7 %collective-permute-start.8 = (bf16[128,1024]{1,0:T(8,128)(2,1)S(1)}, bf16[128,1024]{1,0:T(8,128)(2,1)S(1)}, u32[]{:S(2)}, u32[]{:S(2)}) collective-permute-start(bf16[128,1024]{1,0:T(8,128)(2,1)S(1)} %bitcast.85), channel_id=1, source_target_pairs={{0,32},{32,64},{64,96},{96,0},{1,33},{33,65},{65,97},{97,1},{2,34}... | collective-permute-start | bytes 786440 | tf_op jit(solution)/shard_map/ppermute | solution.py:18
  82.8 29.2 %collective-permute-start.18 = (bf16[128,1024]{1,0:T(8,128)(2,1)S(1)}, bf16[128,1024]{1,0:T(8,128)(2,1)S(1)}, u32[]{:S(2)}, u32[]{:S(2)}) collective-permute-start(bf16[128,1024]{1,0:T(8,128)(2,1)S(1)} %diag_step.3.refs_0_), channel_id=1, source_target_pairs={{0,4},{4,8},{8,12},{12,0},{1,5},{5,9},{9,13},{13,1},{2,6},{6,10},{... | collective-permute-start | bytes 786440 | tf_op jit(solution)/shard_map/ppermute | solution.py:18
  84.1 28.0 %collective-permute-start.19 = (bf16[128,1024]{1,0:T(8,128)(2,1)S(1)}, bf16[128,1024]{1,0:T(8,128)(2,1)S(1)}, u32[]{:S(2)}, u32[]{:S(2)}) collective-permute-start(bf16[128,1024]{1,0:T(8,128)(2,1)S(1)} %diag_step.3.refs_0_), channel_id=1, source_target_pairs={{0,8},{4,12},{8,0},{12,4},{1,9},{5,13},{9,1},{13,5},{2,10},{6,14},... | collective-permute-start | bytes 786440 | tf_op jit(solution)/shard_map/ppermute | solution.py:18
  88.8 32.7 %collective-permute-start.28 = (bf16[256,512]{1,0:T(8,128)(2,1)S(1)}, bf16[256,512]{1,0:T(8,128)(2,1)S(1)}, u32[]{:S(2)}, u32[]{:S(2)}) collective-permute-start(bf16[256,512]{1,0:T(8,128)(2,1)S(1)} %add_bitcast_fusion.2.refs_4_), channel_id=1, source_target_pairs={{0,1},{1,2},{2,3},{3,0},{4,5},{5,6},{6,7},{7,4},{8,9},{9,10},{10,1... | collective-permute-start | bytes 786440 | tf_op jit(solution)/shard_map/ppermute | solution.py:18
  88.9 18.9 %collective-permute-start.23 = (bf16[3,256,128]{2,1,0:T(8,128)(2,1)S(1)}, bf16[3,256,128]{2,1,0:T(8,128)(2,1)S(1)}, u32[]{:S(2)}, u32[]{:S(2)}) collective-permute-start(bf16[3,256,128]{2,1,0:T(8,128)(2,1)S(1)} %get-tuple-element.47), channel_id=1, source_target_pairs={{0,2},{1,3},{2,0},{3,1},{4,6},{5,7},{6,4},{7,5},{8,10},{9,11},{10,... | collective-permute-start | bytes 589832 | tf_op jit(solution)/shard_map/ppermute | solution.py:18
  94.5 13.3 %collective-permute-start.24 = (bf16[3,256,128]{2,1,0:T(8,128)(2,1)S(1)}, bf16[3,256,128]{2,1,0:T(8,128)(2,1)S(1)}, u32[]{:S(2)}, u32[]{:S(2)}) collective-permute-start(bf16[3,256,128]{2,1,0:T(8,128)(2,1)S(1)} %get-tuple-element.46), channel_id=1, source_target_pairs={{0,3},{1,0},{2,1},{3,2},{4,7},{5,4},{6,5},{7,6},{8,11},{9,8},{10,9... | collective-permute-start | bytes 589832 | tf_op jit(solution)/shard_map/ppermute | solution.py:18
  107.7 30.9 %collective-permute-start.20 = (bf16[128,1024]{1,0:T(8,128)(2,1)S(1)}, bf16[128,1024]{1,0:T(8,128)(2,1)S(1)}, u32[]{:S(2)}, u32[]{:S(2)}) collective-permute-start(bf16[128,1024]{1,0:T(8,128)(2,1)S(1)} %diag_step.3.refs_0_), channel_id=1, source_target_pairs={{0,12},{4,0},{8,4},{12,8},{1,13},{5,1},{9,5},{13,9},{2,14},{6,2},{... | collective-permute-start | bytes 786440 | tf_op jit(solution)/shard_map/ppermute | solution.py:18
  107.7 14.0 %collective-permute-start.29 = (bf16[256,512]{1,0:T(8,128)(2,1)S(1)}, bf16[256,512]{1,0:T(8,128)(2,1)}, u32[]{:S(2)}, u32[]{:S(2)}) collective-permute-start(bf16[256,512]{1,0:T(8,128)(2,1)S(1)} %add_bitcast_fusion.2.refs_4_), channel_id=1, source_target_pairs={{0,2},{1,3},{2,0},{3,1},{4,6},{5,7},{6,4},{7,5},{8,10},{9,11},{10,... | collective-permute-start | bytes 786440 | tf_op jit(solution)/shard_map/ppermute | solution.py:18
  112.0 18.5 %collective-permute-start.30 = (bf16[256,512]{1,0:T(8,128)(2,1)S(1)}, bf16[256,512]{1,0:T(8,128)(2,1)}, u32[]{:S(2)}, u32[]{:S(2)}) collective-permute-start(bf16[256,512]{1,0:T(8,128)(2,1)S(1)} %add_bitcast_fusion.2.refs_4_), channel_id=1, source_target_pairs={{0,3},{1,0},{2,1},{3,2},{4,7},{5,4},{6,5},{7,6},{8,11},{9,8},{10,9... | collective-permute-start | bytes 786440 | tf_op jit(solution)/shard_map/ppermute | solution.py:18
  112.1 29.5 %collective-permute-start.31 = (bf16[256,512]{1,0:T(8,128)(2,1)S(1)}, bf16[256,512]{1,0:T(8,128)(2,1)}, u32[]{:S(2)}, u32[]{:S(2)}) collective-permute-start(bf16[256,512]{1,0:T(8,128)(2,1)S(1)} %add_bitcast_fusion.2.refs_4_), channel_id=1, source_target_pairs={{0,16},{16,0},{1,17},{17,1},{2,18},{18,2},{3,19},{19,3},{4,20},{20... | collective-permute-start | bytes 786440 | tf_op jit(solution)/shard_map/ppermute | solution.py:22
  121.5 22.4 %collective-permute-start.32 = (bf16[256,512]{1,0:T(8,128)(2,1)S(1)}, bf16[256,512]{1,0:T(8,128)(2,1)}, u32[]{:S(2)}, u32[]{:S(2)}) collective-permute-start(bf16[256,512]{1,0:T(8,128)(2,1)S(1)} %collective-permute-done.28.refs_5_), channel_id=1, source_target_pairs={{0,16},{16,0},{1,17},{17,1},{2,18},{18,2},{3,19},{19,3},{4,20},{20... | collective-permute-start | bytes 786440 | tf_op jit(solution)/shard_map/ppermute | solution.py:22
  121.7 22.7 %collective-permute-start.33 = (bf16[256,512]{1,0:T(8,128)(2,1)}, bf16[256,512]{1,0:T(8,128)(2,1)}, u32[]{:S(2)}, u32[]{:S(2)}) collective-permute-start(bf16[256,512]{1,0:T(8,128)(2,1)} %collective-permute-done.29.refs_6_), channel_id=1, source_target_pairs={{0,16},{16,0},{1,17},{17,1},{2,18},{18,2},{3,19},{19,3},{4,20},{20... | collective-permute-start | bytes 786440 | tf_op jit(solution)/shard_map/ppermute | solution.py:22
  130.5 13.8 %collective-permute-start.34 = (bf16[256,512]{1,0:T(8,128)(2,1)}, bf16[256,512]{1,0:T(8,128)(2,1)}, u32[]{:S(2)}, u32[]{:S(2)}) collective-permute-start(bf16[256,512]{1,0:T(8,128)(2,1)} %collective-permute-done.30.refs_7_), channel_id=1, source_target_pairs={{0,16},{16,0},{1,17},{17,1},{2,18},{18,2},{3,19},{19,3},{4,20},{20... | collective-permute-start | bytes 786440 | tf_op jit(solution)/shard_map/ppermute | solution.py:22
  141.6 14.3 %collective-permute-start.26 = (bf16[128,1024]{1,0:T(8,128)(2,1)S(1)}, bf16[128,1024]{1,0:T(8,128)(2,1)S(1)}, u32[]{:S(2)}, u32[]{:S(2)}) collective-permute-start(bf16[128,1024]{1,0:T(8,128)(2,1)S(1)} %get-tuple-element.20.refs_0_), channel_id=1, source_target_pairs={{0,64},{32,96},{64,0},{96,32},{1,65},{33,97},{65,1},{97,33},{2,66}... | collective-permute-start | bytes 786440 | tf_op jit(solution)/shard_map/ppermute | solution.py:18
  162.9 19.4 %collective-permute-start.42 = (bf16[256,512]{1,0:T(8,128)(2,1)S(1)}, bf16[256,512]{1,0:T(8,128)(2,1)S(1)}, u32[]{:S(2)}, u32[]{:S(2)}) collective-permute-start(bf16[256,512]{1,0:T(8,128)(2,1)S(1)} %add_bitcast_fusion.1.refs_4_), channel_id=1, source_target_pairs={{0,2},{1,3},{2,0},{3,1},{4,6},{5,7},{6,4},{7,5},{8,10},{9,11},{10,... | collective-permute-start | bytes 786440 | tf_op jit(solution)/shard_map/ppermute | solution.py:18
  164.0 18.4 %collective-permute-start.43 = (bf16[256,512]{1,0:T(8,128)(2,1)S(1)}, bf16[256,512]{1,0:T(8,128)(2,1)S(1)}, u32[]{:S(2)}, u32[]{:S(2)}) collective-permute-start(bf16[256,512]{1,0:T(8,128)(2,1)S(1)} %add_bitcast_fusion.1.refs_4_), channel_id=1, source_target_pairs={{0,3},{1,0},{2,1},{3,2},{4,7},{5,4},{6,5},{7,6},{8,11},{9,8},{10,9... | collective-permute-start | bytes 786440 | tf_op jit(solution)/shard_map/ppermute | solution.py:18
  167.4 15.5 %collective-permute-start.37 = (bf16[128,1024]{1,0:T(8,128)(2,1)S(1)}, bf16[128,1024]{1,0:T(8,128)(2,1)}, u32[]{:S(2)}, u32[]{:S(2)}) collective-permute-start(bf16[128,1024]{1,0:T(8,128)(2,1)S(1)} %diag_step.4.refs_0_), channel_id=1, source_target_pairs={{0,12},{4,0},{8,4},{12,8},{1,13},{5,1},{9,5},{13,9},{2,14},{6,2},{... | collective-permute-start | bytes 786440 | tf_op jit(solution)/shard_map/ppermute | solution.py:18
  172.1 15.4 %collective-permute-start.44 = (bf16[256,512]{1,0:T(8,128)(2,1)S(1)}, bf16[256,512]{1,0:T(8,128)(2,1)S(1)}, u32[]{:S(2)}, u32[]{:S(2)}) collective-permute-start(bf16[256,512]{1,0:T(8,128)(2,1)S(1)} %add_bitcast_fusion.1.refs_4_), channel_id=1, source_target_pairs={{0,16},{16,0},{1,17},{17,1},{2,18},{18,2},{3,19},{19,3},{4,20},{20... | collective-permute-start | bytes 786440 | tf_op jit(solution)/shard_map/ppermute | solution.py:22
  175.0 15.7 %collective-permute-start.45 = (bf16[256,512]{1,0:T(8,128)(2,1)S(1)}, bf16[256,512]{1,0:T(8,128)(2,1)S(1)}, u32[]{:S(2)}, u32[]{:S(2)}) collective-permute-start(bf16[256,512]{1,0:T(8,128)(2,1)S(1)} %collective-permute-done.41.refs_5_), channel_id=1, source_target_pairs={{0,16},{16,0},{1,17},{17,1},{2,18},{18,2},{3,19},{19,3},{4,20},{20... | collective-permute-start | bytes 786440 | tf_op jit(solution)/shard_map/ppermute | solution.py:22
  187.6 15.1 %collective-permute-start.39 = (bf16[128,1024]{1,0:T(8,128)(2,1)S(1)}, bf16[128,1024]{1,0:T(8,128)(2,1)S(1)}, u32[]{:S(2)}, u32[]{:S(2)}) collective-permute-start(bf16[128,1024]{1,0:T(8,128)(2,1)S(1)} %get-tuple-element.23.refs_0_), channel_id=1, source_target_pairs={{0,64},{32,96},{64,0},{96,32},{1,65},{33,97},{65,1},{97,33},{2,66}... | collective-permute-start | bytes 786440 | tf_op jit(solution)/shard_map/ppermute | solution.py:18
  203.8 14.3 %collective-permute-start.48 = (bf16[128,1024]{1,0:T(8,128)(2,1)S(1)}, bf16[128,1024]{1,0:T(8,128)(2,1)S(1)}, u32[]{:S(2)}, u32[]{:S(2)}) collective-permute-start(bf16[128,1024]{1,0:T(8,128)(2,1)S(1)} %diag_step.5.refs_0_), channel_id=1, source_target_pairs={{0,4},{4,8},{8,12},{12,0},{1,5},{5,9},{9,13},{13,1},{2,6},{6,10},{... | collective-permute-start | bytes 786440 | tf_op jit(solution)/shard_map/ppermute | solution.py:18
  205.4 13.4 %collective-permute-start.49 = (bf16[128,1024]{1,0:T(8,128)(2,1)S(1)}, bf16[128,1024]{1,0:T(8,128)(2,1)S(1)}, u32[]{:S(2)}, u32[]{:S(2)}) collective-permute-start(bf16[128,1024]{1,0:T(8,128)(2,1)S(1)} %diag_step.5.refs_0_), channel_id=1, source_target_pairs={{0,8},{4,12},{8,0},{12,4},{1,9},{5,13},{9,1},{13,5},{2,10},{6,14},... | collective-permute-start | bytes 786440 | tf_op jit(solution)/shard_map/ppermute | solution.py:18
  218.8 13.5 %collective-permute-start.57 = (bf16[256,512]{1,0:T(8,128)(2,1)S(1)}, bf16[256,512]{1,0:T(8,128)(2,1)}, u32[]{:S(2)}, u32[]{:S(2)}) collective-permute-start(bf16[256,512]{1,0:T(8,128)(2,1)S(1)} %add_bitcast_fusion.refs_4_), channel_id=1, source_target_pairs={{0,16},{16,0},{1,17},{17,1},{2,18},{18,2},{3,19},{19,3},{4,20},{20... | collective-permute-start | bytes 786440 | tf_op jit(solution)/shard_map/ppermute | solution.py:22
  220.8 14.6 %collective-permute-start.58 = (bf16[256,512]{1,0:T(8,128)(2,1)S(1)}, bf16[256,512]{1,0:T(8,128)(2,1)}, u32[]{:S(2)}, u32[]{:S(2)}) collective-permute-start(bf16[256,512]{1,0:T(8,128)(2,1)S(1)} %collective-permute-done.54.refs_5_), channel_id=1, source_target_pairs={{0,16},{16,0},{1,17},{17,1},{2,18},{18,2},{3,19},{19,3},{4,20},{20... | collective-permute-start | bytes 786440 | tf_op jit(solution)/shard_map/ppermute | solution.py:22
  232.3 15.2 %collective-permute-start.52 = (bf16[128,1024]{1,0:T(8,128)(2,1)S(1)}, bf16[128,1024]{1,0:T(8,128)(2,1)S(1)}, u32[]{:S(2)}, u32[]{:S(2)}) collective-permute-start(bf16[128,1024]{1,0:T(8,128)(2,1)S(1)} %get-tuple-element.29.refs_0_), channel_id=1, source_target_pairs={{0,64},{32,96},{64,0},{96,32},{1,65},{33,97},{65,1},{97,33},{2,66}... | collective-permute-start | bytes 786440 | tf_op jit(solution)/shard_map/ppermute | solution.py:18
  (46 other events, 377.0 us)
Sparse Core Ops, SparseCore 0:
  9.1 30.4 all-gather.5
  41.3 38.6 all-gather.7
  81.8 59.1 all-gather.9

commit v3 on v2

--- a/solution.py
+++ b/solution.py
@@ -43,8 +43,8 @@
     return total
 
 
-def params(**extra):
-    return pltpu.CompilerParams(vmem_limit_bytes=VMEM_LIMIT, **extra)
+def params(limit=VMEM_LIMIT):
+    return pltpu.CompilerParams(vmem_limit_bytes=limit)
 
 
 def cost(flops, moved):
@@ -57,6 +57,7 @@
 
 SCALARS = pl.BlockSpec(memory_space=pltpu.SMEM)
 VMEM = pl.BlockSpec(memory_space=pltpu.VMEM)
+HBM = pl.BlockSpec(memory_space=pltpu.HBM)
 
 
 def turn(place, pieces, dtype):
@@ -109,7 +110,7 @@
             jax.ShapeDtypeStruct((128, 1024), dtype),
             jax.ShapeDtypeStruct((128, 1024), BF16),
         ),
-        in_specs=[VMEM] * count + [VMEM, pl.BlockSpec(memory_space=pltpu.HBM)],
+        in_specs=[VMEM] * count + [VMEM, HBM],
         out_specs=(VMEM, VMEM),
         scratch_shapes=[
             pltpu.VMEM((2, 4, 512, 256), BF16),
@@ -133,7 +134,7 @@
         out[:, pl.ds(pl.multiple_of(side * 512, 512), 512)] = total.astype(BF16)
 
 
-def diag_step(place, pieces, tiles):
+def diag_near(place, pieces, tiles):
     def kernel(place_ref, *refs):
         out, vec = refs[12:]
         vec[...] = add_up(refs[:4]).astype(BF16)
@@ -147,16 +148,67 @@
         scratch_shapes=[pltpu.VMEM((128, 1024), BF16)],
         compiler_params=params(),
         cost_estimate=cost(2 * 128 * 1024 * 1024, 4 << 20),
+        name="diag_near",
+    )(place, *pieces, *tiles)
+
+
+def fetch_diag(tiles_ref, at, tile, sems):
+    copies = [
+        pltpu.make_async_copy(
+            tiles_ref.at[side, :, pl.ds(at * 512, 512), :], tile.at[side], sems.at[side]
+        )
+        for side in range(2)
+    ]
+    for copy in copies:
+        copy.start()
+    return copies
+
+
+def times_fetched(copies, vec, tile, out):
+    for side, copy in enumerate(copies):
+        copy.wait()
+        for half in range(2):
+            rows = slice(half * 256, (half + 1) * 256)
+            total = None
+            for x in range(4):
+                left = vec[:, x * 256 : (x + 1) * 256]
+                term = jnp.dot(left, tile[side, x, rows], preferred_element_type=F32)
+                total = term if total is None else total + term
+            start = side * 512 + half * 256
+            out[:, start : start + 256] = total.astype(BF16)
+
+
+DIAG_SCRATCH = [
+    pltpu.VMEM((128, 1024), BF16),
+    pltpu.VMEM((2, 4, 512, 256), BF16),
+    pltpu.SemaphoreType.DMA((2,)),
+]
+
+
+def diag_step(pieces, tiles, at):
+    def kernel(v0, v1, v2, v3, tiles_ref, out, vec, tile, sems):
+        copies = fetch_diag(tiles_ref, at, tile, sems)
+        vec[...] = add_up((v0, v1, v2, v3)).astype(BF16)
+        times_fetched(copies, vec, tile, out)
+
+    return pl.pallas_call(
+        kernel,
+        out_shape=jax.ShapeDtypeStruct((128, 1024), BF16),
+        in_specs=[VMEM] * 4 + [HBM],
+        out_specs=VMEM,
+        scratch_shapes=DIAG_SCRATCH,
+        compiler_params=params(),
+        cost_estimate=cost(2 * 128 * 1024 * 1024, 4 << 20),
         name="diag_step",
-    )(place, *pieces, *tiles)
-
-
-def last_step(place, pieces, tiles):
-    def kernel(place_ref, *refs):
-        vec, full = refs[16:]
-        vec[...] = add_up(refs[:4]).astype(BF16)
-        times_diag(place_ref, vec, refs[4:12], full)
-        for by, out in enumerate(refs[12:16]):
+    )(*pieces, tiles)
+
+
+def last_step(place, pieces, tiles, at):
+    def kernel(place_ref, v0, v1, v2, v3, tiles_ref, o0, o1, o2, o3, vec, tile, sems, full):
+        copies = fetch_diag(tiles_ref, at, tile, sems)
+        vec[...] = add_up((v0, v1, v2, v3)).astype(BF16)
+        times_fetched(copies, vec, tile, full)
+        for by, out in enumerate((o0, o1, o2, o3)):
             start = lax.rem(place_ref[1] + by, 4) * 128
             out[:, :128] = full[:, pl.ds(pl.multiple_of(start, 128), 128)]
             out[:, 128:] = full[:, pl.ds(pl.multiple_of(start + 512, 128), 128)]
@@ -164,13 +216,55 @@
     return pl.pallas_call(
         kernel,
         out_shape=(jax.ShapeDtypeStruct((128, 256), BF16),) * 4,
-        in_specs=[SCALARS] + [VMEM] * 12,
+        in_specs=[SCALARS] + [VMEM] * 4 + [HBM],
         out_specs=(VMEM,) * 4,
-        scratch_shapes=[pltpu.VMEM((128, 1024), BF16), pltpu.VMEM((128, 1024), BF16)],
+        scratch_shapes=DIAG_SCRATCH + [pltpu.VMEM((128, 1024), BF16)],
         compiler_params=params(),
         cost_estimate=cost(2 * 128 * 1024 * 1024, 4 << 20),
         name="last_step",
-    )(place, *pieces, *tiles)
+    )(place, *pieces, tiles)
+
+
+def stage(lower_tiles, inverse_diag, order, owners, event):
+    rows = 512 * len(order) + (0 if owners is None else 16)
+    moves = []
+    for at, (kind, index) in enumerate(order):
+        if kind == "L":
+            moves.append((0, index, slice(None), at * 512, 512))
+        else:
+            moves.append((1, index, slice(0, 256), at * 512, 256))
+            moves.append((1, index, slice(256, 512), at * 512 + 256, 256))
+    extra = [value for value in (owners, event) if value is not None]
+
+    def kernel(lower_ref, diag_ref, *refs):
+        out, sems = refs[len(extra) :]
+        copies = [
+            pltpu.make_async_copy(
+                (lower_ref, diag_ref)[which].at[index, :, lanes],
+                out.at[pl.ds(start, height)],
+                sems.at[number],
+            )
+            for number, (which, index, lanes, start, height) in enumerate(moves)
+        ]
+        if owners is not None:
+            copies.append(
+                pltpu.make_async_copy(refs[0], out.at[pl.ds(rows - 16, 16)], sems.at[len(moves)])
+            )
+        for copy in copies:
+            copy.start()
+        for copy in copies:
+            copy.wait()
+
+    return pl.pallas_call(
+        kernel,
+        out_shape=jax.ShapeDtypeStruct((rows, 256), BF16),
+        in_specs=[HBM] * (2 + len(extra)),
+        out_specs=HBM,
+        scratch_shapes=[pltpu.SemaphoreType.DMA((len(moves) + 1,))],
+        compiler_params=params(60 * 1024 * 1024),
+        cost_estimate=cost(0, 2 * rows * 512),
+        name="stage",
+    )(lower_tiles, inverse_diag, *extra)
 
 
 def chosen(target, block):
@@ -252,13 +346,7 @@
     )(received.reshape(4, 2, 4, 4, 16, 128))
 
 
-def slots_of(owners, core, x):
-    pair = swap(owners)
-    both = jnp.where(core == 0, jnp.stack([owners, pair]), jnp.stack([pair, owners]))
-    around = [both] + [shift(both, "x", -by) for by in (1, 2, 3)]
-    twice = jnp.stack(around + around)
-    ordered = lax.dynamic_slice_in_dim(twice, lax.rem(4 - x, 4), 4, axis=0)
-    named = ordered.transpose(1, 0, 2).reshape(8, 128)
+def slots_of(named):
     same = named[:, :, None] == named[:, None, :]
     earlier = jnp.arange(128)[None, :, None] > jnp.arange(128)[None, None, :]
     ranks = jnp.sum((same & earlier).astype(jnp.int32), axis=2)
@@ -266,19 +354,13 @@
     return target.reshape(8, 4, 32).transpose(1, 0, 2).reshape(4, 1, 256)
 
 
-def gathered(parts):
-    rows = sum(part.shape[0] for part in parts)
-    joined = jnp.concatenate(parts, axis=0) if len(parts) > 1 else parts[0]
+def gathered(joined):
+    rows = joined.shape[0]
     return lax.all_gather(joined, ("core", "x"), axis=0, tiled=False).reshape(2, 4, rows, 256)
 
 
-def after(value, event):
-    return value + (event[0, 0] * 0).astype(value.dtype)
-
-
-def collected(tile):
-    around = spread(tile, "x")
-    return around + tuple(swap(piece) for piece in around)
+def nothing(*arrays):
+    return sum(array[0, 0] for array in arrays) * 0
 
 
 def local(pivot_rhs, bound_sol, border_tiles, lower_tiles, inverse_diag, owner_map):
@@ -286,58 +368,46 @@
     place = jnp.stack([core, y, x, z]).astype(jnp.int32)
     lead = jnp.where((z == 0) & (core == 0), 1.0, 0.0).astype(F32)
 
-    def lower(j, k):
-        return lower_tiles[pair_slot(j, k)]
-
-    early = gathered([lower(3, 2)])
-    middle = gathered([lower(3, 1), lower(2, 1)])
-    late = gathered([lower(3, 0), lower(2, 0), lower(1, 0)])
-
-    flat = lax.optimization_barrier(border_tiles.reshape(border_tiles.shape[0], -1))
-
-    def border(tiles):
-        return lax.dot_general(
-            tiles, bound_sol, (((0,), (0,)), ((), ())), preferred_element_type=F32
-        )
-
-    def paired(part):
-        axis = part.ndim - 1
-        away = lax.dynamic_slice_in_dim(part, (1 - core) * 512, 512, axis=axis)
-        home = lax.dynamic_slice_in_dim(part, core * 512, 512, axis=axis)
-        return (home + swap(away)).astype(BF16)
-
-    def dealt(part):
-        cut = [
-            lax.dynamic_slice_in_dim(part, lax.rem(x + by, 4) * 128, 128, axis=2)
-            for by in range(4)
-        ]
-        return deal(cut, "x")
-
-    top = lead * pivot_rhs[3] - border(flat[:, 768:])
-    top = paired(top[None])
-    tiles3 = collected(after(inverse_diag[3], top[0]))
-    residual = turn(place, dealt(top), BF16)[0]
-    over_z = spread(residual, "z")
-    rest = border(after(flat[:, :768], residual)).reshape(3, 256, 1024)
-    base = turn(place, dealt(paired(lead * pivot_rhs[:3] - rest)), F32)
-    pieces = spread(diag_step(place, over_z, tiles3), "y")
-    tiles2 = collected(after(inverse_diag[2], pieces[0]))
+    def tile(j, k):
+        return ("L", pair_slot(j, k))
+
+    order = [tile(3, 2), ("D", 2), tile(3, 1), tile(2, 1), ("D", 1)]
+    early = gathered(stage(lower_tiles, inverse_diag, order, None, None))
+    around = spread(inverse_diag[3], "x")
+
+    term = lead * pivot_rhs - lax.dot_general(
+        border_tiles, bound_sol, (((0,), (0,)), ((), ())), preferred_element_type=F32
+    )
+    away = lax.dynamic_slice_in_dim(term, (1 - core) * 512, 512, axis=2).astype(BF16)
+    away = away + nothing(*around[1:])
+    tiles3 = around + tuple(swap(piece) for piece in around)
+    home = lax.dynamic_slice_in_dim(term, core * 512, 512, axis=2)
+    both = (home + swap(away).astype(F32)).astype(BF16)
+    cut = [
+        lax.dynamic_slice_in_dim(both, lax.rem(x + by, 4) * 128, 128, axis=2) for by in range(4)
+    ]
+
+    owners = jnp.pad(owner_map[0, :, 0].astype(BF16)[None], ((0, 15), (0, 128)))
+    order = [tile(3, 0), tile(2, 0), tile(1, 0), ("D", 0)]
+    late = gathered(stage(lower_tiles, inverse_diag, order, owners, both))
+    named = late[:, :, 2048, :128].astype(jnp.int32).reshape(8, 128)
+
+    base = turn(place, deal(cut, "x"), F32)
+    over_z = spread(base[3].astype(BF16), "z")
+    pieces = spread(diag_near(place, over_z, tiles3), "y")
     residual, x3 = lower_step(base[2], pieces, early, 0, BF16)
     over_z = spread(residual, "z")
-    target = slots_of(owner_map[0, :, 0], core, x)
-    pieces = spread(diag_step(place, over_z, tiles2), "y")
-    base1, _ = lower_step(base[1], (x3,), middle, 0, F32)
-    tiles1 = collected(after(inverse_diag[1], pieces[0]))
-    residual, x2 = lower_step(base1, pieces, middle, 1, BF16)
+    pieces = spread(diag_step(over_z, early, 1), "y")
+    base1, _ = lower_step(base[1], (x3,), early, 2, F32)
+    residual, x2 = lower_step(base1, pieces, early, 3, BF16)
     over_z = spread(residual, "z")
-    pieces = spread(diag_step(place, over_z, tiles1), "y")
+    pieces = spread(diag_step(over_z, early, 4), "y")
     base0, _ = lower_step(base[0], (x3,), late, 0, F32)
     base0, _ = lower_step(base0, (x2,), late, 1, F32)
-    tiles0 = collected(after(inverse_diag[0], pieces[0]))
     residual, x1 = lower_step(base0, pieces, late, 2, BF16)
     over_z = spread(residual, "z")
-    packed, still = pack_known(place, target, (x1, x2, x3))
-    rows = deal(last_step(place, over_z, tiles0), "y")
+    packed, still = pack_known(place, slots_of(named), (x1, x2, x3))
+    rows = deal(last_step(place, over_z, late, 3), "y")
     packed = pack_last(still, rows, packed).reshape(128, 16, 128)
     received = lax.all_to_all(
         packed, ("z", "core", "y", "x"), split_axis=0, concat_axis=0, tiled=True

time: 288 us -> 295 us (1.024)
  Pallas kernels: 25.2 us -> 101 us
  starting transfers between devices: 105 us -> 56.3 us
  local copies, waits for them, and re-layouts: 17.1 us -> 3.79 us
  waiting for transfers between devices: 84.6 us -> 75.6 us
    pallas_call x0 -> x3, Pallas kernels: none -> 75.1 us  [the longest x2 74 us: stage(): pl.pallas_call(kernel, out_shape=jax.ShapeDtypeStruct((rows, 256), BF16),...]
    ppermute x19 -> x5, starting transfers between devices: 48.4 us -> 3.73 us  [swap(): return lax.ppermute(value, 'core', [(0, 1), (1, 0)])]
    unnamed x23 -> x4, local copies, waits for them, and re-layouts: 11.4 us -> 0.01 us
    ppermute x45 -> x30, waiting for transfers between devices: 82.1 us -> 73.4 us  [shift(): return lax.ppermute(value, axis, [(i, (i + by) % 4) for i in range(4)])]
    ppermute x45 -> x30, starting transfers between devices: 56 us -> 52.5 us  [shift(): return lax.ppermute(value, axis, [(i, (i + by) % 4) for i in range(4)])]
    convert_element_type x2 -> x3, other arithmetic: 0.36 us -> 3.63 us  [the longest x1 2.9 us: local(): both = (home + swap(away).astype(F32)).astype(BF16)]
    dot_general x2 -> x1, matrix products: 10.5 us -> 11.3 us  [local(): lax.dot_general(border_tiles, bound_sol, (((0,), (0,)), ((), ())), prefer...]
  transfers between devices with their start and end apart: 67 -> 37, of which waited for: 22 -> 23; matrix products, arithmetic and copies ran while one was open for 9% -> 7% of each run, Pallas kernels for 7% -> 18%
where the time goes in v3:
time: 295 us; the launch traced here: 294 us
  Pallas kernels  101 us (34%)
  waiting for transfers between devices  75.6 us (26%)
  starting transfers between devices  56.3 us (19%)
  blocking collectives  23.5 us (8%)
  between operations  15.7 us (5%)
  matrix products  11.3 us (4%)
  other arithmetic  6.94 us (2%)
  local copies, waits for them, and re-layouts  3.79 us (1%)
    pallas_call x2, Pallas kernels, stage(): pl.pallas_call(kernel, out_shape=jax.ShapeDtypeStruct((rows, 256), BF16),...  74 us
    ppermute x30, waiting for transfers between devices, shift(): return lax.ppermute(value, axis, [(i, (i + by) % 4) for i in range(4)])  73.4 us
    ppermute x30, starting transfers between devices, shift(): return lax.ppermute(value, axis, [(i, (i + by) % 4) for i in range(4)])  52.5 us
    all_to_all x1, blocking collectives, local(): lax.all_to_all(packed, ('z', 'core', 'y', 'x'), split_axis=0, concat_axis...  23.5 us
    pallas_call x6, Pallas kernels, lower_step(): pl.pallas_call(kernel, out_shape=(jax.ShapeDtypeStruct((128, 1024), dtype...  13.6 us
    dot_general x1, matrix products, local(): lax.dot_general(border_tiles, bound_sol, (((0,), (0,)), ((), ())), prefer...  11.3 us
  transfers between devices with their start and end apart: 37, of which 23 were waited for; matrix products, arithmetic and copies ran while one was open for 7% of the time, Pallas kernels for 18%

profile of v3, /device:TPU:1, one launch (start us, length us, event | category | flops | bytes accessed | tf_op | source)
XLA Modules:
  0.0 293.9 jit_solution(9611305964302893751)
XLA Ops:
  6.5 40.9 %stage.3 = bf16[2560,256]{1,0:T(8,128)(2,1)} custom-call(bf16[6,512,256]{2,1,0:T(8,128)(2,1)} %lower_ref.3, bf16[4,256,512]{2,1,0:T(8,128)(2,1)} %diag_ref.3), custom_call_target="tpu_custom_call" | custom-call | bytes 2621440 | tf_op jit(solution)/shard_map/stage/pallas_call | solution.py:258
  50.6 2.5 collective-permute-start.1
  54.2 11.3 %multiply_subtract_fusion = f32[4,256,1024]{2,1,0:T(8,128)} fusion(f32[4,256,1024]{2,1,0:T(8,128)} %param.6, f32[]{:T(128)S(6)} %select_n.22, bf16[2048,1024]{1,0:T(8,128)(2,1)} %param.7, bf16[2048,4,256]{2,1,0:T(4,128)(2,1)} %param.8), kind=kOutput, calls=%fused_computation.3 | convolution fusion | flops 4297064448 | bytes 16777220 | tf_op jit(solution)/shard_map/dot_general | solution.py:378
  75.4 2.9 add_convert_fusion.refs_1_
  78.3 33.2 %stage.2 = bf16[2064,256]{1,0:T(8,128)(2,1)} custom-call(bf16[6,512,256]{2,1,0:T(8,128)(2,1)} %lower_ref.3, bf16[4,256,512]{2,1,0:T(8,128)(2,1)} %diag_ref.3, bf16[16,256]{1,0:T(8,128)(2,1)} %pad.4.refs_0_, bf16[4,256,512]{2,1,0:T(8,128)(2,1)} %add_convert_fusion.refs_1_), custom_call_target="tpu_custom_call" | custom-call | bytes 2113536 | tf_op jit(solution)/shard_map/stage/pallas_call | solution.py:258
  115.6 10.7 %collective-permute-done.4.v1 = bf16[4,256,128]{2,1,0:T(8,128)(2,1)S(1)} collective-permute-done((bf16[4,256,128]{2,1,0:T(8,128)(2,1)S(1)}, bf16[4,256,128]{2,1,0:T(8,128)(2,1)S(1)}, u32[]{:S(2)}, u32[]{:S(2)}) %collective-permute-start.4) | collective-permute-done | bytes 262176 | tf_op jit(solution)/shard_map/ppermute | solution.py:18
  128.3 2.2 collective-permute-start.7
  130.6 5.0 %collective-permute-start.8 = (bf16[128,1024]{1,0:T(8,128)(2,1)S(1)}, bf16[128,1024]{1,0:T(8,128)(2,1)S(1)}, u32[]{:S(2)}, u32[]{:S(2)}) collective-permute-start(bf16[128,1024]{1,0:T(8,128)(2,1)S(1)} %fusion.8.refs_0_), channel_id=1, source_target_pairs={{0,64},{32,96},{64,0},{96,32},{1,65},{33,97},{65,1},{97,33},{2,66}... | collective-permute-start | bytes 786440 | tf_op jit(solution)/shard_map/ppermute | solution.py:18
  135.6 3.6 %collective-permute-done.7.refs_1_ = bf16[128,1024]{1,0:T(8,128)(2,1)S(1)} collective-permute-done((bf16[128,1024]{1,0:T(8,128)(2,1)S(1)}, bf16[128,1024]{1,0:T(8,128)(2,1)S(1)}, u32[]{:S(2)}, u32[]{:S(2)}) %collective-permute-start.7) | collective-permute-done | bytes 262176 | tf_op jit(solution)/shard_map/ppermute | solution.py:18
  139.1 6.4 %collective-permute-done.8.refs_2_ = bf16[128,1024]{1,0:T(8,128)(2,1)S(1)} collective-permute-done((bf16[128,1024]{1,0:T(8,128)(2,1)S(1)}, bf16[128,1024]{1,0:T(8,128)(2,1)S(1)}, u32[]{:S(2)}, u32[]{:S(2)}) %collective-permute-start.8) | collective-permute-done | bytes 262176 | tf_op jit(solution)/shard_map/ppermute | solution.py:18
  148.5 2.8 collective-permute-start.15
  154.4 6.2 %collective-permute-done.15.refs_2_ = bf16[128,1024]{1,0:T(8,128)(2,1)S(1)} collective-permute-done((bf16[128,1024]{1,0:T(8,128)(2,1)S(1)}, bf16[128,1024]{1,0:T(8,128)(2,1)S(1)}, u32[]{:S(2)}, u32[]{:S(2)}) %collective-permute-start.15) | collective-permute-done | bytes 262176 | tf_op jit(solution)/shard_map/ppermute | solution.py:18
  162.9 5.1 %collective-permute-start.17 = (bf16[128,1024]{1,0:T(8,128)(2,1)S(1)}, bf16[128,1024]{1,0:T(8,128)(2,1)S(1)}, u32[]{:S(2)}, u32[]{:S(2)}) collective-permute-start(bf16[128,1024]{1,0:T(8,128)(2,1)S(1)} %get-tuple-element.20.v0), channel_id=1, source_target_pairs={{0,32},{32,64},{64,96},{96,0},{1,33},{33,65},{65,97},{97,1},{2,34}... | collective-permute-start | bytes 786440 | tf_op jit(solution)/shard_map/ppermute | solution.py:18
  170.6 2.5 collective-permute-done.17.v1
  173.1 6.5 %collective-permute-done.18.v2 = bf16[128,1024]{1,0:T(8,128)(2,1)S(1)} collective-permute-done((bf16[128,1024]{1,0:T(8,128)(2,1)S(1)}, bf16[128,1024]{1,0:T(8,128)(2,1)S(1)}, u32[]{:S(2)}, u32[]{:S(2)}) %collective-permute-start.18) | collective-permute-done | bytes 262176 | tf_op jit(solution)/shard_map/ppermute | solution.py:18
  183.6 3.4 %collective-permute-start.21 = (bf16[128,1024]{1,0:T(8,128)(2,1)S(1)}, bf16[128,1024]{1,0:T(8,128)(2,1)S(1)}, u32[]{:S(2)}, u32[]{:S(2)}) collective-permute-start(bf16[128,1024]{1,0:T(8,128)(2,1)S(1)} %diag_step.2.refs_0_), channel_id=1, source_target_pairs={{0,8},{4,12},{8,0},{12,4},{1,9},{5,13},{9,1},{13,5},{2,10},{6,14},... | collective-permute-start | bytes 786440 | tf_op jit(solution)/shard_map/ppermute | solution.py:18
  187.0 2.5 lower_step.7
  191.1 6.5 %collective-permute-done.21.refs_2_ = bf16[128,1024]{1,0:T(8,128)(2,1)S(1)} collective-permute-done((bf16[128,1024]{1,0:T(8,128)(2,1)S(1)}, bf16[128,1024]{1,0:T(8,128)(2,1)S(1)}, u32[]{:S(2)}, u32[]{:S(2)}) %collective-permute-start.21) | collective-permute-done | bytes 262176 | tf_op jit(solution)/shard_map/ppermute | solution.py:18
  201.6 3.0 %collective-permute-start.24 = (bf16[128,1024]{1,0:T(8,128)(2,1)S(1)}, bf16[128,1024]{1,0:T(8,128)(2,1)S(1)}, u32[]{:S(2)}, u32[]{:S(2)}) collective-permute-start(bf16[128,1024]{1,0:T(8,128)(2,1)S(1)} %get-tuple-element.23.v0), channel_id=1, source_target_pairs={{0,64},{32,96},{64,0},{96,32},{1,65},{33,97},{65,1},{97,33},{2,66}... | collective-permute-start | bytes 786440 | tf_op jit(solution)/shard_map/ppermute | solution.py:18
  204.6 3.9 %collective-permute-done.23.v1 = bf16[128,1024]{1,0:T(8,128)(2,1)S(1)} collective-permute-done((bf16[128,1024]{1,0:T(8,128)(2,1)S(1)}, bf16[128,1024]{1,0:T(8,128)(2,1)S(1)}, u32[]{:S(2)}, u32[]{:S(2)}) %collective-permute-start.23) | collective-permute-done | bytes 262176 | tf_op jit(solution)/shard_map/ppermute | solution.py:18
  208.5 6.7 %collective-permute-done.24.v2 = bf16[128,1024]{1,0:T(8,128)(2,1)S(1)} collective-permute-done((bf16[128,1024]{1,0:T(8,128)(2,1)S(1)}, bf16[128,1024]{1,0:T(8,128)(2,1)S(1)}, u32[]{:S(2)}, u32[]{:S(2)}) %collective-permute-start.24) | collective-permute-done | bytes 262176 | tf_op jit(solution)/shard_map/ppermute | solution.py:18
  219.2 2.8 collective-permute-start.27
  222.1 2.5 lower_step.9
  224.6 2.5 lower_step.10
  227.1 5.5 %collective-permute-done.27.refs_2_ = bf16[128,1024]{1,0:T(8,128)(2,1)S(1)} collective-permute-done((bf16[128,1024]{1,0:T(8,128)(2,1)S(1)}, bf16[128,1024]{1,0:T(8,128)(2,1)S(1)}, u32[]{:S(2)}, u32[]{:S(2)}) %collective-permute-start.27) | collective-permute-done | bytes 262176 | tf_op jit(solution)/shard_map/ppermute | solution.py:18
  234.9 2.3 collective-permute-start.29
  237.2 2.3 collective-permute-start.30
  243.4 6.8 %collective-permute-done.30.v2 = bf16[128,1024]{1,0:T(8,128)(2,1)S(1)} collective-permute-done((bf16[128,1024]{1,0:T(8,128)(2,1)S(1)}, bf16[128,1024]{1,0:T(8,128)(2,1)S(1)}, u32[]{:S(2)}, u32[]{:S(2)}) %collective-permute-start.30) | collective-permute-done | bytes 262176 | tf_op jit(solution)/shard_map/ppermute | solution.py:18
  250.4 2.5 last_step.1
  254.8 2.8 collective-permute-start.33
  257.7 3.0 %pack_known.1 = (bf16[2048,128]{1,0:T(8,128)(2,1)S(1)}, bf16[2048,256]{1,0:T(8,128)(2,1)S(1)}) custom-call(s32[4]{0:T(128)S(1)} %pad_add_fusion.place_ref, s32[4,1,256]{2,1,0:T(1,128)S(1)} %reshape.77.target_ref, bf16[128,1024]{1,0:T(8,128)(2,1)S(1)} %get-tuple-element.27.x1, bf16[128,1024]{1,0:T(8,128)(2,1)S(1)} %get-tuple-element.24.refs_0_.x2, ...), custom_call_target="tpu_custom_call" | custom-call | flops 402653184 | bytes 2097152 | tf_op jit(solution)/shard_map/pack_known/pallas_call | solution.py:293
  262.0 23.5 %all_to_all.5 = bf16[128,16,128]{2,1,0:T(8,128)(2,1)S(1)} all-to-all(bf16[128,16,128]{2,1,0:T(8,128)(2,1)S(1)} %bitcast.30), channel_id=1, replica_groups=mesh['z'=4,'core'=2,'y'=4,'x'=4] {'z','core','y','x'}, dimensions={0} | all-to-all | bytes 1048576 | tf_op jit(solution)/shard_map/all_to_all | solution.py:412
  (88 shorter events, 54.0 us)
Async XLA Ops:
  6.5 154.4 %all-gather.7.cloned.1.call-start = ((), (), s32[]{:S(2)}) async-start(), calls=%async_computation.2 | async-start | bytes 11796480 | tf_op jit(solution)/shard_map/all_gather | solution.py:359
  47.4 174.6 %all-gather.5.cloned.1.call-start = ((), (), s32[]{:S(2)}) async-start(), calls=%async_computation.1 | async-start | bytes 9510912 | tf_op jit(solution)/shard_map/all_gather | solution.py:359
  48.5 17.0 %collective-permute-start = (bf16[256,512]{1,0:T(8,128)(2,1)S(1)}, bf16[256,512]{1,0:T(8,128)(2,1)S(1)}, u32[]{:S(2)}, u32[]{:S(2)}) collective-permute-start(bf16[256,512]{1,0:T(8,128)(2,1)S(1)} %slice_bitcast_fusion.3.refs_4_), channel_id=1, source_target_pairs={{0,1},{1,2},{2,3},{3,0},{4,5},{5,6},{6,7},{7,4},{8,9},{9,10},{10,1... | collective-permute-start | bytes 786440 | tf_op jit(solution)/shard_map/ppermute | solution.py:18
  50.6 15.4 %collective-permute-start.1 = (bf16[256,512]{1,0:T(8,128)(2,1)S(1)}, bf16[256,512]{1,0:T(8,128)(2,1)S(1)}, u32[]{:S(2)}, u32[]{:S(2)}) collective-permute-start(bf16[256,512]{1,0:T(8,128)(2,1)S(1)} %slice_bitcast_fusion.3.refs_4_), channel_id=1, source_target_pairs={{0,2},{1,3},{2,0},{3,1},{4,6},{5,7},{6,4},{7,5},{8,10},{9,11},{10,... | collective-permute-start | bytes 786440 | tf_op jit(solution)/shard_map/ppermute | solution.py:18
  53.0 14.9 %collective-permute-start.2 = (bf16[256,512]{1,0:T(8,128)(2,1)S(1)}, bf16[256,512]{1,0:T(8,128)(2,1)S(1)}, u32[]{:S(2)}, u32[]{:S(2)}) collective-permute-start(bf16[256,512]{1,0:T(8,128)(2,1)S(1)} %slice_bitcast_fusion.3.refs_4_), channel_id=1, source_target_pairs={{0,3},{1,0},{2,1},{3,2},{4,7},{5,4},{6,5},{7,6},{8,11},{9,8},{10,9... | collective-permute-start | bytes 786440 | tf_op jit(solution)/shard_map/ppermute | solution.py:18
  111.8 14.4 %collective-permute-start.4 = (bf16[4,256,128]{2,1,0:T(8,128)(2,1)S(1)}, bf16[4,256,128]{2,1,0:T(8,128)(2,1)S(1)}, u32[]{:S(2)}, u32[]{:S(2)}) collective-permute-start(bf16[4,256,128]{2,1,0:T(8,128)(2,1)S(1)} %get-tuple-element.40), channel_id=1, source_target_pairs={{0,1},{1,2},{2,3},{3,0},{4,5},{5,6},{6,7},{7,4},{8,9},{9,10},{10,1... | collective-permute-start | bytes 786440 | tf_op jit(solution)/shard_map/ppermute | solution.py:18
  111.9 15.5 %collective-permute-start.5 = (bf16[4,256,128]{2,1,0:T(8,128)(2,1)S(1)}, bf16[4,256,128]{2,1,0:T(8,128)(2,1)S(1)}, u32[]{:S(2)}, u32[]{:S(2)}) collective-permute-start(bf16[4,256,128]{2,1,0:T(8,128)(2,1)S(1)} %get-tuple-element.39), channel_id=1, source_target_pairs={{0,2},{1,3},{2,0},{3,1},{4,6},{5,7},{6,4},{7,5},{8,10},{9,11},{10,... | collective-permute-start | bytes 786440 | tf_op jit(solution)/shard_map/ppermute | solution.py:18
  112.6 14.9 %collective-permute-start.6 = (bf16[4,256,128]{2,1,0:T(8,128)(2,1)S(1)}, bf16[4,256,128]{2,1,0:T(8,128)(2,1)S(1)}, u32[]{:S(2)}, u32[]{:S(2)}) collective-permute-start(bf16[4,256,128]{2,1,0:T(8,128)(2,1)S(1)} %get-tuple-element.38), channel_id=1, source_target_pairs={{0,3},{1,0},{2,1},{3,2},{4,7},{5,4},{6,5},{7,6},{8,11},{9,8},{10,9... | collective-permute-start | bytes 786440 | tf_op jit(solution)/shard_map/ppermute | solution.py:18
  114.5 16.0 %collective-permute-start.10 = (bf16[256,512]{1,0:T(8,128)(2,1)S(1)}, bf16[256,512]{1,0:T(8,128)(2,1)S(1)}, u32[]{:S(2)}, u32[]{:S(2)}) collective-permute-start(bf16[256,512]{1,0:T(8,128)(2,1)S(1)} %slice_bitcast_fusion.3.refs_4_), channel_id=1, source_target_pairs={{0,16},{16,0},{1,17},{17,1},{2,18},{18,2},{3,19},{19,3},{4,20},{20... | collective-permute-start | bytes 786440 | tf_op jit(solution)/shard_map/ppermute | solution.py:22
  115.5 20.1 %collective-permute-start.11 = (bf16[256,512]{1,0:T(8,128)(2,1)S(1)}, bf16[256,512]{1,0:T(8,128)(2,1)S(1)}, u32[]{:S(2)}, u32[]{:S(2)}) collective-permute-start(bf16[256,512]{1,0:T(8,128)(2,1)S(1)} %collective-permute-done.refs_5_), channel_id=1, source_target_pairs={{0,16},{16,0},{1,17},{17,1},{2,18},{18,2},{3,19},{19,3},{4,20},{20... | collective-permute-start | bytes 786440 | tf_op jit(solution)/shard_map/ppermute | solution.py:22
  126.2 9.3 %collective-permute-start.12 = (bf16[256,512]{1,0:T(8,128)(2,1)S(1)}, bf16[256,512]{1,0:T(8,128)(2,1)S(1)}, u32[]{:S(2)}, u32[]{:S(2)}) collective-permute-start(bf16[256,512]{1,0:T(8,128)(2,1)S(1)} %collective-permute-done.1.refs_6_), channel_id=1, source_target_pairs={{0,16},{16,0},{1,17},{17,1},{2,18},{18,2},{3,19},{19,3},{4,20},{20... | collective-permute-start | bytes 786440 | tf_op jit(solution)/shard_map/ppermute | solution.py:22
  127.4 8.1 %collective-permute-start.13 = (bf16[256,512]{1,0:T(8,128)(2,1)S(1)}, bf16[256,512]{1,0:T(8,128)(2,1)S(1)}, u32[]{:S(2)}, u32[]{:S(2)}) collective-permute-start(bf16[256,512]{1,0:T(8,128)(2,1)S(1)} %collective-permute-done.2.refs_7_), channel_id=1, source_target_pairs={{0,16},{16,0},{1,17},{17,1},{2,18},{18,2},{3,19},{19,3},{4,20},{20... | collective-permute-start | bytes 786440 | tf_op jit(solution)/shard_map/ppermute | solution.py:22
  128.3 10.8 %collective-permute-start.7 = (bf16[128,1024]{1,0:T(8,128)(2,1)S(1)}, bf16[128,1024]{1,0:T(8,128)(2,1)S(1)}, u32[]{:S(2)}, u32[]{:S(2)}) collective-permute-start(bf16[128,1024]{1,0:T(8,128)(2,1)S(1)} %fusion.8.refs_0_), channel_id=1, source_target_pairs={{0,32},{32,64},{64,96},{96,0},{1,33},{33,65},{65,97},{97,1},{2,34}... | collective-permute-start | bytes 786440 | tf_op jit(solution)/shard_map/ppermute | solution.py:18
  130.6 15.0 %collective-permute-start.8 = (bf16[128,1024]{1,0:T(8,128)(2,1)S(1)}, bf16[128,1024]{1,0:T(8,128)(2,1)S(1)}, u32[]{:S(2)}, u32[]{:S(2)}) collective-permute-start(bf16[128,1024]{1,0:T(8,128)(2,1)S(1)} %fusion.8.refs_0_), channel_id=1, source_target_pairs={{0,64},{32,96},{64,0},{96,32},{1,65},{33,97},{65,1},{97,33},{2,66}... | collective-permute-start | bytes 786440 | tf_op jit(solution)/shard_map/ppermute | solution.py:18
  135.5 10.4 %collective-permute-start.9 = (bf16[128,1024]{1,0:T(8,128)(2,1)S(1)}, bf16[128,1024]{1,0:T(8,128)(2,1)S(1)}, u32[]{:S(2)}, u32[]{:S(2)}) collective-permute-start(bf16[128,1024]{1,0:T(8,128)(2,1)S(1)} %fusion.8.refs_0_), channel_id=1, source_target_pairs={{0,96},{32,0},{64,32},{96,64},{1,97},{33,1},{65,33},{97,65},{2,98}... | collective-permute-start | bytes 786440 | tf_op jit(solution)/shard_map/ppermute | solution.py:18
  148.5 12.1 %collective-permute-start.15 = (bf16[128,1024]{1,0:T(8,128)(2,1)S(1)}, bf16[128,1024]{1,0:T(8,128)(2,1)S(1)}, u32[]{:S(2)}, u32[]{:S(2)}) collective-permute-start(bf16[128,1024]{1,0:T(8,128)(2,1)S(1)} %diag_near.1.refs_0_), channel_id=1, source_target_pairs={{0,8},{4,12},{8,0},{12,4},{1,9},{5,13},{9,1},{13,5},{2,10},{6,14},... | collective-permute-start | bytes 786440 | tf_op jit(solution)/shard_map/ppermute | solution.py:18
  151.3 9.6 %collective-permute-start.16 = (bf16[128,1024]{1,0:T(8,128)(2,1)S(1)}, bf16[128,1024]{1,0:T(8,128)(2,1)S(1)}, u32[]{:S(2)}, u32[]{:S(2)}) collective-permute-start(bf16[128,1024]{1,0:T(8,128)(2,1)S(1)} %diag_near.1.refs_0_), channel_id=1, source_target_pairs={{0,12},{4,0},{8,4},{12,8},{1,13},{5,1},{9,5},{13,9},{2,14},{6,2},{... | collective-permute-start | bytes 786440 | tf_op jit(solution)/shard_map/ppermute | solution.py:18
  162.9 10.1 %collective-permute-start.17 = (bf16[128,1024]{1,0:T(8,128)(2,1)S(1)}, bf16[128,1024]{1,0:T(8,128)(2,1)S(1)}, u32[]{:S(2)}, u32[]{:S(2)}) collective-permute-start(bf16[128,1024]{1,0:T(8,128)(2,1)S(1)} %get-tuple-element.20.v0), channel_id=1, source_target_pairs={{0,32},{32,64},{64,96},{96,0},{1,33},{33,65},{65,97},{97,1},{2,34}... | collective-permute-start | bytes 786440 | tf_op jit(solution)/shard_map/ppermute | solution.py:18
  168.1 11.5 %collective-permute-start.18 = (bf16[128,1024]{1,0:T(8,128)(2,1)S(1)}, bf16[128,1024]{1,0:T(8,128)(2,1)S(1)}, u32[]{:S(2)}, u32[]{:S(2)}) collective-permute-start(bf16[128,1024]{1,0:T(8,128)(2,1)S(1)} %get-tuple-element.20.v0), channel_id=1, source_target_pairs={{0,64},{32,96},{64,0},{96,32},{1,65},{33,97},{65,1},{97,33},{2,66}... | collective-permute-start | bytes 786440 | tf_op jit(solution)/shard_map/ppermute | solution.py:18
  169.3 10.6 %collective-permute-start.19 = (bf16[128,1024]{1,0:T(8,128)(2,1)S(1)}, bf16[128,1024]{1,0:T(8,128)(2,1)S(1)}, u32[]{:S(2)}, u32[]{:S(2)}) collective-permute-start(bf16[128,1024]{1,0:T(8,128)(2,1)S(1)} %get-tuple-element.20.v0), channel_id=1, source_target_pairs={{0,96},{32,0},{64,32},{96,64},{1,97},{33,1},{65,33},{97,65},{2,98}... | collective-permute-start | bytes 786440 | tf_op jit(solution)/shard_map/ppermute | solution.py:18
  181.8 9.3 %collective-permute-start.20 = (bf16[128,1024]{1,0:T(8,128)(2,1)S(1)}, bf16[128,1024]{1,0:T(8,128)(2,1)S(1)}, u32[]{:S(2)}, u32[]{:S(2)}) collective-permute-start(bf16[128,1024]{1,0:T(8,128)(2,1)S(1)} %diag_step.2.refs_0_), channel_id=1, source_target_pairs={{0,4},{4,8},{8,12},{12,0},{1,5},{5,9},{9,13},{13,1},{2,6},{6,10},{... | collective-permute-start | bytes 786440 | tf_op jit(solution)/shard_map/ppermute | solution.py:18
  183.6 14.0 %collective-permute-start.21 = (bf16[128,1024]{1,0:T(8,128)(2,1)S(1)}, bf16[128,1024]{1,0:T(8,128)(2,1)S(1)}, u32[]{:S(2)}, u32[]{:S(2)}) collective-permute-start(bf16[128,1024]{1,0:T(8,128)(2,1)S(1)} %diag_step.2.refs_0_), channel_id=1, source_target_pairs={{0,8},{4,12},{8,0},{12,4},{1,9},{5,13},{9,1},{13,5},{2,10},{6,14},... | collective-permute-start | bytes 786440 | tf_op jit(solution)/shard_map/ppermute | solution.py:18
  187.0 10.8 %collective-permute-start.22 = (bf16[128,1024]{1,0:T(8,128)(2,1)S(1)}, bf16[128,1024]{1,0:T(8,128)(2,1)S(1)}, u32[]{:S(2)}, u32[]{:S(2)}) collective-permute-start(bf16[128,1024]{1,0:T(8,128)(2,1)S(1)} %diag_step.2.refs_0_), channel_id=1, source_target_pairs={{0,12},{4,0},{8,4},{12,8},{1,13},{5,1},{9,5},{13,9},{2,14},{6,2},{... | collective-permute-start | bytes 786440 | tf_op jit(solution)/shard_map/ppermute | solution.py:18
  199.9 8.6 %collective-permute-start.23 = (bf16[128,1024]{1,0:T(8,128)(2,1)S(1)}, bf16[128,1024]{1,0:T(8,128)(2,1)S(1)}, u32[]{:S(2)}, u32[]{:S(2)}) collective-permute-start(bf16[128,1024]{1,0:T(8,128)(2,1)S(1)} %get-tuple-element.23.v0), channel_id=1, source_target_pairs={{0,32},{32,64},{64,96},{96,0},{1,33},{33,65},{65,97},{97,1},{2,34}... | collective-permute-start | bytes 786440 | tf_op jit(solution)/shard_map/ppermute | solution.py:18
  201.6 13.7 %collective-permute-start.24 = (bf16[128,1024]{1,0:T(8,128)(2,1)S(1)}, bf16[128,1024]{1,0:T(8,128)(2,1)S(1)}, u32[]{:S(2)}, u32[]{:S(2)}) collective-permute-start(bf16[128,1024]{1,0:T(8,128)(2,1)S(1)} %get-tuple-element.23.v0), channel_id=1, source_target_pairs={{0,64},{32,96},{64,0},{96,32},{1,65},{33,97},{65,1},{97,33},{2,66}... | collective-permute-start | bytes 786440 | tf_op jit(solution)/shard_map/ppermute | solution.py:18
  204.6 10.8 %collective-permute-start.25 = (bf16[128,1024]{1,0:T(8,128)(2,1)S(1)}, bf16[128,1024]{1,0:T(8,128)(2,1)S(1)}, u32[]{:S(2)}, u32[]{:S(2)}) collective-permute-start(bf16[128,1024]{1,0:T(8,128)(2,1)S(1)} %get-tuple-element.23.v0), channel_id=1, source_target_pairs={{0,96},{32,0},{64,32},{96,64},{1,97},{33,1},{65,33},{97,65},{2,98}... | collective-permute-start | bytes 786440 | tf_op jit(solution)/shard_map/ppermute | solution.py:18
  217.3 9.7 %collective-permute-start.26 = (bf16[128,1024]{1,0:T(8,128)(2,1)S(1)}, bf16[128,1024]{1,0:T(8,128)(2,1)S(1)}, u32[]{:S(2)}, u32[]{:S(2)}) collective-permute-start(bf16[128,1024]{1,0:T(8,128)(2,1)S(1)} %diag_step.3.refs_0_), channel_id=1, source_target_pairs={{0,4},{4,8},{8,12},{12,0},{1,5},{5,9},{9,13},{13,1},{2,6},{6,10},{... | collective-permute-start | bytes 786440 | tf_op jit(solution)/shard_map/ppermute | solution.py:18
  219.2 13.4 %collective-permute-start.27 = (bf16[128,1024]{1,0:T(8,128)(2,1)S(1)}, bf16[128,1024]{1,0:T(8,128)(2,1)S(1)}, u32[]{:S(2)}, u32[]{:S(2)}) collective-permute-start(bf16[128,1024]{1,0:T(8,128)(2,1)S(1)} %diag_step.3.refs_0_), channel_id=1, source_target_pairs={{0,8},{4,12},{8,0},{12,4},{1,9},{5,13},{9,1},{13,5},{2,10},{6,14},... | collective-permute-start | bytes 786440 | tf_op jit(solution)/shard_map/ppermute | solution.py:18
  222.0 10.8 %collective-permute-start.28 = (bf16[128,1024]{1,0:T(8,128)(2,1)S(1)}, bf16[128,1024]{1,0:T(8,128)(2,1)S(1)}, u32[]{:S(2)}, u32[]{:S(2)}) collective-permute-start(bf16[128,1024]{1,0:T(8,128)(2,1)S(1)} %diag_step.3.refs_0_), channel_id=1, source_target_pairs={{0,12},{4,0},{8,4},{12,8},{1,13},{5,1},{9,5},{13,9},{2,14},{6,2},{... | collective-permute-start | bytes 786440 | tf_op jit(solution)/shard_map/ppermute | solution.py:18
  234.9 8.5 %collective-permute-start.29 = (bf16[128,1024]{1,0:T(8,128)(2,1)S(1)}, bf16[128,1024]{1,0:T(8,128)(2,1)S(1)}, u32[]{:S(2)}, u32[]{:S(2)}) collective-permute-start(bf16[128,1024]{1,0:T(8,128)(2,1)S(1)} %get-tuple-element.29.v0), channel_id=1, source_target_pairs={{0,32},{32,64},{64,96},{96,0},{1,33},{33,65},{65,97},{97,1},{2,34}... | collective-permute-start | bytes 786440 | tf_op jit(solution)/shard_map/ppermute | solution.py:18
  237.2 12.9 %collective-permute-start.30 = (bf16[128,1024]{1,0:T(8,128)(2,1)S(1)}, bf16[128,1024]{1,0:T(8,128)(2,1)S(1)}, u32[]{:S(2)}, u32[]{:S(2)}) collective-permute-start(bf16[128,1024]{1,0:T(8,128)(2,1)S(1)} %get-tuple-element.29.v0), channel_id=1, source_target_pairs={{0,64},{32,96},{64,0},{96,32},{1,65},{33,97},{65,1},{97,33},{2,66}... | collective-permute-start | bytes 786440 | tf_op jit(solution)/shard_map/ppermute | solution.py:18
  239.5 10.8 %collective-permute-start.31 = (bf16[128,1024]{1,0:T(8,128)(2,1)S(1)}, bf16[128,1024]{1,0:T(8,128)(2,1)S(1)}, u32[]{:S(2)}, u32[]{:S(2)}) collective-permute-start(bf16[128,1024]{1,0:T(8,128)(2,1)S(1)} %get-tuple-element.29.v0), channel_id=1, source_target_pairs={{0,96},{32,0},{64,32},{96,64},{1,97},{33,1},{65,33},{97,65},{2,98}... | collective-permute-start | bytes 786440 | tf_op jit(solution)/shard_map/ppermute | solution.py:18
  (7 other events, 81.3 us)
Sparse Core Ops, SparseCore 0:
  47.6 62.1 all-gather.6
  111.7 51.6 all-gather.4

commit v4 on v3

--- a/solution.py
+++ b/solution.py
@@ -122,36 +122,6 @@
     )(*pieces, base, tiles)
 
 
-def times_diag(place_ref, vec, tiles, out):
-    core, x = place_ref[0], place_ref[2]
-    for side, group in ((core, tiles[:4]), (1 - core, tiles[4:])):
-        total = None
-        for step, tile in enumerate(group):
-            start = lax.rem(x + 4 - step, 4) * 256
-            left = vec[:, pl.ds(pl.multiple_of(start, 256), 256)]
-            term = jnp.dot(left, tile[...], preferred_element_type=F32)
-            total = term if total is None else total + term
-        out[:, pl.ds(pl.multiple_of(side * 512, 512), 512)] = total.astype(BF16)
-
-
-def diag_near(place, pieces, tiles):
-    def kernel(place_ref, *refs):
-        out, vec = refs[12:]
-        vec[...] = add_up(refs[:4]).astype(BF16)
-        times_diag(place_ref, vec, refs[4:12], out)
-
-    return pl.pallas_call(
-        kernel,
-        out_shape=jax.ShapeDtypeStruct((128, 1024), BF16),
-        in_specs=[SCALARS] + [VMEM] * 12,
-        out_specs=VMEM,
-        scratch_shapes=[pltpu.VMEM((128, 1024), BF16)],
-        compiler_params=params(),
-        cost_estimate=cost(2 * 128 * 1024 * 1024, 4 << 20),
-        name="diag_near",
-    )(place, *pieces, *tiles)
-
-
 def fetch_diag(tiles_ref, at, tile, sems):
     copies = [
         pltpu.make_async_copy(
@@ -219,52 +189,56 @@
         in_specs=[SCALARS] + [VMEM] * 4 + [HBM],
         out_specs=(VMEM,) * 4,
         scratch_shapes=DIAG_SCRATCH + [pltpu.VMEM((128, 1024), BF16)],
-        compiler_params=params(),
+        compiler_params=params(52 * 1024 * 1024),
         cost_estimate=cost(2 * 128 * 1024 * 1024, 4 << 20),
         name="last_step",
     )(place, *pieces, tiles)
 
 
-def stage(lower_tiles, inverse_diag, order, owners, event):
-    rows = 512 * len(order) + (0 if owners is None else 16)
+def stage(lower_tiles, inverse_diag, orders, owners):
     moves = []
-    for at, (kind, index) in enumerate(order):
-        if kind == "L":
-            moves.append((0, index, slice(None), at * 512, 512))
-        else:
-            moves.append((1, index, slice(0, 256), at * 512, 256))
-            moves.append((1, index, slice(256, 512), at * 512 + 256, 256))
-    extra = [value for value in (owners, event) if value is not None]
-
-    def kernel(lower_ref, diag_ref, *refs):
-        out, sems = refs[len(extra) :]
-        copies = [
-            pltpu.make_async_copy(
-                (lower_ref, diag_ref)[which].at[index, :, lanes],
-                out.at[pl.ds(start, height)],
-                sems.at[number],
-            )
-            for number, (which, index, lanes, start, height) in enumerate(moves)
+    for number, order in enumerate(orders):
+        for at, (kind, index) in enumerate(order):
+            if kind == "L":
+                moves.append((0, index, slice(None), number, at * 512, 512))
+            else:
+                moves.append((1, index, slice(0, 256), number, at * 512, 256))
+                moves.append((1, index, slice(256, 512), number, at * 512 + 256, 256))
+    heights = [512 * len(order) for order in orders]
+    heights[-1] += 16
+    count = len(orders)
+
+    def kernel(lower_ref, diag_ref, owners_ref, *refs):
+        outs, held, sems = refs[:count], refs[count : 2 * count], refs[2 * count]
+        plan = [
+            ((lower_ref, diag_ref)[which].at[index, :, lanes], number, pl.ds(start, height))
+            for which, index, lanes, number, start, height in moves
         ]
-        if owners is not None:
-            copies.append(
-                pltpu.make_async_copy(refs[0], out.at[pl.ds(rows - 16, 16)], sems.at[len(moves)])
-            )
-        for copy in copies:
+        plan.append((owners_ref, count - 1, pl.ds(heights[-1] - 16, 16)))
+        into, onward = [], []
+        for at, (source, number, where) in enumerate(plan):
+            middle = held[number].at[where]
+            into.append(pltpu.make_async_copy(source, middle, sems.at[0, at]))
+            onward.append(pltpu.make_async_copy(middle, outs[number].at[where], sems.at[1, at]))
+        for copy in into:
             copy.start()
-        for copy in copies:
+        for first, second in zip(into, onward):
+            first.wait()
+            second.start()
+        for copy in onward:
             copy.wait()
 
     return pl.pallas_call(
         kernel,
-        out_shape=jax.ShapeDtypeStruct((rows, 256), BF16),
-        in_specs=[HBM] * (2 + len(extra)),
-        out_specs=HBM,
-        scratch_shapes=[pltpu.SemaphoreType.DMA((len(moves) + 1,))],
+        out_shape=tuple(jax.ShapeDtypeStruct((height, 256), BF16) for height in heights),
+        in_specs=[HBM] * 3,
+        out_specs=(HBM,) * count,
+        scratch_shapes=[pltpu.VMEM((height, 256), BF16) for height in heights]
+        + [pltpu.SemaphoreType.DMA((2, len(moves) + 1))],
         compiler_params=params(60 * 1024 * 1024),
-        cost_estimate=cost(0, 2 * rows * 512),
+        cost_estimate=cost(0, 6 << 20),
         name="stage",
-    )(lower_tiles, inverse_diag, *extra)
+    )(lower_tiles, inverse_diag, owners)
 
 
 def chosen(target, block):
@@ -359,10 +333,6 @@
     return lax.all_gather(joined, ("core", "x"), axis=0, tiled=False).reshape(2, 4, rows, 256)
 
 
-def nothing(*arrays):
-    return sum(array[0, 0] for array in arrays) * 0
-
-
 def local(pivot_rhs, bound_sol, border_tiles, lower_tiles, inverse_diag, owner_map):
     z, core, y, x = (lax.axis_index(name) for name in ("z", "core", "y", "x"))
     place = jnp.stack([core, y, x, z]).astype(jnp.int32)
@@ -371,43 +341,48 @@
     def tile(j, k):
         return ("L", pair_slot(j, k))
 
-    order = [tile(3, 2), ("D", 2), tile(3, 1), tile(2, 1), ("D", 1)]
-    early = gathered(stage(lower_tiles, inverse_diag, order, None, None))
-    around = spread(inverse_diag[3], "x")
-
-    term = lead * pivot_rhs - lax.dot_general(
-        border_tiles, bound_sol, (((0,), (0,)), ((), ())), preferred_element_type=F32
-    )
-    away = lax.dynamic_slice_in_dim(term, (1 - core) * 512, 512, axis=2).astype(BF16)
-    away = away + nothing(*around[1:])
-    tiles3 = around + tuple(swap(piece) for piece in around)
-    home = lax.dynamic_slice_in_dim(term, core * 512, 512, axis=2)
-    both = (home + swap(away).astype(F32)).astype(BF16)
+    owners = jnp.pad(owner_map[0, :, 0].astype(BF16)[None], ((0, 15), (0, 128)))
+    orders = [
+        [("D", 3), tile(3, 2), ("D", 2), tile(3, 1)],
+        [tile(2, 1), ("D", 1), tile(3, 0)],
+        [tile(2, 0), tile(1, 0), ("D", 0)],
+    ]
+    early, middle, late = map(gathered, stage(lower_tiles, inverse_diag, orders, owners))
+    named = late[:, :, 1536, :128].astype(jnp.int32).reshape(8, 128)
+
+    def term(side):
+        start = side * 512
+        rhs = lax.dynamic_slice_in_dim(pivot_rhs, start, 512, axis=2)
+        bound = lax.dynamic_slice_in_dim(bound_sol, start, 512, axis=1)
+        product = lax.dot_general(
+            border_tiles, bound, (((0,), (0,)), ((), ())), preferred_element_type=F32
+        )
+        return (lead * rhs - product).astype(BF16)
+
+    away = swap(term(1 - core))
+    home = lax.optimization_barrier(term(core))
+    both = (home.astype(F32) + away.astype(F32)).astype(BF16)
     cut = [
         lax.dynamic_slice_in_dim(both, lax.rem(x + by, 4) * 128, 128, axis=2) for by in range(4)
     ]
 
-    owners = jnp.pad(owner_map[0, :, 0].astype(BF16)[None], ((0, 15), (0, 128)))
-    order = [tile(3, 0), tile(2, 0), tile(1, 0), ("D", 0)]
-    late = gathered(stage(lower_tiles, inverse_diag, order, owners, both))
-    named = late[:, :, 2048, :128].astype(jnp.int32).reshape(8, 128)
-
     base = turn(place, deal(cut, "x"), F32)
-    over_z = spread(base[3].astype(BF16), "z")
-    pieces = spread(diag_near(place, over_z, tiles3), "y")
-    residual, x3 = lower_step(base[2], pieces, early, 0, BF16)
+    base3 = base[3].astype(BF16)
+    over_z = spread(base3, "z")
+    pieces = spread(diag_step(over_z, early, 0), "y")
+    residual, x3 = lower_step(base[2], pieces, early, 1, BF16)
     over_z = spread(residual, "z")
-    pieces = spread(diag_step(over_z, early, 1), "y")
-    base1, _ = lower_step(base[1], (x3,), early, 2, F32)
-    residual, x2 = lower_step(base1, pieces, early, 3, BF16)
+    pieces = spread(diag_step(over_z, early, 2), "y")
+    base1, _ = lower_step(base[1], (x3,), early, 3, F32)
+    residual, x2 = lower_step(base1, pieces, middle, 0, BF16)
     over_z = spread(residual, "z")
-    pieces = spread(diag_step(over_z, early, 4), "y")
-    base0, _ = lower_step(base[0], (x3,), late, 0, F32)
-    base0, _ = lower_step(base0, (x2,), late, 1, F32)
-    residual, x1 = lower_step(base0, pieces, late, 2, BF16)
+    base0, _ = lower_step(base[0], (x3,), middle, 2, F32)
+    pieces = spread(diag_step(over_z, middle, 1), "y")
+    base0, _ = lower_step(base0, (x2,), late, 0, F32)
+    residual, x1 = lower_step(base0, pieces, late, 1, BF16)
     over_z = spread(residual, "z")
     packed, still = pack_known(place, slots_of(named), (x1, x2, x3))
-    rows = deal(last_step(place, over_z, late, 3), "y")
+    rows = deal(last_step(place, over_z, late, 2), "y")
     packed = pack_last(still, rows, packed).reshape(128, 16, 128)
     received = lax.all_to_all(
         packed, ("z", "core", "y", "x"), split_axis=0, concat_axis=0, tiled=True

time: 295 us -> 223 us (0.76)
  Pallas kernels: 101 us -> 30.4 us
  waiting for transfers between devices: 75.6 us -> 94 us
  starting transfers between devices: 56.3 us -> 46.8 us
  other arithmetic: 6.94 us -> 2.95 us
    pallas_call x3 -> x1, Pallas kernels: 75.1 us -> 2.74 us  [stage(): pl.pallas_call(kernel, out_shape=tuple((jax.ShapeDtypeStruct((height, 256...]
    all_gather x2 -> x3, waiting for transfers between devices: 0.02 us -> 11.8 us  [gathered(): lax.all_gather(joined, ('core', 'x'), axis=0, tiled=False)]
    ppermute x30 -> x27, waiting for transfers between devices: 73.4 us -> 80.8 us  [shift(): return lax.ppermute(value, axis, [(i, (i + by) % 4) for i in range(4)])]
    ppermute x30 -> x27, starting transfers between devices: 52.5 us -> 45.2 us  [shift(): return lax.ppermute(value, axis, [(i, (i + by) % 4) for i in range(4)])]
    dot_general x1 -> x2, matrix products: 11.3 us -> 11.8 us  [term(): lax.dot_general(border_tiles, bound, (((0,), (0,)), ((), ())), preferred_...]
  transfers between devices with their start and end apart: 37 -> 31, of which waited for: 23 -> 18; matrix products, arithmetic and copies ran while one was open for 7% -> 7% of each run, Pallas kernels for 18% -> 10%
where the time goes in v4:
time: 223 us; the launch traced here: 222 us
  waiting for transfers between devices  94 us (42%)
  starting transfers between devices  46.8 us (21%)
  Pallas kernels  30.4 us (14%)
  blocking collectives  22 us (10%)
  between operations  13.4 us (6%)
  matrix products  11.8 us (5%)
  other arithmetic  2.95 us (1%)
    ppermute x27, waiting for transfers between devices, shift(): return lax.ppermute(value, axis, [(i, (i + by) % 4) for i in range(4)])  80.8 us
    ppermute x27, starting transfers between devices, shift(): return lax.ppermute(value, axis, [(i, (i + by) % 4) for i in range(4)])  45.2 us
    all_to_all x1, blocking collectives, local(): lax.all_to_all(packed, ('z', 'core', 'y', 'x'), split_axis=0, concat_axis...  22 us
    pallas_call x6, Pallas kernels, lower_step(): pl.pallas_call(kernel, out_shape=(jax.ShapeDtypeStruct((128, 1024), dtype...  13.6 us
    all_gather x3, waiting for transfers between devices, gathered(): lax.all_gather(joined, ('core', 'x'), axis=0, tiled=False)  11.8 us
    dot_general x2, matrix products, term(): lax.dot_general(border_tiles, bound, (((0,), (0,)), ((), ())), preferred_...  11.8 us
    pallas_call x3, Pallas kernels, diag_step(): pl.pallas_call(kernel, out_shape=jax.ShapeDtypeStruct((128, 1024), BF16),...  5.72 us
  transfers between devices with their start and end apart: 31, of which 18 were waited for; matrix products, arithmetic and copies ran while one was open for 7% of the time, Pallas kernels for 10%

profile of v4, /device:TPU:1, one launch (start us, length us, event | category | flops | bytes accessed | tf_op | source)
XLA Modules:
  0.0 222.5 jit_solution(2939692926105019526)
XLA Ops:
  7.8 2.7 %stage.1 = (bf16[2048,256]{1,0:T(8,128)(2,1)}, bf16[1536,256]{1,0:T(8,128)(2,1)}, bf16[1552,256]{1,0:T(8,128)(2,1)}) custom-call(bf16[6,512,256]{2,1,0:T(8,128)(2,1)} %lower_ref.1, bf16[4,256,512]{2,1,0:T(8,128)(2,1)} %diag_ref.1, bf16[16,256]{1,0:T(8,128)(2,1)} %pad.4.owners_ref), custom_call_target="tpu_custom_call" | custom-call | bytes 6291456 | tf_op jit(solution)/shard_map/stage/pallas_call | solution.py:231
  12.1 5.9 %fusion.6 = bf16[4,256,512]{2,1,0:T(8,128)(2,1)S(1)} fusion(f32[4,256,1024]{2,1,0:T(8,128)} %param.6, s32[]{:T(128)S(6)} %select_n.26, bf16[2048,4,256]{2,1,0:T(4,128)(2,1)} %param.8, bf16[2048,1024]{1,0:T(8,128)(2,1)} %param.7, f32[]{:T(128)S(6)} %select_n.24), kind=kOutput, calls=%fused_computation.7 | convolution fusion | flops 2149056512 | bytes 9438720 | tf_op jit(solution)/shard_map/dot_general | solution.py:357
  19.4 5.9 %fusion.7 = bf16[4,256,512]{2,1,0:T(8,128)(2,1)S(1)} fusion(f32[4,256,1024]{2,1,0:T(8,128)} %param.6, s32[]{:T(128)S(6)} %select_n.25, bf16[2048,4,256]{2,1,0:T(4,128)(2,1)} %param.8, bf16[2048,1024]{1,0:T(8,128)(2,1)} %param.7, f32[]{:T(128)S(6)} %select_n.24), kind=kOutput, calls=%fused_computation.9 | convolution fusion | flops 2149056512 | bytes 9438720 | tf_op jit(solution)/shard_map/dot_general | solution.py:357
  27.2 2.5 %collective-permute-start.2 = (bf16[4,256,128]{2,1,0:T(8,128)(2,1)S(1)}, bf16[4,256,128]{2,1,0:T(8,128)(2,1)S(1)}, u32[]{:S(2)}, u32[]{:S(2)}) collective-permute-start(bf16[4,256,128]{2,1,0:T(8,128)(2,1)S(1)} %get-tuple-element.45), channel_id=1, source_target_pairs={{0,2},{1,3},{2,0},{3,1},{4,6},{5,7},{6,4},{7,5},{8,10},{9,11},{10,... | collective-permute-start | bytes 786440 | tf_op jit(solution)/shard_map/ppermute | solution.py:18
  30.9 9.9 %collective-permute-done.1.v1 = bf16[4,256,128]{2,1,0:T(8,128)(2,1)S(1)} collective-permute-done((bf16[4,256,128]{2,1,0:T(8,128)(2,1)S(1)}, bf16[4,256,128]{2,1,0:T(8,128)(2,1)S(1)}, u32[]{:S(2)}, u32[]{:S(2)}) %collective-permute-start.1) | collective-permute-done | bytes 262176 | tf_op jit(solution)/shard_map/ppermute | solution.py:18
  40.8 12.3 %collective-permute-done.2.v2 = bf16[4,256,128]{2,1,0:T(8,128)(2,1)S(1)} collective-permute-done((bf16[4,256,128]{2,1,0:T(8,128)(2,1)S(1)}, bf16[4,256,128]{2,1,0:T(8,128)(2,1)S(1)}, u32[]{:S(2)}, u32[]{:S(2)}) %collective-permute-start.2) | collective-permute-done | bytes 262176 | tf_op jit(solution)/shard_map/ppermute | solution.py:18
  56.0 3.5 %collective-permute-start.5 = (bf16[128,1024]{1,0:T(8,128)(2,1)S(1)}, bf16[128,1024]{1,0:T(8,128)(2,1)S(1)}, u32[]{:S(2)}, u32[]{:S(2)}) collective-permute-start(bf16[128,1024]{1,0:T(8,128)(2,1)S(1)} %fusion.18.v0), channel_id=1, source_target_pairs={{0,64},{32,96},{64,0},{96,32},{1,65},{33,97},{65,1},{97,33},{2,66}... | collective-permute-start | bytes 786440 | tf_op jit(solution)/shard_map/ppermute | solution.py:18
  60.1 4.2 %collective-permute-done.4.v1 = bf16[128,1024]{1,0:T(8,128)(2,1)S(1)} collective-permute-done((bf16[128,1024]{1,0:T(8,128)(2,1)S(1)}, bf16[128,1024]{1,0:T(8,128)(2,1)S(1)}, u32[]{:S(2)}, u32[]{:S(2)}) %collective-permute-start.4) | collective-permute-done | bytes 262176 | tf_op jit(solution)/shard_map/ppermute | solution.py:18
  64.3 6.4 %collective-permute-done.5.v2 = bf16[128,1024]{1,0:T(8,128)(2,1)S(1)} collective-permute-done((bf16[128,1024]{1,0:T(8,128)(2,1)S(1)}, bf16[128,1024]{1,0:T(8,128)(2,1)S(1)}, u32[]{:S(2)}, u32[]{:S(2)}) %collective-permute-start.5) | collective-permute-done | bytes 262176 | tf_op jit(solution)/shard_map/ppermute | solution.py:18
  70.7 4.6 %all-gather.9.cloned.1.call-done = bf16[16384,256]{1,0:T(8,128)(2,1)} async-done(((bf16[2048,256]{1,0:T(8,128)(2,1)}), bf16[16384,256]{1,0:T(8,128)(2,1)}) %all-gather.9.cloned.1.call-update) | async-done | bytes 8388624 | tf_op jit(solution)/shard_map/all_gather | solution.py:333
  78.4 2.4 %collective-permute-start.8 = (bf16[128,1024]{1,0:T(8,128)(2,1)S(1)}, bf16[128,1024]{1,0:T(8,128)(2,1)S(1)}, u32[]{:S(2)}, u32[]{:S(2)}) collective-permute-start(bf16[128,1024]{1,0:T(8,128)(2,1)S(1)} %diag_step.3.refs_0_), channel_id=1, source_target_pairs={{0,8},{4,12},{8,0},{12,4},{1,9},{5,13},{9,1},{13,5},{2,10},{6,14},... | collective-permute-start | bytes 786440 | tf_op jit(solution)/shard_map/ppermute | solution.py:18
  82.2 3.9 %collective-permute-done.7.refs_1_ = bf16[128,1024]{1,0:T(8,128)(2,1)S(1)} collective-permute-done((bf16[128,1024]{1,0:T(8,128)(2,1)S(1)}, bf16[128,1024]{1,0:T(8,128)(2,1)S(1)}, u32[]{:S(2)}, u32[]{:S(2)}) %collective-permute-start.7) | collective-permute-done | bytes 262176 | tf_op jit(solution)/shard_map/ppermute | solution.py:18
  86.1 6.6 %collective-permute-done.8.refs_2_ = bf16[128,1024]{1,0:T(8,128)(2,1)S(1)} collective-permute-done((bf16[128,1024]{1,0:T(8,128)(2,1)S(1)}, bf16[128,1024]{1,0:T(8,128)(2,1)S(1)}, u32[]{:S(2)}, u32[]{:S(2)}) %collective-permute-start.8) | collective-permute-done | bytes 262176 | tf_op jit(solution)/shard_map/ppermute | solution.py:18
  96.1 2.6 %collective-permute-start.11 = (bf16[128,1024]{1,0:T(8,128)(2,1)S(1)}, bf16[128,1024]{1,0:T(8,128)(2,1)S(1)}, u32[]{:S(2)}, u32[]{:S(2)}) collective-permute-start(bf16[128,1024]{1,0:T(8,128)(2,1)S(1)} %get-tuple-element.25.v0), channel_id=1, source_target_pairs={{0,64},{32,96},{64,0},{96,32},{1,65},{33,97},{65,1},{97,33},{2,66}... | collective-permute-start | bytes 786440 | tf_op jit(solution)/shard_map/ppermute | solution.py:18
  99.7 3.1 %collective-permute-done.10.v1 = bf16[128,1024]{1,0:T(8,128)(2,1)S(1)} collective-permute-done((bf16[128,1024]{1,0:T(8,128)(2,1)S(1)}, bf16[128,1024]{1,0:T(8,128)(2,1)S(1)}, u32[]{:S(2)}, u32[]{:S(2)}) %collective-permute-start.10) | collective-permute-done | bytes 262176 | tf_op jit(solution)/shard_map/ppermute | solution.py:18
  102.8 6.7 %collective-permute-done.11.v2 = bf16[128,1024]{1,0:T(8,128)(2,1)S(1)} collective-permute-done((bf16[128,1024]{1,0:T(8,128)(2,1)S(1)}, bf16[128,1024]{1,0:T(8,128)(2,1)S(1)}, u32[]{:S(2)}, u32[]{:S(2)}) %collective-permute-start.11) | collective-permute-done | bytes 262176 | tf_op jit(solution)/shard_map/ppermute | solution.py:18
  112.5 3.6 %collective-permute-start.14 = (bf16[128,1024]{1,0:T(8,128)(2,1)S(1)}, bf16[128,1024]{1,0:T(8,128)(2,1)S(1)}, u32[]{:S(2)}, u32[]{:S(2)}) collective-permute-start(bf16[128,1024]{1,0:T(8,128)(2,1)S(1)} %diag_step.4.refs_0_), channel_id=1, source_target_pairs={{0,8},{4,12},{8,0},{12,4},{1,9},{5,13},{9,1},{13,5},{2,10},{6,14},... | collective-permute-start | bytes 786440 | tf_op jit(solution)/shard_map/ppermute | solution.py:18
  116.1 2.5 %lower_step.7 = (f32[128,1024]{1,0:T(8,128)S(1)}, bf16[128,1024]{1,0:T(8,128)(2,1)}) custom-call(bf16[128,1024]{1,0:T(8,128)(2,1)S(1)} %get-tuple-element.26.refs_0_.x3, f32[128,1024]{1,0:T(8,128)S(1)} %get-tuple-element.42.refs_1_, bf16[2,4,2048,256]{3,2,1,0:T(8,128)(2,1)} %bitcast.47), custom_call_target="tpu_custom_call" | custom-call | flops 268435456 | bytes 4194304 | tf_op jit(solution)/shard_map/lower_step/pallas_call | solution.py:107
  120.0 6.8 %collective-permute-done.14.refs_2_ = bf16[128,1024]{1,0:T(8,128)(2,1)S(1)} collective-permute-done((bf16[128,1024]{1,0:T(8,128)(2,1)S(1)}, bf16[128,1024]{1,0:T(8,128)(2,1)S(1)}, u32[]{:S(2)}, u32[]{:S(2)}) %collective-permute-start.14) | collective-permute-done | bytes 262176 | tf_op jit(solution)/shard_map/ppermute | solution.py:18
  130.1 3.6 %collective-permute-start.17 = (bf16[128,1024]{1,0:T(8,128)(2,1)S(1)}, bf16[128,1024]{1,0:T(8,128)(2,1)S(1)}, u32[]{:S(2)}, u32[]{:S(2)}) collective-permute-start(bf16[128,1024]{1,0:T(8,128)(2,1)S(1)} %get-tuple-element.29.v0), channel_id=1, source_target_pairs={{0,64},{32,96},{64,0},{96,32},{1,65},{33,97},{65,1},{97,33},{2,66}... | collective-permute-start | bytes 786440 | tf_op jit(solution)/shard_map/ppermute | solution.py:18
  133.7 4.0 %collective-permute-done.16.v1 = bf16[128,1024]{1,0:T(8,128)(2,1)S(1)} collective-permute-done((bf16[128,1024]{1,0:T(8,128)(2,1)S(1)}, bf16[128,1024]{1,0:T(8,128)(2,1)S(1)}, u32[]{:S(2)}, u32[]{:S(2)}) %collective-permute-start.16) | collective-permute-done | bytes 262176 | tf_op jit(solution)/shard_map/ppermute | solution.py:18
  137.7 6.7 %collective-permute-done.17.v2 = bf16[128,1024]{1,0:T(8,128)(2,1)S(1)} collective-permute-done((bf16[128,1024]{1,0:T(8,128)(2,1)S(1)}, bf16[128,1024]{1,0:T(8,128)(2,1)S(1)}, u32[]{:S(2)}, u32[]{:S(2)}) %collective-permute-start.17) | collective-permute-done | bytes 262176 | tf_op jit(solution)/shard_map/ppermute | solution.py:18
  146.5 2.4 %collective-permute-start.19 = (bf16[128,1024]{1,0:T(8,128)(2,1)S(1)}, bf16[128,1024]{1,0:T(8,128)(2,1)S(1)}, u32[]{:S(2)}, u32[]{:S(2)}) collective-permute-start(bf16[128,1024]{1,0:T(8,128)(2,1)S(1)} %diag_step.5.refs_0_), channel_id=1, source_target_pairs={{0,4},{4,8},{8,12},{12,0},{1,5},{5,9},{9,13},{13,1},{2,6},{6,10},{... | collective-permute-start | bytes 786440 | tf_op jit(solution)/shard_map/ppermute | solution.py:18
  151.4 2.5 %lower_step.9 = (f32[128,1024]{1,0:T(8,128)S(1)}, bf16[128,1024]{1,0:T(8,128)(2,1)}) custom-call(bf16[128,1024]{1,0:T(8,128)(2,1)S(1)} %get-tuple-element.26.refs_0_.x3, f32[128,1024]{1,0:T(8,128)S(1)} %get-tuple-element.41.refs_1_, bf16[2,4,1536,256]{3,2,1,0:T(8,128)(2,1)} %bitcast.55), custom_call_target="tpu_custom_call" | custom-call | flops 268435456 | bytes 4194304 | tf_op jit(solution)/shard_map/lower_step/pallas_call | solution.py:107
  153.9 7.2 %all-gather.7.cloned.1.call-done = bf16[12416,256]{1,0:T(8,128)(2,1)} async-done(((bf16[1552,256]{1,0:T(8,128)(2,1)}), bf16[12416,256]{1,0:T(8,128)(2,1)}) %all-gather.7.cloned.1.call-update) | async-done | bytes 6357008 | tf_op jit(solution)/shard_map/all_gather | solution.py:333
  161.1 2.5 %lower_step.10 = (f32[128,1024]{1,0:T(8,128)S(1)}, bf16[128,1024]{1,0:T(8,128)(2,1)}) custom-call(bf16[128,1024]{1,0:T(8,128)(2,1)S(1)} %get-tuple-element.30.refs_0_.x2, f32[128,1024]{1,0:T(8,128)S(1)} %get-tuple-element.31.refs_1_, bf16[2,4,1552,256]{3,2,1,0:T(8,128)(2,1)} %bitcast.48), custom_call_target="tpu_custom_call" | custom-call | flops 268435456 | bytes 4194304 | tf_op jit(solution)/shard_map/lower_step/pallas_call | solution.py:107
  167.0 2.6 %collective-permute-start.23 = (bf16[128,1024]{1,0:T(8,128)(2,1)S(1)}, bf16[128,1024]{1,0:T(8,128)(2,1)S(1)}, u32[]{:S(2)}, u32[]{:S(2)}) collective-permute-start(bf16[128,1024]{1,0:T(8,128)(2,1)S(1)} %get-tuple-element.35.v0), channel_id=1, source_target_pairs={{0,64},{32,96},{64,0},{96,32},{1,65},{33,97},{65,1},{97,33},{2,66}... | collective-permute-start | bytes 786440 | tf_op jit(solution)/shard_map/ppermute | solution.py:18
  174.6 6.6 %collective-permute-done.23.v2 = bf16[128,1024]{1,0:T(8,128)(2,1)S(1)} collective-permute-done((bf16[128,1024]{1,0:T(8,128)(2,1)S(1)}, bf16[128,1024]{1,0:T(8,128)(2,1)S(1)}, u32[]{:S(2)}, u32[]{:S(2)}) %collective-permute-start.23) | collective-permute-done | bytes 262176 | tf_op jit(solution)/shard_map/ppermute | solution.py:18
  181.2 2.5 %last_step.1 = (bf16[128,256]{1,0:T(8,128)(2,1)S(1)}, bf16[128,256]{1,0:T(8,128)(2,1)S(1)}, bf16[128,256]{1,0:T(8,128)(2,1)S(1)}, bf16[128,256]{1,0:T(8,128)(2,1)S(1)}) custom-call(s32[4]{0:T(128)S(1)} %pad_add_fusion.place_ref, bf16[128,1024]{1,0:T(8,128)(2,1)S(1)} %get-tuple-element.35.v0, bf16[128,1024]{1,0:T(8,128)(2,1)S(1)} %collective-permute-done.22.v1, ...), custom_call_target="tpu_custom_call" | custom-call | flops 268435456 | bytes 4194304 | tf_op jit(solution)/shard_map/last_step/pallas_call | solution.py:186
  185.2 2.4 %collective-permute-start.26 = (bf16[128,256]{1,0:T(8,128)(2,1)S(1)}, bf16[128,256]{1,0:T(8,128)(2,1)S(1)}, u32[]{:S(2)}, u32[]{:S(2)}) collective-permute-start(bf16[128,256]{1,0:T(8,128)(2,1)S(1)} %get-tuple-element.38), channel_id=1, source_target_pairs={{0,8},{4,12},{8,0},{12,4},{1,9},{5,13},{9,1},{13,5},{2,10},{6,14},... | collective-permute-start | bytes 196616 | tf_op jit(solution)/shard_map/ppermute | solution.py:18
  188.9 3.0 %pack_known.1 = (bf16[2048,128]{1,0:T(8,128)(2,1)S(1)}, bf16[2048,256]{1,0:T(8,128)(2,1)S(1)}) custom-call(s32[4]{0:T(128)S(1)} %pad_add_fusion.place_ref, s32[4,1,256]{2,1,0:T(1,128)S(1)} %reshape.76.target_ref, bf16[128,1024]{1,0:T(8,128)(2,1)S(1)} %get-tuple-element.33.x1, bf16[128,1024]{1,0:T(8,128)(2,1)S(1)} %get-tuple-element.30.refs_0_.x2, ...), custom_call_target="tpu_custom_call" | custom-call | flops 402653184 | bytes 2097152 | tf_op jit(solution)/shard_map/pack_known/pallas_call | solution.py:267
  192.4 22.0 %all_to_all.5 = bf16[128,16,128]{2,1,0:T(8,128)(2,1)S(1)} all-to-all(bf16[128,16,128]{2,1,0:T(8,128)(2,1)S(1)} %bitcast.43), channel_id=1, replica_groups=mesh['z'=4,'core'=2,'y'=4,'x'=4] {'z','core','y','x'}, dimensions={0} | all-to-all | bytes 1048576 | tf_op jit(solution)/shard_map/all_to_all | solution.py:387
  (68 shorter events, 44.9 us)
Async XLA Ops:
  6.5 68.8 %all-gather.9.cloned.1.call-start = ((), (), s32[]{:S(2)}) async-start(), calls=%async_computation.2 | async-start | bytes 9437184 | tf_op jit(solution)/shard_map/all_gather | solution.py:333
  10.6 108.0 %all-gather.11.cloned.1.call-start = ((), (), s32[]{:S(2)}) async-start(), calls=%async_computation.3 | async-start | bytes 7077888 | tf_op jit(solution)/shard_map/all_gather | solution.py:333
  11.3 149.8 %all-gather.7.cloned.1.call-start = ((), (), s32[]{:S(2)}) async-start(), calls=%async_computation.1 | async-start | bytes 7151616 | tf_op jit(solution)/shard_map/all_gather | solution.py:333
  17.9 7.4 %collective-permute-start = (bf16[4,256,512]{2,1,0:T(8,128)(2,1)S(1)}, bf16[4,256,512]{2,1,0:T(8,128)(2,1)S(1)}, u32[]{:S(2)}, u32[]{:S(2)}) collective-permute-start(bf16[4,256,512]{2,1,0:T(8,128)(2,1)S(1)} %fusion.6), channel_id=1, source_target_pairs={{0,16},{16,0},{1,17},{17,1},{2,18},{18,2},{3,19},{19,3},{4,20},{20... | collective-permute-start | bytes 3145736 | tf_op jit(solution)/shard_map/ppermute | solution.py:22
  25.9 15.0 %collective-permute-start.1 = (bf16[4,256,128]{2,1,0:T(8,128)(2,1)S(1)}, bf16[4,256,128]{2,1,0:T(8,128)(2,1)S(1)}, u32[]{:S(2)}, u32[]{:S(2)}) collective-permute-start(bf16[4,256,128]{2,1,0:T(8,128)(2,1)S(1)} %get-tuple-element.46), channel_id=1, source_target_pairs={{0,1},{1,2},{2,3},{3,0},{4,5},{5,6},{6,7},{7,4},{8,9},{9,10},{10,1... | collective-permute-start | bytes 786440 | tf_op jit(solution)/shard_map/ppermute | solution.py:18
  27.2 26.0 %collective-permute-start.2 = (bf16[4,256,128]{2,1,0:T(8,128)(2,1)S(1)}, bf16[4,256,128]{2,1,0:T(8,128)(2,1)S(1)}, u32[]{:S(2)}, u32[]{:S(2)}) collective-permute-start(bf16[4,256,128]{2,1,0:T(8,128)(2,1)S(1)} %get-tuple-element.45), channel_id=1, source_target_pairs={{0,2},{1,3},{2,0},{3,1},{4,6},{5,7},{6,4},{7,5},{8,10},{9,11},{10,... | collective-permute-start | bytes 786440 | tf_op jit(solution)/shard_map/ppermute | solution.py:18
  29.7 23.5 %collective-permute-start.3 = (bf16[4,256,128]{2,1,0:T(8,128)(2,1)S(1)}, bf16[4,256,128]{2,1,0:T(8,128)(2,1)S(1)}, u32[]{:S(2)}, u32[]{:S(2)}) collective-permute-start(bf16[4,256,128]{2,1,0:T(8,128)(2,1)S(1)} %get-tuple-element.44), channel_id=1, source_target_pairs={{0,3},{1,0},{2,1},{3,2},{4,7},{5,4},{6,5},{7,6},{8,11},{9,8},{10,9... | collective-permute-start | bytes 786440 | tf_op jit(solution)/shard_map/ppermute | solution.py:18
  54.1 10.2 %collective-permute-start.4 = (bf16[128,1024]{1,0:T(8,128)(2,1)S(1)}, bf16[128,1024]{1,0:T(8,128)(2,1)S(1)}, u32[]{:S(2)}, u32[]{:S(2)}) collective-permute-start(bf16[128,1024]{1,0:T(8,128)(2,1)S(1)} %fusion.18.v0), channel_id=1, source_target_pairs={{0,32},{32,64},{64,96},{96,0},{1,33},{33,65},{65,97},{97,1},{2,34}... | collective-permute-start | bytes 786440 | tf_op jit(solution)/shard_map/ppermute | solution.py:18
  56.0 14.7 %collective-permute-start.5 = (bf16[128,1024]{1,0:T(8,128)(2,1)S(1)}, bf16[128,1024]{1,0:T(8,128)(2,1)S(1)}, u32[]{:S(2)}, u32[]{:S(2)}) collective-permute-start(bf16[128,1024]{1,0:T(8,128)(2,1)S(1)} %fusion.18.v0), channel_id=1, source_target_pairs={{0,64},{32,96},{64,0},{96,32},{1,65},{33,97},{65,1},{97,33},{2,66}... | collective-permute-start | bytes 786440 | tf_op jit(solution)/shard_map/ppermute | solution.py:18
  59.5 11.2 %collective-permute-start.6 = (bf16[128,1024]{1,0:T(8,128)(2,1)S(1)}, bf16[128,1024]{1,0:T(8,128)(2,1)S(1)}, u32[]{:S(2)}, u32[]{:S(2)}) collective-permute-start(bf16[128,1024]{1,0:T(8,128)(2,1)S(1)} %fusion.18.v0), channel_id=1, source_target_pairs={{0,96},{32,0},{64,32},{96,64},{1,97},{33,1},{65,33},{97,65},{2,98}... | collective-permute-start | bytes 786440 | tf_op jit(solution)/shard_map/ppermute | solution.py:18
  77.2 8.9 %collective-permute-start.7 = (bf16[128,1024]{1,0:T(8,128)(2,1)S(1)}, bf16[128,1024]{1,0:T(8,128)(2,1)S(1)}, u32[]{:S(2)}, u32[]{:S(2)}) collective-permute-start(bf16[128,1024]{1,0:T(8,128)(2,1)S(1)} %diag_step.3.refs_0_), channel_id=1, source_target_pairs={{0,4},{4,8},{8,12},{12,0},{1,5},{5,9},{9,13},{13,1},{2,6},{6,10},{... | collective-permute-start | bytes 786440 | tf_op jit(solution)/shard_map/ppermute | solution.py:18
  78.4 14.2 %collective-permute-start.8 = (bf16[128,1024]{1,0:T(8,128)(2,1)S(1)}, bf16[128,1024]{1,0:T(8,128)(2,1)S(1)}, u32[]{:S(2)}, u32[]{:S(2)}) collective-permute-start(bf16[128,1024]{1,0:T(8,128)(2,1)S(1)} %diag_step.3.refs_0_), channel_id=1, source_target_pairs={{0,8},{4,12},{8,0},{12,4},{1,9},{5,13},{9,1},{13,5},{2,10},{6,14},... | collective-permute-start | bytes 786440 | tf_op jit(solution)/shard_map/ppermute | solution.py:18
  80.9 11.8 %collective-permute-start.9 = (bf16[128,1024]{1,0:T(8,128)(2,1)S(1)}, bf16[128,1024]{1,0:T(8,128)(2,1)S(1)}, u32[]{:S(2)}, u32[]{:S(2)}) collective-permute-start(bf16[128,1024]{1,0:T(8,128)(2,1)S(1)} %diag_step.3.refs_0_), channel_id=1, source_target_pairs={{0,12},{4,0},{8,4},{12,8},{1,13},{5,1},{9,5},{13,9},{2,14},{6,2},{... | collective-permute-start | bytes 786440 | tf_op jit(solution)/shard_map/ppermute | solution.py:18
  94.7 8.1 %collective-permute-start.10 = (bf16[128,1024]{1,0:T(8,128)(2,1)S(1)}, bf16[128,1024]{1,0:T(8,128)(2,1)S(1)}, u32[]{:S(2)}, u32[]{:S(2)}) collective-permute-start(bf16[128,1024]{1,0:T(8,128)(2,1)S(1)} %get-tuple-element.25.v0), channel_id=1, source_target_pairs={{0,32},{32,64},{64,96},{96,0},{1,33},{33,65},{65,97},{97,1},{2,34}... | collective-permute-start | bytes 786440 | tf_op jit(solution)/shard_map/ppermute | solution.py:18
  96.1 13.5 %collective-permute-start.11 = (bf16[128,1024]{1,0:T(8,128)(2,1)S(1)}, bf16[128,1024]{1,0:T(8,128)(2,1)S(1)}, u32[]{:S(2)}, u32[]{:S(2)}) collective-permute-start(bf16[128,1024]{1,0:T(8,128)(2,1)S(1)} %get-tuple-element.25.v0), channel_id=1, source_target_pairs={{0,64},{32,96},{64,0},{96,32},{1,65},{33,97},{65,1},{97,33},{2,66}... | collective-permute-start | bytes 786440 | tf_op jit(solution)/shard_map/ppermute | solution.py:18
  98.6 10.9 %collective-permute-start.12 = (bf16[128,1024]{1,0:T(8,128)(2,1)S(1)}, bf16[128,1024]{1,0:T(8,128)(2,1)S(1)}, u32[]{:S(2)}, u32[]{:S(2)}) collective-permute-start(bf16[128,1024]{1,0:T(8,128)(2,1)S(1)} %get-tuple-element.25.v0), channel_id=1, source_target_pairs={{0,96},{32,0},{64,32},{96,64},{1,97},{33,1},{65,33},{97,65},{2,98}... | collective-permute-start | bytes 786440 | tf_op jit(solution)/shard_map/ppermute | solution.py:18
  111.5 8.6 %collective-permute-start.13 = (bf16[128,1024]{1,0:T(8,128)(2,1)S(1)}, bf16[128,1024]{1,0:T(8,128)(2,1)S(1)}, u32[]{:S(2)}, u32[]{:S(2)}) collective-permute-start(bf16[128,1024]{1,0:T(8,128)(2,1)S(1)} %diag_step.4.refs_0_), channel_id=1, source_target_pairs={{0,4},{4,8},{8,12},{12,0},{1,5},{5,9},{9,13},{13,1},{2,6},{6,10},{... | collective-permute-start | bytes 786440 | tf_op jit(solution)/shard_map/ppermute | solution.py:18
  112.5 14.3 %collective-permute-start.14 = (bf16[128,1024]{1,0:T(8,128)(2,1)S(1)}, bf16[128,1024]{1,0:T(8,128)(2,1)S(1)}, u32[]{:S(2)}, u32[]{:S(2)}) collective-permute-start(bf16[128,1024]{1,0:T(8,128)(2,1)S(1)} %diag_step.4.refs_0_), channel_id=1, source_target_pairs={{0,8},{4,12},{8,0},{12,4},{1,9},{5,13},{9,1},{13,5},{2,10},{6,14},... | collective-permute-start | bytes 786440 | tf_op jit(solution)/shard_map/ppermute | solution.py:18
  116.1 10.8 %collective-permute-start.15 = (bf16[128,1024]{1,0:T(8,128)(2,1)S(1)}, bf16[128,1024]{1,0:T(8,128)(2,1)S(1)}, u32[]{:S(2)}, u32[]{:S(2)}) collective-permute-start(bf16[128,1024]{1,0:T(8,128)(2,1)S(1)} %diag_step.4.refs_0_), channel_id=1, source_target_pairs={{0,12},{4,0},{8,4},{12,8},{1,13},{5,1},{9,5},{13,9},{2,14},{6,2},{... | collective-permute-start | bytes 786440 | tf_op jit(solution)/shard_map/ppermute | solution.py:18
  129.0 8.8 %collective-permute-start.16 = (bf16[128,1024]{1,0:T(8,128)(2,1)S(1)}, bf16[128,1024]{1,0:T(8,128)(2,1)S(1)}, u32[]{:S(2)}, u32[]{:S(2)}) collective-permute-start(bf16[128,1024]{1,0:T(8,128)(2,1)S(1)} %get-tuple-element.29.v0), channel_id=1, source_target_pairs={{0,32},{32,64},{64,96},{96,0},{1,33},{33,65},{65,97},{97,1},{2,34}... | collective-permute-start | bytes 786440 | tf_op jit(solution)/shard_map/ppermute | solution.py:18
  130.1 14.3 %collective-permute-start.17 = (bf16[128,1024]{1,0:T(8,128)(2,1)S(1)}, bf16[128,1024]{1,0:T(8,128)(2,1)S(1)}, u32[]{:S(2)}, u32[]{:S(2)}) collective-permute-start(bf16[128,1024]{1,0:T(8,128)(2,1)S(1)} %get-tuple-element.29.v0), channel_id=1, source_target_pairs={{0,64},{32,96},{64,0},{96,32},{1,65},{33,97},{65,1},{97,33},{2,66}... | collective-permute-start | bytes 786440 | tf_op jit(solution)/shard_map/ppermute | solution.py:18
  133.7 10.8 %collective-permute-start.18 = (bf16[128,1024]{1,0:T(8,128)(2,1)S(1)}, bf16[128,1024]{1,0:T(8,128)(2,1)S(1)}, u32[]{:S(2)}, u32[]{:S(2)}) collective-permute-start(bf16[128,1024]{1,0:T(8,128)(2,1)S(1)} %get-tuple-element.29.v0), channel_id=1, source_target_pairs={{0,96},{32,0},{64,32},{96,64},{1,97},{33,1},{65,33},{97,65},{2,98}... | collective-permute-start | bytes 786440 | tf_op jit(solution)/shard_map/ppermute | solution.py:18
  146.5 17.1 %collective-permute-start.19 = (bf16[128,1024]{1,0:T(8,128)(2,1)S(1)}, bf16[128,1024]{1,0:T(8,128)(2,1)S(1)}, u32[]{:S(2)}, u32[]{:S(2)}) collective-permute-start(bf16[128,1024]{1,0:T(8,128)(2,1)S(1)} %diag_step.5.refs_0_), channel_id=1, source_target_pairs={{0,4},{4,8},{8,12},{12,0},{1,5},{5,9},{9,13},{13,1},{2,6},{6,10},{... | collective-permute-start | bytes 786440 | tf_op jit(solution)/shard_map/ppermute | solution.py:18
  148.9 14.7 %collective-permute-start.20 = (bf16[128,1024]{1,0:T(8,128)(2,1)S(1)}, bf16[128,1024]{1,0:T(8,128)(2,1)S(1)}, u32[]{:S(2)}, u32[]{:S(2)}) collective-permute-start(bf16[128,1024]{1,0:T(8,128)(2,1)S(1)} %diag_step.5.refs_0_), channel_id=1, source_target_pairs={{0,8},{4,12},{8,0},{12,4},{1,9},{5,13},{9,1},{13,5},{2,10},{6,14},... | collective-permute-start | bytes 786440 | tf_op jit(solution)/shard_map/ppermute | solution.py:18
  151.1 12.6 %collective-permute-start.21 = (bf16[128,1024]{1,0:T(8,128)(2,1)S(1)}, bf16[128,1024]{1,0:T(8,128)(2,1)S(1)}, u32[]{:S(2)}, u32[]{:S(2)}) collective-permute-start(bf16[128,1024]{1,0:T(8,128)(2,1)S(1)} %diag_step.5.refs_0_), channel_id=1, source_target_pairs={{0,12},{4,0},{8,4},{12,8},{1,13},{5,1},{9,5},{13,9},{2,14},{6,2},{... | collective-permute-start | bytes 786440 | tf_op jit(solution)/shard_map/ppermute | solution.py:18
  165.7 8.9 %collective-permute-start.22 = (bf16[128,1024]{1,0:T(8,128)(2,1)S(1)}, bf16[128,1024]{1,0:T(8,128)(2,1)S(1)}, u32[]{:S(2)}, u32[]{:S(2)}) collective-permute-start(bf16[128,1024]{1,0:T(8,128)(2,1)S(1)} %get-tuple-element.35.v0), channel_id=1, source_target_pairs={{0,32},{32,64},{64,96},{96,0},{1,33},{33,65},{65,97},{97,1},{2,34}... | collective-permute-start | bytes 786440 | tf_op jit(solution)/shard_map/ppermute | solution.py:18
  167.0 14.2 %collective-permute-start.23 = (bf16[128,1024]{1,0:T(8,128)(2,1)S(1)}, bf16[128,1024]{1,0:T(8,128)(2,1)S(1)}, u32[]{:S(2)}, u32[]{:S(2)}) collective-permute-start(bf16[128,1024]{1,0:T(8,128)(2,1)S(1)} %get-tuple-element.35.v0), channel_id=1, source_target_pairs={{0,64},{32,96},{64,0},{96,32},{1,65},{33,97},{65,1},{97,33},{2,66}... | collective-permute-start | bytes 786440 | tf_op jit(solution)/shard_map/ppermute | solution.py:18
  169.6 11.6 %collective-permute-start.24 = (bf16[128,1024]{1,0:T(8,128)(2,1)S(1)}, bf16[128,1024]{1,0:T(8,128)(2,1)S(1)}, u32[]{:S(2)}, u32[]{:S(2)}) collective-permute-start(bf16[128,1024]{1,0:T(8,128)(2,1)S(1)} %get-tuple-element.35.v0), channel_id=1, source_target_pairs={{0,96},{32,0},{64,32},{96,64},{1,97},{33,1},{65,33},{97,65},{2,98}... | collective-permute-start | bytes 786440 | tf_op jit(solution)/shard_map/ppermute | solution.py:18
  183.7 8.3 %collective-permute-start.25 = (bf16[128,256]{1,0:T(8,128)(2,1)S(1)}, bf16[128,256]{1,0:T(8,128)(2,1)S(1)}, u32[]{:S(2)}, u32[]{:S(2)}) collective-permute-start(bf16[128,256]{1,0:T(8,128)(2,1)S(1)} %get-tuple-element.37), channel_id=1, source_target_pairs={{0,4},{4,8},{8,12},{12,0},{1,5},{5,9},{9,13},{13,1},{2,6},{6,10},{... | collective-permute-start | bytes 196616 | tf_op jit(solution)/shard_map/ppermute | solution.py:18
  185.2 6.8 %collective-permute-start.26 = (bf16[128,256]{1,0:T(8,128)(2,1)S(1)}, bf16[128,256]{1,0:T(8,128)(2,1)S(1)}, u32[]{:S(2)}, u32[]{:S(2)}) collective-permute-start(bf16[128,256]{1,0:T(8,128)(2,1)S(1)} %get-tuple-element.38), channel_id=1, source_target_pairs={{0,8},{4,12},{8,0},{12,4},{1,9},{5,13},{9,1},{13,5},{2,10},{6,14},... | collective-permute-start | bytes 196616 | tf_op jit(solution)/shard_map/ppermute | solution.py:18
  187.6 4.4 %collective-permute-start.27 = (bf16[128,256]{1,0:T(8,128)(2,1)S(1)}, bf16[128,256]{1,0:T(8,128)(2,1)S(1)}, u32[]{:S(2)}, u32[]{:S(2)}) collective-permute-start(bf16[128,256]{1,0:T(8,128)(2,1)S(1)} %get-tuple-element.39), channel_id=1, source_target_pairs={{0,12},{4,0},{8,4},{12,8},{1,13},{5,1},{9,5},{13,9},{2,14},{6,2},{... | collective-permute-start | bytes 196616 | tf_op jit(solution)/shard_map/ppermute | solution.py:18
Sparse Core Ops, SparseCore 0:
  10.7 64.5 all-gather.8
  77.0 41.0 all-gather.10
  119.8 41.2 all-gather.6

commit v5 on v4

--- a/solution.py
+++ b/solution.py
@@ -22,6 +22,11 @@
     return lax.ppermute(value, "core", [(0, 1), (1, 0)])
 
 
+def along_x(value, core, by):
+    pairs = [(core * 4 + i, core * 4 + (i + by) % 4) for i in range(4)]
+    return lax.ppermute(value, ("core", "x"), pairs)
+
+
 def spread(value, axis):
     far = shift(value, axis, 2)
     right = shift(value, axis, 1)
@@ -60,25 +65,91 @@
 HBM = pl.BlockSpec(memory_space=pltpu.HBM)
 
 
-def turn(place, pieces, dtype):
-    blocks = pieces[0].shape[0]
-
-    def kernel(place_ref, v0, v1, v2, v3, out):
-        for step, ref in enumerate((v0, v1, v2, v3)):
-            start = lax.rem(place_ref[2] + 4 - step, 4) * 256
-            lanes = pl.ds(pl.multiple_of(start, 256), 256)
-            for k in range(blocks):
-                out[k, :, lanes] = ref[k].astype(F32).T.astype(dtype)
-
-    return pl.pallas_call(
-        kernel,
-        out_shape=jax.ShapeDtypeStruct((blocks, 128, 1024), dtype),
-        in_specs=[SCALARS] + [VMEM] * 4,
+def first_product(place, pieces, mine, other, rest):
+    def kernel(place_ref, v0, v1, v2, v3, mine_ref, other_ref, rest_ref, *refs):
+        outs, turned = refs[:4], refs[4]
+        core, x = place_ref[0], place_ref[2]
+        turned[...] = add_up((v0, v1, v2, v3)).T.astype(BF16)
+        for step, out in enumerate(outs):
+            start = pl.multiple_of(lax.rem(x + step, 4) * 128, 128)
+            left = turned[pl.ds(start, 128), :]
+            for side, tile in ((core, mine_ref), (1 - core, other_ref)):
+                product = jnp.dot(left, tile[...], preferred_element_type=F32).astype(BF16)
+                for block in range(4):
+                    rows = pl.ds(pl.multiple_of((side * 4 + block) * 128, 128), 128)
+                    out[rows, :] = product[:, block * 128 : (block + 1) * 128]
+            for k in range(3):
+                out[1024 + k * 256 : 1280 + k * 256, :] = rest_ref[k, :, pl.ds(start, 128)]
+
+    return pl.pallas_call(
+        kernel,
+        out_shape=(jax.ShapeDtypeStruct((1792, 128), BF16),) * 4,
+        in_specs=[SCALARS] + [VMEM] * 7,
+        out_specs=(VMEM,) * 4,
+        scratch_shapes=[pltpu.VMEM((512, 256), BF16)],
+        compiler_params=params(),
+        cost_estimate=cost(2 * 512 * 256 * 1024, 4 << 20),
+        name="first_product",
+    )(place, *pieces, mine, other, rest)
+
+
+def by_core(place_ref, parcels, body):
+    own, zero, one = parcels[0], parcels[1:4], parcels[4:7]
+
+    @pl.when(place_ref[0] == 0)
+    def _():
+        body((own, *zero))
+
+    @pl.when(place_ref[0] == 1)
+    def _():
+        body((own, *one))
+
+
+def first_sum(place, parcels):
+    def kernel(place_ref, *refs):
+        out = refs[7]
+
+        def body(parts):
+            for block in range(8):
+                rows = slice(block * 128, (block + 1) * 128)
+                out[:, rows] = add_up([part.at[rows] for part in parts]).astype(BF16)
+
+        by_core(place_ref, refs[:7], body)
+
+    return pl.pallas_call(
+        kernel,
+        out_shape=jax.ShapeDtypeStruct((128, 1024), BF16),
+        in_specs=[SCALARS] + [VMEM] * 7,
         out_specs=VMEM,
         compiler_params=params(),
-        cost_estimate=cost(blocks * 128 * 1024, blocks << 20),
+        cost_estimate=cost(4 * 128 * 1024, 2 << 20),
+        name="first_sum",
+    )(place, *parcels)
+
+
+def turn(place, parcels):
+    def kernel(place_ref, *refs):
+        out = refs[7]
+
+        def body(parts):
+            for step, part in enumerate(parts):
+                start = lax.rem(place_ref[2] + 4 - step, 4) * 256
+                lanes = pl.ds(pl.multiple_of(start, 256), 256)
+                for k in range(3):
+                    rows = part[1024 + k * 256 : 1280 + k * 256, :]
+                    out[k, :, lanes] = rows.astype(F32).T
+
+        by_core(place_ref, refs[:7], body)
+
+    return pl.pallas_call(
+        kernel,
+        out_shape=jax.ShapeDtypeStruct((3, 128, 1024), F32),
+        in_specs=[SCALARS] + [VMEM] * 7,
+        out_specs=VMEM,
+        compiler_params=params(),
+        cost_estimate=cost(3 * 128 * 1024, 4 << 20),
         name="turn",
-    )(place, *pieces)
+    )(place, *parcels)
 
 
 def lower_step(base, pieces, tiles, at, dtype):
@@ -343,12 +414,12 @@
 
     owners = jnp.pad(owner_map[0, :, 0].astype(BF16)[None], ((0, 15), (0, 128)))
     orders = [
-        [("D", 3), tile(3, 2), ("D", 2), tile(3, 1)],
-        [tile(2, 1), ("D", 1), tile(3, 0)],
-        [tile(2, 0), tile(1, 0), ("D", 0)],
+        [tile(3, 2), ("D", 2), tile(3, 1), tile(2, 1), ("D", 1)],
+        [tile(3, 0), tile(2, 0), tile(1, 0), ("D", 0)],
     ]
-    early, middle, late = map(gathered, stage(lower_tiles, inverse_diag, orders, owners))
-    named = late[:, :, 1536, :128].astype(jnp.int32).reshape(8, 128)
+    early, late = map(gathered, stage(lower_tiles, inverse_diag, orders, owners))
+    named = late[:, :, 2048, :128].astype(jnp.int32).reshape(8, 128)
+    other = swap(inverse_diag[3])
 
     def term(side):
         start = side * 512
@@ -362,27 +433,27 @@
     away = swap(term(1 - core))
     home = lax.optimization_barrier(term(core))
     both = (home.astype(F32) + away.astype(F32)).astype(BF16)
-    cut = [
-        lax.dynamic_slice_in_dim(both, lax.rem(x + by, 4) * 128, 128, axis=2) for by in range(4)
-    ]
-
-    base = turn(place, deal(cut, "x"), F32)
-    base3 = base[3].astype(BF16)
-    over_z = spread(base3, "z")
-    pieces = spread(diag_step(over_z, early, 0), "y")
-    residual, x3 = lower_step(base[2], pieces, early, 1, BF16)
+    over_z = spread(both[3], "z")
+    own, *parcels = first_product(place, over_z, inverse_diag[3], other, both[:3])
+    zero = [along_x(parcels[by - 1], 0, by) for by in (1, 2, 3)]
+    token = lax.ppermute(sum(parcel[:8] for parcel in zero), "core", [(0, 1)])
+    one = [along_x(parcels[by - 1] + token[0, 0] * 0, 1, by) for by in (1, 2, 3)]
+    parcels = (own, *zero, *one)
+    pieces = spread(first_sum(place, parcels), "y")
+    base = turn(place, parcels)
+    residual, x3 = lower_step(base[2], pieces, early, 0, BF16)
     over_z = spread(residual, "z")
-    pieces = spread(diag_step(over_z, early, 2), "y")
-    base1, _ = lower_step(base[1], (x3,), early, 3, F32)
-    residual, x2 = lower_step(base1, pieces, middle, 0, BF16)
+    pieces = spread(diag_step(over_z, early, 1), "y")
+    base1, _ = lower_step(base[1], (x3,), early, 2, F32)
+    residual, x2 = lower_step(base1, pieces, early, 3, BF16)
     over_z = spread(residual, "z")
-    base0, _ = lower_step(base[0], (x3,), middle, 2, F32)
-    pieces = spread(diag_step(over_z, middle, 1), "y")
-    base0, _ = lower_step(base0, (x2,), late, 0, F32)
-    residual, x1 = lower_step(base0, pieces, late, 1, BF16)
+    pieces = spread(diag_step(over_z, early, 4), "y")
+    base0, _ = lower_step(base[0], (x3,), late, 0, F32)
+    base0, _ = lower_step(base0, (x2,), late, 1, F32)
+    residual, x1 = lower_step(base0, pieces, late, 2, BF16)
     over_z = spread(residual, "z")
     packed, still = pack_known(place, slots_of(named), (x1, x2, x3))
-    rows = deal(last_step(place, over_z, late, 2), "y")
+    rows = deal(last_step(place, over_z, late, 3), "y")
     packed = pack_last(still, rows, packed).reshape(128, 16, 128)
     received = lax.all_to_all(
         packed, ("z", "core", "y", "x"), split_axis=0, concat_axis=0, tiled=True

time: 223 us -> 245 us (1.099)
  waiting for transfers between devices: 94 us -> 109 us
  starting transfers between devices: 46.8 us -> 53.1 us
    ppermute x0 -> x7, waiting for transfers between devices: none -> 54.8 us  [the longest x1 35.5 us: local(): token = lax.ppermute(sum((parcel[:8] for parcel in zero)), 'core', [(0, 1)])]
    ppermute x27 -> x24, waiting for transfers between devices: 80.8 us -> 53.5 us  [shift(): return lax.ppermute(value, axis, [(i, (i + by) % 4) for i in range(4)])]
    all_gather x3 -> x2, waiting for transfers between devices: 11.8 us -> 0.02 us  [gathered(): lax.all_gather(joined, ('core', 'x'), axis=0, tiled=False)]
    ppermute x0 -> x7, starting transfers between devices: none -> 11.6 us  [the longest x6 10.3 us: along_x(): return lax.ppermute(value, ('core', 'x'), pairs)]
    ppermute x27 -> x24, starting transfers between devices: 45.2 us -> 39.8 us  [shift(): return lax.ppermute(value, axis, [(i, (i + by) % 4) for i in range(4)])]
    pallas_call x3 -> x2, Pallas kernels: 5.72 us -> 3.74 us  [diag_step(): pl.pallas_call(kernel, out_shape=jax.ShapeDtypeStruct((128, 1024), BF16),...]
  transfers between devices with their start and end apart: 31 -> 35, of which waited for: 18 -> 21; matrix products, arithmetic and copies ran while one was open for 7% -> 7% of each run, Pallas kernels for 10% -> 9%
where the time goes in v5:
time: 245 us
  waiting for transfers between devices  109 us (44%)
  starting transfers between devices  53.1 us (22%)
  Pallas kernels  30.3 us (12%)
  blocking collectives  20.3 us (8%)
  between operations  14.4 us (6%)
  matrix products  11.9 us (5%)
  other arithmetic  3.08 us (1%)
  local copies, waits for them, and re-layouts  2.51 us (1%)
    ppermute x24, waiting for transfers between devices, shift(): return lax.ppermute(value, axis, [(i, (i + by) % 4) for i in range(4)])  53.5 us
    ppermute x24, starting transfers between devices, shift(): return lax.ppermute(value, axis, [(i, (i + by) % 4) for i in range(4)])  39.8 us
    ppermute x1, waiting for transfers between devices, local(): token = lax.ppermute(sum((parcel[:8] for parcel in zero)), 'core', [(0, 1)])  35.5 us
    all_to_all x1, blocking collectives, local(): lax.all_to_all(packed, ('z', 'core', 'y', 'x'), split_axis=0, concat_axis...  20.3 us
    ppermute x6, waiting for transfers between devices, along_x(): return lax.ppermute(value, ('core', 'x'), pairs)  19.3 us
    pallas_call x6, Pallas kernels, lower_step(): pl.pallas_call(kernel, out_shape=(jax.ShapeDtypeStruct((128, 1024), dtype...  13.7 us
    dot_general x2, matrix products, term(): lax.dot_general(border_tiles, bound, (((0,), (0,)), ((), ())), preferred_...  11.9 us
    ppermute x6, starting transfers between devices, along_x(): return lax.ppermute(value, ('core', 'x'), pairs)  10.3 us
  transfers between devices with their start and end apart: 35, of which 21 were waited for; matrix products, arithmetic and copies ran while one was open for 7% of the time, Pallas kernels for 9%

profile of v5, /device:TPU:1, one launch (start us, length us, event | category | flops | bytes accessed | tf_op | source)
XLA Modules:
  0.0 244.6 jit_solution(15207631158414055084)
XLA Ops:
  7.8 2.7 %stage.1 = (bf16[2560,256]{1,0:T(8,128)(2,1)}, bf16[2064,256]{1,0:T(8,128)(2,1)}) custom-call(bf16[6,512,256]{2,1,0:T(8,128)(2,1)} %lower_ref.1, bf16[4,256,512]{2,1,0:T(8,128)(2,1)} %diag_ref.1, bf16[16,256]{1,0:T(8,128)(2,1)} %pad.4.owners_ref), custom_call_target="tpu_custom_call" | custom-call | bytes 6291456 | tf_op jit(solution)/shard_map/stage/pallas_call | solution.py:302
  11.3 5.9 %fusion.6 = bf16[4,256,512]{2,1,0:T(8,128)(2,1)S(1)} fusion(f32[4,256,1024]{2,1,0:T(8,128)} %param.6, s32[]{:T(128)S(6)} %select_n.14, bf16[2048,4,256]{2,1,0:T(4,128)(2,1)} %param.8, bf16[2048,1024]{1,0:T(8,128)(2,1)} %param.7, f32[]{:T(128)S(6)} %select_n.12), kind=kOutput, calls=%fused_computation.7 | convolution fusion | flops 2149056512 | bytes 9438720 | tf_op jit(solution)/shard_map/dot_general | solution.py:428
  19.7 6.0 %fusion.7 = bf16[4,256,512]{2,1,0:T(8,128)(2,1)S(1)} fusion(f32[4,256,1024]{2,1,0:T(8,128)} %param.6, s32[]{:T(128)S(6)} %select_n.13, bf16[2048,4,256]{2,1,0:T(4,128)(2,1)} %param.8, bf16[2048,1024]{1,0:T(8,128)(2,1)} %param.7, f32[]{:T(128)S(6)} %select_n.12), kind=kOutput, calls=%fused_computation.9 | convolution fusion | flops 2149056512 | bytes 9438720 | tf_op jit(solution)/shard_map/dot_general | solution.py:428
  27.9 3.6 %collective-permute-start.2 = (bf16[256,512]{1,0:T(8,128)(2,1)S(1)}, bf16[256,512]{1,0:T(8,128)(2,1)S(1)}, u32[]{:S(2)}, u32[]{:S(2)}) collective-permute-start(bf16[256,512]{1,0:T(8,128)(2,1)S(1)} %slice_bitcast_fusion.3.v0), channel_id=1, source_target_pairs={{0,64},{32,96},{64,0},{96,32},{1,65},{33,97},{65,1},{97,33},{2,66}... | collective-permute-start | bytes 786440 | tf_op jit(solution)/shard_map/ppermute | solution.py:18
  32.2 4.4 %collective-permute-done.1.v1 = bf16[256,512]{1,0:T(8,128)(2,1)S(1)} collective-permute-done((bf16[256,512]{1,0:T(8,128)(2,1)S(1)}, bf16[256,512]{1,0:T(8,128)(2,1)S(1)}, u32[]{:S(2)}, u32[]{:S(2)}) %collective-permute-start.1) | collective-permute-done | bytes 262176 | tf_op jit(solution)/shard_map/ppermute | solution.py:18
  36.6 6.4 %collective-permute-done.2.v2 = bf16[256,512]{1,0:T(8,128)(2,1)S(1)} collective-permute-done((bf16[256,512]{1,0:T(8,128)(2,1)S(1)}, bf16[256,512]{1,0:T(8,128)(2,1)S(1)}, u32[]{:S(2)}, u32[]{:S(2)}) %collective-permute-start.2) | collective-permute-done | bytes 262176 | tf_op jit(solution)/shard_map/ppermute | solution.py:18
  47.7 35.5 %collective-permute-done.8 = bf16[8,128]{1,0:T(8,128)(2,1)S(1)} collective-permute-done((bf16[8,128]{1,0:T(8,128)(2,1)S(1)}, bf16[8,128]{1,0:T(8,128)(2,1)S(1)}, u32[]{:S(2)}, u32[]{:S(2)}) %collective-permute-start.8) | collective-permute-done | bytes 2080 | tf_op jit(solution)/shard_map/ppermute | solution.py:439
  86.4 3.6 %collective-permute-start.10 = (bf16[1792,128]{1,0:T(8,128)(2,1)S(1)}, bf16[1792,128]{1,0:T(8,128)(2,1)S(1)}, u32[]{:S(2)}, u32[]{:S(2)}) collective-permute-start(bf16[1792,128]{1,0:T(8,128)(2,1)S(1)} %broadcast_add_fusion.1), channel_id=1, source_target_pairs={{16,18},{17,19},{18,16},{19,17},{20,22},{21,23},{22,20},{23,21},{2... | collective-permute-start | bytes 1376264 | tf_op jit(solution)/shard_map/ppermute | solution.py:27
  90.0 2.8 %collective-permute-start.9 = (bf16[1792,128]{1,0:T(8,128)(2,1)S(1)}, bf16[1792,128]{1,0:T(8,128)(2,1)S(1)}, u32[]{:S(2)}, u32[]{:S(2)}) collective-permute-start(bf16[1792,128]{1,0:T(8,128)(2,1)S(1)} %broadcast_add_fusion.2), channel_id=1, source_target_pairs={{16,17},{17,18},{18,19},{19,16},{20,21},{21,22},{22,23},{23,20},{2... | collective-permute-start | bytes 1376264 | tf_op jit(solution)/shard_map/ppermute | solution.py:27
  94.0 3.4 %collective-permute-done.10.refs_5_ = bf16[1792,128]{1,0:T(8,128)(2,1)S(1)} collective-permute-done((bf16[1792,128]{1,0:T(8,128)(2,1)S(1)}, bf16[1792,128]{1,0:T(8,128)(2,1)S(1)}, u32[]{:S(2)}, u32[]{:S(2)}) %collective-permute-start.10) | collective-permute-done | bytes 458784 | tf_op jit(solution)/shard_map/ppermute | solution.py:27
  97.4 14.6 %collective-permute-done.9.refs_4_ = bf16[1792,128]{1,0:T(8,128)(2,1)S(1)} collective-permute-done((bf16[1792,128]{1,0:T(8,128)(2,1)S(1)}, bf16[1792,128]{1,0:T(8,128)(2,1)S(1)}, u32[]{:S(2)}, u32[]{:S(2)}) %collective-permute-start.9) | collective-permute-done | bytes 458784 | tf_op jit(solution)/shard_map/ppermute | solution.py:27
  113.6 2.4 collective-permute-start.13
  120.1 5.8 %collective-permute-done.13.refs_2_ = bf16[128,1024]{1,0:T(8,128)(2,1)S(1)} collective-permute-done((bf16[128,1024]{1,0:T(8,128)(2,1)S(1)}, bf16[128,1024]{1,0:T(8,128)(2,1)S(1)}, u32[]{:S(2)}, u32[]{:S(2)}) %collective-permute-start.13) | collective-permute-done | bytes 262176 | tf_op jit(solution)/shard_map/ppermute | solution.py:18
  129.3 3.3 %collective-permute-start.16 = (bf16[128,1024]{1,0:T(8,128)(2,1)S(1)}, bf16[128,1024]{1,0:T(8,128)(2,1)S(1)}, u32[]{:S(2)}, u32[]{:S(2)}) collective-permute-start(bf16[128,1024]{1,0:T(8,128)(2,1)S(1)} %get-tuple-element.32.v0), channel_id=1, source_target_pairs={{0,64},{32,96},{64,0},{96,32},{1,65},{33,97},{65,1},{97,33},{2,66}... | collective-permute-start | bytes 786440 | tf_op jit(solution)/shard_map/ppermute | solution.py:18
  133.3 2.3 collective-permute-done.15.v1
  135.7 6.2 %collective-permute-done.16.v2 = bf16[128,1024]{1,0:T(8,128)(2,1)S(1)} collective-permute-done((bf16[128,1024]{1,0:T(8,128)(2,1)S(1)}, bf16[128,1024]{1,0:T(8,128)(2,1)S(1)}, u32[]{:S(2)}, u32[]{:S(2)}) %collective-permute-start.16) | collective-permute-done | bytes 262176 | tf_op jit(solution)/shard_map/ppermute | solution.py:18
  143.9 4.5 %collective-permute-start.18 = (bf16[128,1024]{1,0:T(8,128)(2,1)S(1)}, bf16[128,1024]{1,0:T(8,128)(2,1)S(1)}, u32[]{:S(2)}, u32[]{:S(2)}) collective-permute-start(bf16[128,1024]{1,0:T(8,128)(2,1)S(1)} %diag_step.2.refs_0_), channel_id=1, source_target_pairs={{0,4},{4,8},{8,12},{12,0},{1,5},{5,9},{9,13},{13,1},{2,6},{6,10},{... | collective-permute-start | bytes 786440 | tf_op jit(solution)/shard_map/ppermute | solution.py:18
  150.9 2.5 %lower_step.7 = (f32[128,1024]{1,0:T(8,128)S(1)}, bf16[128,1024]{1,0:T(8,128)(2,1)}) custom-call(bf16[128,1024]{1,0:T(8,128)(2,1)S(1)} %get-tuple-element.33.refs_0_.x3, f32[128,1024]{1,0:T(8,128)S(1)} %get-tuple-element.48.refs_1_, bf16[2,4,2560,256]{3,2,1,0:T(8,128)(2,1)} %bitcast.48), custom_call_target="tpu_custom_call" | custom-call | flops 268435456 | bytes 4194304 | tf_op jit(solution)/shard_map/lower_step/pallas_call | solution.py:178
  153.7 6.5 %collective-permute-done.19.refs_2_ = bf16[128,1024]{1,0:T(8,128)(2,1)S(1)} collective-permute-done((bf16[128,1024]{1,0:T(8,128)(2,1)S(1)}, bf16[128,1024]{1,0:T(8,128)(2,1)S(1)}, u32[]{:S(2)}, u32[]{:S(2)}) %collective-permute-start.19) | collective-permute-done | bytes 262176 | tf_op jit(solution)/shard_map/ppermute | solution.py:18
  162.8 2.7 %collective-permute-start.21 = (bf16[128,1024]{1,0:T(8,128)(2,1)S(1)}, bf16[128,1024]{1,0:T(8,128)(2,1)S(1)}, u32[]{:S(2)}, u32[]{:S(2)}) collective-permute-start(bf16[128,1024]{1,0:T(8,128)(2,1)S(1)} %get-tuple-element.35.v0), channel_id=1, source_target_pairs={{0,32},{32,64},{64,96},{96,0},{1,33},{33,65},{65,97},{97,1},{2,34}... | collective-permute-start | bytes 786440 | tf_op jit(solution)/shard_map/ppermute | solution.py:18
  165.5 2.8 %collective-permute-start.22 = (bf16[128,1024]{1,0:T(8,128)(2,1)S(1)}, bf16[128,1024]{1,0:T(8,128)(2,1)S(1)}, u32[]{:S(2)}, u32[]{:S(2)}) collective-permute-start(bf16[128,1024]{1,0:T(8,128)(2,1)S(1)} %get-tuple-element.35.v0), channel_id=1, source_target_pairs={{0,64},{32,96},{64,0},{96,32},{1,65},{33,97},{65,1},{97,33},{2,66}... | collective-permute-start | bytes 786440 | tf_op jit(solution)/shard_map/ppermute | solution.py:18
  168.3 4.1 %collective-permute-done.21.v1 = bf16[128,1024]{1,0:T(8,128)(2,1)S(1)} collective-permute-done((bf16[128,1024]{1,0:T(8,128)(2,1)S(1)}, bf16[128,1024]{1,0:T(8,128)(2,1)S(1)}, u32[]{:S(2)}, u32[]{:S(2)}) %collective-permute-start.21) | collective-permute-done | bytes 262176 | tf_op jit(solution)/shard_map/ppermute | solution.py:18
  172.4 6.5 %collective-permute-done.22.v2 = bf16[128,1024]{1,0:T(8,128)(2,1)S(1)} collective-permute-done((bf16[128,1024]{1,0:T(8,128)(2,1)S(1)}, bf16[128,1024]{1,0:T(8,128)(2,1)S(1)}, u32[]{:S(2)}, u32[]{:S(2)}) %collective-permute-start.22) | collective-permute-done | bytes 262176 | tf_op jit(solution)/shard_map/ppermute | solution.py:18
  182.7 3.0 %collective-permute-start.25 = (bf16[128,1024]{1,0:T(8,128)(2,1)S(1)}, bf16[128,1024]{1,0:T(8,128)(2,1)S(1)}, u32[]{:S(2)}, u32[]{:S(2)}) collective-permute-start(bf16[128,1024]{1,0:T(8,128)(2,1)S(1)} %diag_step.3.refs_0_), channel_id=1, source_target_pairs={{0,8},{4,12},{8,0},{12,4},{1,9},{5,13},{9,1},{13,5},{2,10},{6,14},... | collective-permute-start | bytes 786440 | tf_op jit(solution)/shard_map/ppermute | solution.py:18
  185.8 2.5 %lower_step.9 = (f32[128,1024]{1,0:T(8,128)S(1)}, bf16[128,1024]{1,0:T(8,128)(2,1)}) custom-call(bf16[128,1024]{1,0:T(8,128)(2,1)S(1)} %get-tuple-element.33.refs_0_.x3, f32[128,1024]{1,0:T(8,128)S(1)} %get-tuple-element.47.refs_1_, bf16[2,4,2064,256]{3,2,1,0:T(8,128)(2,1)} %bitcast.51), custom_call_target="tpu_custom_call" | custom-call | flops 268435456 | bytes 4194304 | tf_op jit(solution)/shard_map/lower_step/pallas_call | solution.py:178
  188.3 2.5 %lower_step.10 = (f32[128,1024]{1,0:T(8,128)S(1)}, bf16[128,1024]{1,0:T(8,128)(2,1)}) custom-call(bf16[128,1024]{1,0:T(8,128)(2,1)S(1)} %get-tuple-element.36.refs_0_.x2, f32[128,1024]{1,0:T(8,128)S(1)} %get-tuple-element.37.refs_1_, bf16[2,4,2064,256]{3,2,1,0:T(8,128)(2,1)} %bitcast.52), custom_call_target="tpu_custom_call" | custom-call | flops 268435456 | bytes 4194304 | tf_op jit(solution)/shard_map/lower_step/pallas_call | solution.py:178
  190.8 2.9 %collective-permute-done.25.refs_2_ = bf16[128,1024]{1,0:T(8,128)(2,1)S(1)} collective-permute-done((bf16[128,1024]{1,0:T(8,128)(2,1)S(1)}, bf16[128,1024]{1,0:T(8,128)(2,1)S(1)}, u32[]{:S(2)}, u32[]{:S(2)}) %collective-permute-start.25) | collective-permute-done | bytes 262176 | tf_op jit(solution)/shard_map/ppermute | solution.py:18
  197.3 2.4 collective-permute-start.28
  202.3 4.0 %collective-permute-done.28.v2 = bf16[128,1024]{1,0:T(8,128)(2,1)S(1)} collective-permute-done((bf16[128,1024]{1,0:T(8,128)(2,1)S(1)}, bf16[128,1024]{1,0:T(8,128)(2,1)S(1)}, u32[]{:S(2)}, u32[]{:S(2)}) %collective-permute-start.28) | collective-permute-done | bytes 262176 | tf_op jit(solution)/shard_map/ppermute | solution.py:18
  206.3 2.5 %last_step.1 = (bf16[128,256]{1,0:T(8,128)(2,1)S(1)}, bf16[128,256]{1,0:T(8,128)(2,1)S(1)}, bf16[128,256]{1,0:T(8,128)(2,1)S(1)}, bf16[128,256]{1,0:T(8,128)(2,1)S(1)}) custom-call(s32[4]{0:T(128)S(1)} %pad_add_fusion.place_ref, bf16[128,1024]{1,0:T(8,128)(2,1)S(1)} %get-tuple-element.41.v0, bf16[128,1024]{1,0:T(8,128)(2,1)S(1)} %collective-permute-done.27.v1, ...), custom_call_target="tpu_custom_call" | custom-call | flops 268435456 | bytes 4194304 | tf_op jit(solution)/shard_map/last_step/pallas_call | solution.py:257
  212.5 3.0 %pack_known.1 = (bf16[2048,128]{1,0:T(8,128)(2,1)S(1)}, bf16[2048,256]{1,0:T(8,128)(2,1)S(1)}) custom-call(s32[4]{0:T(128)S(1)} %pad_add_fusion.place_ref, s32[4,1,256]{2,1,0:T(1,128)S(1)} %reshape.74.target_ref, bf16[128,1024]{1,0:T(8,128)(2,1)S(1)} %get-tuple-element.39.x1, bf16[128,1024]{1,0:T(8,128)(2,1)S(1)} %get-tuple-element.36.refs_0_.x2, ...), custom_call_target="tpu_custom_call" | custom-call | flops 402653184 | bytes 2097152 | tf_op jit(solution)/shard_map/pack_known/pallas_call | solution.py:338
  216.0 20.3 %all_to_all.5 = bf16[128,16,128]{2,1,0:T(8,128)(2,1)S(1)} all-to-all(bf16[128,16,128]{2,1,0:T(8,128)(2,1)S(1)} %bitcast.45), channel_id=1, replica_groups=mesh['z'=4,'core'=2,'y'=4,'x'=4] {'z','core','y','x'}, dimensions={0} | all-to-all | bytes 1048576 | tf_op jit(solution)/shard_map/all_to_all | solution.py:458
  (82 shorter events, 48.6 us)
Async XLA Ops:
  6.5 120.1 %all-gather.7.cloned.1.call-start = ((), (), s32[]{:S(2)}) async-start(), calls=%async_computation.2 | async-start | bytes 11796480 | tf_op jit(solution)/shard_map/all_gather | solution.py:404
  10.5 175.3 %all-gather.5.cloned.1.call-start = ((), (), s32[]{:S(2)}) async-start(), calls=%async_computation.1 | async-start | bytes 9510912 | tf_op jit(solution)/shard_map/all_gather | solution.py:404
  17.1 8.6 %collective-permute-start = (bf16[4,256,512]{2,1,0:T(8,128)(2,1)S(1)}, bf16[4,256,512]{2,1,0:T(8,128)(2,1)S(1)}, u32[]{:S(2)}, u32[]{:S(2)}) collective-permute-start(bf16[4,256,512]{2,1,0:T(8,128)(2,1)S(1)} %fusion.6), channel_id=1, source_target_pairs={{0,16},{16,0},{1,17},{17,1},{2,18},{18,2},{3,19},{19,3},{4,20},{20... | collective-permute-start | bytes 3145736 | tf_op jit(solution)/shard_map/ppermute | solution.py:22
  19.6 12.6 %collective-permute-start.4 = (bf16[256,512]{1,0:T(8,128)(2,1)S(1)}, bf16[256,512]{1,0:T(8,128)(2,1)S(1)}, u32[]{:S(2)}, u32[]{:S(2)}) collective-permute-start(bf16[256,512]{1,0:T(8,128)(2,1)S(1)} %slice_bitcast_fusion.4.mine_ref), channel_id=1, source_target_pairs={{0,16},{16,0},{1,17},{17,1},{2,18},{18,2},{3,19},{19,3},{4,20},{20... | collective-permute-start | bytes 786440 | tf_op jit(solution)/shard_map/ppermute | solution.py:22
  26.1 10.5 %collective-permute-start.1 = (bf16[256,512]{1,0:T(8,128)(2,1)S(1)}, bf16[256,512]{1,0:T(8,128)(2,1)S(1)}, u32[]{:S(2)}, u32[]{:S(2)}) collective-permute-start(bf16[256,512]{1,0:T(8,128)(2,1)S(1)} %slice_bitcast_fusion.3.v0), channel_id=1, source_target_pairs={{0,32},{32,64},{64,96},{96,0},{1,33},{33,65},{65,97},{97,1},{2,34}... | collective-permute-start | bytes 786440 | tf_op jit(solution)/shard_map/ppermute | solution.py:18
  27.9 15.0 %collective-permute-start.2 = (bf16[256,512]{1,0:T(8,128)(2,1)S(1)}, bf16[256,512]{1,0:T(8,128)(2,1)S(1)}, u32[]{:S(2)}, u32[]{:S(2)}) collective-permute-start(bf16[256,512]{1,0:T(8,128)(2,1)S(1)} %slice_bitcast_fusion.3.v0), channel_id=1, source_target_pairs={{0,64},{32,96},{64,0},{96,32},{1,65},{33,97},{65,1},{97,33},{2,66}... | collective-permute-start | bytes 786440 | tf_op jit(solution)/shard_map/ppermute | solution.py:18
  31.5 11.5 %collective-permute-start.3 = (bf16[256,512]{1,0:T(8,128)(2,1)S(1)}, bf16[256,512]{1,0:T(8,128)(2,1)S(1)}, u32[]{:S(2)}, u32[]{:S(2)}) collective-permute-start(bf16[256,512]{1,0:T(8,128)(2,1)S(1)} %slice_bitcast_fusion.3.v0), channel_id=1, source_target_pairs={{0,96},{32,0},{64,32},{96,64},{1,97},{33,1},{65,33},{97,65},{2,98}... | collective-permute-start | bytes 786440 | tf_op jit(solution)/shard_map/ppermute | solution.py:18
  46.4 36.8 %collective-permute-start.8 = (bf16[8,128]{1,0:T(8,128)(2,1)S(1)}, bf16[8,128]{1,0:T(8,128)(2,1)S(1)}, u32[]{:S(2)}, u32[]{:S(2)}) collective-permute-start(bf16[8,128]{1,0:T(8,128)(2,1)S(1)} %slice_add_fusion), channel_id=1, source_target_pairs={{0,16},{1,17},{2,18},{3,19},{4,20},{5,21},{6,22},{7,23},{8,24},{9,... | collective-permute-start | bytes 6152 | tf_op jit(solution)/shard_map/ppermute | solution.py:439
  84.5 9.5 %collective-permute-start.11 = (bf16[1792,128]{1,0:T(8,128)(2,1)S(1)}, bf16[1792,128]{1,0:T(8,128)(2,1)S(1)}, u32[]{:S(2)}, u32[]{:S(2)}) collective-permute-start(bf16[1792,128]{1,0:T(8,128)(2,1)S(1)} %broadcast_add_fusion), channel_id=1, source_target_pairs={{16,19},{17,16},{18,17},{19,18},{20,23},{21,20},{22,21},{23,22},{2... | collective-permute-start | bytes 1376264 | tf_op jit(solution)/shard_map/ppermute | solution.py:27
  86.4 11.0 %collective-permute-start.10 = (bf16[1792,128]{1,0:T(8,128)(2,1)S(1)}, bf16[1792,128]{1,0:T(8,128)(2,1)S(1)}, u32[]{:S(2)}, u32[]{:S(2)}) collective-permute-start(bf16[1792,128]{1,0:T(8,128)(2,1)S(1)} %broadcast_add_fusion.1), channel_id=1, source_target_pairs={{16,18},{17,19},{18,16},{19,17},{20,22},{21,23},{22,20},{23,21},{2... | collective-permute-start | bytes 1376264 | tf_op jit(solution)/shard_map/ppermute | solution.py:27
  90.0 22.1 %collective-permute-start.9 = (bf16[1792,128]{1,0:T(8,128)(2,1)S(1)}, bf16[1792,128]{1,0:T(8,128)(2,1)S(1)}, u32[]{:S(2)}, u32[]{:S(2)}) collective-permute-start(bf16[1792,128]{1,0:T(8,128)(2,1)S(1)} %broadcast_add_fusion.2), channel_id=1, source_target_pairs={{16,17},{17,18},{18,19},{19,16},{20,21},{21,22},{22,23},{23,20},{2... | collective-permute-start | bytes 1376264 | tf_op jit(solution)/shard_map/ppermute | solution.py:27
  112.7 7.4 %collective-permute-start.12 = (bf16[128,1024]{1,0:T(8,128)(2,1)S(1)}, bf16[128,1024]{1,0:T(8,128)(2,1)S(1)}, u32[]{:S(2)}, u32[]{:S(2)}) collective-permute-start(bf16[128,1024]{1,0:T(8,128)(2,1)S(1)} %first_sum.1.refs_0_), channel_id=1, source_target_pairs={{0,4},{4,8},{8,12},{12,0},{1,5},{5,9},{9,13},{13,1},{2,6},{6,10},{... | collective-permute-start | bytes 786440 | tf_op jit(solution)/shard_map/ppermute | solution.py:18
  113.6 12.4 %collective-permute-start.13 = (bf16[128,1024]{1,0:T(8,128)(2,1)S(1)}, bf16[128,1024]{1,0:T(8,128)(2,1)S(1)}, u32[]{:S(2)}, u32[]{:S(2)}) collective-permute-start(bf16[128,1024]{1,0:T(8,128)(2,1)S(1)} %first_sum.1.refs_0_), channel_id=1, source_target_pairs={{0,8},{4,12},{8,0},{12,4},{1,9},{5,13},{9,1},{13,5},{2,10},{6,14},... | collective-permute-start | bytes 786440 | tf_op jit(solution)/shard_map/ppermute | solution.py:18
  116.0 10.6 %collective-permute-start.14 = (bf16[128,1024]{1,0:T(8,128)(2,1)S(1)}, bf16[128,1024]{1,0:T(8,128)(2,1)S(1)}, u32[]{:S(2)}, u32[]{:S(2)}) collective-permute-start(bf16[128,1024]{1,0:T(8,128)(2,1)S(1)} %first_sum.1.refs_0_), channel_id=1, source_target_pairs={{0,12},{4,0},{8,4},{12,8},{1,13},{5,1},{9,5},{13,9},{2,14},{6,2},{... | collective-permute-start | bytes 786440 | tf_op jit(solution)/shard_map/ppermute | solution.py:18
  128.7 6.9 %collective-permute-start.15 = (bf16[128,1024]{1,0:T(8,128)(2,1)S(1)}, bf16[128,1024]{1,0:T(8,128)(2,1)S(1)}, u32[]{:S(2)}, u32[]{:S(2)}) collective-permute-start(bf16[128,1024]{1,0:T(8,128)(2,1)S(1)} %get-tuple-element.32.v0), channel_id=1, source_target_pairs={{0,32},{32,64},{64,96},{96,0},{1,33},{33,65},{65,97},{97,1},{2,34}... | collective-permute-start | bytes 786440 | tf_op jit(solution)/shard_map/ppermute | solution.py:18
  129.3 12.6 %collective-permute-start.16 = (bf16[128,1024]{1,0:T(8,128)(2,1)S(1)}, bf16[128,1024]{1,0:T(8,128)(2,1)S(1)}, u32[]{:S(2)}, u32[]{:S(2)}) collective-permute-start(bf16[128,1024]{1,0:T(8,128)(2,1)S(1)} %get-tuple-element.32.v0), channel_id=1, source_target_pairs={{0,64},{32,96},{64,0},{96,32},{1,65},{33,97},{65,1},{97,33},{2,66}... | collective-permute-start | bytes 786440 | tf_op jit(solution)/shard_map/ppermute | solution.py:18
  132.6 9.4 %collective-permute-start.17 = (bf16[128,1024]{1,0:T(8,128)(2,1)S(1)}, bf16[128,1024]{1,0:T(8,128)(2,1)S(1)}, u32[]{:S(2)}, u32[]{:S(2)}) collective-permute-start(bf16[128,1024]{1,0:T(8,128)(2,1)S(1)} %get-tuple-element.32.v0), channel_id=1, source_target_pairs={{0,96},{32,0},{64,32},{96,64},{1,97},{33,1},{65,33},{97,65},{2,98}... | collective-permute-start | bytes 786440 | tf_op jit(solution)/shard_map/ppermute | solution.py:18
  143.9 9.8 %collective-permute-start.18 = (bf16[128,1024]{1,0:T(8,128)(2,1)S(1)}, bf16[128,1024]{1,0:T(8,128)(2,1)S(1)}, u32[]{:S(2)}, u32[]{:S(2)}) collective-permute-start(bf16[128,1024]{1,0:T(8,128)(2,1)S(1)} %diag_step.2.refs_0_), channel_id=1, source_target_pairs={{0,4},{4,8},{8,12},{12,0},{1,5},{5,9},{9,13},{13,1},{2,6},{6,10},{... | collective-permute-start | bytes 786440 | tf_op jit(solution)/shard_map/ppermute | solution.py:18
  148.4 11.8 %collective-permute-start.19 = (bf16[128,1024]{1,0:T(8,128)(2,1)S(1)}, bf16[128,1024]{1,0:T(8,128)(2,1)S(1)}, u32[]{:S(2)}, u32[]{:S(2)}) collective-permute-start(bf16[128,1024]{1,0:T(8,128)(2,1)S(1)} %diag_step.2.refs_0_), channel_id=1, source_target_pairs={{0,8},{4,12},{8,0},{12,4},{1,9},{5,13},{9,1},{13,5},{2,10},{6,14},... | collective-permute-start | bytes 786440 | tf_op jit(solution)/shard_map/ppermute | solution.py:18
  150.1 10.6 %collective-permute-start.20 = (bf16[128,1024]{1,0:T(8,128)(2,1)S(1)}, bf16[128,1024]{1,0:T(8,128)(2,1)S(1)}, u32[]{:S(2)}, u32[]{:S(2)}) collective-permute-start(bf16[128,1024]{1,0:T(8,128)(2,1)S(1)} %diag_step.2.refs_0_), channel_id=1, source_target_pairs={{0,12},{4,0},{8,4},{12,8},{1,13},{5,1},{9,5},{13,9},{2,14},{6,2},{... | collective-permute-start | bytes 786440 | tf_op jit(solution)/shard_map/ppermute | solution.py:18
  162.8 9.6 %collective-permute-start.21 = (bf16[128,1024]{1,0:T(8,128)(2,1)S(1)}, bf16[128,1024]{1,0:T(8,128)(2,1)S(1)}, u32[]{:S(2)}, u32[]{:S(2)}) collective-permute-start(bf16[128,1024]{1,0:T(8,128)(2,1)S(1)} %get-tuple-element.35.v0), channel_id=1, source_target_pairs={{0,32},{32,64},{64,96},{96,0},{1,33},{33,65},{65,97},{97,1},{2,34}... | collective-permute-start | bytes 786440 | tf_op jit(solution)/shard_map/ppermute | solution.py:18
  165.5 13.4 %collective-permute-start.22 = (bf16[128,1024]{1,0:T(8,128)(2,1)S(1)}, bf16[128,1024]{1,0:T(8,128)(2,1)S(1)}, u32[]{:S(2)}, u32[]{:S(2)}) collective-permute-start(bf16[128,1024]{1,0:T(8,128)(2,1)S(1)} %get-tuple-element.35.v0), channel_id=1, source_target_pairs={{0,64},{32,96},{64,0},{96,32},{1,65},{33,97},{65,1},{97,33},{2,66}... | collective-permute-start | bytes 786440 | tf_op jit(solution)/shard_map/ppermute | solution.py:18
  168.3 10.8 %collective-permute-start.23 = (bf16[128,1024]{1,0:T(8,128)(2,1)S(1)}, bf16[128,1024]{1,0:T(8,128)(2,1)S(1)}, u32[]{:S(2)}, u32[]{:S(2)}) collective-permute-start(bf16[128,1024]{1,0:T(8,128)(2,1)S(1)} %get-tuple-element.35.v0), channel_id=1, source_target_pairs={{0,96},{32,0},{64,32},{96,64},{1,97},{33,1},{65,33},{97,65},{2,98}... | collective-permute-start | bytes 786440 | tf_op jit(solution)/shard_map/ppermute | solution.py:18
  181.1 9.7 %collective-permute-start.24 = (bf16[128,1024]{1,0:T(8,128)(2,1)S(1)}, bf16[128,1024]{1,0:T(8,128)(2,1)S(1)}, u32[]{:S(2)}, u32[]{:S(2)}) collective-permute-start(bf16[128,1024]{1,0:T(8,128)(2,1)S(1)} %diag_step.3.refs_0_), channel_id=1, source_target_pairs={{0,4},{4,8},{8,12},{12,0},{1,5},{5,9},{9,13},{13,1},{2,6},{6,10},{... | collective-permute-start | bytes 786440 | tf_op jit(solution)/shard_map/ppermute | solution.py:18
  182.7 11.0 %collective-permute-start.25 = (bf16[128,1024]{1,0:T(8,128)(2,1)S(1)}, bf16[128,1024]{1,0:T(8,128)(2,1)S(1)}, u32[]{:S(2)}, u32[]{:S(2)}) collective-permute-start(bf16[128,1024]{1,0:T(8,128)(2,1)S(1)} %diag_step.3.refs_0_), channel_id=1, source_target_pairs={{0,8},{4,12},{8,0},{12,4},{1,9},{5,13},{9,1},{13,5},{2,10},{6,14},... | collective-permute-start | bytes 786440 | tf_op jit(solution)/shard_map/ppermute | solution.py:18
  185.7 8.0 %collective-permute-start.26 = (bf16[128,1024]{1,0:T(8,128)(2,1)S(1)}, bf16[128,1024]{1,0:T(8,128)(2,1)S(1)}, u32[]{:S(2)}, u32[]{:S(2)}) collective-permute-start(bf16[128,1024]{1,0:T(8,128)(2,1)S(1)} %diag_step.3.refs_0_), channel_id=1, source_target_pairs={{0,12},{4,0},{8,4},{12,8},{1,13},{5,1},{9,5},{13,9},{2,14},{6,2},{... | collective-permute-start | bytes 786440 | tf_op jit(solution)/shard_map/ppermute | solution.py:18
  195.8 6.6 %collective-permute-start.27 = (bf16[128,1024]{1,0:T(8,128)(2,1)S(1)}, bf16[128,1024]{1,0:T(8,128)(2,1)S(1)}, u32[]{:S(2)}, u32[]{:S(2)}) collective-permute-start(bf16[128,1024]{1,0:T(8,128)(2,1)S(1)} %get-tuple-element.41.v0), channel_id=1, source_target_pairs={{0,32},{32,64},{64,96},{96,0},{1,33},{33,65},{65,97},{97,1},{2,34}... | collective-permute-start | bytes 786440 | tf_op jit(solution)/shard_map/ppermute | solution.py:18
  197.3 9.0 %collective-permute-start.28 = (bf16[128,1024]{1,0:T(8,128)(2,1)S(1)}, bf16[128,1024]{1,0:T(8,128)(2,1)S(1)}, u32[]{:S(2)}, u32[]{:S(2)}) collective-permute-start(bf16[128,1024]{1,0:T(8,128)(2,1)S(1)} %get-tuple-element.41.v0), channel_id=1, source_target_pairs={{0,64},{32,96},{64,0},{96,32},{1,65},{33,97},{65,1},{97,33},{2,66}... | collective-permute-start | bytes 786440 | tf_op jit(solution)/shard_map/ppermute | solution.py:18
  199.7 6.6 %collective-permute-start.29 = (bf16[128,1024]{1,0:T(8,128)(2,1)S(1)}, bf16[128,1024]{1,0:T(8,128)(2,1)S(1)}, u32[]{:S(2)}, u32[]{:S(2)}) collective-permute-start(bf16[128,1024]{1,0:T(8,128)(2,1)S(1)} %get-tuple-element.41.v0), channel_id=1, source_target_pairs={{0,96},{32,0},{64,32},{96,64},{1,97},{33,1},{65,33},{97,65},{2,98}... | collective-permute-start | bytes 786440 | tf_op jit(solution)/shard_map/ppermute | solution.py:18
  208.8 6.7 %collective-permute-start.30 = (bf16[128,256]{1,0:T(8,128)(2,1)S(1)}, bf16[128,256]{1,0:T(8,128)(2,1)S(1)}, u32[]{:S(2)}, u32[]{:S(2)}) collective-permute-start(bf16[128,256]{1,0:T(8,128)(2,1)S(1)} %get-tuple-element.43), channel_id=1, source_target_pairs={{0,4},{4,8},{8,12},{12,0},{1,5},{5,9},{9,13},{13,1},{2,6},{6,10},{... | collective-permute-start | bytes 196616 | tf_op jit(solution)/shard_map/ppermute | solution.py:18
  209.6 5.9 %collective-permute-start.31 = (bf16[128,256]{1,0:T(8,128)(2,1)S(1)}, bf16[128,256]{1,0:T(8,128)(2,1)S(1)}, u32[]{:S(2)}, u32[]{:S(2)}) collective-permute-start(bf16[128,256]{1,0:T(8,128)(2,1)S(1)} %get-tuple-element.44), channel_id=1, source_target_pairs={{0,8},{4,12},{8,0},{12,4},{1,9},{5,13},{9,1},{13,5},{2,10},{6,14},... | collective-permute-start | bytes 196616 | tf_op jit(solution)/shard_map/ppermute | solution.py:18
  211.9 3.6 %collective-permute-start.32 = (bf16[128,256]{1,0:T(8,128)(2,1)S(1)}, bf16[128,256]{1,0:T(8,128)(2,1)S(1)}, u32[]{:S(2)}, u32[]{:S(2)}) collective-permute-start(bf16[128,256]{1,0:T(8,128)(2,1)S(1)} %get-tuple-element.45), channel_id=1, source_target_pairs={{0,12},{4,0},{8,4},{12,8},{1,13},{5,1},{9,5},{13,9},{2,14},{6,2},{... | collective-permute-start | bytes 196616 | tf_op jit(solution)/shard_map/ppermute | solution.py:18
  (3 other events, 4.2 us)
Sparse Core Ops, SparseCore 0:
  10.6 70.9 all-gather.6
  83.4 54.8 all-gather.4

commit v6 on v4

--- a/solution.py
+++ b/solution.py
@@ -60,23 +60,46 @@
 HBM = pl.BlockSpec(memory_space=pltpu.HBM)
 
 
-def turn(place, pieces, dtype):
-    blocks = pieces[0].shape[0]
-
+def first_product(place, pieces, mine, other):
+    def kernel(place_ref, v0, v1, v2, v3, mine_ref, other_ref, *refs):
+        outs, turned = refs[:4], refs[4]
+        core, x = place_ref[0], place_ref[2]
+        turned[...] = add_up((v0, v1, v2, v3)).T.astype(BF16)
+        for step, out in enumerate(outs):
+            start = pl.multiple_of(lax.rem(x + step, 4) * 128, 128)
+            left = turned[pl.ds(start, 128), :]
+            for side, tile in ((core, mine_ref), (1 - core, other_ref)):
+                product = jnp.dot(left, tile[...], preferred_element_type=F32)
+                lanes = pl.ds(pl.multiple_of(side * 512, 512), 512)
+                out[:, lanes] = product.astype(BF16)
+
+    return pl.pallas_call(
+        kernel,
+        out_shape=(jax.ShapeDtypeStruct((128, 1024), BF16),) * 4,
+        in_specs=[SCALARS] + [VMEM] * 6,
+        out_specs=(VMEM,) * 4,
+        scratch_shapes=[pltpu.VMEM((512, 256), BF16)],
+        compiler_params=params(),
+        cost_estimate=cost(2 * 512 * 256 * 1024, 3 << 20),
+        name="first_product",
+    )(place, *pieces, mine, other)
+
+
+def turn(place, pieces):
     def kernel(place_ref, v0, v1, v2, v3, out):
         for step, ref in enumerate((v0, v1, v2, v3)):
             start = lax.rem(place_ref[2] + 4 - step, 4) * 256
             lanes = pl.ds(pl.multiple_of(start, 256), 256)
-            for k in range(blocks):
-                out[k, :, lanes] = ref[k].astype(F32).T.astype(dtype)
-
-    return pl.pallas_call(
-        kernel,
-        out_shape=jax.ShapeDtypeStruct((blocks, 128, 1024), dtype),
+            for k in range(3):
+                out[k, :, lanes] = ref[k].astype(F32).T
+
+    return pl.pallas_call(
+        kernel,
+        out_shape=jax.ShapeDtypeStruct((3, 128, 1024), F32),
         in_specs=[SCALARS] + [VMEM] * 4,
         out_specs=VMEM,
         compiler_params=params(),
-        cost_estimate=cost(blocks * 128 * 1024, blocks << 20),
+        cost_estimate=cost(3 * 128 * 1024, 3 << 20),
         name="turn",
     )(place, *pieces)
 
@@ -343,12 +366,12 @@
 
     owners = jnp.pad(owner_map[0, :, 0].astype(BF16)[None], ((0, 15), (0, 128)))
     orders = [
-        [("D", 3), tile(3, 2), ("D", 2), tile(3, 1)],
-        [tile(2, 1), ("D", 1), tile(3, 0)],
-        [tile(2, 0), tile(1, 0), ("D", 0)],
+        [tile(3, 2), ("D", 2), tile(3, 1), tile(2, 1), ("D", 1)],
+        [tile(3, 0), tile(2, 0), tile(1, 0), ("D", 0)],
     ]
-    early, middle, late = map(gathered, stage(lower_tiles, inverse_diag, orders, owners))
-    named = late[:, :, 1536, :128].astype(jnp.int32).reshape(8, 128)
+    early, late = map(gathered, stage(lower_tiles, inverse_diag, orders, owners))
+    named = late[:, :, 2048, :128].astype(jnp.int32).reshape(8, 128)
+    other = swap(inverse_diag[3])
 
     def term(side):
         start = side * 512
@@ -362,27 +385,29 @@
     away = swap(term(1 - core))
     home = lax.optimization_barrier(term(core))
     both = (home.astype(F32) + away.astype(F32)).astype(BF16)
+    over_z = spread(both[3], "z")
+    products = first_product(place, over_z, inverse_diag[3], other)
+    rest = both[:3] + over_z[1][0, 0] * 0
     cut = [
-        lax.dynamic_slice_in_dim(both, lax.rem(x + by, 4) * 128, 128, axis=2) for by in range(4)
+        lax.dynamic_slice_in_dim(rest, lax.rem(x + by, 4) * 128, 128, axis=2) for by in range(4)
     ]
-
-    base = turn(place, deal(cut, "x"), F32)
-    base3 = base[3].astype(BF16)
-    over_z = spread(base3, "z")
-    pieces = spread(diag_step(over_z, early, 0), "y")
-    residual, x3 = lower_step(base[2], pieces, early, 1, BF16)
+    base = turn(place, deal(cut, "x"))
+    over_x = deal(products, "x")
+    partial = sum(piece.astype(F32) for piece in over_x).astype(BF16)
+    pieces = spread(partial, "y")
+    residual, x3 = lower_step(base[2], pieces, early, 0, BF16)
     over_z = spread(residual, "z")
-    pieces = spread(diag_step(over_z, early, 2), "y")
-    base1, _ = lower_step(base[1], (x3,), early, 3, F32)
-    residual, x2 = lower_step(base1, pieces, middle, 0, BF16)
+    pieces = spread(diag_step(over_z, early, 1), "y")
+    base1, _ = lower_step(base[1], (x3,), early, 2, F32)
+    residual, x2 = lower_step(base1, pieces, early, 3, BF16)
     over_z = spread(residual, "z")
-    base0, _ = lower_step(base[0], (x3,), middle, 2, F32)
-    pieces = spread(diag_step(over_z, middle, 1), "y")
-    base0, _ = lower_step(base0, (x2,), late, 0, F32)
-    residual, x1 = lower_step(base0, pieces, late, 1, BF16)
+    pieces = spread(diag_step(over_z, early, 4), "y")
+    base0, _ = lower_step(base[0], (x3,), late, 0, F32)
+    base0, _ = lower_step(base0, (x2,), late, 1, F32)
+    residual, x1 = lower_step(base0, pieces, late, 2, BF16)
     over_z = spread(residual, "z")
     packed, still = pack_known(place, slots_of(named), (x1, x2, x3))
-    rows = deal(last_step(place, over_z, late, 2), "y")
+    rows = deal(last_step(place, over_z, late, 3), "y")
     packed = pack_last(still, rows, packed).reshape(128, 16, 128)
     received = lax.all_to_all(
         packed, ("z", "core", "y", "x"), split_axis=0, concat_axis=0, tiled=True

time: 223 us -> 230 us (1.031)
  starting transfers between devices: 46.8 us -> 54.1 us
    all_gather x3 -> x2, waiting for transfers between devices: 11.8 us -> 0.02 us  [gathered(): lax.all_gather(joined, ('core', 'x'), axis=0, tiled=False)]
    ppermute x27 -> x30, waiting for transfers between devices: 80.8 us -> 91 us  [shift(): return lax.ppermute(value, axis, [(i, (i + by) % 4) for i in range(4)])]
    ppermute x27 -> x30, starting transfers between devices: 45.2 us -> 52.2 us  [shift(): return lax.ppermute(value, axis, [(i, (i + by) % 4) for i in range(4)])]
    pallas_call x3 -> x2, Pallas kernels: 5.72 us -> 3.77 us  [diag_step(): pl.pallas_call(kernel, out_shape=jax.ShapeDtypeStruct((128, 1024), BF16),...]
  transfers between devices with their start and end apart: 31 -> 34, of which waited for: 18 -> 22; matrix products, arithmetic and copies ran while one was open for 7% -> 7% of each run, Pallas kernels for 10% -> 9%
where the time goes in v6:
time: 230 us; the launch traced here: 229 us
  waiting for transfers between devices  91.7 us (40%)
  starting transfers between devices  54.1 us (24%)
  Pallas kernels  29.5 us (13%)
  blocking collectives  21.9 us (10%)
  between operations  14.3 us (6%)
  matrix products  11.7 us (5%)
  other arithmetic  3.19 us (1%)
  local copies, waits for them, and re-layouts  2.66 us (1%)
    ppermute x30, waiting for transfers between devices, shift(): return lax.ppermute(value, axis, [(i, (i + by) % 4) for i in range(4)])  91 us
    ppermute x30, starting transfers between devices, shift(): return lax.ppermute(value, axis, [(i, (i + by) % 4) for i in range(4)])  52.2 us
    all_to_all x1, blocking collectives, local(): lax.all_to_all(packed, ('z', 'core', 'y', 'x'), split_axis=0, concat_axis...  21.9 us
    pallas_call x6, Pallas kernels, lower_step(): pl.pallas_call(kernel, out_shape=(jax.ShapeDtypeStruct((128, 1024), dtype...  13.6 us
    dot_general x2, matrix products, term(): lax.dot_general(border_tiles, bound, (((0,), (0,)), ((), ())), preferred_...  11.7 us
  transfers between devices with their start and end apart: 34, of which 22 were waited for; matrix products, arithmetic and copies ran while one was open for 7% of the time, Pallas kernels for 9%

profile of v6, /device:TPU:1, one launch (start us, length us, event | category | flops | bytes accessed | tf_op | source)
XLA Modules:
  0.0 229.0 jit_solution(12368568429847885785)
XLA Ops:
  7.8 2.7 %stage.1 = (bf16[2560,256]{1,0:T(8,128)(2,1)}, bf16[2064,256]{1,0:T(8,128)(2,1)}) custom-call(bf16[6,512,256]{2,1,0:T(8,128)(2,1)} %lower_ref.1, bf16[4,256,512]{2,1,0:T(8,128)(2,1)} %diag_ref.1, bf16[16,256]{1,0:T(8,128)(2,1)} %pad.4.owners_ref), custom_call_target="tpu_custom_call" | custom-call | bytes 6291456 | tf_op jit(solution)/shard_map/stage/pallas_call | solution.py:254
  11.3 5.9 %fusion.6 = bf16[4,256,512]{2,1,0:T(8,128)(2,1)S(1)} fusion(f32[4,256,1024]{2,1,0:T(8,128)} %param.6, s32[]{:T(128)S(6)} %select_n.26, bf16[2048,4,256]{2,1,0:T(4,128)(2,1)} %param.8, bf16[2048,1024]{1,0:T(8,128)(2,1)} %param.7, f32[]{:T(128)S(6)} %select_n.24), kind=kOutput, calls=%fused_computation.7 | convolution fusion | flops 2149056512 | bytes 9438720 | tf_op jit(solution)/shard_map/dot_general | solution.py:380
  18.6 5.8 %fusion.7 = bf16[4,256,512]{2,1,0:T(8,128)(2,1)S(1)} fusion(f32[4,256,1024]{2,1,0:T(8,128)} %param.6, s32[]{:T(128)S(6)} %select_n.25, bf16[2048,4,256]{2,1,0:T(4,128)(2,1)} %param.8, bf16[2048,1024]{1,0:T(8,128)(2,1)} %param.7, f32[]{:T(128)S(6)} %select_n.24), kind=kOutput, calls=%fused_computation.9 | convolution fusion | flops 2149056512 | bytes 9438720 | tf_op jit(solution)/shard_map/dot_general | solution.py:380
  28.0 3.3 %collective-permute-start.2 = (bf16[256,512]{1,0:T(8,128)(2,1)S(1)}, bf16[256,512]{1,0:T(8,128)(2,1)S(1)}, u32[]{:S(2)}, u32[]{:S(2)}) collective-permute-start(bf16[256,512]{1,0:T(8,128)(2,1)S(1)} %slice_bitcast_fusion.3.v0), channel_id=1, source_target_pairs={{0,64},{32,96},{64,0},{96,32},{1,65},{33,97},{65,1},{97,33},{2,66}... | collective-permute-start | bytes 786440 | tf_op jit(solution)/shard_map/ppermute | solution.py:18
  32.0 3.7 %collective-permute-done.1.v1 = bf16[256,512]{1,0:T(8,128)(2,1)S(1)} collective-permute-done((bf16[256,512]{1,0:T(8,128)(2,1)S(1)}, bf16[256,512]{1,0:T(8,128)(2,1)S(1)}, u32[]{:S(2)}, u32[]{:S(2)}) %collective-permute-start.1) | collective-permute-done | bytes 262176 | tf_op jit(solution)/shard_map/ppermute | solution.py:18
  38.4 3.8 %collective-permute-done.2.v2 = bf16[256,512]{1,0:T(8,128)(2,1)S(1)} collective-permute-done((bf16[256,512]{1,0:T(8,128)(2,1)S(1)}, bf16[256,512]{1,0:T(8,128)(2,1)S(1)}, u32[]{:S(2)}, u32[]{:S(2)}) %collective-permute-start.2) | collective-permute-done | bytes 262176 | tf_op jit(solution)/shard_map/ppermute | solution.py:18
  44.9 2.5 %collective-permute-start.6 = (bf16[128,1024]{1,0:T(8,128)(2,1)S(1)}, bf16[128,1024]{1,0:T(8,128)(2,1)S(1)}, u32[]{:S(2)}, u32[]{:S(2)}) collective-permute-start(bf16[128,1024]{1,0:T(8,128)(2,1)S(1)} %get-tuple-element.29), channel_id=1, source_target_pairs={{0,2},{1,3},{2,0},{3,1},{4,6},{5,7},{6,4},{7,5},{8,10},{9,11},{10,... | collective-permute-start | bytes 786440 | tf_op jit(solution)/shard_map/ppermute | solution.py:18
  51.2 29.9 %collective-permute-done.12.v2 = bf16[3,256,128]{2,1,0:T(8,128)(2,1)S(1)} collective-permute-done((bf16[3,256,128]{2,1,0:T(8,128)(2,1)S(1)}, bf16[3,256,128]{2,1,0:T(8,128)(2,1)S(1)}, u32[]{:S(2)}, u32[]{:S(2)}) %collective-permute-start.12) | collective-permute-done | bytes 196640 | tf_op jit(solution)/shard_map/ppermute | solution.py:18
  81.1 5.9 %collective-permute-done.13.v3 = bf16[3,256,128]{2,1,0:T(8,128)(2,1)S(1)} collective-permute-done((bf16[3,256,128]{2,1,0:T(8,128)(2,1)S(1)}, bf16[3,256,128]{2,1,0:T(8,128)(2,1)S(1)}, u32[]{:S(2)}, u32[]{:S(2)}) %collective-permute-start.13) | collective-permute-done | bytes 196640 | tf_op jit(solution)/shard_map/ppermute | solution.py:18
  88.0 2.9 %collective-permute-start.10 = (bf16[128,1024]{1,0:T(8,128)(2,1)S(1)}, bf16[128,1024]{1,0:T(8,128)(2,1)S(1)}, u32[]{:S(2)}, u32[]{:S(2)}) collective-permute-start(bf16[128,1024]{1,0:T(8,128)(2,1)S(1)} %add_convert_fusion.1.refs_0_), channel_id=1, source_target_pairs={{0,12},{4,0},{8,4},{12,8},{1,13},{5,1},{9,5},{13,9},{2,14},{6,2},{... | collective-permute-start | bytes 786440 | tf_op jit(solution)/shard_map/ppermute | solution.py:18
  94.2 5.6 %collective-permute-done.8.refs_1_ = bf16[128,1024]{1,0:T(8,128)(2,1)S(1)} collective-permute-done((bf16[128,1024]{1,0:T(8,128)(2,1)S(1)}, bf16[128,1024]{1,0:T(8,128)(2,1)S(1)}, u32[]{:S(2)}, u32[]{:S(2)}) %collective-permute-start.8) | collective-permute-done | bytes 262176 | tf_op jit(solution)/shard_map/ppermute | solution.py:18
  103.8 2.5 %collective-permute-start.14 = (bf16[128,1024]{1,0:T(8,128)(2,1)S(1)}, bf16[128,1024]{1,0:T(8,128)(2,1)S(1)}, u32[]{:S(2)}, u32[]{:S(2)}) collective-permute-start(bf16[128,1024]{1,0:T(8,128)(2,1)S(1)} %get-tuple-element.32.v0), channel_id=1, source_target_pairs={{0,32},{32,64},{64,96},{96,0},{1,33},{33,65},{65,97},{97,1},{2,34}... | collective-permute-start | bytes 786440 | tf_op jit(solution)/shard_map/ppermute | solution.py:18
  106.3 3.1 %collective-permute-start.15 = (bf16[128,1024]{1,0:T(8,128)(2,1)S(1)}, bf16[128,1024]{1,0:T(8,128)(2,1)S(1)}, u32[]{:S(2)}, u32[]{:S(2)}) collective-permute-start(bf16[128,1024]{1,0:T(8,128)(2,1)S(1)} %get-tuple-element.32.v0), channel_id=1, source_target_pairs={{0,64},{32,96},{64,0},{96,32},{1,65},{33,97},{65,1},{97,33},{2,66}... | collective-permute-start | bytes 786440 | tf_op jit(solution)/shard_map/ppermute | solution.py:18
  109.5 3.0 %collective-permute-done.14.v1 = bf16[128,1024]{1,0:T(8,128)(2,1)S(1)} collective-permute-done((bf16[128,1024]{1,0:T(8,128)(2,1)S(1)}, bf16[128,1024]{1,0:T(8,128)(2,1)S(1)}, u32[]{:S(2)}, u32[]{:S(2)}) %collective-permute-start.14) | collective-permute-done | bytes 262176 | tf_op jit(solution)/shard_map/ppermute | solution.py:18
  112.4 5.2 %collective-permute-done.15.v2 = bf16[128,1024]{1,0:T(8,128)(2,1)S(1)} collective-permute-done((bf16[128,1024]{1,0:T(8,128)(2,1)S(1)}, bf16[128,1024]{1,0:T(8,128)(2,1)S(1)}, u32[]{:S(2)}, u32[]{:S(2)}) %collective-permute-start.15) | collective-permute-done | bytes 262176 | tf_op jit(solution)/shard_map/ppermute | solution.py:18
  125.2 2.5 %lower_step.7 = (f32[128,1024]{1,0:T(8,128)S(1)}, bf16[128,1024]{1,0:T(8,128)(2,1)}) custom-call(bf16[128,1024]{1,0:T(8,128)(2,1)S(1)} %get-tuple-element.33.refs_0_.x3, f32[128,1024]{1,0:T(8,128)S(1)} %get-tuple-element.48.refs_1_, bf16[2,4,2560,256]{3,2,1,0:T(8,128)(2,1)} %bitcast.48), custom_call_target="tpu_custom_call" | custom-call | flops 268435456 | bytes 4194304 | tf_op jit(solution)/shard_map/lower_step/pallas_call | solution.py:130
  127.7 4.5 %collective-permute-done.18.refs_2_ = bf16[128,1024]{1,0:T(8,128)(2,1)S(1)} collective-permute-done((bf16[128,1024]{1,0:T(8,128)(2,1)S(1)}, bf16[128,1024]{1,0:T(8,128)(2,1)S(1)}, u32[]{:S(2)}, u32[]{:S(2)}) %collective-permute-start.18) | collective-permute-done | bytes 262176 | tf_op jit(solution)/shard_map/ppermute | solution.py:18
  134.3 3.2 %collective-permute-start.20 = (bf16[128,1024]{1,0:T(8,128)(2,1)S(1)}, bf16[128,1024]{1,0:T(8,128)(2,1)S(1)}, u32[]{:S(2)}, u32[]{:S(2)}) collective-permute-start(bf16[128,1024]{1,0:T(8,128)(2,1)S(1)} %get-tuple-element.35.v0), channel_id=1, source_target_pairs={{0,32},{32,64},{64,96},{96,0},{1,33},{33,65},{65,97},{97,1},{2,34}... | collective-permute-start | bytes 786440 | tf_op jit(solution)/shard_map/ppermute | solution.py:18
  137.5 3.4 %collective-permute-start.21 = (bf16[128,1024]{1,0:T(8,128)(2,1)S(1)}, bf16[128,1024]{1,0:T(8,128)(2,1)S(1)}, u32[]{:S(2)}, u32[]{:S(2)}) collective-permute-start(bf16[128,1024]{1,0:T(8,128)(2,1)S(1)} %get-tuple-element.35.v0), channel_id=1, source_target_pairs={{0,64},{32,96},{64,0},{96,32},{1,65},{33,97},{65,1},{97,33},{2,66}... | collective-permute-start | bytes 786440 | tf_op jit(solution)/shard_map/ppermute | solution.py:18
  140.9 3.2 %collective-permute-done.20.v1 = bf16[128,1024]{1,0:T(8,128)(2,1)S(1)} collective-permute-done((bf16[128,1024]{1,0:T(8,128)(2,1)S(1)}, bf16[128,1024]{1,0:T(8,128)(2,1)S(1)}, u32[]{:S(2)}, u32[]{:S(2)}) %collective-permute-start.20) | collective-permute-done | bytes 262176 | tf_op jit(solution)/shard_map/ppermute | solution.py:18
  144.1 6.5 %collective-permute-done.21.v2 = bf16[128,1024]{1,0:T(8,128)(2,1)S(1)} collective-permute-done((bf16[128,1024]{1,0:T(8,128)(2,1)S(1)}, bf16[128,1024]{1,0:T(8,128)(2,1)S(1)}, u32[]{:S(2)}, u32[]{:S(2)}) %collective-permute-start.21) | collective-permute-done | bytes 262176 | tf_op jit(solution)/shard_map/ppermute | solution.py:18
  153.2 2.8 %collective-permute-start.23 = (bf16[128,1024]{1,0:T(8,128)(2,1)S(1)}, bf16[128,1024]{1,0:T(8,128)(2,1)S(1)}, u32[]{:S(2)}, u32[]{:S(2)}) collective-permute-start(bf16[128,1024]{1,0:T(8,128)(2,1)S(1)} %diag_step.3.refs_0_), channel_id=1, source_target_pairs={{0,4},{4,8},{8,12},{12,0},{1,5},{5,9},{9,13},{13,1},{2,6},{6,10},{... | collective-permute-start | bytes 786440 | tf_op jit(solution)/shard_map/ppermute | solution.py:18
  158.5 2.5 %lower_step.9 = (f32[128,1024]{1,0:T(8,128)S(1)}, bf16[128,1024]{1,0:T(8,128)(2,1)}) custom-call(bf16[128,1024]{1,0:T(8,128)(2,1)S(1)} %get-tuple-element.33.refs_0_.x3, f32[128,1024]{1,0:T(8,128)S(1)} %get-tuple-element.47.refs_1_, bf16[2,4,2064,256]{3,2,1,0:T(8,128)(2,1)} %bitcast.51), custom_call_target="tpu_custom_call" | custom-call | flops 268435456 | bytes 4194304 | tf_op jit(solution)/shard_map/lower_step/pallas_call | solution.py:130
  161.0 2.5 %lower_step.10 = (f32[128,1024]{1,0:T(8,128)S(1)}, bf16[128,1024]{1,0:T(8,128)(2,1)}) custom-call(bf16[128,1024]{1,0:T(8,128)(2,1)S(1)} %get-tuple-element.36.refs_0_.x2, f32[128,1024]{1,0:T(8,128)S(1)} %get-tuple-element.37.refs_1_, bf16[2,4,2064,256]{3,2,1,0:T(8,128)(2,1)} %bitcast.52), custom_call_target="tpu_custom_call" | custom-call | flops 268435456 | bytes 4194304 | tf_op jit(solution)/shard_map/lower_step/pallas_call | solution.py:130
  163.6 4.4 %collective-permute-done.24.refs_2_ = bf16[128,1024]{1,0:T(8,128)(2,1)S(1)} collective-permute-done((bf16[128,1024]{1,0:T(8,128)(2,1)S(1)}, bf16[128,1024]{1,0:T(8,128)(2,1)S(1)}, u32[]{:S(2)}, u32[]{:S(2)}) %collective-permute-start.24) | collective-permute-done | bytes 262176 | tf_op jit(solution)/shard_map/ppermute | solution.py:18
  170.3 2.8 %collective-permute-start.26 = (bf16[128,1024]{1,0:T(8,128)(2,1)S(1)}, bf16[128,1024]{1,0:T(8,128)(2,1)S(1)}, u32[]{:S(2)}, u32[]{:S(2)}) collective-permute-start(bf16[128,1024]{1,0:T(8,128)(2,1)S(1)} %get-tuple-element.41.v0), channel_id=1, source_target_pairs={{0,32},{32,64},{64,96},{96,0},{1,33},{33,65},{65,97},{97,1},{2,34}... | collective-permute-start | bytes 786440 | tf_op jit(solution)/shard_map/ppermute | solution.py:18
  173.1 3.2 %collective-permute-start.27 = (bf16[128,1024]{1,0:T(8,128)(2,1)S(1)}, bf16[128,1024]{1,0:T(8,128)(2,1)S(1)}, u32[]{:S(2)}, u32[]{:S(2)}) collective-permute-start(bf16[128,1024]{1,0:T(8,128)(2,1)S(1)} %get-tuple-element.41.v0), channel_id=1, source_target_pairs={{0,64},{32,96},{64,0},{96,32},{1,65},{33,97},{65,1},{97,33},{2,66}... | collective-permute-start | bytes 786440 | tf_op jit(solution)/shard_map/ppermute | solution.py:18
  180.3 6.5 %collective-permute-done.27.v2 = bf16[128,1024]{1,0:T(8,128)(2,1)S(1)} collective-permute-done((bf16[128,1024]{1,0:T(8,128)(2,1)S(1)}, bf16[128,1024]{1,0:T(8,128)(2,1)S(1)}, u32[]{:S(2)}, u32[]{:S(2)}) %collective-permute-start.27) | collective-permute-done | bytes 262176 | tf_op jit(solution)/shard_map/ppermute | solution.py:18
  187.1 2.5 %last_step.1 = (bf16[128,256]{1,0:T(8,128)(2,1)S(1)}, bf16[128,256]{1,0:T(8,128)(2,1)S(1)}, bf16[128,256]{1,0:T(8,128)(2,1)S(1)}, bf16[128,256]{1,0:T(8,128)(2,1)S(1)}) custom-call(s32[4]{0:T(128)S(1)} %pad_add_fusion.place_ref, bf16[128,1024]{1,0:T(8,128)(2,1)S(1)} %get-tuple-element.41.v0, bf16[128,1024]{1,0:T(8,128)(2,1)S(1)} %collective-permute-done.26.v1, ...), custom_call_target="tpu_custom_call" | custom-call | flops 268435456 | bytes 4194304 | tf_op jit(solution)/shard_map/last_step/pallas_call | solution.py:209
  189.6 2.4 %collective-permute-start.29 = (bf16[128,256]{1,0:T(8,128)(2,1)S(1)}, bf16[128,256]{1,0:T(8,128)(2,1)S(1)}, u32[]{:S(2)}, u32[]{:S(2)}) collective-permute-start(bf16[128,256]{1,0:T(8,128)(2,1)S(1)} %get-tuple-element.43), channel_id=1, source_target_pairs={{0,4},{4,8},{8,12},{12,0},{1,5},{5,9},{9,13},{13,1},{2,6},{6,10},{... | collective-permute-start | bytes 196616 | tf_op jit(solution)/shard_map/ppermute | solution.py:18
  194.7 3.0 %pack_known.1 = (bf16[2048,128]{1,0:T(8,128)(2,1)S(1)}, bf16[2048,256]{1,0:T(8,128)(2,1)S(1)}) custom-call(s32[4]{0:T(128)S(1)} %pad_add_fusion.place_ref, s32[4,1,256]{2,1,0:T(1,128)S(1)} %reshape.74.target_ref, bf16[128,1024]{1,0:T(8,128)(2,1)S(1)} %get-tuple-element.39.x1, bf16[128,1024]{1,0:T(8,128)(2,1)S(1)} %get-tuple-element.36.refs_0_.x2, ...), custom_call_target="tpu_custom_call" | custom-call | flops 402653184 | bytes 2097152 | tf_op jit(solution)/shard_map/pack_known/pallas_call | solution.py:290
  198.8 21.9 %all_to_all.5 = bf16[128,16,128]{2,1,0:T(8,128)(2,1)S(1)} all-to-all(bf16[128,16,128]{2,1,0:T(8,128)(2,1)S(1)} %bitcast.45), channel_id=1, replica_groups=mesh['z'=4,'core'=2,'y'=4,'x'=4] {'z','core','y','x'}, dimensions={0} | all-to-all | bytes 1048576 | tf_op jit(solution)/shard_map/all_to_all | solution.py:412
  (77 shorter events, 51.1 us)
Async XLA Ops:
  6.5 95.2 %all-gather.7.cloned.1.call-start = ((), (), s32[]{:S(2)}) async-start(), calls=%async_computation.2 | async-start | bytes 11796480 | tf_op jit(solution)/shard_map/all_gather | solution.py:356
  10.5 148.0 %all-gather.5.cloned.1.call-start = ((), (), s32[]{:S(2)}) async-start(), calls=%async_computation.1 | async-start | bytes 9510912 | tf_op jit(solution)/shard_map/all_gather | solution.py:356
  17.1 7.4 %collective-permute-start = (bf16[4,256,512]{2,1,0:T(8,128)(2,1)S(1)}, bf16[4,256,512]{2,1,0:T(8,128)(2,1)S(1)}, u32[]{:S(2)}, u32[]{:S(2)}) collective-permute-start(bf16[4,256,512]{2,1,0:T(8,128)(2,1)S(1)} %fusion.6), channel_id=1, source_target_pairs={{0,16},{16,0},{1,17},{17,1},{2,18},{18,2},{3,19},{19,3},{4,20},{20... | collective-permute-start | bytes 3145736 | tf_op jit(solution)/shard_map/ppermute | solution.py:22
  24.8 10.9 %collective-permute-start.1 = (bf16[256,512]{1,0:T(8,128)(2,1)S(1)}, bf16[256,512]{1,0:T(8,128)(2,1)S(1)}, u32[]{:S(2)}, u32[]{:S(2)}) collective-permute-start(bf16[256,512]{1,0:T(8,128)(2,1)S(1)} %slice_bitcast_fusion.3.v0), channel_id=1, source_target_pairs={{0,32},{32,64},{64,96},{96,0},{1,33},{33,65},{65,97},{97,1},{2,34}... | collective-permute-start | bytes 786440 | tf_op jit(solution)/shard_map/ppermute | solution.py:18
  27.6 10.8 %collective-permute-start.4 = (bf16[256,512]{1,0:T(8,128)(2,1)S(1)}, bf16[256,512]{1,0:T(8,128)(2,1)S(1)}, u32[]{:S(2)}, u32[]{:S(2)}) collective-permute-start(bf16[256,512]{1,0:T(8,128)(2,1)S(1)} %slice_bitcast_fusion.4.mine_ref), channel_id=1, source_target_pairs={{0,16},{16,0},{1,17},{17,1},{2,18},{18,2},{3,19},{19,3},{4,20},{20... | collective-permute-start | bytes 786440 | tf_op jit(solution)/shard_map/ppermute | solution.py:22
  28.0 14.2 %collective-permute-start.2 = (bf16[256,512]{1,0:T(8,128)(2,1)S(1)}, bf16[256,512]{1,0:T(8,128)(2,1)S(1)}, u32[]{:S(2)}, u32[]{:S(2)}) collective-permute-start(bf16[256,512]{1,0:T(8,128)(2,1)S(1)} %slice_bitcast_fusion.3.v0), channel_id=1, source_target_pairs={{0,64},{32,96},{64,0},{96,32},{1,65},{33,97},{65,1},{97,33},{2,66}... | collective-permute-start | bytes 786440 | tf_op jit(solution)/shard_map/ppermute | solution.py:18
  31.3 11.1 %collective-permute-start.3 = (bf16[256,512]{1,0:T(8,128)(2,1)S(1)}, bf16[256,512]{1,0:T(8,128)(2,1)S(1)}, u32[]{:S(2)}, u32[]{:S(2)}) collective-permute-start(bf16[256,512]{1,0:T(8,128)(2,1)S(1)} %slice_bitcast_fusion.3.v0), channel_id=1, source_target_pairs={{0,96},{32,0},{64,32},{96,64},{1,97},{33,1},{65,33},{97,65},{2,98}... | collective-permute-start | bytes 786440 | tf_op jit(solution)/shard_map/ppermute | solution.py:18
  37.1 12.2 %collective-permute-start.11 = (bf16[3,256,128]{2,1,0:T(8,128)(2,1)S(1)}, bf16[3,256,128]{2,1,0:T(8,128)(2,1)S(1)}, u32[]{:S(2)}, u32[]{:S(2)}) collective-permute-start(bf16[3,256,128]{2,1,0:T(8,128)(2,1)S(1)} %get-tuple-element.52), channel_id=1, source_target_pairs={{0,1},{1,2},{2,3},{3,0},{4,5},{5,6},{6,7},{7,4},{8,9},{9,10},{10,1... | collective-permute-start | bytes 589832 | tf_op jit(solution)/shard_map/ppermute | solution.py:18
  43.6 44.2 %collective-permute-start.5 = (bf16[128,1024]{1,0:T(8,128)(2,1)S(1)}, bf16[128,1024]{1,0:T(8,128)(2,1)S(1)}, u32[]{:S(2)}, u32[]{:S(2)}) collective-permute-start(bf16[128,1024]{1,0:T(8,128)(2,1)S(1)} %get-tuple-element.28), channel_id=1, source_target_pairs={{0,1},{1,2},{2,3},{3,0},{4,5},{5,6},{6,7},{7,4},{8,9},{9,10},{10,1... | collective-permute-start | bytes 786440 | tf_op jit(solution)/shard_map/ppermute | solution.py:18
  44.9 42.9 %collective-permute-start.6 = (bf16[128,1024]{1,0:T(8,128)(2,1)S(1)}, bf16[128,1024]{1,0:T(8,128)(2,1)S(1)}, u32[]{:S(2)}, u32[]{:S(2)}) collective-permute-start(bf16[128,1024]{1,0:T(8,128)(2,1)S(1)} %get-tuple-element.29), channel_id=1, source_target_pairs={{0,2},{1,3},{2,0},{3,1},{4,6},{5,7},{6,4},{7,5},{8,10},{9,11},{10,... | collective-permute-start | bytes 786440 | tf_op jit(solution)/shard_map/ppermute | solution.py:18
  47.4 40.4 %collective-permute-start.7 = (bf16[128,1024]{1,0:T(8,128)(2,1)S(1)}, bf16[128,1024]{1,0:T(8,128)(2,1)S(1)}, u32[]{:S(2)}, u32[]{:S(2)}) collective-permute-start(bf16[128,1024]{1,0:T(8,128)(2,1)S(1)} %get-tuple-element.30), channel_id=1, source_target_pairs={{0,3},{1,0},{2,1},{3,2},{4,7},{5,4},{6,5},{7,6},{8,11},{9,8},{10,9... | collective-permute-start | bytes 786440 | tf_op jit(solution)/shard_map/ppermute | solution.py:18
  48.5 32.6 %collective-permute-start.12 = (bf16[3,256,128]{2,1,0:T(8,128)(2,1)S(1)}, bf16[3,256,128]{2,1,0:T(8,128)(2,1)S(1)}, u32[]{:S(2)}, u32[]{:S(2)}) collective-permute-start(bf16[3,256,128]{2,1,0:T(8,128)(2,1)S(1)} %get-tuple-element.51), channel_id=1, source_target_pairs={{0,2},{1,3},{2,0},{3,1},{4,6},{5,7},{6,4},{7,5},{8,10},{9,11},{10,... | collective-permute-start | bytes 589832 | tf_op jit(solution)/shard_map/ppermute | solution.py:18
  49.3 37.6 %collective-permute-start.13 = (bf16[3,256,128]{2,1,0:T(8,128)(2,1)S(1)}, bf16[3,256,128]{2,1,0:T(8,128)(2,1)S(1)}, u32[]{:S(2)}, u32[]{:S(2)}) collective-permute-start(bf16[3,256,128]{2,1,0:T(8,128)(2,1)S(1)} %get-tuple-element.50), channel_id=1, source_target_pairs={{0,3},{1,0},{2,1},{3,2},{4,7},{5,4},{6,5},{7,6},{8,11},{9,8},{10,9... | collective-permute-start | bytes 589832 | tf_op jit(solution)/shard_map/ppermute | solution.py:18
  88.0 6.2 %collective-permute-start.10 = (bf16[128,1024]{1,0:T(8,128)(2,1)S(1)}, bf16[128,1024]{1,0:T(8,128)(2,1)S(1)}, u32[]{:S(2)}, u32[]{:S(2)}) collective-permute-start(bf16[128,1024]{1,0:T(8,128)(2,1)S(1)} %add_convert_fusion.1.refs_0_), channel_id=1, source_target_pairs={{0,12},{4,0},{8,4},{12,8},{1,13},{5,1},{9,5},{13,9},{2,14},{6,2},{... | collective-permute-start | bytes 786440 | tf_op jit(solution)/shard_map/ppermute | solution.py:18
  90.9 8.9 %collective-permute-start.8 = (bf16[128,1024]{1,0:T(8,128)(2,1)S(1)}, bf16[128,1024]{1,0:T(8,128)(2,1)S(1)}, u32[]{:S(2)}, u32[]{:S(2)}) collective-permute-start(bf16[128,1024]{1,0:T(8,128)(2,1)S(1)} %add_convert_fusion.1.refs_0_), channel_id=1, source_target_pairs={{0,4},{4,8},{8,12},{12,0},{1,5},{5,9},{9,13},{13,1},{2,6},{6,10},{... | collective-permute-start | bytes 786440 | tf_op jit(solution)/shard_map/ppermute | solution.py:18
  90.9 10.9 %collective-permute-start.9 = (bf16[128,1024]{1,0:T(8,128)(2,1)S(1)}, bf16[128,1024]{1,0:T(8,128)(2,1)S(1)}, u32[]{:S(2)}, u32[]{:S(2)}) collective-permute-start(bf16[128,1024]{1,0:T(8,128)(2,1)S(1)} %add_convert_fusion.1.refs_0_), channel_id=1, source_target_pairs={{0,8},{4,12},{8,0},{12,4},{1,9},{5,13},{9,1},{13,5},{2,10},{6,14},... | collective-permute-start | bytes 786440 | tf_op jit(solution)/shard_map/ppermute | solution.py:18
  103.8 8.7 %collective-permute-start.14 = (bf16[128,1024]{1,0:T(8,128)(2,1)S(1)}, bf16[128,1024]{1,0:T(8,128)(2,1)S(1)}, u32[]{:S(2)}, u32[]{:S(2)}) collective-permute-start(bf16[128,1024]{1,0:T(8,128)(2,1)S(1)} %get-tuple-element.32.v0), channel_id=1, source_target_pairs={{0,32},{32,64},{64,96},{96,0},{1,33},{33,65},{65,97},{97,1},{2,34}... | collective-permute-start | bytes 786440 | tf_op jit(solution)/shard_map/ppermute | solution.py:18
  106.3 11.3 %collective-permute-start.15 = (bf16[128,1024]{1,0:T(8,128)(2,1)S(1)}, bf16[128,1024]{1,0:T(8,128)(2,1)S(1)}, u32[]{:S(2)}, u32[]{:S(2)}) collective-permute-start(bf16[128,1024]{1,0:T(8,128)(2,1)S(1)} %get-tuple-element.32.v0), channel_id=1, source_target_pairs={{0,64},{32,96},{64,0},{96,32},{1,65},{33,97},{65,1},{97,33},{2,66}... | collective-permute-start | bytes 786440 | tf_op jit(solution)/shard_map/ppermute | solution.py:18
  109.4 8.6 %collective-permute-start.16 = (bf16[128,1024]{1,0:T(8,128)(2,1)S(1)}, bf16[128,1024]{1,0:T(8,128)(2,1)S(1)}, u32[]{:S(2)}, u32[]{:S(2)}) collective-permute-start(bf16[128,1024]{1,0:T(8,128)(2,1)S(1)} %get-tuple-element.32.v0), channel_id=1, source_target_pairs={{0,96},{32,0},{64,32},{96,64},{1,97},{33,1},{65,33},{97,65},{2,98}... | collective-permute-start | bytes 786440 | tf_op jit(solution)/shard_map/ppermute | solution.py:18
  120.0 7.7 %collective-permute-start.17 = (bf16[128,1024]{1,0:T(8,128)(2,1)S(1)}, bf16[128,1024]{1,0:T(8,128)(2,1)S(1)}, u32[]{:S(2)}, u32[]{:S(2)}) collective-permute-start(bf16[128,1024]{1,0:T(8,128)(2,1)S(1)} %diag_step.2.refs_0_), channel_id=1, source_target_pairs={{0,4},{4,8},{8,12},{12,0},{1,5},{5,9},{9,13},{13,1},{2,6},{6,10},{... | collective-permute-start | bytes 786440 | tf_op jit(solution)/shard_map/ppermute | solution.py:18
  121.0 11.2 %collective-permute-start.18 = (bf16[128,1024]{1,0:T(8,128)(2,1)S(1)}, bf16[128,1024]{1,0:T(8,128)(2,1)S(1)}, u32[]{:S(2)}, u32[]{:S(2)}) collective-permute-start(bf16[128,1024]{1,0:T(8,128)(2,1)S(1)} %diag_step.2.refs_0_), channel_id=1, source_target_pairs={{0,8},{4,12},{8,0},{12,4},{1,9},{5,13},{9,1},{13,5},{2,10},{6,14},... | collective-permute-start | bytes 786440 | tf_op jit(solution)/shard_map/ppermute | solution.py:18
  123.2 9.1 %collective-permute-start.19 = (bf16[128,1024]{1,0:T(8,128)(2,1)S(1)}, bf16[128,1024]{1,0:T(8,128)(2,1)S(1)}, u32[]{:S(2)}, u32[]{:S(2)}) collective-permute-start(bf16[128,1024]{1,0:T(8,128)(2,1)S(1)} %diag_step.2.refs_0_), channel_id=1, source_target_pairs={{0,12},{4,0},{8,4},{12,8},{1,13},{5,1},{9,5},{13,9},{2,14},{6,2},{... | collective-permute-start | bytes 786440 | tf_op jit(solution)/shard_map/ppermute | solution.py:18
  134.3 9.8 %collective-permute-start.20 = (bf16[128,1024]{1,0:T(8,128)(2,1)S(1)}, bf16[128,1024]{1,0:T(8,128)(2,1)S(1)}, u32[]{:S(2)}, u32[]{:S(2)}) collective-permute-start(bf16[128,1024]{1,0:T(8,128)(2,1)S(1)} %get-tuple-element.35.v0), channel_id=1, source_target_pairs={{0,32},{32,64},{64,96},{96,0},{1,33},{33,65},{65,97},{97,1},{2,34}... | collective-permute-start | bytes 786440 | tf_op jit(solution)/shard_map/ppermute | solution.py:18
  137.5 13.2 %collective-permute-start.21 = (bf16[128,1024]{1,0:T(8,128)(2,1)S(1)}, bf16[128,1024]{1,0:T(8,128)(2,1)S(1)}, u32[]{:S(2)}, u32[]{:S(2)}) collective-permute-start(bf16[128,1024]{1,0:T(8,128)(2,1)S(1)} %get-tuple-element.35.v0), channel_id=1, source_target_pairs={{0,64},{32,96},{64,0},{96,32},{1,65},{33,97},{65,1},{97,33},{2,66}... | collective-permute-start | bytes 786440 | tf_op jit(solution)/shard_map/ppermute | solution.py:18
  140.9 10.5 %collective-permute-start.22 = (bf16[128,1024]{1,0:T(8,128)(2,1)S(1)}, bf16[128,1024]{1,0:T(8,128)(2,1)S(1)}, u32[]{:S(2)}, u32[]{:S(2)}) collective-permute-start(bf16[128,1024]{1,0:T(8,128)(2,1)S(1)} %get-tuple-element.35.v0), channel_id=1, source_target_pairs={{0,96},{32,0},{64,32},{96,64},{1,97},{33,1},{65,33},{97,65},{2,98}... | collective-permute-start | bytes 786440 | tf_op jit(solution)/shard_map/ppermute | solution.py:18
  153.2 10.4 %collective-permute-start.23 = (bf16[128,1024]{1,0:T(8,128)(2,1)S(1)}, bf16[128,1024]{1,0:T(8,128)(2,1)S(1)}, u32[]{:S(2)}, u32[]{:S(2)}) collective-permute-start(bf16[128,1024]{1,0:T(8,128)(2,1)S(1)} %diag_step.3.refs_0_), channel_id=1, source_target_pairs={{0,4},{4,8},{8,12},{12,0},{1,5},{5,9},{9,13},{13,1},{2,6},{6,10},{... | collective-permute-start | bytes 786440 | tf_op jit(solution)/shard_map/ppermute | solution.py:18
  156.0 12.0 %collective-permute-start.24 = (bf16[128,1024]{1,0:T(8,128)(2,1)S(1)}, bf16[128,1024]{1,0:T(8,128)(2,1)S(1)}, u32[]{:S(2)}, u32[]{:S(2)}) collective-permute-start(bf16[128,1024]{1,0:T(8,128)(2,1)S(1)} %diag_step.3.refs_0_), channel_id=1, source_target_pairs={{0,8},{4,12},{8,0},{12,4},{1,9},{5,13},{9,1},{13,5},{2,10},{6,14},... | collective-permute-start | bytes 786440 | tf_op jit(solution)/shard_map/ppermute | solution.py:18
  158.1 10.2 %collective-permute-start.25 = (bf16[128,1024]{1,0:T(8,128)(2,1)S(1)}, bf16[128,1024]{1,0:T(8,128)(2,1)S(1)}, u32[]{:S(2)}, u32[]{:S(2)}) collective-permute-start(bf16[128,1024]{1,0:T(8,128)(2,1)S(1)} %diag_step.3.refs_0_), channel_id=1, source_target_pairs={{0,12},{4,0},{8,4},{12,8},{1,13},{5,1},{9,5},{13,9},{2,14},{6,2},{... | collective-permute-start | bytes 786440 | tf_op jit(solution)/shard_map/ppermute | solution.py:18
  170.3 10.1 %collective-permute-start.26 = (bf16[128,1024]{1,0:T(8,128)(2,1)S(1)}, bf16[128,1024]{1,0:T(8,128)(2,1)S(1)}, u32[]{:S(2)}, u32[]{:S(2)}) collective-permute-start(bf16[128,1024]{1,0:T(8,128)(2,1)S(1)} %get-tuple-element.41.v0), channel_id=1, source_target_pairs={{0,32},{32,64},{64,96},{96,0},{1,33},{33,65},{65,97},{97,1},{2,34}... | collective-permute-start | bytes 786440 | tf_op jit(solution)/shard_map/ppermute | solution.py:18
  173.1 13.7 %collective-permute-start.27 = (bf16[128,1024]{1,0:T(8,128)(2,1)S(1)}, bf16[128,1024]{1,0:T(8,128)(2,1)S(1)}, u32[]{:S(2)}, u32[]{:S(2)}) collective-permute-start(bf16[128,1024]{1,0:T(8,128)(2,1)S(1)} %get-tuple-element.41.v0), channel_id=1, source_target_pairs={{0,64},{32,96},{64,0},{96,32},{1,65},{33,97},{65,1},{97,33},{2,66}... | collective-permute-start | bytes 786440 | tf_op jit(solution)/shard_map/ppermute | solution.py:18
  176.3 10.8 %collective-permute-start.28 = (bf16[128,1024]{1,0:T(8,128)(2,1)S(1)}, bf16[128,1024]{1,0:T(8,128)(2,1)S(1)}, u32[]{:S(2)}, u32[]{:S(2)}) collective-permute-start(bf16[128,1024]{1,0:T(8,128)(2,1)S(1)} %get-tuple-element.41.v0), channel_id=1, source_target_pairs={{0,96},{32,0},{64,32},{96,64},{1,97},{33,1},{65,33},{97,65},{2,98}... | collective-permute-start | bytes 786440 | tf_op jit(solution)/shard_map/ppermute | solution.py:18
  189.6 8.1 %collective-permute-start.29 = (bf16[128,256]{1,0:T(8,128)(2,1)S(1)}, bf16[128,256]{1,0:T(8,128)(2,1)S(1)}, u32[]{:S(2)}, u32[]{:S(2)}) collective-permute-start(bf16[128,256]{1,0:T(8,128)(2,1)S(1)} %get-tuple-element.43), channel_id=1, source_target_pairs={{0,4},{4,8},{8,12},{12,0},{1,5},{5,9},{9,13},{13,1},{2,6},{6,10},{... | collective-permute-start | bytes 196616 | tf_op jit(solution)/shard_map/ppermute | solution.py:18
  (2 other events, 9.7 us)
Sparse Core Ops, SparseCore 0:
  10.6 81.7 all-gather.6
  94.1 50.2 all-gather.4

commit v7 on v6

--- a/solution.py
+++ b/solution.py
@@ -237,24 +237,32 @@
             ((lower_ref, diag_ref)[which].at[index, :, lanes], number, pl.ds(start, height))
             for which, index, lanes, number, start, height in moves
         ]
-        plan.append((owners_ref, count - 1, pl.ds(heights[-1] - 16, 16)))
+        named = pl.ds(heights[-1] - 16, 16)
+        spread_out = jnp.broadcast_to(owners_ref[...].astype(F32), (16, 128)).astype(BF16)
+        held[-1][named, :128] = spread_out
+        held[-1][named, 128:] = jnp.zeros((16, 128), BF16)
         into, onward = [], []
         for at, (source, number, where) in enumerate(plan):
             middle = held[number].at[where]
             into.append(pltpu.make_async_copy(source, middle, sems.at[0, at]))
             onward.append(pltpu.make_async_copy(middle, outs[number].at[where], sems.at[1, at]))
+        last = pltpu.make_async_copy(
+            held[-1].at[named], outs[-1].at[named], sems.at[1, len(moves)]
+        )
         for copy in into:
             copy.start()
+        last.start()
         for first, second in zip(into, onward):
             first.wait()
             second.start()
         for copy in onward:
             copy.wait()
+        last.wait()
 
     return pl.pallas_call(
         kernel,
         out_shape=tuple(jax.ShapeDtypeStruct((height, 256), BF16) for height in heights),
-        in_specs=[HBM] * 3,
+        in_specs=[HBM, HBM, VMEM],
         out_specs=(HBM,) * count,
         scratch_shapes=[pltpu.VMEM((height, 256), BF16) for height in heights]
         + [pltpu.SemaphoreType.DMA((2, len(moves) + 1))],
@@ -364,12 +372,13 @@
     def tile(j, k):
         return ("L", pair_slot(j, k))
 
-    owners = jnp.pad(owner_map[0, :, 0].astype(BF16)[None], ((0, 15), (0, 128)))
+    owners = owner_map[:, :, 0]
     orders = [
-        [tile(3, 2), ("D", 2), tile(3, 1), tile(2, 1), ("D", 1)],
+        [tile(3, 2), ("D", 2)],
+        [tile(3, 1), tile(2, 1), ("D", 1)],
         [tile(3, 0), tile(2, 0), tile(1, 0), ("D", 0)],
     ]
-    early, late = map(gathered, stage(lower_tiles, inverse_diag, orders, owners))
+    early, middle, late = map(gathered, stage(lower_tiles, inverse_diag, orders, owners))
     named = late[:, :, 2048, :128].astype(jnp.int32).reshape(8, 128)
     other = swap(inverse_diag[3])
 
@@ -398,10 +407,10 @@
     residual, x3 = lower_step(base[2], pieces, early, 0, BF16)
     over_z = spread(residual, "z")
     pieces = spread(diag_step(over_z, early, 1), "y")
-    base1, _ = lower_step(base[1], (x3,), early, 2, F32)
-    residual, x2 = lower_step(base1, pieces, early, 3, BF16)
+    base1, _ = lower_step(base[1], (x3,), middle, 0, F32)
+    residual, x2 = lower_step(base1, pieces, middle, 1, BF16)
     over_z = spread(residual, "z")
-    pieces = spread(diag_step(over_z, early, 4), "y")
+    pieces = spread(diag_step(over_z, middle, 2), "y")
     base0, _ = lower_step(base[0], (x3,), late, 0, F32)
     base0, _ = lower_step(base0, (x2,), late, 1, F32)
     residual, x1 = lower_step(base0, pieces, late, 2, BF16)

time: 230 us -> 214 us (0.930)
  waiting for transfers between devices: 91.7 us -> 68.9 us
  starting transfers between devices: 54.1 us -> 61.5 us
    ppermute x30, waiting for transfers between devices: 91 us -> 62.7 us  [shift(): return lax.ppermute(value, axis, [(i, (i + by) % 4) for i in range(4)])]
    ppermute x30, starting transfers between devices: 52.2 us -> 59.5 us  [shift(): return lax.ppermute(value, axis, [(i, (i + by) % 4) for i in range(4)])]
    all_gather x2 -> x3, waiting for transfers between devices: 0.02 us -> 4.78 us  [gathered(): lax.all_gather(joined, ('core', 'x'), axis=0, tiled=False)]
  transfers between devices with their start and end apart: 34 -> 35, of which waited for: 22 -> 20; matrix products, arithmetic and copies ran while one was open for 7% -> 8% of each run, Pallas kernels for 9% -> 9%
where the time goes in v7:
time: 214 us
  waiting for transfers between devices  68.9 us (32%)
  starting transfers between devices  61.5 us (29%)
  Pallas kernels  29.5 us (14%)
  blocking collectives  23.8 us (11%)
  between operations  14 us (7%)
  matrix products  11.7 us (5%)
  other arithmetic  2.54 us (1%)
    ppermute x30, waiting for transfers between devices, shift(): return lax.ppermute(value, axis, [(i, (i + by) % 4) for i in range(4)])  62.7 us
    ppermute x30, starting transfers between devices, shift(): return lax.ppermute(value, axis, [(i, (i + by) % 4) for i in range(4)])  59.5 us
    all_to_all x1, blocking collectives, local(): lax.all_to_all(packed, ('z', 'core', 'y', 'x'), split_axis=0, concat_axis...  23.8 us
    pallas_call x6, Pallas kernels, lower_step(): pl.pallas_call(kernel, out_shape=(jax.ShapeDtypeStruct((128, 1024), dtype...  14 us
    dot_general x2, matrix products, term(): lax.dot_general(border_tiles, bound, (((0,), (0,)), ((), ())), preferred_...  11.7 us
    all_gather x3, waiting for transfers between devices, gathered(): lax.all_gather(joined, ('core', 'x'), axis=0, tiled=False)  4.78 us
  transfers between devices with their start and end apart: 35, of which 20 were waited for; matrix products, arithmetic and copies ran while one was open for 8% of the time, Pallas kernels for 9%

profile of v7, /device:TPU:1, one launch (start us, length us, event | category | flops | bytes accessed | tf_op | source)
XLA Modules:
  0.0 214.0 jit_solution(8857720140416559720)
XLA Ops:
  6.5 3.3 %stage.1 = (bf16[1024,256]{1,0:T(8,128)(2,1)}, bf16[1536,256]{1,0:T(8,128)(2,1)}, bf16[2064,256]{1,0:T(8,128)(2,1)}) custom-call(bf16[6,512,256]{2,1,0:T(8,128)(2,1)} %lower_ref.1, bf16[4,256,512]{2,1,0:T(8,128)(2,1)} %diag_ref.1, s32[1,128]{1,0:T(1,128)} %bitcast.58), custom_call_target="tpu_custom_call" | custom-call | bytes 6291456 | tf_op jit(solution)/shard_map/stage/pallas_call | solution.py:262
  11.3 5.9 %fusion.6 = bf16[4,256,512]{2,1,0:T(8,128)(2,1)S(1)} fusion(f32[4,256,1024]{2,1,0:T(8,128)} %param.6, s32[]{:T(128)S(6)} %select_n.26, bf16[2048,4,256]{2,1,0:T(4,128)(2,1)} %param.8, bf16[2048,1024]{1,0:T(8,128)(2,1)} %param.7, f32[]{:T(128)S(6)} %select_n.24), kind=kOutput, calls=%fused_computation.7 | convolution fusion | flops 2149056512 | bytes 9438720 | tf_op jit(solution)/shard_map/dot_general | solution.py:389
  18.7 5.9 %fusion.7 = bf16[4,256,512]{2,1,0:T(8,128)(2,1)S(1)} fusion(f32[4,256,1024]{2,1,0:T(8,128)} %param.6, s32[]{:T(128)S(6)} %select_n.25, bf16[2048,4,256]{2,1,0:T(4,128)(2,1)} %param.8, bf16[2048,1024]{1,0:T(8,128)(2,1)} %param.7, f32[]{:T(128)S(6)} %select_n.24), kind=kOutput, calls=%fused_computation.9 | convolution fusion | flops 2149056512 | bytes 9438720 | tf_op jit(solution)/shard_map/dot_general | solution.py:389
  28.0 3.4 %collective-permute-start.2 = (bf16[256,512]{1,0:T(8,128)(2,1)S(1)}, bf16[256,512]{1,0:T(8,128)(2,1)S(1)}, u32[]{:S(2)}, u32[]{:S(2)}) collective-permute-start(bf16[256,512]{1,0:T(8,128)(2,1)S(1)} %slice_bitcast_fusion.3.v0), channel_id=1, source_target_pairs={{0,64},{32,96},{64,0},{96,32},{1,65},{33,97},{65,1},{97,33},{2,66}... | collective-permute-start | bytes 786440 | tf_op jit(solution)/shard_map/ppermute | solution.py:18
  32.1 3.7 %collective-permute-done.1.v1 = bf16[256,512]{1,0:T(8,128)(2,1)S(1)} collective-permute-done((bf16[256,512]{1,0:T(8,128)(2,1)S(1)}, bf16[256,512]{1,0:T(8,128)(2,1)S(1)}, u32[]{:S(2)}, u32[]{:S(2)}) %collective-permute-start.1) | collective-permute-done | bytes 262176 | tf_op jit(solution)/shard_map/ppermute | solution.py:18
  38.5 3.8 %collective-permute-done.2.v2 = bf16[256,512]{1,0:T(8,128)(2,1)S(1)} collective-permute-done((bf16[256,512]{1,0:T(8,128)(2,1)S(1)}, bf16[256,512]{1,0:T(8,128)(2,1)S(1)}, u32[]{:S(2)}, u32[]{:S(2)}) %collective-permute-start.2) | collective-permute-done | bytes 262176 | tf_op jit(solution)/shard_map/ppermute | solution.py:18
  43.7 2.6 %collective-permute-start.7 = (bf16[128,1024]{1,0:T(8,128)(2,1)S(1)}, bf16[128,1024]{1,0:T(8,128)(2,1)S(1)}, u32[]{:S(2)}, u32[]{:S(2)}) collective-permute-start(bf16[128,1024]{1,0:T(8,128)(2,1)S(1)} %get-tuple-element.31), channel_id=1, source_target_pairs={{0,3},{1,0},{2,1},{3,2},{4,7},{5,4},{6,5},{7,6},{8,11},{9,8},{10,9... | collective-permute-start | bytes 786440 | tf_op jit(solution)/shard_map/ppermute | solution.py:18
  51.3 13.0 %collective-permute-done.12.v2 = bf16[3,256,128]{2,1,0:T(8,128)(2,1)S(1)} collective-permute-done((bf16[3,256,128]{2,1,0:T(8,128)(2,1)S(1)}, bf16[3,256,128]{2,1,0:T(8,128)(2,1)S(1)}, u32[]{:S(2)}, u32[]{:S(2)}) %collective-permute-start.12) | collective-permute-done | bytes 196640 | tf_op jit(solution)/shard_map/ppermute | solution.py:18
  64.3 3.6 %collective-permute-done.13.v3 = bf16[3,256,128]{2,1,0:T(8,128)(2,1)S(1)} collective-permute-done((bf16[3,256,128]{2,1,0:T(8,128)(2,1)S(1)}, bf16[3,256,128]{2,1,0:T(8,128)(2,1)S(1)}, u32[]{:S(2)}, u32[]{:S(2)}) %collective-permute-start.13) | collective-permute-done | bytes 196640 | tf_op jit(solution)/shard_map/ppermute | solution.py:18
  70.3 2.9 %collective-permute-start.9 = (bf16[128,1024]{1,0:T(8,128)(2,1)S(1)}, bf16[128,1024]{1,0:T(8,128)(2,1)S(1)}, u32[]{:S(2)}, u32[]{:S(2)}) collective-permute-start(bf16[128,1024]{1,0:T(8,128)(2,1)S(1)} %add_convert_fusion.1.refs_0_), channel_id=1, source_target_pairs={{0,8},{4,12},{8,0},{12,4},{1,9},{5,13},{9,1},{13,5},{2,10},{6,14},... | collective-permute-start | bytes 786440 | tf_op jit(solution)/shard_map/ppermute | solution.py:18
  76.2 3.7 %collective-permute-done.9.refs_2_ = bf16[128,1024]{1,0:T(8,128)(2,1)S(1)} collective-permute-done((bf16[128,1024]{1,0:T(8,128)(2,1)S(1)}, bf16[128,1024]{1,0:T(8,128)(2,1)S(1)}, u32[]{:S(2)}, u32[]{:S(2)}) %collective-permute-start.9) | collective-permute-done | bytes 262176 | tf_op jit(solution)/shard_map/ppermute | solution.py:18
  82.1 3.4 %collective-permute-start.14 = (bf16[128,1024]{1,0:T(8,128)(2,1)S(1)}, bf16[128,1024]{1,0:T(8,128)(2,1)S(1)}, u32[]{:S(2)}, u32[]{:S(2)}) collective-permute-start(bf16[128,1024]{1,0:T(8,128)(2,1)S(1)} %get-tuple-element.33.v0), channel_id=1, source_target_pairs={{0,32},{32,64},{64,96},{96,0},{1,33},{33,65},{65,97},{97,1},{2,34}... | collective-permute-start | bytes 786440 | tf_op jit(solution)/shard_map/ppermute | solution.py:18
  85.5 4.6 %collective-permute-start.15 = (bf16[128,1024]{1,0:T(8,128)(2,1)S(1)}, bf16[128,1024]{1,0:T(8,128)(2,1)S(1)}, u32[]{:S(2)}, u32[]{:S(2)}) collective-permute-start(bf16[128,1024]{1,0:T(8,128)(2,1)S(1)} %get-tuple-element.33.v0), channel_id=1, source_target_pairs={{0,64},{32,96},{64,0},{96,32},{1,65},{33,97},{65,1},{97,33},{2,66}... | collective-permute-start | bytes 786440 | tf_op jit(solution)/shard_map/ppermute | solution.py:18
  90.1 2.6 %collective-permute-done.14.v1 = bf16[128,1024]{1,0:T(8,128)(2,1)S(1)} collective-permute-done((bf16[128,1024]{1,0:T(8,128)(2,1)S(1)}, bf16[128,1024]{1,0:T(8,128)(2,1)S(1)}, u32[]{:S(2)}, u32[]{:S(2)}) %collective-permute-start.14) | collective-permute-done | bytes 262176 | tf_op jit(solution)/shard_map/ppermute | solution.py:18
  92.7 4.9 %collective-permute-done.15.v2 = bf16[128,1024]{1,0:T(8,128)(2,1)S(1)} collective-permute-done((bf16[128,1024]{1,0:T(8,128)(2,1)S(1)}, bf16[128,1024]{1,0:T(8,128)(2,1)S(1)}, u32[]{:S(2)}, u32[]{:S(2)}) %collective-permute-start.15) | collective-permute-done | bytes 262176 | tf_op jit(solution)/shard_map/ppermute | solution.py:18
  98.6 7.1 %collective-permute-start.17 = (bf16[128,1024]{1,0:T(8,128)(2,1)S(1)}, bf16[128,1024]{1,0:T(8,128)(2,1)S(1)}, u32[]{:S(2)}, u32[]{:S(2)}) collective-permute-start(bf16[128,1024]{1,0:T(8,128)(2,1)S(1)} %diag_step.2.refs_0_), channel_id=1, source_target_pairs={{0,4},{4,8},{8,12},{12,0},{1,5},{5,9},{9,13},{13,1},{2,6},{6,10},{... | collective-permute-start | bytes 786440 | tf_op jit(solution)/shard_map/ppermute | solution.py:18
  108.2 2.7 %lower_step.7 = (f32[128,1024]{1,0:T(8,128)S(1)}, bf16[128,1024]{1,0:T(8,128)(2,1)}) custom-call(bf16[128,1024]{1,0:T(8,128)(2,1)S(1)} %get-tuple-element.34.refs_0_.x3, f32[128,1024]{1,0:T(8,128)S(1)} %get-tuple-element.50.refs_1_, bf16[2,4,1536,256]{3,2,1,0:T(8,128)(2,1)} %bitcast.54), custom_call_target="tpu_custom_call" | custom-call | flops 268435456 | bytes 4194304 | tf_op jit(solution)/shard_map/lower_step/pallas_call | solution.py:130
  110.9 4.4 %collective-permute-done.18.refs_2_ = bf16[128,1024]{1,0:T(8,128)(2,1)S(1)} collective-permute-done((bf16[128,1024]{1,0:T(8,128)(2,1)S(1)}, bf16[128,1024]{1,0:T(8,128)(2,1)S(1)}, u32[]{:S(2)}, u32[]{:S(2)}) %collective-permute-start.18) | collective-permute-done | bytes 262176 | tf_op jit(solution)/shard_map/ppermute | solution.py:18
  117.6 2.6 %collective-permute-start.20 = (bf16[128,1024]{1,0:T(8,128)(2,1)S(1)}, bf16[128,1024]{1,0:T(8,128)(2,1)S(1)}, u32[]{:S(2)}, u32[]{:S(2)}) collective-permute-start(bf16[128,1024]{1,0:T(8,128)(2,1)S(1)} %get-tuple-element.37.v0), channel_id=1, source_target_pairs={{0,32},{32,64},{64,96},{96,0},{1,33},{33,65},{65,97},{97,1},{2,34}... | collective-permute-start | bytes 786440 | tf_op jit(solution)/shard_map/ppermute | solution.py:18
  120.2 3.7 %collective-permute-start.21 = (bf16[128,1024]{1,0:T(8,128)(2,1)S(1)}, bf16[128,1024]{1,0:T(8,128)(2,1)S(1)}, u32[]{:S(2)}, u32[]{:S(2)}) collective-permute-start(bf16[128,1024]{1,0:T(8,128)(2,1)S(1)} %get-tuple-element.37.v0), channel_id=1, source_target_pairs={{0,64},{32,96},{64,0},{96,32},{1,65},{33,97},{65,1},{97,33},{2,66}... | collective-permute-start | bytes 786440 | tf_op jit(solution)/shard_map/ppermute | solution.py:18
  123.9 3.6 %collective-permute-done.20.v1 = bf16[128,1024]{1,0:T(8,128)(2,1)S(1)} collective-permute-done((bf16[128,1024]{1,0:T(8,128)(2,1)S(1)}, bf16[128,1024]{1,0:T(8,128)(2,1)S(1)}, u32[]{:S(2)}, u32[]{:S(2)}) %collective-permute-start.20) | collective-permute-done | bytes 262176 | tf_op jit(solution)/shard_map/ppermute | solution.py:18
  127.4 6.4 %collective-permute-done.21.v2 = bf16[128,1024]{1,0:T(8,128)(2,1)S(1)} collective-permute-done((bf16[128,1024]{1,0:T(8,128)(2,1)S(1)}, bf16[128,1024]{1,0:T(8,128)(2,1)S(1)}, u32[]{:S(2)}, u32[]{:S(2)}) %collective-permute-start.21) | collective-permute-done | bytes 262176 | tf_op jit(solution)/shard_map/ppermute | solution.py:18
  136.5 3.7 %collective-permute-start.23 = (bf16[128,1024]{1,0:T(8,128)(2,1)S(1)}, bf16[128,1024]{1,0:T(8,128)(2,1)S(1)}, u32[]{:S(2)}, u32[]{:S(2)}) collective-permute-start(bf16[128,1024]{1,0:T(8,128)(2,1)S(1)} %diag_step.3.refs_0_), channel_id=1, source_target_pairs={{0,4},{4,8},{8,12},{12,0},{1,5},{5,9},{9,13},{13,1},{2,6},{6,10},{... | collective-permute-start | bytes 786440 | tf_op jit(solution)/shard_map/ppermute | solution.py:18
  142.8 4.8 %all-gather.7.cloned.1.call-done = bf16[16512,256]{1,0:T(8,128)(2,1)} async-done(((bf16[2064,256]{1,0:T(8,128)(2,1)}), bf16[16512,256]{1,0:T(8,128)(2,1)}) %all-gather.7.cloned.1.call-update) | async-done | bytes 8454160 | tf_op jit(solution)/shard_map/all_gather | solution.py:364
  147.5 2.5 %lower_step.9 = (f32[128,1024]{1,0:T(8,128)S(1)}, bf16[128,1024]{1,0:T(8,128)(2,1)}) custom-call(bf16[128,1024]{1,0:T(8,128)(2,1)S(1)} %get-tuple-element.34.refs_0_.x3, f32[128,1024]{1,0:T(8,128)S(1)} %get-tuple-element.49.refs_1_, bf16[2,4,2064,256]{3,2,1,0:T(8,128)(2,1)} %bitcast.48), custom_call_target="tpu_custom_call" | custom-call | flops 268435456 | bytes 4194304 | tf_op jit(solution)/shard_map/lower_step/pallas_call | solution.py:130
  150.1 2.5 %lower_step.10 = (f32[128,1024]{1,0:T(8,128)S(1)}, bf16[128,1024]{1,0:T(8,128)(2,1)}) custom-call(bf16[128,1024]{1,0:T(8,128)(2,1)S(1)} %get-tuple-element.38.refs_0_.x2, f32[128,1024]{1,0:T(8,128)S(1)} %get-tuple-element.39.refs_1_, bf16[2,4,2064,256]{3,2,1,0:T(8,128)(2,1)} %bitcast.49), custom_call_target="tpu_custom_call" | custom-call | flops 268435456 | bytes 4194304 | tf_op jit(solution)/shard_map/lower_step/pallas_call | solution.py:130
  156.2 3.6 %collective-permute-start.27 = (bf16[128,1024]{1,0:T(8,128)(2,1)S(1)}, bf16[128,1024]{1,0:T(8,128)(2,1)S(1)}, u32[]{:S(2)}, u32[]{:S(2)}) collective-permute-start(bf16[128,1024]{1,0:T(8,128)(2,1)S(1)} %get-tuple-element.43.v0), channel_id=1, source_target_pairs={{0,64},{32,96},{64,0},{96,32},{1,65},{33,97},{65,1},{97,33},{2,66}... | collective-permute-start | bytes 786440 | tf_op jit(solution)/shard_map/ppermute | solution.py:18
  163.8 6.7 %collective-permute-done.27.v2 = bf16[128,1024]{1,0:T(8,128)(2,1)S(1)} collective-permute-done((bf16[128,1024]{1,0:T(8,128)(2,1)S(1)}, bf16[128,1024]{1,0:T(8,128)(2,1)S(1)}, u32[]{:S(2)}, u32[]{:S(2)}) %collective-permute-start.27) | collective-permute-done | bytes 262176 | tf_op jit(solution)/shard_map/ppermute | solution.py:18
  170.7 2.5 %last_step.1 = (bf16[128,256]{1,0:T(8,128)(2,1)S(1)}, bf16[128,256]{1,0:T(8,128)(2,1)S(1)}, bf16[128,256]{1,0:T(8,128)(2,1)S(1)}, bf16[128,256]{1,0:T(8,128)(2,1)S(1)}) custom-call(s32[4]{0:T(128)S(1)} %pad_add_fusion.place_ref, bf16[128,1024]{1,0:T(8,128)(2,1)S(1)} %get-tuple-element.43.v0, bf16[128,1024]{1,0:T(8,128)(2,1)S(1)} %collective-permute-done.26.v1, ...), custom_call_target="tpu_custom_call" | custom-call | flops 268435456 | bytes 4194304 | tf_op jit(solution)/shard_map/last_step/pallas_call | solution.py:209
  174.5 3.2 %collective-permute-start.30 = (bf16[128,256]{1,0:T(8,128)(2,1)S(1)}, bf16[128,256]{1,0:T(8,128)(2,1)S(1)}, u32[]{:S(2)}, u32[]{:S(2)}) collective-permute-start(bf16[128,256]{1,0:T(8,128)(2,1)S(1)} %get-tuple-element.46), channel_id=1, source_target_pairs={{0,8},{4,12},{8,0},{12,4},{1,9},{5,13},{9,1},{13,5},{2,10},{6,14},... | collective-permute-start | bytes 196616 | tf_op jit(solution)/shard_map/ppermute | solution.py:18
  177.9 3.0 %pack_known.1 = (bf16[2048,128]{1,0:T(8,128)(2,1)S(1)}, bf16[2048,256]{1,0:T(8,128)(2,1)S(1)}) custom-call(s32[4]{0:T(128)S(1)} %pad_add_fusion.place_ref, s32[4,1,256]{2,1,0:T(1,128)S(1)} %reshape.66.target_ref, bf16[128,1024]{1,0:T(8,128)(2,1)S(1)} %get-tuple-element.41.x1, bf16[128,1024]{1,0:T(8,128)(2,1)S(1)} %get-tuple-element.38.refs_0_.x2, ...), custom_call_target="tpu_custom_call" | custom-call | flops 402653184 | bytes 2097152 | tf_op jit(solution)/shard_map/pack_known/pallas_call | solution.py:298
  182.2 23.8 %all_to_all.5 = bf16[128,16,128]{2,1,0:T(8,128)(2,1)S(1)} all-to-all(bf16[128,16,128]{2,1,0:T(8,128)(2,1)S(1)} %bitcast.47), channel_id=1, replica_groups=mesh['z'=4,'core'=2,'y'=4,'x'=4] {'z','core','y','x'}, dimensions={0} | all-to-all | bytes 1048576 | tf_op jit(solution)/shard_map/all_to_all | solution.py:421
  (80 shorter events, 46.0 us)
Async XLA Ops:
  6.5 73.4 %all-gather.9.cloned.1.call-start = ((), (), s32[]{:S(2)}) async-start(), calls=%async_computation.2 | async-start | bytes 4718592 | tf_op jit(solution)/shard_map/all_gather | solution.py:364
  9.8 98.4 %all-gather.11.cloned.1.call-start = ((), (), s32[]{:S(2)}) async-start(), calls=%async_computation.3 | async-start | bytes 7077888 | tf_op jit(solution)/shard_map/all_gather | solution.py:364
  10.6 137.0 %all-gather.7.cloned.1.call-start = ((), (), s32[]{:S(2)}) async-start(), calls=%async_computation.1 | async-start | bytes 9510912 | tf_op jit(solution)/shard_map/all_gather | solution.py:364
  17.2 7.4 %collective-permute-start = (bf16[4,256,512]{2,1,0:T(8,128)(2,1)S(1)}, bf16[4,256,512]{2,1,0:T(8,128)(2,1)S(1)}, u32[]{:S(2)}, u32[]{:S(2)}) collective-permute-start(bf16[4,256,512]{2,1,0:T(8,128)(2,1)S(1)} %fusion.6), channel_id=1, source_target_pairs={{0,16},{16,0},{1,17},{17,1},{2,18},{18,2},{3,19},{19,3},{4,20},{20... | collective-permute-start | bytes 3145736 | tf_op jit(solution)/shard_map/ppermute | solution.py:22
  24.9 10.9 %collective-permute-start.1 = (bf16[256,512]{1,0:T(8,128)(2,1)S(1)}, bf16[256,512]{1,0:T(8,128)(2,1)S(1)}, u32[]{:S(2)}, u32[]{:S(2)}) collective-permute-start(bf16[256,512]{1,0:T(8,128)(2,1)S(1)} %slice_bitcast_fusion.3.v0), channel_id=1, source_target_pairs={{0,32},{32,64},{64,96},{96,0},{1,33},{33,65},{65,97},{97,1},{2,34}... | collective-permute-start | bytes 786440 | tf_op jit(solution)/shard_map/ppermute | solution.py:18
  27.7 10.8 %collective-permute-start.4 = (bf16[256,512]{1,0:T(8,128)(2,1)S(1)}, bf16[256,512]{1,0:T(8,128)(2,1)S(1)}, u32[]{:S(2)}, u32[]{:S(2)}) collective-permute-start(bf16[256,512]{1,0:T(8,128)(2,1)S(1)} %slice_bitcast_fusion.4.mine_ref), channel_id=1, source_target_pairs={{0,16},{16,0},{1,17},{17,1},{2,18},{18,2},{3,19},{19,3},{4,20},{20... | collective-permute-start | bytes 786440 | tf_op jit(solution)/shard_map/ppermute | solution.py:22
  28.0 14.3 %collective-permute-start.2 = (bf16[256,512]{1,0:T(8,128)(2,1)S(1)}, bf16[256,512]{1,0:T(8,128)(2,1)S(1)}, u32[]{:S(2)}, u32[]{:S(2)}) collective-permute-start(bf16[256,512]{1,0:T(8,128)(2,1)S(1)} %slice_bitcast_fusion.3.v0), channel_id=1, source_target_pairs={{0,64},{32,96},{64,0},{96,32},{1,65},{33,97},{65,1},{97,33},{2,66}... | collective-permute-start | bytes 786440 | tf_op jit(solution)/shard_map/ppermute | solution.py:18
  31.5 11.1 %collective-permute-start.3 = (bf16[256,512]{1,0:T(8,128)(2,1)S(1)}, bf16[256,512]{1,0:T(8,128)(2,1)S(1)}, u32[]{:S(2)}, u32[]{:S(2)}) collective-permute-start(bf16[256,512]{1,0:T(8,128)(2,1)S(1)} %slice_bitcast_fusion.3.v0), channel_id=1, source_target_pairs={{0,96},{32,0},{64,32},{96,64},{1,97},{33,1},{65,33},{97,65},{2,98}... | collective-permute-start | bytes 786440 | tf_op jit(solution)/shard_map/ppermute | solution.py:18
  37.2 12.0 %collective-permute-start.11 = (bf16[3,256,128]{2,1,0:T(8,128)(2,1)S(1)}, bf16[3,256,128]{2,1,0:T(8,128)(2,1)S(1)}, u32[]{:S(2)}, u32[]{:S(2)}) collective-permute-start(bf16[3,256,128]{2,1,0:T(8,128)(2,1)S(1)} %get-tuple-element.54), channel_id=1, source_target_pairs={{0,1},{1,2},{2,3},{3,0},{4,5},{5,6},{6,7},{7,4},{8,9},{9,10},{10,1... | collective-permute-start | bytes 589832 | tf_op jit(solution)/shard_map/ppermute | solution.py:18
  43.7 25.0 %collective-permute-start.7 = (bf16[128,1024]{1,0:T(8,128)(2,1)S(1)}, bf16[128,1024]{1,0:T(8,128)(2,1)S(1)}, u32[]{:S(2)}, u32[]{:S(2)}) collective-permute-start(bf16[128,1024]{1,0:T(8,128)(2,1)S(1)} %get-tuple-element.31), channel_id=1, source_target_pairs={{0,3},{1,0},{2,1},{3,2},{4,7},{5,4},{6,5},{7,6},{8,11},{9,8},{10,9... | collective-permute-start | bytes 786440 | tf_op jit(solution)/shard_map/ppermute | solution.py:18
  46.3 22.5 %collective-permute-start.6 = (bf16[128,1024]{1,0:T(8,128)(2,1)S(1)}, bf16[128,1024]{1,0:T(8,128)(2,1)S(1)}, u32[]{:S(2)}, u32[]{:S(2)}) collective-permute-start(bf16[128,1024]{1,0:T(8,128)(2,1)S(1)} %get-tuple-element.30), channel_id=1, source_target_pairs={{0,2},{1,3},{2,0},{3,1},{4,6},{5,7},{6,4},{7,5},{8,10},{9,11},{10,... | collective-permute-start | bytes 786440 | tf_op jit(solution)/shard_map/ppermute | solution.py:18
  46.8 21.9 %collective-permute-start.5 = (bf16[128,1024]{1,0:T(8,128)(2,1)S(1)}, bf16[128,1024]{1,0:T(8,128)(2,1)S(1)}, u32[]{:S(2)}, u32[]{:S(2)}) collective-permute-start(bf16[128,1024]{1,0:T(8,128)(2,1)S(1)} %get-tuple-element.29), channel_id=1, source_target_pairs={{0,1},{1,2},{2,3},{3,0},{4,5},{5,6},{6,7},{7,4},{8,9},{9,10},{10,1... | collective-permute-start | bytes 786440 | tf_op jit(solution)/shard_map/ppermute | solution.py:18
  47.5 16.9 %collective-permute-start.12 = (bf16[3,256,128]{2,1,0:T(8,128)(2,1)S(1)}, bf16[3,256,128]{2,1,0:T(8,128)(2,1)S(1)}, u32[]{:S(2)}, u32[]{:S(2)}) collective-permute-start(bf16[3,256,128]{2,1,0:T(8,128)(2,1)S(1)} %get-tuple-element.53), channel_id=1, source_target_pairs={{0,2},{1,3},{2,0},{3,1},{4,6},{5,7},{6,4},{7,5},{8,10},{9,11},{10,... | collective-permute-start | bytes 589832 | tf_op jit(solution)/shard_map/ppermute | solution.py:18
  49.3 18.7 %collective-permute-start.13 = (bf16[3,256,128]{2,1,0:T(8,128)(2,1)S(1)}, bf16[3,256,128]{2,1,0:T(8,128)(2,1)S(1)}, u32[]{:S(2)}, u32[]{:S(2)}) collective-permute-start(bf16[3,256,128]{2,1,0:T(8,128)(2,1)S(1)} %get-tuple-element.52), channel_id=1, source_target_pairs={{0,3},{1,0},{2,1},{3,2},{4,7},{5,4},{6,5},{7,6},{8,11},{9,8},{10,9... | collective-permute-start | bytes 589832 | tf_op jit(solution)/shard_map/ppermute | solution.py:18
  68.9 7.2 %collective-permute-start.8 = (bf16[128,1024]{1,0:T(8,128)(2,1)S(1)}, bf16[128,1024]{1,0:T(8,128)(2,1)S(1)}, u32[]{:S(2)}, u32[]{:S(2)}) collective-permute-start(bf16[128,1024]{1,0:T(8,128)(2,1)S(1)} %add_convert_fusion.1.refs_0_), channel_id=1, source_target_pairs={{0,4},{4,8},{8,12},{12,0},{1,5},{5,9},{9,13},{13,1},{2,6},{6,10},{... | collective-permute-start | bytes 786440 | tf_op jit(solution)/shard_map/ppermute | solution.py:18
  70.3 9.6 %collective-permute-start.9 = (bf16[128,1024]{1,0:T(8,128)(2,1)S(1)}, bf16[128,1024]{1,0:T(8,128)(2,1)S(1)}, u32[]{:S(2)}, u32[]{:S(2)}) collective-permute-start(bf16[128,1024]{1,0:T(8,128)(2,1)S(1)} %add_convert_fusion.1.refs_0_), channel_id=1, source_target_pairs={{0,8},{4,12},{8,0},{12,4},{1,9},{5,13},{9,1},{13,5},{2,10},{6,14},... | collective-permute-start | bytes 786440 | tf_op jit(solution)/shard_map/ppermute | solution.py:18
  82.1 10.6 %collective-permute-start.14 = (bf16[128,1024]{1,0:T(8,128)(2,1)S(1)}, bf16[128,1024]{1,0:T(8,128)(2,1)S(1)}, u32[]{:S(2)}, u32[]{:S(2)}) collective-permute-start(bf16[128,1024]{1,0:T(8,128)(2,1)S(1)} %get-tuple-element.33.v0), channel_id=1, source_target_pairs={{0,32},{32,64},{64,96},{96,0},{1,33},{33,65},{65,97},{97,1},{2,34}... | collective-permute-start | bytes 786440 | tf_op jit(solution)/shard_map/ppermute | solution.py:18
  85.5 12.1 %collective-permute-start.15 = (bf16[128,1024]{1,0:T(8,128)(2,1)S(1)}, bf16[128,1024]{1,0:T(8,128)(2,1)S(1)}, u32[]{:S(2)}, u32[]{:S(2)}) collective-permute-start(bf16[128,1024]{1,0:T(8,128)(2,1)S(1)} %get-tuple-element.33.v0), channel_id=1, source_target_pairs={{0,64},{32,96},{64,0},{96,32},{1,65},{33,97},{65,1},{97,33},{2,66}... | collective-permute-start | bytes 786440 | tf_op jit(solution)/shard_map/ppermute | solution.py:18
  90.1 7.5 %collective-permute-start.16 = (bf16[128,1024]{1,0:T(8,128)(2,1)S(1)}, bf16[128,1024]{1,0:T(8,128)(2,1)S(1)}, u32[]{:S(2)}, u32[]{:S(2)}) collective-permute-start(bf16[128,1024]{1,0:T(8,128)(2,1)S(1)} %get-tuple-element.33.v0), channel_id=1, source_target_pairs={{0,96},{32,0},{64,32},{96,64},{1,97},{33,1},{65,33},{97,65},{2,98}... | collective-permute-start | bytes 786440 | tf_op jit(solution)/shard_map/ppermute | solution.py:18
  98.6 12.3 %collective-permute-start.17 = (bf16[128,1024]{1,0:T(8,128)(2,1)S(1)}, bf16[128,1024]{1,0:T(8,128)(2,1)S(1)}, u32[]{:S(2)}, u32[]{:S(2)}) collective-permute-start(bf16[128,1024]{1,0:T(8,128)(2,1)S(1)} %diag_step.2.refs_0_), channel_id=1, source_target_pairs={{0,4},{4,8},{8,12},{12,0},{1,5},{5,9},{9,13},{13,1},{2,6},{6,10},{... | collective-permute-start | bytes 786440 | tf_op jit(solution)/shard_map/ppermute | solution.py:18
  105.7 9.7 %collective-permute-start.18 = (bf16[128,1024]{1,0:T(8,128)(2,1)S(1)}, bf16[128,1024]{1,0:T(8,128)(2,1)S(1)}, u32[]{:S(2)}, u32[]{:S(2)}) collective-permute-start(bf16[128,1024]{1,0:T(8,128)(2,1)S(1)} %diag_step.2.refs_0_), channel_id=1, source_target_pairs={{0,8},{4,12},{8,0},{12,4},{1,9},{5,13},{9,1},{13,5},{2,10},{6,14},... | collective-permute-start | bytes 786440 | tf_op jit(solution)/shard_map/ppermute | solution.py:18
  106.3 9.3 %collective-permute-start.19 = (bf16[128,1024]{1,0:T(8,128)(2,1)S(1)}, bf16[128,1024]{1,0:T(8,128)(2,1)S(1)}, u32[]{:S(2)}, u32[]{:S(2)}) collective-permute-start(bf16[128,1024]{1,0:T(8,128)(2,1)S(1)} %diag_step.2.refs_0_), channel_id=1, source_target_pairs={{0,12},{4,0},{8,4},{12,8},{1,13},{5,1},{9,5},{13,9},{2,14},{6,2},{... | collective-permute-start | bytes 786440 | tf_op jit(solution)/shard_map/ppermute | solution.py:18
  117.6 9.8 %collective-permute-start.20 = (bf16[128,1024]{1,0:T(8,128)(2,1)S(1)}, bf16[128,1024]{1,0:T(8,128)(2,1)S(1)}, u32[]{:S(2)}, u32[]{:S(2)}) collective-permute-start(bf16[128,1024]{1,0:T(8,128)(2,1)S(1)} %get-tuple-element.37.v0), channel_id=1, source_target_pairs={{0,32},{32,64},{64,96},{96,0},{1,33},{33,65},{65,97},{97,1},{2,34}... | collective-permute-start | bytes 786440 | tf_op jit(solution)/shard_map/ppermute | solution.py:18
  120.2 13.6 %collective-permute-start.21 = (bf16[128,1024]{1,0:T(8,128)(2,1)S(1)}, bf16[128,1024]{1,0:T(8,128)(2,1)S(1)}, u32[]{:S(2)}, u32[]{:S(2)}) collective-permute-start(bf16[128,1024]{1,0:T(8,128)(2,1)S(1)} %get-tuple-element.37.v0), channel_id=1, source_target_pairs={{0,64},{32,96},{64,0},{96,32},{1,65},{33,97},{65,1},{97,33},{2,66}... | collective-permute-start | bytes 786440 | tf_op jit(solution)/shard_map/ppermute | solution.py:18
  123.9 10.7 %collective-permute-start.22 = (bf16[128,1024]{1,0:T(8,128)(2,1)S(1)}, bf16[128,1024]{1,0:T(8,128)(2,1)S(1)}, u32[]{:S(2)}, u32[]{:S(2)}) collective-permute-start(bf16[128,1024]{1,0:T(8,128)(2,1)S(1)} %get-tuple-element.37.v0), channel_id=1, source_target_pairs={{0,96},{32,0},{64,32},{96,64},{1,97},{33,1},{65,33},{97,65},{2,98}... | collective-permute-start | bytes 786440 | tf_op jit(solution)/shard_map/ppermute | solution.py:18
  136.5 16.1 %collective-permute-start.23 = (bf16[128,1024]{1,0:T(8,128)(2,1)S(1)}, bf16[128,1024]{1,0:T(8,128)(2,1)S(1)}, u32[]{:S(2)}, u32[]{:S(2)}) collective-permute-start(bf16[128,1024]{1,0:T(8,128)(2,1)S(1)} %diag_step.3.refs_0_), channel_id=1, source_target_pairs={{0,4},{4,8},{8,12},{12,0},{1,5},{5,9},{9,13},{13,1},{2,6},{6,10},{... | collective-permute-start | bytes 786440 | tf_op jit(solution)/shard_map/ppermute | solution.py:18
  140.3 12.5 %collective-permute-start.24 = (bf16[128,1024]{1,0:T(8,128)(2,1)S(1)}, bf16[128,1024]{1,0:T(8,128)(2,1)S(1)}, u32[]{:S(2)}, u32[]{:S(2)}) collective-permute-start(bf16[128,1024]{1,0:T(8,128)(2,1)S(1)} %diag_step.3.refs_0_), channel_id=1, source_target_pairs={{0,8},{4,12},{8,0},{12,4},{1,9},{5,13},{9,1},{13,5},{2,10},{6,14},... | collective-permute-start | bytes 786440 | tf_op jit(solution)/shard_map/ppermute | solution.py:18
  142.1 10.6 %collective-permute-start.25 = (bf16[128,1024]{1,0:T(8,128)(2,1)S(1)}, bf16[128,1024]{1,0:T(8,128)(2,1)S(1)}, u32[]{:S(2)}, u32[]{:S(2)}) collective-permute-start(bf16[128,1024]{1,0:T(8,128)(2,1)S(1)} %diag_step.3.refs_0_), channel_id=1, source_target_pairs={{0,12},{4,0},{8,4},{12,8},{1,13},{5,1},{9,5},{13,9},{2,14},{6,2},{... | collective-permute-start | bytes 786440 | tf_op jit(solution)/shard_map/ppermute | solution.py:18
  154.8 9.0 %collective-permute-start.26 = (bf16[128,1024]{1,0:T(8,128)(2,1)S(1)}, bf16[128,1024]{1,0:T(8,128)(2,1)S(1)}, u32[]{:S(2)}, u32[]{:S(2)}) collective-permute-start(bf16[128,1024]{1,0:T(8,128)(2,1)S(1)} %get-tuple-element.43.v0), channel_id=1, source_target_pairs={{0,32},{32,64},{64,96},{96,0},{1,33},{33,65},{65,97},{97,1},{2,34}... | collective-permute-start | bytes 786440 | tf_op jit(solution)/shard_map/ppermute | solution.py:18
  156.2 14.3 %collective-permute-start.27 = (bf16[128,1024]{1,0:T(8,128)(2,1)S(1)}, bf16[128,1024]{1,0:T(8,128)(2,1)S(1)}, u32[]{:S(2)}, u32[]{:S(2)}) collective-permute-start(bf16[128,1024]{1,0:T(8,128)(2,1)S(1)} %get-tuple-element.43.v0), channel_id=1, source_target_pairs={{0,64},{32,96},{64,0},{96,32},{1,65},{33,97},{65,1},{97,33},{2,66}... | collective-permute-start | bytes 786440 | tf_op jit(solution)/shard_map/ppermute | solution.py:18
  159.8 10.8 %collective-permute-start.28 = (bf16[128,1024]{1,0:T(8,128)(2,1)S(1)}, bf16[128,1024]{1,0:T(8,128)(2,1)S(1)}, u32[]{:S(2)}, u32[]{:S(2)}) collective-permute-start(bf16[128,1024]{1,0:T(8,128)(2,1)S(1)} %get-tuple-element.43.v0), channel_id=1, source_target_pairs={{0,96},{32,0},{64,32},{96,64},{1,97},{33,1},{65,33},{97,65},{2,98}... | collective-permute-start | bytes 786440 | tf_op jit(solution)/shard_map/ppermute | solution.py:18
  173.1 7.7 %collective-permute-start.29 = (bf16[128,256]{1,0:T(8,128)(2,1)S(1)}, bf16[128,256]{1,0:T(8,128)(2,1)S(1)}, u32[]{:S(2)}, u32[]{:S(2)}) collective-permute-start(bf16[128,256]{1,0:T(8,128)(2,1)S(1)} %get-tuple-element.45), channel_id=1, source_target_pairs={{0,4},{4,8},{8,12},{12,0},{1,5},{5,9},{9,13},{13,1},{2,6},{6,10},{... | collective-permute-start | bytes 196616 | tf_op jit(solution)/shard_map/ppermute | solution.py:18
  (4 other events, 34.8 us)
Sparse Core Ops, SparseCore 0:
  9.9 38.2 all-gather.8
  50.0 43.2 all-gather.10
  95.0 52.5 all-gather.6

commit v8 on v7

--- a/solution.py
+++ b/solution.py
@@ -22,6 +22,11 @@
     return lax.ppermute(value, "core", [(0, 1), (1, 0)])
 
 
+def along_x(value, core, by):
+    pairs = [(core * 4 + i, core * 4 + (i + by) % 4) for i in range(4)]
+    return lax.ppermute(value, ("core", "x"), pairs)
+
+
 def spread(value, axis):
     far = shift(value, axis, 2)
     right = shift(value, axis, 1)
@@ -60,9 +65,9 @@
 HBM = pl.BlockSpec(memory_space=pltpu.HBM)
 
 
-def first_product(place, pieces, mine, other):
+def first_product(place, pieces, mine, other, sent):
     def kernel(place_ref, v0, v1, v2, v3, mine_ref, other_ref, *refs):
-        outs, turned = refs[:4], refs[4]
+        outs, turned = refs[len(sent) : len(sent) + 4], refs[len(sent) + 4]
         core, x = place_ref[0], place_ref[2]
         turned[...] = add_up((v0, v1, v2, v3)).T.astype(BF16)
         for step, out in enumerate(outs):
@@ -76,13 +81,30 @@
     return pl.pallas_call(
         kernel,
         out_shape=(jax.ShapeDtypeStruct((128, 1024), BF16),) * 4,
-        in_specs=[SCALARS] + [VMEM] * 6,
+        in_specs=[SCALARS] + [VMEM] * 6 + [pl.BlockSpec(memory_space=pl.ANY)] * len(sent),
         out_specs=(VMEM,) * 4,
         scratch_shapes=[pltpu.VMEM((512, 256), BF16)],
         compiler_params=params(),
         cost_estimate=cost(2 * 512 * 256 * 1024, 3 << 20),
         name="first_product",
-    )(place, *pieces, mine, other)
+    )(place, *pieces, mine, other, *sent)
+
+
+def gate(token, arrays):
+    def kernel(*refs):
+        pass
+
+    count = len(arrays)
+    return pl.pallas_call(
+        kernel,
+        out_shape=tuple(jax.ShapeDtypeStruct(value.shape, value.dtype) for value in arrays),
+        in_specs=[pl.BlockSpec(memory_space=pl.ANY)] * (count + 1),
+        out_specs=(pl.BlockSpec(memory_space=pl.ANY),) * count,
+        input_output_aliases={i + 1: i for i in range(count)},
+        compiler_params=params(),
+        cost_estimate=cost(0, 1024),
+        name="gate",
+    )(token, *arrays)
 
 
 def turn(place, pieces):
@@ -395,14 +417,19 @@
     home = lax.optimization_barrier(term(core))
     both = (home.astype(F32) + away.astype(F32)).astype(BF16)
     over_z = spread(both[3], "z")
-    products = first_product(place, over_z, inverse_diag[3], other)
-    rest = both[:3] + over_z[1][0, 0] * 0
     cut = [
-        lax.dynamic_slice_in_dim(rest, lax.rem(x + by, 4) * 128, 128, axis=2) for by in range(4)
+        lax.dynamic_slice_in_dim(both[:3], lax.rem(x + by, 4) * 128, 128, axis=2)
+        for by in range(4)
     ]
-    base = turn(place, deal(cut, "x"))
-    over_x = deal(products, "x")
-    partial = sum(piece.astype(F32) for piece in over_x).astype(BF16)
+    rest = deal(cut, "x")
+    products = first_product(place, over_z, inverse_diag[3], other, rest[1:])
+    base = turn(place, rest)
+    own, *others = products
+    zero = [along_x(others[by - 1], 0, by) for by in (1, 2, 3)]
+    token = lax.ppermute(sum(piece[:8] for piece in zero), "core", [(0, 1)])
+    others = gate(token, others)
+    one = [along_x(others[by - 1], 1, by) for by in (1, 2, 3)]
+    partial = sum(piece.astype(F32) for piece in (own, *zero, *one)).astype(BF16)
     pieces = spread(partial, "y")
     residual, x3 = lower_step(base[2], pieces, early, 0, BF16)
     over_z = spread(residual, "z")

time: 214 us -> 222 us (1.037)
  waiting for transfers between devices: 68.9 us -> 80.2 us
  starting transfers between devices: 61.5 us -> 54.9 us
  blocking collectives: 23.8 us -> 26.3 us
    ppermute x0 -> x7, waiting for transfers between devices: none -> 33.5 us  [the longest x1 21.1 us: local(): token = lax.ppermute(sum((piece[:8] for piece in zero)), 'core', [(0, 1)])]
    ppermute x30 -> x27, waiting for transfers between devices: 62.7 us -> 43 us  [shift(): return lax.ppermute(value, axis, [(i, (i + by) % 4) for i in range(4)])]
    ppermute x30 -> x27, starting transfers between devices: 59.5 us -> 41.8 us  [shift(): return lax.ppermute(value, axis, [(i, (i + by) % 4) for i in range(4)])]
    ppermute x0 -> x7, starting transfers between devices: none -> 11.5 us  [the longest x6 10.2 us: along_x(): return lax.ppermute(value, ('core', 'x'), pairs)]
    all_to_all x1, blocking collectives: 23.8 us -> 26.3 us  [local(): lax.all_to_all(packed, ('z', 'core', 'y', 'x'), split_axis=0, concat_axis...]
    all_gather x3, waiting for transfers between devices: 4.78 us -> 2.36 us  [gathered(): lax.all_gather(joined, ('core', 'x'), axis=0, tiled=False)]
  transfers between devices with their start and end apart: 35 -> 39, of which waited for: 20 -> 19; matrix products, arithmetic and copies ran while one was open for 8% -> 8% of each run, Pallas kernels for 9% -> 9%
where the time goes in v8:
time: 222 us
  waiting for transfers between devices  80.2 us (36%)
  starting transfers between devices  54.9 us (25%)
  Pallas kernels  29.3 us (13%)
  blocking collectives  26.3 us (12%)
  between operations  13.5 us (6%)
  matrix products  13.1 us (6%)
  other arithmetic  2.64 us (1%)
    ppermute x27, waiting for transfers between devices, shift(): return lax.ppermute(value, axis, [(i, (i + by) % 4) for i in range(4)])  43 us
    ppermute x27, starting transfers between devices, shift(): return lax.ppermute(value, axis, [(i, (i + by) % 4) for i in range(4)])  41.8 us
    all_to_all x1, blocking collectives, local(): lax.all_to_all(packed, ('z', 'core', 'y', 'x'), split_axis=0, concat_axis...  26.3 us
    ppermute x1, waiting for transfers between devices, local(): token = lax.ppermute(sum((piece[:8] for piece in zero)), 'core', [(0, 1)])  21.1 us
    pallas_call x6, Pallas kernels, lower_step(): pl.pallas_call(kernel, out_shape=(jax.ShapeDtypeStruct((128, 1024), dtype...  13.8 us
    dot_general x2, matrix products, term(): lax.dot_general(border_tiles, bound, (((0,), (0,)), ((), ())), preferred_...  13.1 us
    ppermute x6, waiting for transfers between devices, along_x(): return lax.ppermute(value, ('core', 'x'), pairs)  12.5 us
    ppermute x6, starting transfers between devices, along_x(): return lax.ppermute(value, ('core', 'x'), pairs)  10.2 us
  transfers between devices with their start and end apart: 39, of which 19 were waited for; matrix products, arithmetic and copies ran while one was open for 8% of the time, Pallas kernels for 9%

profile of v8, /device:TPU:1, one launch (start us, length us, event | category | flops | bytes accessed | tf_op | source)
XLA Modules:
  0.0 221.6 jit_solution(16831964972099095117)
XLA Ops:
  6.5 3.3 %stage.1 = (bf16[1024,256]{1,0:T(8,128)(2,1)}, bf16[1536,256]{1,0:T(8,128)(2,1)}, bf16[2064,256]{1,0:T(8,128)(2,1)}) custom-call(bf16[6,512,256]{2,1,0:T(8,128)(2,1)} %lower_ref.1, bf16[4,256,512]{2,1,0:T(8,128)(2,1)} %diag_ref.1, s32[1,128]{1,0:T(1,128)} %bitcast.57), custom_call_target="tpu_custom_call" | custom-call | bytes 6291456 | tf_op jit(solution)/shard_map/stage/pallas_call | solution.py:284
  11.4 6.8 %fusion.6 = bf16[4,256,512]{2,1,0:T(8,128)(2,1)} fusion(f32[4,256,1024]{2,1,0:T(8,128)} %param.6, s32[]{:T(128)S(6)} %select_n.26, bf16[2048,4,256]{2,1,0:T(4,128)(2,1)} %param.8, bf16[2048,1024]{1,0:T(8,128)(2,1)} %param.7, f32[]{:T(128)S(6)} %select_n.24), kind=kOutput, calls=%fused_computation.7 | convolution fusion | flops 2149056512 | bytes 9438720 | tf_op jit(solution)/shard_map/dot_general | solution.py:411
  20.7 6.3 %fusion.7 = bf16[4,256,512]{2,1,0:T(8,128)(2,1)S(1)} fusion(f32[4,256,1024]{2,1,0:T(8,128)} %param.6, s32[]{:T(128)S(6)} %select_n.25, bf16[2048,4,256]{2,1,0:T(4,128)(2,1)} %param.8, bf16[2048,1024]{1,0:T(8,128)(2,1)} %param.7, f32[]{:T(128)S(6)} %select_n.24), kind=kOutput, calls=%fused_computation.9 | convolution fusion | flops 2149056512 | bytes 9438720 | tf_op jit(solution)/shard_map/dot_general | solution.py:411
  30.9 3.2 %collective-permute-start.2 = (bf16[256,512]{1,0:T(8,128)(2,1)S(1)}, bf16[256,512]{1,0:T(8,128)(2,1)S(1)}, u32[]{:S(2)}, u32[]{:S(2)}) collective-permute-start(bf16[256,512]{1,0:T(8,128)(2,1)S(1)} %slice_bitcast_fusion.3.v0), channel_id=1, source_target_pairs={{0,64},{32,96},{64,0},{96,32},{1,65},{33,97},{65,1},{97,33},{2,66}... | collective-permute-start | bytes 786440 | tf_op jit(solution)/shard_map/ppermute | solution.py:18
  34.9 2.4 %collective-permute-start.6 = (bf16[3,256,128]{2,1,0:T(8,128)(2,1)S(1)}, bf16[3,256,128]{2,1,0:T(8,128)(2,1)S(1)}, u32[]{:S(2)}, u32[]{:S(2)}) collective-permute-start(bf16[3,256,128]{2,1,0:T(8,128)(2,1)S(1)} %get-tuple-element.60), channel_id=1, source_target_pairs={{0,2},{1,3},{2,0},{3,1},{4,6},{5,7},{6,4},{7,5},{8,10},{9,11},{10,... | collective-permute-start | bytes 589832 | tf_op jit(solution)/shard_map/ppermute | solution.py:18
  37.4 2.4 %collective-permute-done.5.refs_0_.v1 = bf16[3,256,128]{2,1,0:T(8,128)(2,1)S(1)} collective-permute-done((bf16[3,256,128]{2,1,0:T(8,128)(2,1)S(1)}, bf16[3,256,128]{2,1,0:T(8,128)(2,1)S(1)}, u32[]{:S(2)}, u32[]{:S(2)}) %collective-permute-start.5) | collective-permute-done | bytes 196640 | tf_op jit(solution)/shard_map/ppermute | solution.py:18
  41.1 8.0 %collective-permute-done.6.refs_1_.v2 = bf16[3,256,128]{2,1,0:T(8,128)(2,1)S(1)} collective-permute-done((bf16[3,256,128]{2,1,0:T(8,128)(2,1)S(1)}, bf16[3,256,128]{2,1,0:T(8,128)(2,1)S(1)}, u32[]{:S(2)}, u32[]{:S(2)}) %collective-permute-start.6) | collective-permute-done | bytes 196640 | tf_op jit(solution)/shard_map/ppermute | solution.py:18
  55.5 21.1 %collective-permute-done.11.refs_0_ = bf16[8,1024]{1,0:T(8,128)(2,1)S(1)} collective-permute-done((bf16[8,1024]{1,0:T(8,128)(2,1)S(1)}, bf16[8,1024]{1,0:T(8,128)(2,1)S(1)}, u32[]{:S(2)}, u32[]{:S(2)}) %collective-permute-start.11) | collective-permute-done | bytes 16416 | tf_op jit(solution)/shard_map/ppermute | solution.py:429
  78.5 3.5 %collective-permute-start.13 = (bf16[128,1024]{1,0:T(8,128)(2,1)S(1)}, bf16[128,1024]{1,0:T(8,128)(2,1)S(1)}, u32[]{:S(2)}, u32[]{:S(2)}) collective-permute-start(bf16[128,1024]{1,0:T(8,128)(2,1)S(1)} %get-tuple-element.36), channel_id=1, source_target_pairs={{16,18},{17,19},{18,16},{19,17},{20,22},{21,23},{22,20},{23,21},{2... | collective-permute-start | bytes 786440 | tf_op jit(solution)/shard_map/ppermute | solution.py:27
  82.0 2.8 %collective-permute-start.12 = (bf16[128,1024]{1,0:T(8,128)(2,1)S(1)}, bf16[128,1024]{1,0:T(8,128)(2,1)S(1)}, u32[]{:S(2)}, u32[]{:S(2)}) collective-permute-start(bf16[128,1024]{1,0:T(8,128)(2,1)S(1)} %get-tuple-element.35), channel_id=1, source_target_pairs={{16,17},{17,18},{18,19},{19,16},{20,21},{21,22},{22,23},{23,20},{2... | collective-permute-start | bytes 786440 | tf_op jit(solution)/shard_map/ppermute | solution.py:27
  85.6 4.1 %collective-permute-done.14 = bf16[128,1024]{1,0:T(8,128)(2,1)S(1)} collective-permute-done((bf16[128,1024]{1,0:T(8,128)(2,1)S(1)}, bf16[128,1024]{1,0:T(8,128)(2,1)S(1)}, u32[]{:S(2)}, u32[]{:S(2)}) %collective-permute-start.14) | collective-permute-done | bytes 262176 | tf_op jit(solution)/shard_map/ppermute | solution.py:27
  89.6 3.1 %collective-permute-done.13 = bf16[128,1024]{1,0:T(8,128)(2,1)S(1)} collective-permute-done((bf16[128,1024]{1,0:T(8,128)(2,1)S(1)}, bf16[128,1024]{1,0:T(8,128)(2,1)S(1)}, u32[]{:S(2)}, u32[]{:S(2)}) %collective-permute-start.13) | collective-permute-done | bytes 262176 | tf_op jit(solution)/shard_map/ppermute | solution.py:27
  92.7 5.3 %collective-permute-done.12 = bf16[128,1024]{1,0:T(8,128)(2,1)S(1)} collective-permute-done((bf16[128,1024]{1,0:T(8,128)(2,1)S(1)}, bf16[128,1024]{1,0:T(8,128)(2,1)S(1)}, u32[]{:S(2)}, u32[]{:S(2)}) %collective-permute-start.12) | collective-permute-done | bytes 262176 | tf_op jit(solution)/shard_map/ppermute | solution.py:27
  99.3 2.3 %collective-permute-start.16 = (bf16[128,1024]{1,0:T(8,128)(2,1)S(1)}, bf16[128,1024]{1,0:T(8,128)(2,1)S(1)}, u32[]{:S(2)}, u32[]{:S(2)}) collective-permute-start(bf16[128,1024]{1,0:T(8,128)(2,1)S(1)} %add_convert_fusion.1.refs_0_), channel_id=1, source_target_pairs={{0,8},{4,12},{8,0},{12,4},{1,9},{5,13},{9,1},{13,5},{2,10},{6,14},... | collective-permute-start | bytes 786440 | tf_op jit(solution)/shard_map/ppermute | solution.py:18
  104.8 3.3 %collective-permute-done.16.refs_2_ = bf16[128,1024]{1,0:T(8,128)(2,1)S(1)} collective-permute-done((bf16[128,1024]{1,0:T(8,128)(2,1)S(1)}, bf16[128,1024]{1,0:T(8,128)(2,1)S(1)}, u32[]{:S(2)}, u32[]{:S(2)}) %collective-permute-start.16) | collective-permute-done | bytes 262176 | tf_op jit(solution)/shard_map/ppermute | solution.py:18
  108.2 2.2 lower_step.6
  114.2 6.1 %collective-permute-done.18.v1 = bf16[128,1024]{1,0:T(8,128)(2,1)S(1)} collective-permute-done((bf16[128,1024]{1,0:T(8,128)(2,1)S(1)}, bf16[128,1024]{1,0:T(8,128)(2,1)S(1)}, u32[]{:S(2)}, u32[]{:S(2)}) %collective-permute-start.18) | collective-permute-done | bytes 262176 | tf_op jit(solution)/shard_map/ppermute | solution.py:18
  126.4 2.5 %lower_step.7 = (f32[128,1024]{1,0:T(8,128)S(1)}, bf16[128,1024]{1,0:T(8,128)(2,1)}) custom-call(bf16[128,1024]{1,0:T(8,128)(2,1)S(1)} %get-tuple-element.40.refs_0_.x3, f32[128,1024]{1,0:T(8,128)S(1)} %get-tuple-element.56.refs_1_, bf16[2,4,1536,256]{3,2,1,0:T(8,128)(2,1)} %bitcast.53), custom_call_target="tpu_custom_call" | custom-call | flops 268435456 | bytes 4194304 | tf_op jit(solution)/shard_map/lower_step/pallas_call | solution.py:152
  129.0 3.2 %collective-permute-done.22.refs_2_ = bf16[128,1024]{1,0:T(8,128)(2,1)S(1)} collective-permute-done((bf16[128,1024]{1,0:T(8,128)(2,1)S(1)}, bf16[128,1024]{1,0:T(8,128)(2,1)S(1)}, u32[]{:S(2)}, u32[]{:S(2)}) %collective-permute-start.22) | collective-permute-done | bytes 262176 | tf_op jit(solution)/shard_map/ppermute | solution.py:18
  135.2 2.7 %collective-permute-start.25 = (bf16[128,1024]{1,0:T(8,128)(2,1)S(1)}, bf16[128,1024]{1,0:T(8,128)(2,1)S(1)}, u32[]{:S(2)}, u32[]{:S(2)}) collective-permute-start(bf16[128,1024]{1,0:T(8,128)(2,1)S(1)} %get-tuple-element.43.v0), channel_id=1, source_target_pairs={{0,64},{32,96},{64,0},{96,32},{1,65},{33,97},{65,1},{97,33},{2,66}... | collective-permute-start | bytes 786440 | tf_op jit(solution)/shard_map/ppermute | solution.py:18
  137.9 3.3 %collective-permute-done.24.v1 = bf16[128,1024]{1,0:T(8,128)(2,1)S(1)} collective-permute-done((bf16[128,1024]{1,0:T(8,128)(2,1)S(1)}, bf16[128,1024]{1,0:T(8,128)(2,1)S(1)}, u32[]{:S(2)}, u32[]{:S(2)}) %collective-permute-start.24) | collective-permute-done | bytes 262176 | tf_op jit(solution)/shard_map/ppermute | solution.py:18
  141.1 3.3 %collective-permute-done.25.v2 = bf16[128,1024]{1,0:T(8,128)(2,1)S(1)} collective-permute-done((bf16[128,1024]{1,0:T(8,128)(2,1)S(1)}, bf16[128,1024]{1,0:T(8,128)(2,1)S(1)}, u32[]{:S(2)}, u32[]{:S(2)}) %collective-permute-start.25) | collective-permute-done | bytes 262176 | tf_op jit(solution)/shard_map/ppermute | solution.py:18
  148.0 2.1 collective-permute-start.28
  151.1 2.4 %all-gather.7.cloned.1.call-done = bf16[16512,256]{1,0:T(8,128)(2,1)} async-done(((bf16[2064,256]{1,0:T(8,128)(2,1)}), bf16[16512,256]{1,0:T(8,128)(2,1)}) %all-gather.7.cloned.1.call-update) | async-done | bytes 8454160 | tf_op jit(solution)/shard_map/all_gather | solution.py:386
  153.4 2.5 %lower_step.9 = (f32[128,1024]{1,0:T(8,128)S(1)}, bf16[128,1024]{1,0:T(8,128)(2,1)}) custom-call(bf16[128,1024]{1,0:T(8,128)(2,1)S(1)} %get-tuple-element.40.refs_0_.x3, f32[128,1024]{1,0:T(8,128)S(1)} %get-tuple-element.55.refs_1_, bf16[2,4,2064,256]{3,2,1,0:T(8,128)(2,1)} %bitcast.47), custom_call_target="tpu_custom_call" | custom-call | flops 268435456 | bytes 4194304 | tf_op jit(solution)/shard_map/lower_step/pallas_call | solution.py:152
  155.9 2.5 %lower_step.10 = (f32[128,1024]{1,0:T(8,128)S(1)}, bf16[128,1024]{1,0:T(8,128)(2,1)}) custom-call(bf16[128,1024]{1,0:T(8,128)(2,1)S(1)} %get-tuple-element.44.refs_0_.x2, f32[128,1024]{1,0:T(8,128)S(1)} %get-tuple-element.45.refs_1_, bf16[2,4,2064,256]{3,2,1,0:T(8,128)(2,1)} %bitcast.48), custom_call_target="tpu_custom_call" | custom-call | flops 268435456 | bytes 4194304 | tf_op jit(solution)/shard_map/lower_step/pallas_call | solution.py:152
  161.8 2.6 %collective-permute-start.31 = (bf16[128,1024]{1,0:T(8,128)(2,1)S(1)}, bf16[128,1024]{1,0:T(8,128)(2,1)S(1)}, u32[]{:S(2)}, u32[]{:S(2)}) collective-permute-start(bf16[128,1024]{1,0:T(8,128)(2,1)S(1)} %get-tuple-element.49.v0), channel_id=1, source_target_pairs={{0,64},{32,96},{64,0},{96,32},{1,65},{33,97},{65,1},{97,33},{2,66}... | collective-permute-start | bytes 786440 | tf_op jit(solution)/shard_map/ppermute | solution.py:18
  169.4 6.8 %collective-permute-done.31.v2 = bf16[128,1024]{1,0:T(8,128)(2,1)S(1)} collective-permute-done((bf16[128,1024]{1,0:T(8,128)(2,1)S(1)}, bf16[128,1024]{1,0:T(8,128)(2,1)S(1)}, u32[]{:S(2)}, u32[]{:S(2)}) %collective-permute-start.31) | collective-permute-done | bytes 262176 | tf_op jit(solution)/shard_map/ppermute | solution.py:18
  176.2 2.5 %last_step.1 = (bf16[128,256]{1,0:T(8,128)(2,1)S(1)}, bf16[128,256]{1,0:T(8,128)(2,1)S(1)}, bf16[128,256]{1,0:T(8,128)(2,1)S(1)}, bf16[128,256]{1,0:T(8,128)(2,1)S(1)}) custom-call(s32[4]{0:T(128)S(1)} %pad_add_fusion.place_ref, bf16[128,1024]{1,0:T(8,128)(2,1)S(1)} %get-tuple-element.49.v0, bf16[128,1024]{1,0:T(8,128)(2,1)S(1)} %collective-permute-done.30.v1, ...), custom_call_target="tpu_custom_call" | custom-call | flops 268435456 | bytes 4194304 | tf_op jit(solution)/shard_map/last_step/pallas_call | solution.py:231
  180.0 2.4 %collective-permute-start.34 = (bf16[128,256]{1,0:T(8,128)(2,1)S(1)}, bf16[128,256]{1,0:T(8,128)(2,1)S(1)}, u32[]{:S(2)}, u32[]{:S(2)}) collective-permute-start(bf16[128,256]{1,0:T(8,128)(2,1)S(1)} %get-tuple-element.52), channel_id=1, source_target_pairs={{0,8},{4,12},{8,0},{12,4},{1,9},{5,13},{9,1},{13,5},{2,10},{6,14},... | collective-permute-start | bytes 196616 | tf_op jit(solution)/shard_map/ppermute | solution.py:18
  183.7 3.0 %pack_known.1 = (bf16[2048,128]{1,0:T(8,128)(2,1)S(1)}, bf16[2048,256]{1,0:T(8,128)(2,1)S(1)}) custom-call(s32[4]{0:T(128)S(1)} %pad_add_fusion.place_ref, s32[4,1,256]{2,1,0:T(1,128)S(1)} %reshape.64.target_ref, bf16[128,1024]{1,0:T(8,128)(2,1)S(1)} %get-tuple-element.47.x1, bf16[128,1024]{1,0:T(8,128)(2,1)S(1)} %get-tuple-element.44.refs_0_.x2, ...), custom_call_target="tpu_custom_call" | custom-call | flops 402653184 | bytes 2097152 | tf_op jit(solution)/shard_map/pack_known/pallas_call | solution.py:320
  187.2 26.3 %all_to_all.5 = bf16[128,16,128]{2,1,0:T(8,128)(2,1)S(1)} all-to-all(bf16[128,16,128]{2,1,0:T(8,128)(2,1)S(1)} %bitcast.46), channel_id=1, replica_groups=mesh['z'=4,'core'=2,'y'=4,'x'=4] {'z','core','y','x'}, dimensions={0} | all-to-all | bytes 1048576 | tf_op jit(solution)/shard_map/all_to_all | solution.py:448
  (89 shorter events, 53.9 us)
Async XLA Ops:
  6.5 101.7 %all-gather.9.cloned.1.call-start = ((), (), s32[]{:S(2)}) async-start(), calls=%async_computation.2 | async-start | bytes 4718592 | tf_op jit(solution)/shard_map/all_gather | solution.py:386
  9.9 116.6 %all-gather.11.cloned.1.call-start = ((), (), s32[]{:S(2)}) async-start(), calls=%async_computation.3 | async-start | bytes 7077888 | tf_op jit(solution)/shard_map/all_gather | solution.py:386
  10.6 142.8 %all-gather.7.cloned.1.call-start = ((), (), s32[]{:S(2)}) async-start(), calls=%async_computation.1 | async-start | bytes 9510912 | tf_op jit(solution)/shard_map/all_gather | solution.py:386
  18.2 8.9 %collective-permute-start = (bf16[4,256,512]{2,1,0:T(8,128)(2,1)}, bf16[4,256,512]{2,1,0:T(8,128)(2,1)S(1)}, u32[]{:S(2)}, u32[]{:S(2)}) collective-permute-start(bf16[4,256,512]{2,1,0:T(8,128)(2,1)} %fusion.6), channel_id=1, source_target_pairs={{0,16},{16,0},{1,17},{17,1},{2,18},{18,2},{3,19},{19,3},{4,20},{20... | collective-permute-start | bytes 3145736 | tf_op jit(solution)/shard_map/ppermute | solution.py:22
  20.6 14.3 %collective-permute-start.4 = (bf16[256,512]{1,0:T(8,128)(2,1)S(1)}, bf16[256,512]{1,0:T(8,128)(2,1)S(1)}, u32[]{:S(2)}, u32[]{:S(2)}) collective-permute-start(bf16[256,512]{1,0:T(8,128)(2,1)S(1)} %slice_bitcast_fusion.4.mine_ref), channel_id=1, source_target_pairs={{0,16},{16,0},{1,17},{17,1},{2,18},{18,2},{3,19},{19,3},{4,20},{20... | collective-permute-start | bytes 786440 | tf_op jit(solution)/shard_map/ppermute | solution.py:22
  27.6 12.2 %collective-permute-start.5 = (bf16[3,256,128]{2,1,0:T(8,128)(2,1)S(1)}, bf16[3,256,128]{2,1,0:T(8,128)(2,1)S(1)}, u32[]{:S(2)}, u32[]{:S(2)}) collective-permute-start(bf16[3,256,128]{2,1,0:T(8,128)(2,1)S(1)} %get-tuple-element.61), channel_id=1, source_target_pairs={{0,1},{1,2},{2,3},{3,0},{4,5},{5,6},{6,7},{7,4},{8,9},{9,10},{10,1... | collective-permute-start | bytes 589832 | tf_op jit(solution)/shard_map/ppermute | solution.py:18
  28.9 22.0 %collective-permute-start.1 = (bf16[256,512]{1,0:T(8,128)(2,1)S(1)}, bf16[256,512]{1,0:T(8,128)(2,1)S(1)}, u32[]{:S(2)}, u32[]{:S(2)}) collective-permute-start(bf16[256,512]{1,0:T(8,128)(2,1)S(1)} %slice_bitcast_fusion.3.v0), channel_id=1, source_target_pairs={{0,32},{32,64},{64,96},{96,0},{1,33},{33,65},{65,97},{97,1},{2,34}... | collective-permute-start | bytes 786440 | tf_op jit(solution)/shard_map/ppermute | solution.py:18
  30.9 20.0 %collective-permute-start.2 = (bf16[256,512]{1,0:T(8,128)(2,1)S(1)}, bf16[256,512]{1,0:T(8,128)(2,1)S(1)}, u32[]{:S(2)}, u32[]{:S(2)}) collective-permute-start(bf16[256,512]{1,0:T(8,128)(2,1)S(1)} %slice_bitcast_fusion.3.v0), channel_id=1, source_target_pairs={{0,64},{32,96},{64,0},{96,32},{1,65},{33,97},{65,1},{97,33},{2,66}... | collective-permute-start | bytes 786440 | tf_op jit(solution)/shard_map/ppermute | solution.py:18
  34.1 16.8 %collective-permute-start.3 = (bf16[256,512]{1,0:T(8,128)(2,1)S(1)}, bf16[256,512]{1,0:T(8,128)(2,1)S(1)}, u32[]{:S(2)}, u32[]{:S(2)}) collective-permute-start(bf16[256,512]{1,0:T(8,128)(2,1)S(1)} %slice_bitcast_fusion.3.v0), channel_id=1, source_target_pairs={{0,96},{32,0},{64,32},{96,64},{1,97},{33,1},{65,33},{97,65},{2,98}... | collective-permute-start | bytes 786440 | tf_op jit(solution)/shard_map/ppermute | solution.py:18
  34.9 14.1 %collective-permute-start.6 = (bf16[3,256,128]{2,1,0:T(8,128)(2,1)S(1)}, bf16[3,256,128]{2,1,0:T(8,128)(2,1)S(1)}, u32[]{:S(2)}, u32[]{:S(2)}) collective-permute-start(bf16[3,256,128]{2,1,0:T(8,128)(2,1)S(1)} %get-tuple-element.60), channel_id=1, source_target_pairs={{0,2},{1,3},{2,0},{3,1},{4,6},{5,7},{6,4},{7,5},{8,10},{9,11},{10,... | collective-permute-start | bytes 589832 | tf_op jit(solution)/shard_map/ppermute | solution.py:18
  39.8 11.1 %collective-permute-start.7 = (bf16[3,256,128]{2,1,0:T(8,128)(2,1)S(1)}, bf16[3,256,128]{2,1,0:T(8,128)(2,1)S(1)}, u32[]{:S(2)}, u32[]{:S(2)}) collective-permute-start(bf16[3,256,128]{2,1,0:T(8,128)(2,1)S(1)} %get-tuple-element.59), channel_id=1, source_target_pairs={{0,3},{1,0},{2,1},{3,2},{4,7},{5,4},{6,5},{7,6},{8,11},{9,8},{10,9... | collective-permute-start | bytes 589832 | tf_op jit(solution)/shard_map/ppermute | solution.py:18
  54.2 22.4 %collective-permute-start.11 = (bf16[8,1024]{1,0:T(8,128)(2,1)S(1)}, bf16[8,1024]{1,0:T(8,128)(2,1)S(1)}, u32[]{:S(2)}, u32[]{:S(2)}) collective-permute-start(bf16[8,1024]{1,0:T(8,128)(2,1)S(1)} %slice_add_fusion), channel_id=1, source_target_pairs={{0,16},{1,17},{2,18},{3,19},{4,20},{5,21},{6,22},{7,23},{8,24},{9,... | collective-permute-start | bytes 49160 | tf_op jit(solution)/shard_map/ppermute | solution.py:429
  76.5 13.1 %collective-permute-start.14 = (bf16[128,1024]{1,0:T(8,128)(2,1)S(1)}, bf16[128,1024]{1,0:T(8,128)(2,1)S(1)}, u32[]{:S(2)}, u32[]{:S(2)}) collective-permute-start(bf16[128,1024]{1,0:T(8,128)(2,1)S(1)} %get-tuple-element.37), channel_id=1, source_target_pairs={{16,19},{17,16},{18,17},{19,18},{20,23},{21,20},{22,21},{23,22},{2... | collective-permute-start | bytes 786440 | tf_op jit(solution)/shard_map/ppermute | solution.py:27
  78.5 14.2 %collective-permute-start.13 = (bf16[128,1024]{1,0:T(8,128)(2,1)S(1)}, bf16[128,1024]{1,0:T(8,128)(2,1)S(1)}, u32[]{:S(2)}, u32[]{:S(2)}) collective-permute-start(bf16[128,1024]{1,0:T(8,128)(2,1)S(1)} %get-tuple-element.36), channel_id=1, source_target_pairs={{16,18},{17,19},{18,16},{19,17},{20,22},{21,23},{22,20},{23,21},{2... | collective-permute-start | bytes 786440 | tf_op jit(solution)/shard_map/ppermute | solution.py:27
  82.0 16.0 %collective-permute-start.12 = (bf16[128,1024]{1,0:T(8,128)(2,1)S(1)}, bf16[128,1024]{1,0:T(8,128)(2,1)S(1)}, u32[]{:S(2)}, u32[]{:S(2)}) collective-permute-start(bf16[128,1024]{1,0:T(8,128)(2,1)S(1)} %get-tuple-element.35), channel_id=1, source_target_pairs={{16,17},{17,18},{18,19},{19,16},{20,21},{21,22},{22,23},{23,20},{2... | collective-permute-start | bytes 786440 | tf_op jit(solution)/shard_map/ppermute | solution.py:27
  99.3 8.8 %collective-permute-start.16 = (bf16[128,1024]{1,0:T(8,128)(2,1)S(1)}, bf16[128,1024]{1,0:T(8,128)(2,1)S(1)}, u32[]{:S(2)}, u32[]{:S(2)}) collective-permute-start(bf16[128,1024]{1,0:T(8,128)(2,1)S(1)} %add_convert_fusion.1.refs_0_), channel_id=1, source_target_pairs={{0,8},{4,12},{8,0},{12,4},{1,9},{5,13},{9,1},{13,5},{2,10},{6,14},... | collective-permute-start | bytes 786440 | tf_op jit(solution)/shard_map/ppermute | solution.py:18
  110.4 9.9 %collective-permute-start.18 = (bf16[128,1024]{1,0:T(8,128)(2,1)S(1)}, bf16[128,1024]{1,0:T(8,128)(2,1)S(1)}, u32[]{:S(2)}, u32[]{:S(2)}) collective-permute-start(bf16[128,1024]{1,0:T(8,128)(2,1)S(1)} %get-tuple-element.39.v0), channel_id=1, source_target_pairs={{0,32},{32,64},{64,96},{96,0},{1,33},{33,65},{65,97},{97,1},{2,34}... | collective-permute-start | bytes 786440 | tf_op jit(solution)/shard_map/ppermute | solution.py:18
  111.7 8.6 %collective-permute-start.19 = (bf16[128,1024]{1,0:T(8,128)(2,1)S(1)}, bf16[128,1024]{1,0:T(8,128)(2,1)S(1)}, u32[]{:S(2)}, u32[]{:S(2)}) collective-permute-start(bf16[128,1024]{1,0:T(8,128)(2,1)S(1)} %get-tuple-element.39.v0), channel_id=1, source_target_pairs={{0,64},{32,96},{64,0},{96,32},{1,65},{33,97},{65,1},{97,33},{2,66}... | collective-permute-start | bytes 786440 | tf_op jit(solution)/shard_map/ppermute | solution.py:18
  112.9 8.0 %collective-permute-start.20 = (bf16[128,1024]{1,0:T(8,128)(2,1)S(1)}, bf16[128,1024]{1,0:T(8,128)(2,1)S(1)}, u32[]{:S(2)}, u32[]{:S(2)}) collective-permute-start(bf16[128,1024]{1,0:T(8,128)(2,1)S(1)} %get-tuple-element.39.v0), channel_id=1, source_target_pairs={{0,96},{32,0},{64,32},{96,64},{1,97},{33,1},{65,33},{97,65},{2,98}... | collective-permute-start | bytes 786440 | tf_op jit(solution)/shard_map/ppermute | solution.py:18
  121.9 7.1 %collective-permute-start.21 = (bf16[128,1024]{1,0:T(8,128)(2,1)S(1)}, bf16[128,1024]{1,0:T(8,128)(2,1)S(1)}, u32[]{:S(2)}, u32[]{:S(2)}) collective-permute-start(bf16[128,1024]{1,0:T(8,128)(2,1)S(1)} %diag_step.2.refs_0_), channel_id=1, source_target_pairs={{0,4},{4,8},{8,12},{12,0},{1,5},{5,9},{9,13},{13,1},{2,6},{6,10},{... | collective-permute-start | bytes 786440 | tf_op jit(solution)/shard_map/ppermute | solution.py:18
  123.4 8.7 %collective-permute-start.22 = (bf16[128,1024]{1,0:T(8,128)(2,1)S(1)}, bf16[128,1024]{1,0:T(8,128)(2,1)S(1)}, u32[]{:S(2)}, u32[]{:S(2)}) collective-permute-start(bf16[128,1024]{1,0:T(8,128)(2,1)S(1)} %diag_step.2.refs_0_), channel_id=1, source_target_pairs={{0,8},{4,12},{8,0},{12,4},{1,9},{5,13},{9,1},{13,5},{2,10},{6,14},... | collective-permute-start | bytes 786440 | tf_op jit(solution)/shard_map/ppermute | solution.py:18
  134.2 6.9 %collective-permute-start.24 = (bf16[128,1024]{1,0:T(8,128)(2,1)S(1)}, bf16[128,1024]{1,0:T(8,128)(2,1)S(1)}, u32[]{:S(2)}, u32[]{:S(2)}) collective-permute-start(bf16[128,1024]{1,0:T(8,128)(2,1)S(1)} %get-tuple-element.43.v0), channel_id=1, source_target_pairs={{0,32},{32,64},{64,96},{96,0},{1,33},{33,65},{65,97},{97,1},{2,34}... | collective-permute-start | bytes 786440 | tf_op jit(solution)/shard_map/ppermute | solution.py:18
  135.2 9.3 %collective-permute-start.25 = (bf16[128,1024]{1,0:T(8,128)(2,1)S(1)}, bf16[128,1024]{1,0:T(8,128)(2,1)S(1)}, u32[]{:S(2)}, u32[]{:S(2)}) collective-permute-start(bf16[128,1024]{1,0:T(8,128)(2,1)S(1)} %get-tuple-element.43.v0), channel_id=1, source_target_pairs={{0,64},{32,96},{64,0},{96,32},{1,65},{33,97},{65,1},{97,33},{2,66}... | collective-permute-start | bytes 786440 | tf_op jit(solution)/shard_map/ppermute | solution.py:18
  137.9 6.7 %collective-permute-start.26 = (bf16[128,1024]{1,0:T(8,128)(2,1)S(1)}, bf16[128,1024]{1,0:T(8,128)(2,1)S(1)}, u32[]{:S(2)}, u32[]{:S(2)}) collective-permute-start(bf16[128,1024]{1,0:T(8,128)(2,1)S(1)} %get-tuple-element.43.v0), channel_id=1, source_target_pairs={{0,96},{32,0},{64,32},{96,64},{1,97},{33,1},{65,33},{97,65},{2,98}... | collective-permute-start | bytes 786440 | tf_op jit(solution)/shard_map/ppermute | solution.py:18
  146.4 12.0 %collective-permute-start.27 = (bf16[128,1024]{1,0:T(8,128)(2,1)S(1)}, bf16[128,1024]{1,0:T(8,128)(2,1)S(1)}, u32[]{:S(2)}, u32[]{:S(2)}) collective-permute-start(bf16[128,1024]{1,0:T(8,128)(2,1)S(1)} %diag_step.3.refs_0_), channel_id=1, source_target_pairs={{0,4},{4,8},{8,12},{12,0},{1,5},{5,9},{9,13},{13,1},{2,6},{6,10},{... | collective-permute-start | bytes 786440 | tf_op jit(solution)/shard_map/ppermute | solution.py:18
  148.0 10.5 %collective-permute-start.28 = (bf16[128,1024]{1,0:T(8,128)(2,1)S(1)}, bf16[128,1024]{1,0:T(8,128)(2,1)S(1)}, u32[]{:S(2)}, u32[]{:S(2)}) collective-permute-start(bf16[128,1024]{1,0:T(8,128)(2,1)S(1)} %diag_step.3.refs_0_), channel_id=1, source_target_pairs={{0,8},{4,12},{8,0},{12,4},{1,9},{5,13},{9,1},{13,5},{2,10},{6,14},... | collective-permute-start | bytes 786440 | tf_op jit(solution)/shard_map/ppermute | solution.py:18
  150.1 8.4 %collective-permute-start.29 = (bf16[128,1024]{1,0:T(8,128)(2,1)S(1)}, bf16[128,1024]{1,0:T(8,128)(2,1)S(1)}, u32[]{:S(2)}, u32[]{:S(2)}) collective-permute-start(bf16[128,1024]{1,0:T(8,128)(2,1)S(1)} %diag_step.3.refs_0_), channel_id=1, source_target_pairs={{0,12},{4,0},{8,4},{12,8},{1,13},{5,1},{9,5},{13,9},{2,14},{6,2},{... | collective-permute-start | bytes 786440 | tf_op jit(solution)/shard_map/ppermute | solution.py:18
  160.5 8.9 %collective-permute-start.30 = (bf16[128,1024]{1,0:T(8,128)(2,1)S(1)}, bf16[128,1024]{1,0:T(8,128)(2,1)S(1)}, u32[]{:S(2)}, u32[]{:S(2)}) collective-permute-start(bf16[128,1024]{1,0:T(8,128)(2,1)S(1)} %get-tuple-element.49.v0), channel_id=1, source_target_pairs={{0,32},{32,64},{64,96},{96,0},{1,33},{33,65},{65,97},{97,1},{2,34}... | collective-permute-start | bytes 786440 | tf_op jit(solution)/shard_map/ppermute | solution.py:18
  161.8 14.4 %collective-permute-start.31 = (bf16[128,1024]{1,0:T(8,128)(2,1)S(1)}, bf16[128,1024]{1,0:T(8,128)(2,1)S(1)}, u32[]{:S(2)}, u32[]{:S(2)}) collective-permute-start(bf16[128,1024]{1,0:T(8,128)(2,1)S(1)} %get-tuple-element.49.v0), channel_id=1, source_target_pairs={{0,64},{32,96},{64,0},{96,32},{1,65},{33,97},{65,1},{97,33},{2,66}... | collective-permute-start | bytes 786440 | tf_op jit(solution)/shard_map/ppermute | solution.py:18
  164.4 11.8 %collective-permute-start.32 = (bf16[128,1024]{1,0:T(8,128)(2,1)S(1)}, bf16[128,1024]{1,0:T(8,128)(2,1)S(1)}, u32[]{:S(2)}, u32[]{:S(2)}) collective-permute-start(bf16[128,1024]{1,0:T(8,128)(2,1)S(1)} %get-tuple-element.49.v0), channel_id=1, source_target_pairs={{0,96},{32,0},{64,32},{96,64},{1,97},{33,1},{65,33},{97,65},{2,98}... | collective-permute-start | bytes 786440 | tf_op jit(solution)/shard_map/ppermute | solution.py:18
  178.7 8.0 %collective-permute-start.33 = (bf16[128,256]{1,0:T(8,128)(2,1)S(1)}, bf16[128,256]{1,0:T(8,128)(2,1)S(1)}, u32[]{:S(2)}, u32[]{:S(2)}) collective-permute-start(bf16[128,256]{1,0:T(8,128)(2,1)S(1)} %get-tuple-element.51), channel_id=1, source_target_pairs={{0,4},{4,8},{8,12},{12,0},{1,5},{5,9},{9,13},{13,1},{2,6},{6,10},{... | collective-permute-start | bytes 196616 | tf_op jit(solution)/shard_map/ppermute | solution.py:18
  180.0 6.8 %collective-permute-start.34 = (bf16[128,256]{1,0:T(8,128)(2,1)S(1)}, bf16[128,256]{1,0:T(8,128)(2,1)S(1)}, u32[]{:S(2)}, u32[]{:S(2)}) collective-permute-start(bf16[128,256]{1,0:T(8,128)(2,1)S(1)} %get-tuple-element.52), channel_id=1, source_target_pairs={{0,8},{4,12},{8,0},{12,4},{1,9},{5,13},{9,1},{13,5},{2,10},{6,14},... | collective-permute-start | bytes 196616 | tf_op jit(solution)/shard_map/ppermute | solution.py:18
  (8 other events, 41.0 us)
Sparse Core Ops, SparseCore 0:
  10.0 44.1 all-gather.8
  55.9 47.4 all-gather.10
  105.1 48.2 all-gather.6

commit v9 on v8

--- a/solution.py
+++ b/solution.py
@@ -22,9 +22,9 @@
     return lax.ppermute(value, "core", [(0, 1), (1, 0)])
 
 
-def along_x(value, core, by):
+def along_y(value, core, by):
     pairs = [(core * 4 + i, core * 4 + (i + by) % 4) for i in range(4)]
-    return lax.ppermute(value, ("core", "x"), pairs)
+    return lax.ppermute(value, ("core", "y"), pairs)
 
 
 def spread(value, axis):
@@ -62,53 +62,83 @@
 
 SCALARS = pl.BlockSpec(memory_space=pltpu.SMEM)
 VMEM = pl.BlockSpec(memory_space=pltpu.VMEM)
+ANY = pl.BlockSpec(memory_space=pl.ANY)
 HBM = pl.BlockSpec(memory_space=pltpu.HBM)
 
 
 def first_product(place, pieces, mine, other, sent):
-    def kernel(place_ref, v0, v1, v2, v3, mine_ref, other_ref, *refs):
-        outs, turned = refs[len(sent) : len(sent) + 4], refs[len(sent) + 4]
-        core, x = place_ref[0], place_ref[2]
-        turned[...] = add_up((v0, v1, v2, v3)).T.astype(BF16)
-        for step, out in enumerate(outs):
-            start = pl.multiple_of(lax.rem(x + step, 4) * 128, 128)
-            left = turned[pl.ds(start, 128), :]
-            for side, tile in ((core, mine_ref), (1 - core, other_ref)):
-                product = jnp.dot(left, tile[...], preferred_element_type=F32)
-                lanes = pl.ds(pl.multiple_of(side * 512, 512), 512)
-                out[:, lanes] = product.astype(BF16)
-
-    return pl.pallas_call(
-        kernel,
-        out_shape=(jax.ShapeDtypeStruct((128, 1024), BF16),) * 4,
-        in_specs=[SCALARS] + [VMEM] * 6 + [pl.BlockSpec(memory_space=pl.ANY)] * len(sent),
+    def kernel(place_ref, v0, v1, v2, v3, mine_ref, other_ref, _, *refs):
+        outs, full = refs[:4], refs[4]
+        core, y = place_ref[0], place_ref[1]
+        turned = add_up((v0, v1, v2, v3)).T.astype(BF16)
+        for side, tile in ((core, mine_ref), (1 - core, other_ref)):
+            product = jnp.dot(turned, tile[...], preferred_element_type=F32)
+            full[:, pl.ds(pl.multiple_of(side * 512, 512), 512)] = product.astype(BF16)
+        for by, out in enumerate(outs):
+            start = lax.rem(y + by, 4) * 128
+            out[:, :128] = full[:, pl.ds(pl.multiple_of(start, 128), 128)]
+            out[:, 128:] = full[:, pl.ds(pl.multiple_of(start + 512, 128), 128)]
+
+    return pl.pallas_call(
+        kernel,
+        out_shape=(jax.ShapeDtypeStruct((512, 256), BF16),) * 4,
+        in_specs=[SCALARS] + [VMEM] * 6 + [ANY],
         out_specs=(VMEM,) * 4,
-        scratch_shapes=[pltpu.VMEM((512, 256), BF16)],
+        scratch_shapes=[pltpu.VMEM((512, 1024), BF16)],
         compiler_params=params(),
         cost_estimate=cost(2 * 512 * 256 * 1024, 3 << 20),
         name="first_product",
-    )(place, *pieces, mine, other, *sent)
-
-
-def gate(token, arrays):
+    )(place, *pieces, mine, other, sent)
+
+
+def first_sum(place, own, zero, one):
+    def kernel(place_ref, own_ref, *refs):
+        outs = refs[6:]
+
+        def body(parts):
+            for step, out in enumerate(outs):
+                start = lax.rem(place_ref[2] + step, 4) * 128
+                rows = pl.ds(pl.multiple_of(start, 128), 128)
+                out[...] = add_up([part.at[rows] for part in (own_ref, *parts)]).astype(BF16)
+
+        @pl.when(place_ref[0] == 0)
+        def _():
+            body(refs[:3])
+
+        @pl.when(place_ref[0] == 1)
+        def _():
+            body(refs[3:6])
+
+    return pl.pallas_call(
+        kernel,
+        out_shape=(jax.ShapeDtypeStruct((128, 256), BF16),) * 4,
+        in_specs=[SCALARS] + [VMEM] * 7,
+        out_specs=(VMEM,) * 4,
+        compiler_params=params(),
+        cost_estimate=cost(4 * 512 * 256, 1 << 20),
+        name="first_sum",
+    )(place, own, *zero, *one)
+
+
+def gate(events, arrays):
     def kernel(*refs):
         pass
 
-    count = len(arrays)
+    count, first = len(arrays), len(events)
     return pl.pallas_call(
         kernel,
         out_shape=tuple(jax.ShapeDtypeStruct(value.shape, value.dtype) for value in arrays),
-        in_specs=[pl.BlockSpec(memory_space=pl.ANY)] * (count + 1),
-        out_specs=(pl.BlockSpec(memory_space=pl.ANY),) * count,
-        input_output_aliases={i + 1: i for i in range(count)},
+        in_specs=[ANY] * (first + count),
+        out_specs=(ANY,) * count,
+        input_output_aliases={first + i: i for i in range(count)},
         compiler_params=params(),
         cost_estimate=cost(0, 1024),
         name="gate",
-    )(token, *arrays)
-
-
-def turn(place, pieces):
-    def kernel(place_ref, v0, v1, v2, v3, out):
+    )(*events, *arrays)
+
+
+def turn(place, pieces, event):
+    def kernel(place_ref, v0, v1, v2, v3, _, out):
         for step, ref in enumerate((v0, v1, v2, v3)):
             start = lax.rem(place_ref[2] + 4 - step, 4) * 256
             lanes = pl.ds(pl.multiple_of(start, 256), 256)
@@ -118,18 +148,21 @@
     return pl.pallas_call(
         kernel,
         out_shape=jax.ShapeDtypeStruct((3, 128, 1024), F32),
-        in_specs=[SCALARS] + [VMEM] * 4,
+        in_specs=[SCALARS] + [VMEM] * 4 + [pl.BlockSpec(memory_space=pl.ANY)],
         out_specs=VMEM,
         compiler_params=params(),
         cost_estimate=cost(3 * 128 * 1024, 3 << 20),
         name="turn",
-    )(place, *pieces)
-
-
-def lower_step(base, pieces, tiles, at, dtype):
+    )(place, *pieces, event)
+
+
+def lower_step(base, pieces, tiles, at, dtype, place=None):
     count = len(pieces)
+    where = [] if place is None else [place]
 
     def kernel(*refs):
+        place_ref = refs[0]
+        refs = refs[len(where) :]
         parts = refs[:count]
         base_ref, tiles_ref, out, kept, tile, sems = refs[count:]
         copies = [
@@ -140,7 +173,13 @@
         ]
         for copy in copies:
             copy.start()
-        kept[...] = add_up(parts).astype(BF16)
+        if where:
+            for step, part in enumerate(parts):
+                start = lax.rem(place_ref[1] + 4 - step, 4) * 128
+                kept[:, pl.ds(pl.multiple_of(start, 128), 128)] = part[:, :128]
+                kept[:, pl.ds(pl.multiple_of(start + 512, 128), 128)] = part[:, 128:]
+        else:
+            kept[...] = add_up(parts).astype(BF16)
         for i, copy in enumerate(copies):
             lanes = slice(i * 256, (i + 1) * 256)
             copy.wait()
@@ -155,7 +194,7 @@
             jax.ShapeDtypeStruct((128, 1024), dtype),
             jax.ShapeDtypeStruct((128, 1024), BF16),
         ),
-        in_specs=[VMEM] * count + [VMEM, HBM],
+        in_specs=[SCALARS] * len(where) + [VMEM] * (count + 1) + [HBM],
         out_specs=(VMEM, VMEM),
         scratch_shapes=[
             pltpu.VMEM((2, 4, 512, 256), BF16),
@@ -164,7 +203,7 @@
         compiler_params=params(),
         cost_estimate=cost(2 * 128 * 1024 * 1024, 4 << 20),
         name="lower_step",
-    )(*pieces, base, tiles)
+    )(*where, *pieces, base, tiles)
 
 
 def fetch_diag(tiles_ref, at, tile, sems):
@@ -396,11 +435,10 @@
 
     owners = owner_map[:, :, 0]
     orders = [
-        [tile(3, 2), ("D", 2)],
-        [tile(3, 1), tile(2, 1), ("D", 1)],
+        [tile(3, 2), ("D", 2), tile(3, 1), tile(2, 1), ("D", 1)],
         [tile(3, 0), tile(2, 0), tile(1, 0), ("D", 0)],
     ]
-    early, middle, late = map(gathered, stage(lower_tiles, inverse_diag, orders, owners))
+    early, late = map(gathered, stage(lower_tiles, inverse_diag, orders, owners))
     named = late[:, :, 2048, :128].astype(jnp.int32).reshape(8, 128)
     other = swap(inverse_diag[3])
 
@@ -422,22 +460,22 @@
         for by in range(4)
     ]
     rest = deal(cut, "x")
-    products = first_product(place, over_z, inverse_diag[3], other, rest[1:])
-    base = turn(place, rest)
-    own, *others = products
-    zero = [along_x(others[by - 1], 0, by) for by in (1, 2, 3)]
+    own, *others = first_product(place, over_z, inverse_diag[3], other, rest[1])
+    zero = [along_y(others[by - 1], 0, by) for by in (1, 2, 3)]
     token = lax.ppermute(sum(piece[:8] for piece in zero), "core", [(0, 1)])
-    others = gate(token, others)
-    one = [along_x(others[by - 1], 1, by) for by in (1, 2, 3)]
-    partial = sum(piece.astype(F32) for piece in (own, *zero, *one)).astype(BF16)
-    pieces = spread(partial, "y")
-    residual, x3 = lower_step(base[2], pieces, early, 0, BF16)
+    others = gate((token, *rest[2:]), others)
+    one = [along_y(others[by - 1], 1, by) for by in (1, 2, 3)]
+    over_x = deal(first_sum(place, own, zero, one), "x")
+    quarter = sum(piece.astype(F32) for piece in over_x).astype(BF16)
+    base = turn(place, rest, quarter)
+    quarters = spread(quarter, "y")
+    residual, x3 = lower_step(base[2], quarters, early, 0, BF16, place)
     over_z = spread(residual, "z")
     pieces = spread(diag_step(over_z, early, 1), "y")
-    base1, _ = lower_step(base[1], (x3,), middle, 0, F32)
-    residual, x2 = lower_step(base1, pieces, middle, 1, BF16)
+    base1, _ = lower_step(base[1], (x3,), early, 2, F32)
+    residual, x2 = lower_step(base1, pieces, early, 3, BF16)
     over_z = spread(residual, "z")
-    pieces = spread(diag_step(over_z, middle, 2), "y")
+    pieces = spread(diag_step(over_z, early, 4), "y")
     base0, _ = lower_step(base[0], (x3,), late, 0, F32)
     base0, _ = lower_step(base0, (x2,), late, 1, F32)
     residual, x1 = lower_step(base0, pieces, late, 2, BF16)

time: 222 us -> 224 us (level)
  blocking collectives: 26.3 us -> 21.9 us
  waiting for transfers between devices: 80.2 us -> 83 us
    ppermute x27 -> x30, waiting for transfers between devices: 43 us -> 74.9 us  [shift(): return lax.ppermute(value, axis, [(i, (i + by) % 4) for i in range(4)])]
    ppermute x1, waiting for transfers between devices: 21.1 us -> 2.45 us  [local(): token = lax.ppermute(sum((piece[:8] for piece in zero)), 'core', [(0, 1)])]
    ppermute x6, waiting for transfers between devices: 12.5 us -> 4.96 us  [along_y(): return lax.ppermute(value, ('core', 'y'), pairs)]
    all_to_all x1, blocking collectives: 26.3 us -> 21.9 us  [local(): lax.all_to_all(packed, ('z', 'core', 'y', 'x'), split_axis=0, concat_axis...]
    all_gather x3 -> x2, waiting for transfers between devices: 2.36 us -> 0.02 us  [gathered(): lax.all_gather(joined, ('core', 'x'), axis=0, tiled=False)]
    ppermute x27 -> x30, starting transfers between devices: 41.8 us -> 42.3 us  [shift(): return lax.ppermute(value, axis, [(i, (i + by) % 4) for i in range(4)])]
  transfers between devices with their start and end apart: 39 -> 41, of which waited for: 19 -> 25; matrix products, arithmetic and copies ran while one was open for 8% -> 8% of each run, Pallas kernels for 9% -> 10%
where the time goes in v9:
time: 224 us
  waiting for transfers between devices  83 us (37%)
  starting transfers between devices  56.6 us (25%)
  Pallas kernels  31.5 us (14%)
  blocking collectives  21.9 us (10%)
  between operations  13.8 us (6%)
  matrix products  13.2 us (6%)
  other arithmetic  2.37 us (1%)
    ppermute x30, waiting for transfers between devices, shift(): return lax.ppermute(value, axis, [(i, (i + by) % 4) for i in range(4)])  74.9 us
    ppermute x30, starting transfers between devices, shift(): return lax.ppermute(value, axis, [(i, (i + by) % 4) for i in range(4)])  42.3 us
    all_to_all x1, blocking collectives, local(): lax.all_to_all(packed, ('z', 'core', 'y', 'x'), split_axis=0, concat_axis...  21.9 us
    pallas_call x6, Pallas kernels, lower_step(): pl.pallas_call(kernel, out_shape=(jax.ShapeDtypeStruct((128, 1024), dtype...  14.2 us
    dot_general x2, matrix products, term(): lax.dot_general(border_tiles, bound, (((0,), (0,)), ((), ())), preferred_...  13.2 us
    ppermute x6, starting transfers between devices, along_y(): return lax.ppermute(value, ('core', 'y'), pairs)  11.4 us
    ppermute x6, waiting for transfers between devices, along_y(): return lax.ppermute(value, ('core', 'y'), pairs)  4.96 us
  transfers between devices with their start and end apart: 41, of which 25 were waited for; matrix products, arithmetic and copies ran while one was open for 8% of the time, Pallas kernels for 10%

profile of v9, /device:TPU:1, one launch (start us, length us, event | category | flops | bytes accessed | tf_op | source)
XLA Modules:
  0.0 223.8 jit_solution(7783919105861690528)
XLA Ops:
  6.5 3.3 %stage.1 = (bf16[2560,256]{1,0:T(8,128)(2,1)}, bf16[2064,256]{1,0:T(8,128)(2,1)}) custom-call(bf16[6,512,256]{2,1,0:T(8,128)(2,1)} %lower_ref.1, bf16[4,256,512]{2,1,0:T(8,128)(2,1)} %diag_ref.1, s32[1,128]{1,0:T(1,128)} %bitcast.56), custom_call_target="tpu_custom_call" | custom-call | bytes 6291456 | tf_op jit(solution)/shard_map/stage/pallas_call | solution.py:323
  10.6 6.8 %fusion.6 = bf16[4,256,512]{2,1,0:T(8,128)(2,1)} fusion(f32[4,256,1024]{2,1,0:T(8,128)} %param.6, s32[]{:T(128)S(6)} %select_n.26, bf16[2048,4,256]{2,1,0:T(4,128)(2,1)} %param.8, bf16[2048,1024]{1,0:T(8,128)(2,1)} %param.7, f32[]{:T(128)S(6)} %select_n.24), kind=kOutput, calls=%fused_computation.7 | convolution fusion | flops 2149056512 | bytes 9438720 | tf_op jit(solution)/shard_map/dot_general | solution.py:449
  20.0 6.3 %fusion.7 = bf16[4,256,512]{2,1,0:T(8,128)(2,1)S(1)} fusion(f32[4,256,1024]{2,1,0:T(8,128)} %param.6, s32[]{:T(128)S(6)} %select_n.25, bf16[2048,4,256]{2,1,0:T(4,128)(2,1)} %param.8, bf16[2048,1024]{1,0:T(8,128)(2,1)} %param.7, f32[]{:T(128)S(6)} %select_n.24), kind=kOutput, calls=%fused_computation.9 | convolution fusion | flops 2149056512 | bytes 9438720 | tf_op jit(solution)/shard_map/dot_general | solution.py:449
  28.6 3.6 %collective-permute-start.2 = (bf16[256,512]{1,0:T(8,128)(2,1)S(1)}, bf16[256,512]{1,0:T(8,128)(2,1)S(1)}, u32[]{:S(2)}, u32[]{:S(2)}) collective-permute-start(bf16[256,512]{1,0:T(8,128)(2,1)S(1)} %slice_bitcast_fusion.3.v0), channel_id=1, source_target_pairs={{0,64},{32,96},{64,0},{96,32},{1,65},{33,97},{65,1},{97,33},{2,66}... | collective-permute-start | bytes 786440 | tf_op jit(solution)/shard_map/ppermute | solution.py:18
  34.4 10.5 %collective-permute-done.5._.v1 = bf16[3,256,128]{2,1,0:T(8,128)(2,1)S(1)} collective-permute-done((bf16[3,256,128]{2,1,0:T(8,128)(2,1)S(1)}, bf16[3,256,128]{2,1,0:T(8,128)(2,1)S(1)}, u32[]{:S(2)}, u32[]{:S(2)}) %collective-permute-start.5) | collective-permute-done | bytes 196640 | tf_op jit(solution)/shard_map/ppermute | solution.py:18
  52.1 6.8 %collective-permute-done.10.refs_1_.v2 = bf16[3,256,128]{2,1,0:T(8,128)(2,1)S(1)} collective-permute-done((bf16[3,256,128]{2,1,0:T(8,128)(2,1)S(1)}, bf16[3,256,128]{2,1,0:T(8,128)(2,1)S(1)}, u32[]{:S(2)}, u32[]{:S(2)}) %collective-permute-start.10) | collective-permute-done | bytes 196640 | tf_op jit(solution)/shard_map/ppermute | solution.py:18
  58.9 5.6 %collective-permute-done.11.refs_2_.v3 = bf16[3,256,128]{2,1,0:T(8,128)(2,1)S(1)} collective-permute-done((bf16[3,256,128]{2,1,0:T(8,128)(2,1)S(1)}, bf16[3,256,128]{2,1,0:T(8,128)(2,1)S(1)}, u32[]{:S(2)}, u32[]{:S(2)}) %collective-permute-start.11) | collective-permute-done | bytes 196640 | tf_op jit(solution)/shard_map/ppermute | solution.py:18
  64.4 2.5 %collective-permute-done.9.refs_0_ = bf16[8,256]{1,0:T(8,128)(2,1)S(1)} collective-permute-done((bf16[8,256]{1,0:T(8,128)(2,1)S(1)}, bf16[8,256]{1,0:T(8,128)(2,1)S(1)}, u32[]{:S(2)}, u32[]{:S(2)}) %collective-permute-start.9) | collective-permute-done | bytes 4128 | tf_op jit(solution)/shard_map/ppermute | solution.py:465
  66.9 2.7 %collective-permute-start.12 = (bf16[512,256]{1,0:T(8,128)(2,1)S(1)}, bf16[512,256]{1,0:T(8,128)(2,1)S(1)}, u32[]{:S(2)}, u32[]{:S(2)}) collective-permute-start(bf16[512,256]{1,0:T(8,128)(2,1)S(1)} %get-tuple-element.38), channel_id=1, source_target_pairs={{16,20},{20,24},{24,28},{28,16},{17,21},{21,25},{25,29},{29,17},{1... | collective-permute-start | bytes 786440 | tf_op jit(solution)/shard_map/ppermute | solution.py:27
  69.6 4.6 %collective-permute-start.13 = (bf16[512,256]{1,0:T(8,128)(2,1)S(1)}, bf16[512,256]{1,0:T(8,128)(2,1)S(1)}, u32[]{:S(2)}, u32[]{:S(2)}) collective-permute-start(bf16[512,256]{1,0:T(8,128)(2,1)S(1)} %get-tuple-element.39), channel_id=1, source_target_pairs={{16,24},{20,28},{24,16},{28,20},{17,25},{21,29},{25,17},{29,21},{1... | collective-permute-start | bytes 786440 | tf_op jit(solution)/shard_map/ppermute | solution.py:27
  76.3 2.5 %collective-permute-done.13.refs_4_ = bf16[512,256]{1,0:T(8,128)(2,1)S(1)} collective-permute-done((bf16[512,256]{1,0:T(8,128)(2,1)S(1)}, bf16[512,256]{1,0:T(8,128)(2,1)S(1)}, u32[]{:S(2)}, u32[]{:S(2)}) %collective-permute-start.13) | collective-permute-done | bytes 262176 | tf_op jit(solution)/shard_map/ppermute | solution.py:27
  78.8 2.5 %collective-permute-done.14.refs_5_ = bf16[512,256]{1,0:T(8,128)(2,1)S(1)} collective-permute-done((bf16[512,256]{1,0:T(8,128)(2,1)S(1)}, bf16[512,256]{1,0:T(8,128)(2,1)S(1)}, u32[]{:S(2)}, u32[]{:S(2)}) %collective-permute-start.14) | collective-permute-done | bytes 262176 | tf_op jit(solution)/shard_map/ppermute | solution.py:27
  94.6 2.6 %lower_step.6 = (bf16[128,1024]{1,0:T(8,128)(2,1)S(1)}, bf16[128,1024]{1,0:T(8,128)(2,1)S(1)}) custom-call(s32[4]{0:T(128)S(1)} %pad_add_fusion.place_ref.refs_0_, bf16[128,256]{1,0:T(8,128)(2,1)S(1)} %add_convert_fusion.1._.refs_1_, bf16[128,256]{1,0:T(8,128)(2,1)S(1)} %collective-permute-done.18.refs_2_, ...), custom_call_target="tpu_custom_call" | custom-call | flops 268435456 | bytes 4194304 | tf_op jit(solution)/shard_map/lower_step/pallas_call | solution.py:191
  98.3 2.6 %collective-permute-start.22 = (bf16[128,1024]{1,0:T(8,128)(2,1)S(1)}, bf16[128,1024]{1,0:T(8,128)(2,1)S(1)}, u32[]{:S(2)}, u32[]{:S(2)}) collective-permute-start(bf16[128,1024]{1,0:T(8,128)(2,1)S(1)} %get-tuple-element.46.v0), channel_id=1, source_target_pairs={{0,64},{32,96},{64,0},{96,32},{1,65},{33,97},{65,1},{97,33},{2,66}... | collective-permute-start | bytes 786440 | tf_op jit(solution)/shard_map/ppermute | solution.py:18
  101.1 5.0 %collective-permute-done.21.v1 = bf16[128,1024]{1,0:T(8,128)(2,1)S(1)} collective-permute-done((bf16[128,1024]{1,0:T(8,128)(2,1)S(1)}, bf16[128,1024]{1,0:T(8,128)(2,1)S(1)}, u32[]{:S(2)}, u32[]{:S(2)}) %collective-permute-start.21) | collective-permute-done | bytes 262176 | tf_op jit(solution)/shard_map/ppermute | solution.py:18
  106.1 6.9 %collective-permute-done.22.v2 = bf16[128,1024]{1,0:T(8,128)(2,1)S(1)} collective-permute-done((bf16[128,1024]{1,0:T(8,128)(2,1)S(1)}, bf16[128,1024]{1,0:T(8,128)(2,1)S(1)}, u32[]{:S(2)}, u32[]{:S(2)}) %collective-permute-start.22) | collective-permute-done | bytes 262176 | tf_op jit(solution)/shard_map/ppermute | solution.py:18
  114.9 2.8 %collective-permute-start.25 = (bf16[128,1024]{1,0:T(8,128)(2,1)S(1)}, bf16[128,1024]{1,0:T(8,128)(2,1)S(1)}, u32[]{:S(2)}, u32[]{:S(2)}) collective-permute-start(bf16[128,1024]{1,0:T(8,128)(2,1)S(1)} %diag_step.2.refs_0_), channel_id=1, source_target_pairs={{0,8},{4,12},{8,0},{12,4},{1,9},{5,13},{9,1},{13,5},{2,10},{6,14},... | collective-permute-start | bytes 786440 | tf_op jit(solution)/shard_map/ppermute | solution.py:18
  117.9 2.5 %lower_step.7 = (f32[128,1024]{1,0:T(8,128)S(1)}, bf16[128,1024]{1,0:T(8,128)(2,1)}) custom-call(bf16[128,1024]{1,0:T(8,128)(2,1)S(1)} %get-tuple-element.47.refs_0_.x3, f32[128,1024]{1,0:T(8,128)S(1)} %get-tuple-element.62.refs_1_, bf16[2,4,2560,256]{3,2,1,0:T(8,128)(2,1)} %bitcast.46), custom_call_target="tpu_custom_call" | custom-call | flops 268435456 | bytes 4194304 | tf_op jit(solution)/shard_map/lower_step/pallas_call | solution.py:191
  120.5 3.9 %collective-permute-done.24.refs_1_ = bf16[128,1024]{1,0:T(8,128)(2,1)S(1)} collective-permute-done((bf16[128,1024]{1,0:T(8,128)(2,1)S(1)}, bf16[128,1024]{1,0:T(8,128)(2,1)S(1)}, u32[]{:S(2)}, u32[]{:S(2)}) %collective-permute-start.24) | collective-permute-done | bytes 262176 | tf_op jit(solution)/shard_map/ppermute | solution.py:18
  124.4 3.8 %collective-permute-done.25.refs_2_ = bf16[128,1024]{1,0:T(8,128)(2,1)S(1)} collective-permute-done((bf16[128,1024]{1,0:T(8,128)(2,1)S(1)}, bf16[128,1024]{1,0:T(8,128)(2,1)S(1)}, u32[]{:S(2)}, u32[]{:S(2)}) %collective-permute-start.25) | collective-permute-done | bytes 262176 | tf_op jit(solution)/shard_map/ppermute | solution.py:18
  133.5 2.6 %collective-permute-start.28 = (bf16[128,1024]{1,0:T(8,128)(2,1)S(1)}, bf16[128,1024]{1,0:T(8,128)(2,1)S(1)}, u32[]{:S(2)}, u32[]{:S(2)}) collective-permute-start(bf16[128,1024]{1,0:T(8,128)(2,1)S(1)} %get-tuple-element.49.v0), channel_id=1, source_target_pairs={{0,64},{32,96},{64,0},{96,32},{1,65},{33,97},{65,1},{97,33},{2,66}... | collective-permute-start | bytes 786440 | tf_op jit(solution)/shard_map/ppermute | solution.py:18
  136.1 4.2 %collective-permute-done.27.v1 = bf16[128,1024]{1,0:T(8,128)(2,1)S(1)} collective-permute-done((bf16[128,1024]{1,0:T(8,128)(2,1)S(1)}, bf16[128,1024]{1,0:T(8,128)(2,1)S(1)}, u32[]{:S(2)}, u32[]{:S(2)}) %collective-permute-start.27) | collective-permute-done | bytes 262176 | tf_op jit(solution)/shard_map/ppermute | solution.py:18
  140.2 6.5 %collective-permute-done.28.v2 = bf16[128,1024]{1,0:T(8,128)(2,1)S(1)} collective-permute-done((bf16[128,1024]{1,0:T(8,128)(2,1)S(1)}, bf16[128,1024]{1,0:T(8,128)(2,1)S(1)}, u32[]{:S(2)}, u32[]{:S(2)}) %collective-permute-start.28) | collective-permute-done | bytes 262176 | tf_op jit(solution)/shard_map/ppermute | solution.py:18
  153.6 2.5 %lower_step.9 = (f32[128,1024]{1,0:T(8,128)S(1)}, bf16[128,1024]{1,0:T(8,128)(2,1)}) custom-call(bf16[128,1024]{1,0:T(8,128)(2,1)S(1)} %get-tuple-element.47.refs_0_.x3, f32[128,1024]{1,0:T(8,128)S(1)} %get-tuple-element.61.refs_1_, bf16[2,4,2064,256]{3,2,1,0:T(8,128)(2,1)} %bitcast.49), custom_call_target="tpu_custom_call" | custom-call | flops 268435456 | bytes 4194304 | tf_op jit(solution)/shard_map/lower_step/pallas_call | solution.py:191
  156.2 2.5 %lower_step.10 = (f32[128,1024]{1,0:T(8,128)S(1)}, bf16[128,1024]{1,0:T(8,128)(2,1)}) custom-call(bf16[128,1024]{1,0:T(8,128)(2,1)S(1)} %get-tuple-element.50.refs_0_.x2, f32[128,1024]{1,0:T(8,128)S(1)} %get-tuple-element.51.refs_1_, bf16[2,4,2064,256]{3,2,1,0:T(8,128)(2,1)} %bitcast.50), custom_call_target="tpu_custom_call" | custom-call | flops 268435456 | bytes 4194304 | tf_op jit(solution)/shard_map/lower_step/pallas_call | solution.py:191
  158.7 5.6 %collective-permute-done.31.refs_2_ = bf16[128,1024]{1,0:T(8,128)(2,1)S(1)} collective-permute-done((bf16[128,1024]{1,0:T(8,128)(2,1)S(1)}, bf16[128,1024]{1,0:T(8,128)(2,1)S(1)}, u32[]{:S(2)}, u32[]{:S(2)}) %collective-permute-start.31) | collective-permute-done | bytes 262176 | tf_op jit(solution)/shard_map/ppermute | solution.py:18
  168.5 2.5 %collective-permute-start.34 = (bf16[128,1024]{1,0:T(8,128)(2,1)S(1)}, bf16[128,1024]{1,0:T(8,128)(2,1)S(1)}, u32[]{:S(2)}, u32[]{:S(2)}) collective-permute-start(bf16[128,1024]{1,0:T(8,128)(2,1)S(1)} %get-tuple-element.55.v0), channel_id=1, source_target_pairs={{0,64},{32,96},{64,0},{96,32},{1,65},{33,97},{65,1},{97,33},{2,66}... | collective-permute-start | bytes 786440 | tf_op jit(solution)/shard_map/ppermute | solution.py:18
  174.9 6.8 %collective-permute-done.34.v2 = bf16[128,1024]{1,0:T(8,128)(2,1)S(1)} collective-permute-done((bf16[128,1024]{1,0:T(8,128)(2,1)S(1)}, bf16[128,1024]{1,0:T(8,128)(2,1)S(1)}, u32[]{:S(2)}, u32[]{:S(2)}) %collective-permute-start.34) | collective-permute-done | bytes 262176 | tf_op jit(solution)/shard_map/ppermute | solution.py:18
  181.9 2.5 %last_step.1 = (bf16[128,256]{1,0:T(8,128)(2,1)S(1)}, bf16[128,256]{1,0:T(8,128)(2,1)S(1)}, bf16[128,256]{1,0:T(8,128)(2,1)S(1)}, bf16[128,256]{1,0:T(8,128)(2,1)S(1)}) custom-call(s32[4]{0:T(128)S(1)} %pad_add_fusion.place_ref.refs_0_, bf16[128,1024]{1,0:T(8,128)(2,1)S(1)} %get-tuple-element.55.v0, bf16[128,1024]{1,0:T(8,128)(2,1)S(1)} %collective-permute-done.33.v1, ...), custom_call_target="tpu_custom_call" | custom-call | flops 268435456 | bytes 4194304 | tf_op jit(solution)/shard_map/last_step/pallas_call | solution.py:270
  186.5 2.5 %collective-permute-start.37 = (bf16[128,256]{1,0:T(8,128)(2,1)S(1)}, bf16[128,256]{1,0:T(8,128)(2,1)S(1)}, u32[]{:S(2)}, u32[]{:S(2)}) collective-permute-start(bf16[128,256]{1,0:T(8,128)(2,1)S(1)} %get-tuple-element.58), channel_id=1, source_target_pairs={{0,8},{4,12},{8,0},{12,4},{1,9},{5,13},{9,1},{13,5},{2,10},{6,14},... | collective-permute-start | bytes 196616 | tf_op jit(solution)/shard_map/ppermute | solution.py:18
  189.2 3.0 %pack_known.1 = (bf16[2048,128]{1,0:T(8,128)(2,1)S(1)}, bf16[2048,256]{1,0:T(8,128)(2,1)S(1)}) custom-call(s32[4]{0:T(128)S(1)} %pad_add_fusion.place_ref.refs_0_, s32[4,1,256]{2,1,0:T(1,128)S(1)} %reshape.61.target_ref, bf16[128,1024]{1,0:T(8,128)(2,1)S(1)} %get-tuple-element.53.x1, bf16[128,1024]{1,0:T(8,128)(2,1)S(1)} %get-tuple-element.50.refs_0_.x2, ...), custom_call_target="tpu_custom_call" | custom-call | flops 402653184 | bytes 2097152 | tf_op jit(solution)/shard_map/pack_known/pallas_call | solution.py:359
  193.6 21.9 %all_to_all.5 = bf16[128,16,128]{2,1,0:T(8,128)(2,1)S(1)} all-to-all(bf16[128,16,128]{2,1,0:T(8,128)(2,1)S(1)} %bitcast.43), channel_id=1, replica_groups=mesh['z'=4,'core'=2,'y'=4,'x'=4] {'z','core','y','x'}, dimensions={0} | all-to-all | bytes 1048576 | tf_op jit(solution)/shard_map/all_to_all | solution.py:486
  (91 shorter events, 59.4 us)
Async XLA Ops:
  6.5 88.0 %all-gather.7.cloned.1.call-start = ((), (), s32[]{:S(2)}) async-start(), calls=%async_computation.2 | async-start | bytes 11796480 | tf_op jit(solution)/shard_map/all_gather | solution.py:425
  9.9 143.8 %all-gather.5.cloned.1.call-start = ((), (), s32[]{:S(2)}) async-start(), calls=%async_computation.1 | async-start | bytes 9510912 | tf_op jit(solution)/shard_map/all_gather | solution.py:425
  17.5 8.9 %collective-permute-start = (bf16[4,256,512]{2,1,0:T(8,128)(2,1)}, bf16[4,256,512]{2,1,0:T(8,128)(2,1)S(1)}, u32[]{:S(2)}, u32[]{:S(2)}) collective-permute-start(bf16[4,256,512]{2,1,0:T(8,128)(2,1)} %fusion.6), channel_id=1, source_target_pairs={{0,16},{16,0},{1,17},{17,1},{2,18},{18,2},{3,19},{19,3},{4,20},{20... | collective-permute-start | bytes 3145736 | tf_op jit(solution)/shard_map/ppermute | solution.py:22
  19.9 14.5 %collective-permute-start.4 = (bf16[256,512]{1,0:T(8,128)(2,1)S(1)}, bf16[256,512]{1,0:T(8,128)(2,1)S(1)}, u32[]{:S(2)}, u32[]{:S(2)}) collective-permute-start(bf16[256,512]{1,0:T(8,128)(2,1)S(1)} %slice_bitcast_fusion.4.mine_ref), channel_id=1, source_target_pairs={{0,16},{16,0},{1,17},{17,1},{2,18},{18,2},{3,19},{19,3},{4,20},{20... | collective-permute-start | bytes 786440 | tf_op jit(solution)/shard_map/ppermute | solution.py:22
  26.8 18.1 %collective-permute-start.1 = (bf16[256,512]{1,0:T(8,128)(2,1)S(1)}, bf16[256,512]{1,0:T(8,128)(2,1)S(1)}, u32[]{:S(2)}, u32[]{:S(2)}) collective-permute-start(bf16[256,512]{1,0:T(8,128)(2,1)S(1)} %slice_bitcast_fusion.3.v0), channel_id=1, source_target_pairs={{0,32},{32,64},{64,96},{96,0},{1,33},{33,65},{65,97},{97,1},{2,34}... | collective-permute-start | bytes 786440 | tf_op jit(solution)/shard_map/ppermute | solution.py:18
  28.6 16.3 %collective-permute-start.2 = (bf16[256,512]{1,0:T(8,128)(2,1)S(1)}, bf16[256,512]{1,0:T(8,128)(2,1)S(1)}, u32[]{:S(2)}, u32[]{:S(2)}) collective-permute-start(bf16[256,512]{1,0:T(8,128)(2,1)S(1)} %slice_bitcast_fusion.3.v0), channel_id=1, source_target_pairs={{0,64},{32,96},{64,0},{96,32},{1,65},{33,97},{65,1},{97,33},{2,66}... | collective-permute-start | bytes 786440 | tf_op jit(solution)/shard_map/ppermute | solution.py:18
  32.2 12.7 %collective-permute-start.3 = (bf16[256,512]{1,0:T(8,128)(2,1)S(1)}, bf16[256,512]{1,0:T(8,128)(2,1)S(1)}, u32[]{:S(2)}, u32[]{:S(2)}) collective-permute-start(bf16[256,512]{1,0:T(8,128)(2,1)S(1)} %slice_bitcast_fusion.3.v0), channel_id=1, source_target_pairs={{0,96},{32,0},{64,32},{96,64},{1,97},{33,1},{65,33},{97,65},{2,98}... | collective-permute-start | bytes 786440 | tf_op jit(solution)/shard_map/ppermute | solution.py:18
  33.0 11.9 %collective-permute-start.5 = (bf16[3,256,128]{2,1,0:T(8,128)(2,1)S(1)}, bf16[3,256,128]{2,1,0:T(8,128)(2,1)S(1)}, u32[]{:S(2)}, u32[]{:S(2)}) collective-permute-start(bf16[3,256,128]{2,1,0:T(8,128)(2,1)S(1)} %get-tuple-element.67), channel_id=1, source_target_pairs={{0,1},{1,2},{2,3},{3,0},{4,5},{5,6},{6,7},{7,4},{8,9},{9,10},{10,1... | collective-permute-start | bytes 589832 | tf_op jit(solution)/shard_map/ppermute | solution.py:18
  48.3 10.6 %collective-permute-start.10 = (bf16[3,256,128]{2,1,0:T(8,128)(2,1)S(1)}, bf16[3,256,128]{2,1,0:T(8,128)(2,1)S(1)}, u32[]{:S(2)}, u32[]{:S(2)}) collective-permute-start(bf16[3,256,128]{2,1,0:T(8,128)(2,1)S(1)} %get-tuple-element.66), channel_id=1, source_target_pairs={{0,2},{1,3},{2,0},{3,1},{4,6},{5,7},{6,4},{7,5},{8,10},{9,11},{10,... | collective-permute-start | bytes 589832 | tf_op jit(solution)/shard_map/ppermute | solution.py:18
  50.0 14.5 %collective-permute-start.11 = (bf16[3,256,128]{2,1,0:T(8,128)(2,1)S(1)}, bf16[3,256,128]{2,1,0:T(8,128)(2,1)S(1)}, u32[]{:S(2)}, u32[]{:S(2)}) collective-permute-start(bf16[3,256,128]{2,1,0:T(8,128)(2,1)S(1)} %get-tuple-element.65), channel_id=1, source_target_pairs={{0,3},{1,0},{2,1},{3,2},{4,7},{5,4},{6,5},{7,6},{8,11},{9,8},{10,9... | collective-permute-start | bytes 589832 | tf_op jit(solution)/shard_map/ppermute | solution.py:18
  50.8 16.1 %collective-permute-start.9 = (bf16[8,256]{1,0:T(8,128)(2,1)S(1)}, bf16[8,256]{1,0:T(8,128)(2,1)S(1)}, u32[]{:S(2)}, u32[]{:S(2)}) collective-permute-start(bf16[8,256]{1,0:T(8,128)(2,1)S(1)} %slice_add_fusion), channel_id=1, source_target_pairs={{0,16},{1,17},{2,18},{3,19},{4,20},{5,21},{6,22},{7,23},{8,24},{9,... | collective-permute-start | bytes 12296 | tf_op jit(solution)/shard_map/ppermute | solution.py:465
  66.9 9.4 %collective-permute-start.12 = (bf16[512,256]{1,0:T(8,128)(2,1)S(1)}, bf16[512,256]{1,0:T(8,128)(2,1)S(1)}, u32[]{:S(2)}, u32[]{:S(2)}) collective-permute-start(bf16[512,256]{1,0:T(8,128)(2,1)S(1)} %get-tuple-element.38), channel_id=1, source_target_pairs={{16,20},{20,24},{24,28},{28,16},{17,21},{21,25},{25,29},{29,17},{1... | collective-permute-start | bytes 786440 | tf_op jit(solution)/shard_map/ppermute | solution.py:27
  69.6 9.2 %collective-permute-start.13 = (bf16[512,256]{1,0:T(8,128)(2,1)S(1)}, bf16[512,256]{1,0:T(8,128)(2,1)S(1)}, u32[]{:S(2)}, u32[]{:S(2)}) collective-permute-start(bf16[512,256]{1,0:T(8,128)(2,1)S(1)} %get-tuple-element.39), channel_id=1, source_target_pairs={{16,24},{20,28},{24,16},{28,20},{17,25},{21,29},{25,17},{29,21},{1... | collective-permute-start | bytes 786440 | tf_op jit(solution)/shard_map/ppermute | solution.py:27
  74.1 7.1 %collective-permute-start.14 = (bf16[512,256]{1,0:T(8,128)(2,1)S(1)}, bf16[512,256]{1,0:T(8,128)(2,1)S(1)}, u32[]{:S(2)}, u32[]{:S(2)}) collective-permute-start(bf16[512,256]{1,0:T(8,128)(2,1)S(1)} %get-tuple-element.40), channel_id=1, source_target_pairs={{16,28},{20,16},{24,20},{28,24},{17,29},{21,17},{25,21},{29,25},{1... | collective-permute-start | bytes 786440 | tf_op jit(solution)/shard_map/ppermute | solution.py:27
  88.2 5.5 %collective-permute-start.19 = (bf16[128,256]{1,0:T(8,128)(2,1)S(1)}, bf16[128,256]{1,0:T(8,128)(2,1)S(1)}, u32[]{:S(2)}, u32[]{:S(2)}) collective-permute-start(bf16[128,256]{1,0:T(8,128)(2,1)S(1)} %add_convert_fusion.1._.refs_1_), channel_id=1, source_target_pairs={{0,8},{4,12},{8,0},{12,4},{1,9},{5,13},{9,1},{13,5},{2,10},{6,14},... | collective-permute-start | bytes 196616 | tf_op jit(solution)/shard_map/ppermute | solution.py:18
  97.2 8.9 %collective-permute-start.21 = (bf16[128,1024]{1,0:T(8,128)(2,1)S(1)}, bf16[128,1024]{1,0:T(8,128)(2,1)S(1)}, u32[]{:S(2)}, u32[]{:S(2)}) collective-permute-start(bf16[128,1024]{1,0:T(8,128)(2,1)S(1)} %get-tuple-element.46.v0), channel_id=1, source_target_pairs={{0,32},{32,64},{64,96},{96,0},{1,33},{33,65},{65,97},{97,1},{2,34}... | collective-permute-start | bytes 786440 | tf_op jit(solution)/shard_map/ppermute | solution.py:18
  98.3 14.6 %collective-permute-start.22 = (bf16[128,1024]{1,0:T(8,128)(2,1)S(1)}, bf16[128,1024]{1,0:T(8,128)(2,1)S(1)}, u32[]{:S(2)}, u32[]{:S(2)}) collective-permute-start(bf16[128,1024]{1,0:T(8,128)(2,1)S(1)} %get-tuple-element.46.v0), channel_id=1, source_target_pairs={{0,64},{32,96},{64,0},{96,32},{1,65},{33,97},{65,1},{97,33},{2,66}... | collective-permute-start | bytes 786440 | tf_op jit(solution)/shard_map/ppermute | solution.py:18
  100.9 12.0 %collective-permute-start.23 = (bf16[128,1024]{1,0:T(8,128)(2,1)S(1)}, bf16[128,1024]{1,0:T(8,128)(2,1)S(1)}, u32[]{:S(2)}, u32[]{:S(2)}) collective-permute-start(bf16[128,1024]{1,0:T(8,128)(2,1)S(1)} %get-tuple-element.46.v0), channel_id=1, source_target_pairs={{0,96},{32,0},{64,32},{96,64},{1,97},{33,1},{65,33},{97,65},{2,98}... | collective-permute-start | bytes 786440 | tf_op jit(solution)/shard_map/ppermute | solution.py:18
  114.8 9.6 %collective-permute-start.24 = (bf16[128,1024]{1,0:T(8,128)(2,1)S(1)}, bf16[128,1024]{1,0:T(8,128)(2,1)S(1)}, u32[]{:S(2)}, u32[]{:S(2)}) collective-permute-start(bf16[128,1024]{1,0:T(8,128)(2,1)S(1)} %diag_step.2.refs_0_), channel_id=1, source_target_pairs={{0,4},{4,8},{8,12},{12,0},{1,5},{5,9},{9,13},{13,1},{2,6},{6,10},{... | collective-permute-start | bytes 786440 | tf_op jit(solution)/shard_map/ppermute | solution.py:18
  114.9 13.3 %collective-permute-start.25 = (bf16[128,1024]{1,0:T(8,128)(2,1)S(1)}, bf16[128,1024]{1,0:T(8,128)(2,1)S(1)}, u32[]{:S(2)}, u32[]{:S(2)}) collective-permute-start(bf16[128,1024]{1,0:T(8,128)(2,1)S(1)} %diag_step.2.refs_0_), channel_id=1, source_target_pairs={{0,8},{4,12},{8,0},{12,4},{1,9},{5,13},{9,1},{13,5},{2,10},{6,14},... | collective-permute-start | bytes 786440 | tf_op jit(solution)/shard_map/ppermute | solution.py:18
  117.7 11.8 %collective-permute-start.26 = (bf16[128,1024]{1,0:T(8,128)(2,1)S(1)}, bf16[128,1024]{1,0:T(8,128)(2,1)S(1)}, u32[]{:S(2)}, u32[]{:S(2)}) collective-permute-start(bf16[128,1024]{1,0:T(8,128)(2,1)S(1)} %diag_step.2.refs_0_), channel_id=1, source_target_pairs={{0,12},{4,0},{8,4},{12,8},{1,13},{5,1},{9,5},{13,9},{2,14},{6,2},{... | collective-permute-start | bytes 786440 | tf_op jit(solution)/shard_map/ppermute | solution.py:18
  131.5 8.7 %collective-permute-start.27 = (bf16[128,1024]{1,0:T(8,128)(2,1)S(1)}, bf16[128,1024]{1,0:T(8,128)(2,1)S(1)}, u32[]{:S(2)}, u32[]{:S(2)}) collective-permute-start(bf16[128,1024]{1,0:T(8,128)(2,1)S(1)} %get-tuple-element.49.v0), channel_id=1, source_target_pairs={{0,32},{32,64},{64,96},{96,0},{1,33},{33,65},{65,97},{97,1},{2,34}... | collective-permute-start | bytes 786440 | tf_op jit(solution)/shard_map/ppermute | solution.py:18
  133.5 13.2 %collective-permute-start.28 = (bf16[128,1024]{1,0:T(8,128)(2,1)S(1)}, bf16[128,1024]{1,0:T(8,128)(2,1)S(1)}, u32[]{:S(2)}, u32[]{:S(2)}) collective-permute-start(bf16[128,1024]{1,0:T(8,128)(2,1)S(1)} %get-tuple-element.49.v0), channel_id=1, source_target_pairs={{0,64},{32,96},{64,0},{96,32},{1,65},{33,97},{65,1},{97,33},{2,66}... | collective-permute-start | bytes 786440 | tf_op jit(solution)/shard_map/ppermute | solution.py:18
  136.1 10.8 %collective-permute-start.29 = (bf16[128,1024]{1,0:T(8,128)(2,1)S(1)}, bf16[128,1024]{1,0:T(8,128)(2,1)S(1)}, u32[]{:S(2)}, u32[]{:S(2)}) collective-permute-start(bf16[128,1024]{1,0:T(8,128)(2,1)S(1)} %get-tuple-element.49.v0), channel_id=1, source_target_pairs={{0,96},{32,0},{64,32},{96,64},{1,97},{33,1},{65,33},{97,65},{2,98}... | collective-permute-start | bytes 786440 | tf_op jit(solution)/shard_map/ppermute | solution.py:18
  148.8 9.9 %collective-permute-start.30 = (bf16[128,1024]{1,0:T(8,128)(2,1)S(1)}, bf16[128,1024]{1,0:T(8,128)(2,1)S(1)}, u32[]{:S(2)}, u32[]{:S(2)}) collective-permute-start(bf16[128,1024]{1,0:T(8,128)(2,1)S(1)} %diag_step.3.refs_0_), channel_id=1, source_target_pairs={{0,4},{4,8},{8,12},{12,0},{1,5},{5,9},{9,13},{13,1},{2,6},{6,10},{... | collective-permute-start | bytes 786440 | tf_op jit(solution)/shard_map/ppermute | solution.py:18
  151.1 13.2 %collective-permute-start.31 = (bf16[128,1024]{1,0:T(8,128)(2,1)S(1)}, bf16[128,1024]{1,0:T(8,128)(2,1)S(1)}, u32[]{:S(2)}, u32[]{:S(2)}) collective-permute-start(bf16[128,1024]{1,0:T(8,128)(2,1)S(1)} %diag_step.3.refs_0_), channel_id=1, source_target_pairs={{0,8},{4,12},{8,0},{12,4},{1,9},{5,13},{9,1},{13,5},{2,10},{6,14},... | collective-permute-start | bytes 786440 | tf_op jit(solution)/shard_map/ppermute | solution.py:18
  153.5 10.8 %collective-permute-start.32 = (bf16[128,1024]{1,0:T(8,128)(2,1)S(1)}, bf16[128,1024]{1,0:T(8,128)(2,1)S(1)}, u32[]{:S(2)}, u32[]{:S(2)}) collective-permute-start(bf16[128,1024]{1,0:T(8,128)(2,1)S(1)} %diag_step.3.refs_0_), channel_id=1, source_target_pairs={{0,12},{4,0},{8,4},{12,8},{1,13},{5,1},{9,5},{13,9},{2,14},{6,2},{... | collective-permute-start | bytes 786440 | tf_op jit(solution)/shard_map/ppermute | solution.py:18
  166.4 8.5 %collective-permute-start.33 = (bf16[128,1024]{1,0:T(8,128)(2,1)S(1)}, bf16[128,1024]{1,0:T(8,128)(2,1)S(1)}, u32[]{:S(2)}, u32[]{:S(2)}) collective-permute-start(bf16[128,1024]{1,0:T(8,128)(2,1)S(1)} %get-tuple-element.55.v0), channel_id=1, source_target_pairs={{0,32},{32,64},{64,96},{96,0},{1,33},{33,65},{65,97},{97,1},{2,34}... | collective-permute-start | bytes 786440 | tf_op jit(solution)/shard_map/ppermute | solution.py:18
  168.5 13.1 %collective-permute-start.34 = (bf16[128,1024]{1,0:T(8,128)(2,1)S(1)}, bf16[128,1024]{1,0:T(8,128)(2,1)S(1)}, u32[]{:S(2)}, u32[]{:S(2)}) collective-permute-start(bf16[128,1024]{1,0:T(8,128)(2,1)S(1)} %get-tuple-element.55.v0), channel_id=1, source_target_pairs={{0,64},{32,96},{64,0},{96,32},{1,65},{33,97},{65,1},{97,33},{2,66}... | collective-permute-start | bytes 786440 | tf_op jit(solution)/shard_map/ppermute | solution.py:18
  171.1 10.8 %collective-permute-start.35 = (bf16[128,1024]{1,0:T(8,128)(2,1)S(1)}, bf16[128,1024]{1,0:T(8,128)(2,1)S(1)}, u32[]{:S(2)}, u32[]{:S(2)}) collective-permute-start(bf16[128,1024]{1,0:T(8,128)(2,1)S(1)} %get-tuple-element.55.v0), channel_id=1, source_target_pairs={{0,96},{32,0},{64,32},{96,64},{1,97},{33,1},{65,33},{97,65},{2,98}... | collective-permute-start | bytes 786440 | tf_op jit(solution)/shard_map/ppermute | solution.py:18
  184.4 7.9 %collective-permute-start.36 = (bf16[128,256]{1,0:T(8,128)(2,1)S(1)}, bf16[128,256]{1,0:T(8,128)(2,1)S(1)}, u32[]{:S(2)}, u32[]{:S(2)}) collective-permute-start(bf16[128,256]{1,0:T(8,128)(2,1)S(1)} %get-tuple-element.57), channel_id=1, source_target_pairs={{0,4},{4,8},{8,12},{12,0},{1,5},{5,9},{9,13},{13,1},{2,6},{6,10},{... | collective-permute-start | bytes 196616 | tf_op jit(solution)/shard_map/ppermute | solution.py:18
  186.5 5.7 %collective-permute-start.37 = (bf16[128,256]{1,0:T(8,128)(2,1)S(1)}, bf16[128,256]{1,0:T(8,128)(2,1)S(1)}, u32[]{:S(2)}, u32[]{:S(2)}) collective-permute-start(bf16[128,256]{1,0:T(8,128)(2,1)S(1)} %get-tuple-element.58), channel_id=1, source_target_pairs={{0,8},{4,12},{8,0},{12,4},{1,9},{5,13},{9,1},{13,5},{2,10},{6,14},... | collective-permute-start | bytes 196616 | tf_op jit(solution)/shard_map/ppermute | solution.py:18
  (9 other events, 37.5 us)
Sparse Core Ops, SparseCore 0:
  10.0 70.5 all-gather.6
  82.3 50.2 all-gather.4

commit v10 on v9

--- a/solution.py
+++ b/solution.py
@@ -67,8 +67,8 @@
 
 
 def first_product(place, pieces, mine, other, sent):
-    def kernel(place_ref, v0, v1, v2, v3, mine_ref, other_ref, _, *refs):
-        outs, full = refs[:4], refs[4]
+    def kernel(place_ref, v0, v1, v2, v3, mine_ref, other_ref, *refs):
+        outs, full = refs[len(sent) : len(sent) + 4], refs[len(sent) + 4]
         core, y = place_ref[0], place_ref[1]
         turned = add_up((v0, v1, v2, v3)).T.astype(BF16)
         for side, tile in ((core, mine_ref), (1 - core, other_ref)):
@@ -82,13 +82,13 @@
     return pl.pallas_call(
         kernel,
         out_shape=(jax.ShapeDtypeStruct((512, 256), BF16),) * 4,
-        in_specs=[SCALARS] + [VMEM] * 6 + [ANY],
+        in_specs=[SCALARS] + [VMEM] * 6 + [ANY] * len(sent),
         out_specs=(VMEM,) * 4,
         scratch_shapes=[pltpu.VMEM((512, 1024), BF16)],
         compiler_params=params(),
         cost_estimate=cost(2 * 512 * 256 * 1024, 3 << 20),
         name="first_product",
-    )(place, *pieces, mine, other, sent)
+    )(place, *pieces, mine, other, *sent)
 
 
 def first_sum(place, own, zero, one):
@@ -138,20 +138,22 @@
 
 
 def turn(place, pieces, event):
+    blocks = pieces[0].shape[0]
+
     def kernel(place_ref, v0, v1, v2, v3, _, out):
         for step, ref in enumerate((v0, v1, v2, v3)):
             start = lax.rem(place_ref[2] + 4 - step, 4) * 256
             lanes = pl.ds(pl.multiple_of(start, 256), 256)
-            for k in range(3):
+            for k in range(blocks):
                 out[k, :, lanes] = ref[k].astype(F32).T
 
     return pl.pallas_call(
         kernel,
-        out_shape=jax.ShapeDtypeStruct((3, 128, 1024), F32),
+        out_shape=jax.ShapeDtypeStruct((blocks, 128, 1024), F32),
         in_specs=[SCALARS] + [VMEM] * 4 + [pl.BlockSpec(memory_space=pl.ANY)],
         out_specs=VMEM,
         compiler_params=params(),
-        cost_estimate=cost(3 * 128 * 1024, 3 << 20),
+        cost_estimate=cost(blocks * 128 * 1024, blocks << 20),
         name="turn",
     )(place, *pieces, event)
 
@@ -455,22 +457,25 @@
     home = lax.optimization_barrier(term(core))
     both = (home.astype(F32) + away.astype(F32)).astype(BF16)
     over_z = spread(both[3], "z")
-    cut = [
-        lax.dynamic_slice_in_dim(both[:3], lax.rem(x + by, 4) * 128, 128, axis=2)
-        for by in range(4)
-    ]
-    rest = deal(cut, "x")
-    own, *others = first_product(place, over_z, inverse_diag[3], other, rest[1])
+    def cut(part):
+        return [
+            lax.dynamic_slice_in_dim(part, lax.rem(x + by, 4) * 128, 128, axis=2)
+            for by in range(4)
+        ]
+
+    near = deal(cut(both[2:3]), "x")
+    own, *others = first_product(place, over_z, inverse_diag[3], other, near[1:])
     zero = [along_y(others[by - 1], 0, by) for by in (1, 2, 3)]
     token = lax.ppermute(sum(piece[:8] for piece in zero), "core", [(0, 1)])
-    others = gate((token, *rest[2:]), others)
+    others = gate((token,), others)
     one = [along_y(others[by - 1], 1, by) for by in (1, 2, 3)]
     over_x = deal(first_sum(place, own, zero, one), "x")
     quarter = sum(piece.astype(F32) for piece in over_x).astype(BF16)
-    base = turn(place, rest, quarter)
+    base2 = turn(place, near, quarter)[0]
     quarters = spread(quarter, "y")
-    residual, x3 = lower_step(base[2], quarters, early, 0, BF16, place)
+    residual, x3 = lower_step(base2, quarters, early, 0, BF16, place)
     over_z = spread(residual, "z")
+    base = turn(place, deal(gate((x3,), cut(both[:2])), "x"), over_z[2])
     pieces = spread(diag_step(over_z, early, 1), "y")
     base1, _ = lower_step(base[1], (x3,), early, 2, F32)
     residual, x2 = lower_step(base1, pieces, early, 3, BF16)

time: 224 us -> 200 us (0.89)
  waiting for transfers between devices: 83 us -> 57.3 us
    ppermute x30 -> x33, waiting for transfers between devices: 74.9 us -> 32.4 us  [shift(): return lax.ppermute(value, axis, [(i, (i + by) % 4) for i in range(4)])]
    ppermute x1, waiting for transfers between devices: 2.45 us -> 19 us  [local(): token = lax.ppermute(sum((piece[:8] for piece in zero)), 'core', [(0, 1)])]
    ppermute x30 -> x33, starting transfers between devices: 42.3 us -> 43.2 us  [shift(): return lax.ppermute(value, axis, [(i, (i + by) % 4) for i in range(4)])]
  transfers between devices with their start and end apart: 41 -> 44, of which waited for: 25 -> 21; matrix products, arithmetic and copies ran while one was open for 8% -> 9% of each run, Pallas kernels for 10% -> 11%
where the time goes in v10:
time: 200 us; the launch traced here: 199 us
  starting transfers between devices  57.4 us (29%)
  waiting for transfers between devices  57.3 us (29%)
  Pallas kernels  32.2 us (16%)
  blocking collectives  20.2 us (10%)
  between operations  13.8 us (7%)
  matrix products  12.9 us (6%)
  other arithmetic  3.67 us (2%)
    ppermute x33, starting transfers between devices, shift(): return lax.ppermute(value, axis, [(i, (i + by) % 4) for i in range(4)])  43.2 us
    ppermute x33, waiting for transfers between devices, shift(): return lax.ppermute(value, axis, [(i, (i + by) % 4) for i in range(4)])  32.4 us
    all_to_all x1, blocking collectives, local(): lax.all_to_all(packed, ('z', 'core', 'y', 'x'), split_axis=0, concat_axis...  20.2 us
    ppermute x1, waiting for transfers between devices, local(): token = lax.ppermute(sum((piece[:8] for piece in zero)), 'core', [(0, 1)])  19 us
    pallas_call x6, Pallas kernels, lower_step(): pl.pallas_call(kernel, out_shape=(jax.ShapeDtypeStruct((128, 1024), dtype...  14.2 us
    dot_general x2, matrix products, term(): lax.dot_general(border_tiles, bound, (((0,), (0,)), ((), ())), preferred_...  12.9 us
    ppermute x6, starting transfers between devices, along_y(): return lax.ppermute(value, ('core', 'y'), pairs)  11.3 us
    ppermute x6, waiting for transfers between devices, along_y(): return lax.ppermute(value, ('core', 'y'), pairs)  5.19 us
  transfers between devices with their start and end apart: 44, of which 21 were waited for; matrix products, arithmetic and copies ran while one was open for 9% of the time, Pallas kernels for 11%

profile of v10, /device:TPU:1, one launch (start us, length us, event | category | flops | bytes accessed | tf_op | source)
XLA Modules:
  0.0 198.9 jit_solution(13924341958561759823)
XLA Ops:
  6.5 3.3 %stage.1 = (bf16[2560,256]{1,0:T(8,128)(2,1)}, bf16[2064,256]{1,0:T(8,128)(2,1)}) custom-call(bf16[6,512,256]{2,1,0:T(8,128)(2,1)} %lower_ref.1, bf16[4,256,512]{2,1,0:T(8,128)(2,1)} %diag_ref.1, s32[1,128]{1,0:T(1,128)} %bitcast.56), custom_call_target="tpu_custom_call" | custom-call | bytes 6291456 | tf_op jit(solution)/shard_map/stage/pallas_call | solution.py:325
  10.6 5.9 %fusion.6 = bf16[4,256,512]{2,1,0:T(8,128)(2,1)S(1)} fusion(f32[4,256,1024]{2,1,0:T(8,128)} %param.6, s32[]{:T(128)S(6)} %select_n.30, bf16[2048,4,256]{2,1,0:T(4,128)(2,1)} %param.8, bf16[2048,1024]{1,0:T(8,128)(2,1)} %param.7, f32[]{:T(128)S(6)} %select_n.28), kind=kOutput, calls=%fused_computation.7 | convolution fusion | flops 2149056512 | bytes 9438720 | tf_op jit(solution)/shard_map/dot_general | solution.py:451
  19.1 7.0 %fusion.7 = bf16[4,256,512]{2,1,0:T(8,128)(2,1)} fusion(f32[4,256,1024]{2,1,0:T(8,128)} %param.6, s32[]{:T(128)S(6)} %select_n.29, bf16[2048,4,256]{2,1,0:T(4,128)(2,1)} %param.8, bf16[2048,1024]{1,0:T(8,128)(2,1)} %param.7, f32[]{:T(128)S(6)} %select_n.28), kind=kOutput, calls=%fused_computation.9 | convolution fusion | flops 2149056512 | bytes 9438720 | tf_op jit(solution)/shard_map/dot_general | solution.py:451
  29.6 3.5 %collective-permute-start.2 = (bf16[256,512]{1,0:T(8,128)(2,1)S(1)}, bf16[256,512]{1,0:T(8,128)(2,1)S(1)}, u32[]{:S(2)}, u32[]{:S(2)}) collective-permute-start(bf16[256,512]{1,0:T(8,128)(2,1)S(1)} %get-tuple-element.72.v0), channel_id=1, source_target_pairs={{0,64},{32,96},{64,0},{96,32},{1,65},{33,97},{65,1},{97,33},{2,66}... | collective-permute-start | bytes 786440 | tf_op jit(solution)/shard_map/ppermute | solution.py:18
  35.0 2.5 %collective-permute-start.6 = (bf16[1,256,128]{2,1,0:T(8,128)(2,1)S(1)}, bf16[1,256,128]{2,1,0:T(8,128)(2,1)S(1)}, u32[]{:S(2)}, u32[]{:S(2)}) collective-permute-start(bf16[1,256,128]{2,1,0:T(8,128)(2,1)S(1)} %get-tuple-element.79), channel_id=1, source_target_pairs={{0,2},{1,3},{2,0},{3,1},{4,6},{5,7},{6,4},{7,5},{8,10},{9,11},{10,... | collective-permute-start | bytes 196616 | tf_op jit(solution)/shard_map/ppermute | solution.py:18
  37.5 2.5 %collective-permute-done.5.refs_0_.v1 = bf16[1,256,128]{2,1,0:T(8,128)(2,1)S(1)} collective-permute-done((bf16[1,256,128]{2,1,0:T(8,128)(2,1)S(1)}, bf16[1,256,128]{2,1,0:T(8,128)(2,1)S(1)}, u32[]{:S(2)}, u32[]{:S(2)}) %collective-permute-start.5) | collective-permute-done | bytes 65568 | tf_op jit(solution)/shard_map/ppermute | solution.py:18
  41.4 2.3 %collective-permute-done.6.refs_1_.v2 = bf16[1,256,128]{2,1,0:T(8,128)(2,1)S(1)} collective-permute-done((bf16[1,256,128]{2,1,0:T(8,128)(2,1)S(1)}, bf16[1,256,128]{2,1,0:T(8,128)(2,1)S(1)}, u32[]{:S(2)}, u32[]{:S(2)}) %collective-permute-start.6) | collective-permute-done | bytes 65568 | tf_op jit(solution)/shard_map/ppermute | solution.py:18
  49.6 19.0 %collective-permute-done.11.refs_0_ = bf16[8,256]{1,0:T(8,128)(2,1)S(1)} collective-permute-done((bf16[8,256]{1,0:T(8,128)(2,1)S(1)}, bf16[8,256]{1,0:T(8,128)(2,1)S(1)}, u32[]{:S(2)}, u32[]{:S(2)}) %collective-permute-start.11) | collective-permute-done | bytes 4128 | tf_op jit(solution)/shard_map/ppermute | solution.py:469
  70.5 5.4 %collective-permute-start.13 = (bf16[512,256]{1,0:T(8,128)(2,1)S(1)}, bf16[512,256]{1,0:T(8,128)(2,1)S(1)}, u32[]{:S(2)}, u32[]{:S(2)}) collective-permute-start(bf16[512,256]{1,0:T(8,128)(2,1)S(1)} %get-tuple-element.43), channel_id=1, source_target_pairs={{16,24},{20,28},{24,16},{28,20},{17,25},{21,29},{25,17},{29,21},{1... | collective-permute-start | bytes 786440 | tf_op jit(solution)/shard_map/ppermute | solution.py:27
  77.9 2.7 %collective-permute-done.13.refs_4_ = bf16[512,256]{1,0:T(8,128)(2,1)S(1)} collective-permute-done((bf16[512,256]{1,0:T(8,128)(2,1)S(1)}, bf16[512,256]{1,0:T(8,128)(2,1)S(1)}, u32[]{:S(2)}, u32[]{:S(2)}) %collective-permute-start.13) | collective-permute-done | bytes 262176 | tf_op jit(solution)/shard_map/ppermute | solution.py:27
  80.6 2.5 %collective-permute-done.14.refs_5_ = bf16[512,256]{1,0:T(8,128)(2,1)S(1)} collective-permute-done((bf16[512,256]{1,0:T(8,128)(2,1)S(1)}, bf16[512,256]{1,0:T(8,128)(2,1)S(1)}, u32[]{:S(2)}, u32[]{:S(2)}) %collective-permute-start.14) | collective-permute-done | bytes 262176 | tf_op jit(solution)/shard_map/ppermute | solution.py:27
  84.1 4.1 %collective-permute-start.16 = (bf16[128,256]{1,0:T(8,128)(2,1)S(1)}, bf16[128,256]{1,0:T(8,128)(2,1)S(1)}, u32[]{:S(2)}, u32[]{:S(2)}) collective-permute-start(bf16[128,256]{1,0:T(8,128)(2,1)S(1)} %get-tuple-element.47), channel_id=1, source_target_pairs={{0,2},{1,3},{2,0},{3,1},{4,6},{5,7},{6,4},{7,5},{8,10},{9,11},{10,... | collective-permute-start | bytes 196616 | tf_op jit(solution)/shard_map/ppermute | solution.py:18
  90.5 2.3 %collective-permute-done.17 = bf16[128,256]{1,0:T(8,128)(2,1)S(1)} collective-permute-done((bf16[128,256]{1,0:T(8,128)(2,1)S(1)}, bf16[128,256]{1,0:T(8,128)(2,1)S(1)}, u32[]{:S(2)}, u32[]{:S(2)}) %collective-permute-start.17) | collective-permute-done | bytes 65568 | tf_op jit(solution)/shard_map/ppermute | solution.py:18
  96.3 2.1 %collective-permute-done.18.refs_2_ = bf16[128,256]{1,0:T(8,128)(2,1)S(1)} collective-permute-done((bf16[128,256]{1,0:T(8,128)(2,1)S(1)}, bf16[128,256]{1,0:T(8,128)(2,1)S(1)}, u32[]{:S(2)}, u32[]{:S(2)}) %collective-permute-start.18) | collective-permute-done | bytes 65568 | tf_op jit(solution)/shard_map/ppermute | solution.py:18
  99.0 2.6 %lower_step.6 = (bf16[128,1024]{1,0:T(8,128)(2,1)S(1)}, bf16[128,1024]{1,0:T(8,128)(2,1)S(1)}) custom-call(s32[4]{0:T(128)S(1)} %pad_add_fusion.place_ref.refs_0_, bf16[128,256]{1,0:T(8,128)(2,1)S(1)} %add_convert_fusion.1._.refs_1_, bf16[128,256]{1,0:T(8,128)(2,1)S(1)} %collective-permute-done.18.refs_2_, ...), custom_call_target="tpu_custom_call" | custom-call | flops 268435456 | bytes 4194304 | tf_op jit(solution)/shard_map/lower_step/pallas_call | solution.py:193
  102.8 2.3 %collective-permute-start.23 = (bf16[128,1024]{1,0:T(8,128)(2,1)S(1)}, bf16[128,1024]{1,0:T(8,128)(2,1)S(1)}, u32[]{:S(2)}, u32[]{:S(2)}) collective-permute-start(bf16[128,1024]{1,0:T(8,128)(2,1)S(1)} %get-tuple-element.50.v0), channel_id=1, source_target_pairs={{0,96},{32,0},{64,32},{96,64},{1,97},{33,1},{65,33},{97,65},{2,98}... | collective-permute-start | bytes 786440 | tf_op jit(solution)/shard_map/ppermute | solution.py:18
  105.3 2.2 %collective-permute-start.28 = (bf16[2,256,128]{2,1,0:T(8,128)(2,1)S(1)}, bf16[2,256,128]{2,1,0:T(8,128)(2,1)S(1)}, u32[]{:S(2)}, u32[]{:S(2)}) collective-permute-start(bf16[2,256,128]{2,1,0:T(8,128)(2,1)S(1)} %get-tuple-element.54), channel_id=1, source_target_pairs={{0,2},{1,3},{2,0},{3,1},{4,6},{5,7},{6,4},{7,5},{8,10},{9,11},{10,... | collective-permute-start | bytes 393224 | tf_op jit(solution)/shard_map/ppermute | solution.py:18
  111.6 2.0 diag_step.2.refs_0_
  114.3 2.5 %collective-permute-start.25 = (bf16[128,1024]{1,0:T(8,128)(2,1)S(1)}, bf16[128,1024]{1,0:T(8,128)(2,1)S(1)}, u32[]{:S(2)}, u32[]{:S(2)}) collective-permute-start(bf16[128,1024]{1,0:T(8,128)(2,1)S(1)} %diag_step.2.refs_0_), channel_id=1, source_target_pairs={{0,8},{4,12},{8,0},{12,4},{1,9},{5,13},{9,1},{13,5},{2,10},{6,14},... | collective-permute-start | bytes 786440 | tf_op jit(solution)/shard_map/ppermute | solution.py:18
  119.1 2.5 %lower_step.7 = (f32[128,1024]{1,0:T(8,128)S(1)}, bf16[128,1024]{1,0:T(8,128)(2,1)}) custom-call(bf16[128,1024]{1,0:T(8,128)(2,1)S(1)} %get-tuple-element.51.refs_0_.x3, f32[128,1024]{1,0:T(8,128)S(1)} %get-tuple-element.70.refs_1_, bf16[2,4,2560,256]{3,2,1,0:T(8,128)(2,1)} %bitcast.46), custom_call_target="tpu_custom_call" | custom-call | flops 268435456 | bytes 4194304 | tf_op jit(solution)/shard_map/lower_step/pallas_call | solution.py:193
  123.9 2.0 %lower_step.8 = (bf16[128,1024]{1,0:T(8,128)(2,1)S(1)}, bf16[128,1024]{1,0:T(8,128)(2,1)S(1)}) custom-call(bf16[128,1024]{1,0:T(8,128)(2,1)S(1)} %diag_step.2.refs_0_, bf16[128,1024]{1,0:T(8,128)(2,1)S(1)} %collective-permute-done.24.refs_1_, bf16[128,1024]{1,0:T(8,128)(2,1)S(1)} %collective-permute-done.25.refs_2_, ...), custom_call_target="tpu_custom_call" | custom-call | flops 268435456 | bytes 4194304 | tf_op jit(solution)/shard_map/lower_step/pallas_call | solution.py:193
  129.6 5.9 %collective-permute-done.30.v1 = bf16[128,1024]{1,0:T(8,128)(2,1)S(1)} collective-permute-done((bf16[128,1024]{1,0:T(8,128)(2,1)S(1)}, bf16[128,1024]{1,0:T(8,128)(2,1)S(1)}, u32[]{:S(2)}, u32[]{:S(2)}) %collective-permute-start.30) | collective-permute-done | bytes 262176 | tf_op jit(solution)/shard_map/ppermute | solution.py:18
  138.5 3.1 %collective-permute-start.34 = (bf16[128,1024]{1,0:T(8,128)(2,1)S(1)}, bf16[128,1024]{1,0:T(8,128)(2,1)S(1)}, u32[]{:S(2)}, u32[]{:S(2)}) collective-permute-start(bf16[128,1024]{1,0:T(8,128)(2,1)S(1)} %diag_step.3.refs_0_), channel_id=1, source_target_pairs={{0,8},{4,12},{8,0},{12,4},{1,9},{5,13},{9,1},{13,5},{2,10},{6,14},... | collective-permute-start | bytes 786440 | tf_op jit(solution)/shard_map/ppermute | solution.py:18
  141.7 2.5 %lower_step.9 = (f32[128,1024]{1,0:T(8,128)S(1)}, bf16[128,1024]{1,0:T(8,128)(2,1)}) custom-call(bf16[128,1024]{1,0:T(8,128)(2,1)S(1)} %get-tuple-element.51.refs_0_.x3, f32[128,1024]{1,0:T(8,128)S(1)} %get-tuple-element.69.refs_1_, bf16[2,4,2064,256]{3,2,1,0:T(8,128)(2,1)} %bitcast.49), custom_call_target="tpu_custom_call" | custom-call | flops 268435456 | bytes 4194304 | tf_op jit(solution)/shard_map/lower_step/pallas_call | solution.py:193
  144.2 2.5 %lower_step.10 = (f32[128,1024]{1,0:T(8,128)S(1)}, bf16[128,1024]{1,0:T(8,128)(2,1)}) custom-call(bf16[128,1024]{1,0:T(8,128)(2,1)S(1)} %get-tuple-element.58.refs_0_.x2, f32[128,1024]{1,0:T(8,128)S(1)} %get-tuple-element.59.refs_1_, bf16[2,4,2064,256]{3,2,1,0:T(8,128)(2,1)} %bitcast.50), custom_call_target="tpu_custom_call" | custom-call | flops 268435456 | bytes 4194304 | tf_op jit(solution)/shard_map/lower_step/pallas_call | solution.py:193
  148.2 2.0 %lower_step.11 = (bf16[128,1024]{1,0:T(8,128)(2,1)S(1)}, bf16[128,1024]{1,0:T(8,128)(2,1)S(1)}) custom-call(bf16[128,1024]{1,0:T(8,128)(2,1)S(1)} %diag_step.3.refs_0_, bf16[128,1024]{1,0:T(8,128)(2,1)S(1)} %collective-permute-done.33.refs_1_, bf16[128,1024]{1,0:T(8,128)(2,1)S(1)} %collective-permute-done.34.refs_2_, ...), custom_call_target="tpu_custom_call" | custom-call | flops 268435456 | bytes 4194304 | tf_op jit(solution)/shard_map/lower_step/pallas_call | solution.py:193
  151.3 2.6 %collective-permute-start.37 = (bf16[128,1024]{1,0:T(8,128)(2,1)S(1)}, bf16[128,1024]{1,0:T(8,128)(2,1)S(1)}, u32[]{:S(2)}, u32[]{:S(2)}) collective-permute-start(bf16[128,1024]{1,0:T(8,128)(2,1)S(1)} %get-tuple-element.63.v0), channel_id=1, source_target_pairs={{0,64},{32,96},{64,0},{96,32},{1,65},{33,97},{65,1},{97,33},{2,66}... | collective-permute-start | bytes 786440 | tf_op jit(solution)/shard_map/ppermute | solution.py:18
  157.8 2.8 %collective-permute-done.37.v2 = bf16[128,1024]{1,0:T(8,128)(2,1)S(1)} collective-permute-done((bf16[128,1024]{1,0:T(8,128)(2,1)S(1)}, bf16[128,1024]{1,0:T(8,128)(2,1)S(1)}, u32[]{:S(2)}, u32[]{:S(2)}) %collective-permute-start.37) | collective-permute-done | bytes 262176 | tf_op jit(solution)/shard_map/ppermute | solution.py:18
  160.6 2.5 %last_step.1 = (bf16[128,256]{1,0:T(8,128)(2,1)S(1)}, bf16[128,256]{1,0:T(8,128)(2,1)S(1)}, bf16[128,256]{1,0:T(8,128)(2,1)S(1)}, bf16[128,256]{1,0:T(8,128)(2,1)S(1)}) custom-call(s32[4]{0:T(128)S(1)} %pad_add_fusion.place_ref.refs_0_, bf16[128,1024]{1,0:T(8,128)(2,1)S(1)} %get-tuple-element.63.v0, bf16[128,1024]{1,0:T(8,128)(2,1)S(1)} %collective-permute-done.36.v1, ...), custom_call_target="tpu_custom_call" | custom-call | flops 268435456 | bytes 4194304 | tf_op jit(solution)/shard_map/last_step/pallas_call | solution.py:272
  164.0 2.7 %collective-permute-start.40 = (bf16[128,256]{1,0:T(8,128)(2,1)S(1)}, bf16[128,256]{1,0:T(8,128)(2,1)S(1)}, u32[]{:S(2)}, u32[]{:S(2)}) collective-permute-start(bf16[128,256]{1,0:T(8,128)(2,1)S(1)} %get-tuple-element.66), channel_id=1, source_target_pairs={{0,8},{4,12},{8,0},{12,4},{1,9},{5,13},{9,1},{13,5},{2,10},{6,14},... | collective-permute-start | bytes 196616 | tf_op jit(solution)/shard_map/ppermute | solution.py:18
  166.9 3.0 %pack_known.1 = (bf16[2048,128]{1,0:T(8,128)(2,1)S(1)}, bf16[2048,256]{1,0:T(8,128)(2,1)S(1)}) custom-call(s32[4]{0:T(128)S(1)} %pad_add_fusion.place_ref.refs_0_, s32[4,1,256]{2,1,0:T(1,128)S(1)} %reshape.61.target_ref, bf16[128,1024]{1,0:T(8,128)(2,1)S(1)} %get-tuple-element.61.x1, bf16[128,1024]{1,0:T(8,128)(2,1)S(1)} %get-tuple-element.58.refs_0_.x2, ...), custom_call_target="tpu_custom_call" | custom-call | flops 402653184 | bytes 2097152 | tf_op jit(solution)/shard_map/pack_known/pallas_call | solution.py:361
  170.4 20.2 %all_to_all.5 = bf16[128,16,128]{2,1,0:T(8,128)(2,1)S(1)} all-to-all(bf16[128,16,128]{2,1,0:T(8,128)(2,1)S(1)} %bitcast.43), channel_id=1, replica_groups=mesh['z'=4,'core'=2,'y'=4,'x'=4] {'z','core','y','x'}, dimensions={0} | all-to-all | bytes 1048576 | tf_op jit(solution)/shard_map/all_to_all | solution.py:491
  (100 shorter events, 54.1 us)
Async XLA Ops:
  6.5 92.4 %all-gather.7.cloned.1.call-start = ((), (), s32[]{:S(2)}) async-start(), calls=%async_computation.2 | async-start | bytes 11796480 | tf_op jit(solution)/shard_map/all_gather | solution.py:427
  9.9 131.8 %all-gather.5.cloned.1.call-start = ((), (), s32[]{:S(2)}) async-start(), calls=%async_computation.1 | async-start | bytes 9510912 | tf_op jit(solution)/shard_map/all_gather | solution.py:427
  16.5 9.6 %collective-permute-start = (bf16[4,256,512]{2,1,0:T(8,128)(2,1)S(1)}, bf16[4,256,512]{2,1,0:T(8,128)(2,1)S(1)}, u32[]{:S(2)}, u32[]{:S(2)}) collective-permute-start(bf16[4,256,512]{2,1,0:T(8,128)(2,1)S(1)} %fusion.6), channel_id=1, source_target_pairs={{0,16},{16,0},{1,17},{17,1},{2,18},{18,2},{3,19},{19,3},{4,20},{20... | collective-permute-start | bytes 3145736 | tf_op jit(solution)/shard_map/ppermute | solution.py:22
  19.0 16.1 %collective-permute-start.4 = (bf16[256,512]{1,0:T(8,128)(2,1)S(1)}, bf16[256,512]{1,0:T(8,128)(2,1)S(1)}, u32[]{:S(2)}, u32[]{:S(2)}) collective-permute-start(bf16[256,512]{1,0:T(8,128)(2,1)S(1)} %slice_bitcast_fusion.3.mine_ref), channel_id=1, source_target_pairs={{0,16},{16,0},{1,17},{17,1},{2,18},{18,2},{3,19},{19,3},{4,20},{20... | collective-permute-start | bytes 786440 | tf_op jit(solution)/shard_map/ppermute | solution.py:22
  27.8 17.1 %collective-permute-start.1 = (bf16[256,512]{1,0:T(8,128)(2,1)S(1)}, bf16[256,512]{1,0:T(8,128)(2,1)S(1)}, u32[]{:S(2)}, u32[]{:S(2)}) collective-permute-start(bf16[256,512]{1,0:T(8,128)(2,1)S(1)} %get-tuple-element.72.v0), channel_id=1, source_target_pairs={{0,32},{32,64},{64,96},{96,0},{1,33},{33,65},{65,97},{97,1},{2,34}... | collective-permute-start | bytes 786440 | tf_op jit(solution)/shard_map/ppermute | solution.py:18
  29.6 15.3 %collective-permute-start.2 = (bf16[256,512]{1,0:T(8,128)(2,1)S(1)}, bf16[256,512]{1,0:T(8,128)(2,1)S(1)}, u32[]{:S(2)}, u32[]{:S(2)}) collective-permute-start(bf16[256,512]{1,0:T(8,128)(2,1)S(1)} %get-tuple-element.72.v0), channel_id=1, source_target_pairs={{0,64},{32,96},{64,0},{96,32},{1,65},{33,97},{65,1},{97,33},{2,66}... | collective-permute-start | bytes 786440 | tf_op jit(solution)/shard_map/ppermute | solution.py:18
  33.1 11.8 %collective-permute-start.3 = (bf16[256,512]{1,0:T(8,128)(2,1)S(1)}, bf16[256,512]{1,0:T(8,128)(2,1)S(1)}, u32[]{:S(2)}, u32[]{:S(2)}) collective-permute-start(bf16[256,512]{1,0:T(8,128)(2,1)S(1)} %get-tuple-element.72.v0), channel_id=1, source_target_pairs={{0,96},{32,0},{64,32},{96,64},{1,97},{33,1},{65,33},{97,65},{2,98}... | collective-permute-start | bytes 786440 | tf_op jit(solution)/shard_map/ppermute | solution.py:18
  35.0 8.7 %collective-permute-start.6 = (bf16[1,256,128]{2,1,0:T(8,128)(2,1)S(1)}, bf16[1,256,128]{2,1,0:T(8,128)(2,1)S(1)}, u32[]{:S(2)}, u32[]{:S(2)}) collective-permute-start(bf16[1,256,128]{2,1,0:T(8,128)(2,1)S(1)} %get-tuple-element.79), channel_id=1, source_target_pairs={{0,2},{1,3},{2,0},{3,1},{4,6},{5,7},{6,4},{7,5},{8,10},{9,11},{10,... | collective-permute-start | bytes 196616 | tf_op jit(solution)/shard_map/ppermute | solution.py:18
  48.3 20.3 %collective-permute-start.11 = (bf16[8,256]{1,0:T(8,128)(2,1)S(1)}, bf16[8,256]{1,0:T(8,128)(2,1)S(1)}, u32[]{:S(2)}, u32[]{:S(2)}) collective-permute-start(bf16[8,256]{1,0:T(8,128)(2,1)S(1)} %slice_add_fusion), channel_id=1, source_target_pairs={{0,16},{1,17},{2,18},{3,19},{4,20},{5,21},{6,22},{7,23},{8,24},{9,... | collective-permute-start | bytes 12296 | tf_op jit(solution)/shard_map/ppermute | solution.py:469
  68.6 9.3 %collective-permute-start.12 = (bf16[512,256]{1,0:T(8,128)(2,1)S(1)}, bf16[512,256]{1,0:T(8,128)(2,1)S(1)}, u32[]{:S(2)}, u32[]{:S(2)}) collective-permute-start(bf16[512,256]{1,0:T(8,128)(2,1)S(1)} %get-tuple-element.42), channel_id=1, source_target_pairs={{16,20},{20,24},{24,28},{28,16},{17,21},{21,25},{25,29},{29,17},{1... | collective-permute-start | bytes 786440 | tf_op jit(solution)/shard_map/ppermute | solution.py:27
  70.5 10.1 %collective-permute-start.13 = (bf16[512,256]{1,0:T(8,128)(2,1)S(1)}, bf16[512,256]{1,0:T(8,128)(2,1)S(1)}, u32[]{:S(2)}, u32[]{:S(2)}) collective-permute-start(bf16[512,256]{1,0:T(8,128)(2,1)S(1)} %get-tuple-element.43), channel_id=1, source_target_pairs={{16,24},{20,28},{24,16},{28,20},{17,25},{21,29},{25,17},{29,21},{1... | collective-permute-start | bytes 786440 | tf_op jit(solution)/shard_map/ppermute | solution.py:27
  76.0 7.1 %collective-permute-start.14 = (bf16[512,256]{1,0:T(8,128)(2,1)S(1)}, bf16[512,256]{1,0:T(8,128)(2,1)S(1)}, u32[]{:S(2)}, u32[]{:S(2)}) collective-permute-start(bf16[512,256]{1,0:T(8,128)(2,1)S(1)} %get-tuple-element.44), channel_id=1, source_target_pairs={{16,28},{20,16},{24,20},{28,24},{17,29},{21,17},{25,21},{29,25},{1... | collective-permute-start | bytes 786440 | tf_op jit(solution)/shard_map/ppermute | solution.py:27
  84.1 6.4 %collective-permute-start.16 = (bf16[128,256]{1,0:T(8,128)(2,1)S(1)}, bf16[128,256]{1,0:T(8,128)(2,1)S(1)}, u32[]{:S(2)}, u32[]{:S(2)}) collective-permute-start(bf16[128,256]{1,0:T(8,128)(2,1)S(1)} %get-tuple-element.47), channel_id=1, source_target_pairs={{0,2},{1,3},{2,0},{3,1},{4,6},{5,7},{6,4},{7,5},{8,10},{9,11},{10,... | collective-permute-start | bytes 196616 | tf_op jit(solution)/shard_map/ppermute | solution.py:18
  101.6 6.9 %collective-permute-start.22 = (bf16[128,1024]{1,0:T(8,128)(2,1)S(1)}, bf16[128,1024]{1,0:T(8,128)(2,1)S(1)}, u32[]{:S(2)}, u32[]{:S(2)}) collective-permute-start(bf16[128,1024]{1,0:T(8,128)(2,1)S(1)} %get-tuple-element.50.v0), channel_id=1, source_target_pairs={{0,64},{32,96},{64,0},{96,32},{1,65},{33,97},{65,1},{97,33},{2,66}... | collective-permute-start | bytes 786440 | tf_op jit(solution)/shard_map/ppermute | solution.py:18
  101.6 9.9 %collective-permute-start.21 = (bf16[128,1024]{1,0:T(8,128)(2,1)S(1)}, bf16[128,1024]{1,0:T(8,128)(2,1)S(1)}, u32[]{:S(2)}, u32[]{:S(2)}) collective-permute-start(bf16[128,1024]{1,0:T(8,128)(2,1)S(1)} %get-tuple-element.50.v0), channel_id=1, source_target_pairs={{0,32},{32,64},{64,96},{96,0},{1,33},{33,65},{65,97},{97,1},{2,34}... | collective-permute-start | bytes 786440 | tf_op jit(solution)/shard_map/ppermute | solution.py:18
  102.8 8.8 %collective-permute-start.23 = (bf16[128,1024]{1,0:T(8,128)(2,1)S(1)}, bf16[128,1024]{1,0:T(8,128)(2,1)S(1)}, u32[]{:S(2)}, u32[]{:S(2)}) collective-permute-start(bf16[128,1024]{1,0:T(8,128)(2,1)S(1)} %get-tuple-element.50.v0), channel_id=1, source_target_pairs={{0,96},{32,0},{64,32},{96,64},{1,97},{33,1},{65,33},{97,65},{2,98}... | collective-permute-start | bytes 786440 | tf_op jit(solution)/shard_map/ppermute | solution.py:18
  105.2 11.6 %collective-permute-start.27 = (bf16[2,256,128]{2,1,0:T(8,128)(2,1)S(1)}, bf16[2,256,128]{2,1,0:T(8,128)(2,1)S(1)}, u32[]{:S(2)}, u32[]{:S(2)}) collective-permute-start(bf16[2,256,128]{2,1,0:T(8,128)(2,1)S(1)} %get-tuple-element.53), channel_id=1, source_target_pairs={{0,1},{1,2},{2,3},{3,0},{4,5},{5,6},{6,7},{7,4},{8,9},{9,10},{10,1... | collective-permute-start | bytes 393224 | tf_op jit(solution)/shard_map/ppermute | solution.py:18
  105.3 11.6 %collective-permute-start.28 = (bf16[2,256,128]{2,1,0:T(8,128)(2,1)S(1)}, bf16[2,256,128]{2,1,0:T(8,128)(2,1)S(1)}, u32[]{:S(2)}, u32[]{:S(2)}) collective-permute-start(bf16[2,256,128]{2,1,0:T(8,128)(2,1)S(1)} %get-tuple-element.54), channel_id=1, source_target_pairs={{0,2},{1,3},{2,0},{3,1},{4,6},{5,7},{6,4},{7,5},{8,10},{9,11},{10,... | collective-permute-start | bytes 393224 | tf_op jit(solution)/shard_map/ppermute | solution.py:18
  108.5 9.8 %collective-permute-start.29 = (bf16[2,256,128]{2,1,0:T(8,128)(2,1)S(1)}, bf16[2,256,128]{2,1,0:T(8,128)(2,1)S(1)}, u32[]{:S(2)}, u32[]{:S(2)}) collective-permute-start(bf16[2,256,128]{2,1,0:T(8,128)(2,1)S(1)} %get-tuple-element.55), channel_id=1, source_target_pairs={{0,3},{1,0},{2,1},{3,2},{4,7},{5,4},{6,5},{7,6},{8,11},{9,8},{10,9... | collective-permute-start | bytes 393224 | tf_op jit(solution)/shard_map/ppermute | solution.py:18
  113.6 8.1 %collective-permute-start.24 = (bf16[128,1024]{1,0:T(8,128)(2,1)S(1)}, bf16[128,1024]{1,0:T(8,128)(2,1)S(1)}, u32[]{:S(2)}, u32[]{:S(2)}) collective-permute-start(bf16[128,1024]{1,0:T(8,128)(2,1)S(1)} %diag_step.2.refs_0_), channel_id=1, source_target_pairs={{0,4},{4,8},{8,12},{12,0},{1,5},{5,9},{9,13},{13,1},{2,6},{6,10},{... | collective-permute-start | bytes 786440 | tf_op jit(solution)/shard_map/ppermute | solution.py:18
  114.3 9.2 %collective-permute-start.25 = (bf16[128,1024]{1,0:T(8,128)(2,1)S(1)}, bf16[128,1024]{1,0:T(8,128)(2,1)S(1)}, u32[]{:S(2)}, u32[]{:S(2)}) collective-permute-start(bf16[128,1024]{1,0:T(8,128)(2,1)S(1)} %diag_step.2.refs_0_), channel_id=1, source_target_pairs={{0,8},{4,12},{8,0},{12,4},{1,9},{5,13},{9,1},{13,5},{2,10},{6,14},... | collective-permute-start | bytes 786440 | tf_op jit(solution)/shard_map/ppermute | solution.py:18
  116.8 7.1 %collective-permute-start.26 = (bf16[128,1024]{1,0:T(8,128)(2,1)S(1)}, bf16[128,1024]{1,0:T(8,128)(2,1)S(1)}, u32[]{:S(2)}, u32[]{:S(2)}) collective-permute-start(bf16[128,1024]{1,0:T(8,128)(2,1)S(1)} %diag_step.2.refs_0_), channel_id=1, source_target_pairs={{0,12},{4,0},{8,4},{12,8},{1,13},{5,1},{9,5},{13,9},{2,14},{6,2},{... | collective-permute-start | bytes 786440 | tf_op jit(solution)/shard_map/ppermute | solution.py:18
  125.9 9.6 %collective-permute-start.30 = (bf16[128,1024]{1,0:T(8,128)(2,1)S(1)}, bf16[128,1024]{1,0:T(8,128)(2,1)S(1)}, u32[]{:S(2)}, u32[]{:S(2)}) collective-permute-start(bf16[128,1024]{1,0:T(8,128)(2,1)S(1)} %get-tuple-element.57.v0), channel_id=1, source_target_pairs={{0,32},{32,64},{64,96},{96,0},{1,33},{33,65},{65,97},{97,1},{2,34}... | collective-permute-start | bytes 786440 | tf_op jit(solution)/shard_map/ppermute | solution.py:18
  126.9 8.6 %collective-permute-start.31 = (bf16[128,1024]{1,0:T(8,128)(2,1)S(1)}, bf16[128,1024]{1,0:T(8,128)(2,1)S(1)}, u32[]{:S(2)}, u32[]{:S(2)}) collective-permute-start(bf16[128,1024]{1,0:T(8,128)(2,1)S(1)} %get-tuple-element.57.v0), channel_id=1, source_target_pairs={{0,64},{32,96},{64,0},{96,32},{1,65},{33,97},{65,1},{97,33},{2,66}... | collective-permute-start | bytes 786440 | tf_op jit(solution)/shard_map/ppermute | solution.py:18
  127.7 8.5 %collective-permute-start.32 = (bf16[128,1024]{1,0:T(8,128)(2,1)S(1)}, bf16[128,1024]{1,0:T(8,128)(2,1)S(1)}, u32[]{:S(2)}, u32[]{:S(2)}) collective-permute-start(bf16[128,1024]{1,0:T(8,128)(2,1)S(1)} %get-tuple-element.57.v0), channel_id=1, source_target_pairs={{0,96},{32,0},{64,32},{96,64},{1,97},{33,1},{65,33},{97,65},{2,98}... | collective-permute-start | bytes 786440 | tf_op jit(solution)/shard_map/ppermute | solution.py:18
  138.0 8.7 %collective-permute-start.33 = (bf16[128,1024]{1,0:T(8,128)(2,1)S(1)}, bf16[128,1024]{1,0:T(8,128)(2,1)S(1)}, u32[]{:S(2)}, u32[]{:S(2)}) collective-permute-start(bf16[128,1024]{1,0:T(8,128)(2,1)S(1)} %diag_step.3.refs_0_), channel_id=1, source_target_pairs={{0,4},{4,8},{8,12},{12,0},{1,5},{5,9},{9,13},{13,1},{2,6},{6,10},{... | collective-permute-start | bytes 786440 | tf_op jit(solution)/shard_map/ppermute | solution.py:18
  138.5 9.7 %collective-permute-start.34 = (bf16[128,1024]{1,0:T(8,128)(2,1)S(1)}, bf16[128,1024]{1,0:T(8,128)(2,1)S(1)}, u32[]{:S(2)}, u32[]{:S(2)}) collective-permute-start(bf16[128,1024]{1,0:T(8,128)(2,1)S(1)} %diag_step.3.refs_0_), channel_id=1, source_target_pairs={{0,8},{4,12},{8,0},{12,4},{1,9},{5,13},{9,1},{13,5},{2,10},{6,14},... | collective-permute-start | bytes 786440 | tf_op jit(solution)/shard_map/ppermute | solution.py:18
  141.6 6.6 %collective-permute-start.35 = (bf16[128,1024]{1,0:T(8,128)(2,1)S(1)}, bf16[128,1024]{1,0:T(8,128)(2,1)S(1)}, u32[]{:S(2)}, u32[]{:S(2)}) collective-permute-start(bf16[128,1024]{1,0:T(8,128)(2,1)S(1)} %diag_step.3.refs_0_), channel_id=1, source_target_pairs={{0,12},{4,0},{8,4},{12,8},{1,13},{5,1},{9,5},{13,9},{2,14},{6,2},{... | collective-permute-start | bytes 786440 | tf_op jit(solution)/shard_map/ppermute | solution.py:18
  150.3 7.5 %collective-permute-start.36 = (bf16[128,1024]{1,0:T(8,128)(2,1)S(1)}, bf16[128,1024]{1,0:T(8,128)(2,1)S(1)}, u32[]{:S(2)}, u32[]{:S(2)}) collective-permute-start(bf16[128,1024]{1,0:T(8,128)(2,1)S(1)} %get-tuple-element.63.v0), channel_id=1, source_target_pairs={{0,32},{32,64},{64,96},{96,0},{1,33},{33,65},{65,97},{97,1},{2,34}... | collective-permute-start | bytes 786440 | tf_op jit(solution)/shard_map/ppermute | solution.py:18
  151.3 9.3 %collective-permute-start.37 = (bf16[128,1024]{1,0:T(8,128)(2,1)S(1)}, bf16[128,1024]{1,0:T(8,128)(2,1)S(1)}, u32[]{:S(2)}, u32[]{:S(2)}) collective-permute-start(bf16[128,1024]{1,0:T(8,128)(2,1)S(1)} %get-tuple-element.63.v0), channel_id=1, source_target_pairs={{0,64},{32,96},{64,0},{96,32},{1,65},{33,97},{65,1},{97,33},{2,66}... | collective-permute-start | bytes 786440 | tf_op jit(solution)/shard_map/ppermute | solution.py:18
  153.9 6.7 %collective-permute-start.38 = (bf16[128,1024]{1,0:T(8,128)(2,1)S(1)}, bf16[128,1024]{1,0:T(8,128)(2,1)S(1)}, u32[]{:S(2)}, u32[]{:S(2)}) collective-permute-start(bf16[128,1024]{1,0:T(8,128)(2,1)S(1)} %get-tuple-element.63.v0), channel_id=1, source_target_pairs={{0,96},{32,0},{64,32},{96,64},{1,97},{33,1},{65,33},{97,65},{2,98}... | collective-permute-start | bytes 786440 | tf_op jit(solution)/shard_map/ppermute | solution.py:18
  163.1 6.8 %collective-permute-start.39 = (bf16[128,256]{1,0:T(8,128)(2,1)S(1)}, bf16[128,256]{1,0:T(8,128)(2,1)S(1)}, u32[]{:S(2)}, u32[]{:S(2)}) collective-permute-start(bf16[128,256]{1,0:T(8,128)(2,1)S(1)} %get-tuple-element.65), channel_id=1, source_target_pairs={{0,4},{4,8},{8,12},{12,0},{1,5},{5,9},{9,13},{13,1},{2,6},{6,10},{... | collective-permute-start | bytes 196616 | tf_op jit(solution)/shard_map/ppermute | solution.py:18
  (12 other events, 50.0 us)
Sparse Core Ops, SparseCore 0:
  10.0 64.9 all-gather.6
  76.7 55.9 all-gather.4

commit v11 on v10

--- a/solution.py
+++ b/solution.py
@@ -22,9 +22,9 @@
     return lax.ppermute(value, "core", [(0, 1), (1, 0)])
 
 
-def along_y(value, core, by):
-    pairs = [(core * 4 + i, core * 4 + (i + by) % 4) for i in range(4)]
-    return lax.ppermute(value, ("core", "y"), pairs)
+def along_z(value, core, by):
+    pairs = [(i * 2 + core, (i + by) % 4 * 2 + core) for i in range(4)]
+    return lax.ppermute(value, ("z", "core"), pairs)
 
 
 def spread(value, axis):
@@ -66,13 +66,22 @@
 HBM = pl.BlockSpec(memory_space=pltpu.HBM)
 
 
-def first_product(place, pieces, mine, other, sent):
-    def kernel(place_ref, v0, v1, v2, v3, mine_ref, other_ref, *refs):
-        outs, full = refs[len(sent) : len(sent) + 4], refs[len(sent) + 4]
+def first_product(place, own, zero, one, mine, other):
+    def kernel(place_ref, own_ref, *refs):
+        mine_ref, other_ref = refs[6:8]
+        outs, full, turned = refs[8:12], refs[12], refs[13]
         core, y = place_ref[0], place_ref[1]
-        turned = add_up((v0, v1, v2, v3)).T.astype(BF16)
+
+        @pl.when(core == 0)
+        def _():
+            turned[...] = add_up((own_ref, *refs[:3])).T.astype(BF16)
+
+        @pl.when(core == 1)
+        def _():
+            turned[...] = add_up((own_ref, *refs[3:6])).T.astype(BF16)
+
         for side, tile in ((core, mine_ref), (1 - core, other_ref)):
-            product = jnp.dot(turned, tile[...], preferred_element_type=F32)
+            product = jnp.dot(turned[...], tile[...], preferred_element_type=F32)
             full[:, pl.ds(pl.multiple_of(side * 512, 512), 512)] = product.astype(BF16)
         for by, out in enumerate(outs):
             start = lax.rem(y + by, 4) * 128
@@ -82,42 +91,31 @@
     return pl.pallas_call(
         kernel,
         out_shape=(jax.ShapeDtypeStruct((512, 256), BF16),) * 4,
-        in_specs=[SCALARS] + [VMEM] * 6 + [ANY] * len(sent),
+        in_specs=[SCALARS] + [VMEM] * 9,
         out_specs=(VMEM,) * 4,
-        scratch_shapes=[pltpu.VMEM((512, 1024), BF16)],
+        scratch_shapes=[pltpu.VMEM((512, 1024), BF16), pltpu.VMEM((512, 256), BF16)],
         compiler_params=params(),
         cost_estimate=cost(2 * 512 * 256 * 1024, 3 << 20),
         name="first_product",
-    )(place, *pieces, mine, other, *sent)
-
-
-def first_sum(place, own, zero, one):
-    def kernel(place_ref, own_ref, *refs):
-        outs = refs[6:]
-
-        def body(parts):
-            for step, out in enumerate(outs):
-                start = lax.rem(place_ref[2] + step, 4) * 128
-                rows = pl.ds(pl.multiple_of(start, 128), 128)
-                out[...] = add_up([part.at[rows] for part in (own_ref, *parts)]).astype(BF16)
-
-        @pl.when(place_ref[0] == 0)
-        def _():
-            body(refs[:3])
-
-        @pl.when(place_ref[0] == 1)
-        def _():
-            body(refs[3:6])
+    )(place, own, *zero, *one, mine, other)
+
+
+def first_sum(place, pieces, sent):
+    def kernel(place_ref, v0, v1, v2, v3, *refs):
+        for step, out in enumerate(refs[len(sent) :]):
+            start = lax.rem(place_ref[2] + step, 4) * 128
+            rows = pl.ds(pl.multiple_of(start, 128), 128)
+            out[...] = add_up([part.at[rows] for part in (v0, v1, v2, v3)]).astype(BF16)
 
     return pl.pallas_call(
         kernel,
         out_shape=(jax.ShapeDtypeStruct((128, 256), BF16),) * 4,
-        in_specs=[SCALARS] + [VMEM] * 7,
+        in_specs=[SCALARS] + [VMEM] * 4 + [ANY] * len(sent),
         out_specs=(VMEM,) * 4,
         compiler_params=params(),
         cost_estimate=cost(4 * 512 * 256, 1 << 20),
         name="first_sum",
-    )(place, own, *zero, *one)
+    )(place, *pieces, *sent)
 
 
 def gate(events, arrays):
@@ -456,7 +454,6 @@
     away = swap(term(1 - core))
     home = lax.optimization_barrier(term(core))
     both = (home.astype(F32) + away.astype(F32)).astype(BF16)
-    over_z = spread(both[3], "z")
     def cut(part):
         return [
             lax.dynamic_slice_in_dim(part, lax.rem(x + by, 4) * 128, 128, axis=2)
@@ -464,12 +461,13 @@
         ]
 
     near = deal(cut(both[2:3]), "x")
-    own, *others = first_product(place, over_z, inverse_diag[3], other, near[1:])
-    zero = [along_y(others[by - 1], 0, by) for by in (1, 2, 3)]
+    own = both[3]
+    zero = [along_z(own, 0, by) for by in (1, 2, 3)]
     token = lax.ppermute(sum(piece[:8] for piece in zero), "core", [(0, 1)])
-    others = gate((token,), others)
-    one = [along_y(others[by - 1], 1, by) for by in (1, 2, 3)]
-    over_x = deal(first_sum(place, own, zero, one), "x")
+    (held,) = gate((token,), (own,))
+    one = [along_z(held, 1, by) for by in (1, 2, 3)]
+    over_y = deal(first_product(place, own, zero, one, inverse_diag[3], other), "y")
+    over_x = deal(first_sum(place, over_y, near[1:]), "x")
     quarter = sum(piece.astype(F32) for piece in over_x).astype(BF16)
     base2 = turn(place, near, quarter)[0]
     quarters = spread(quarter, "y")

time: 200 us -> 213 us (1.065)
  starting transfers between devices: 57.4 us -> 73.2 us
    ppermute x1, waiting for transfers between devices: 19 us -> 0.01 us  [local(): token = lax.ppermute(sum((piece[:8] for piece in zero)), 'core', [(0, 1)])]
    ppermute x33, waiting for transfers between devices: 32.4 us -> 49.4 us  [shift(): return lax.ppermute(value, axis, [(i, (i + by) % 4) for i in range(4)])]
    ppermute x2, starting transfers between devices: 1.6 us -> 17.2 us  [swap(): return lax.ppermute(value, 'core', [(0, 1), (1, 0)])]
  transfers between devices with their start and end apart: 44 -> 44, of which waited for: 21 -> 27; matrix products, arithmetic and copies ran while one was open for 9% -> 8% of each run, Pallas kernels for 11% -> 11%
where the time goes in v11:
time: 213 us
  starting transfers between devices  73.2 us (34%)
  waiting for transfers between devices  55.7 us (26%)
  Pallas kernels  32.4 us (15%)
  blocking collectives  20.3 us (10%)
  between operations  13.8 us (6%)
  matrix products  11.7 us (5%)
  local copies, waits for them, and re-layouts  3.27 us (2%)
  other arithmetic  2.36 us (1%)
    ppermute x33, waiting for transfers between devices, shift(): return lax.ppermute(value, axis, [(i, (i + by) % 4) for i in range(4)])  49.4 us
    ppermute x33, starting transfers between devices, shift(): return lax.ppermute(value, axis, [(i, (i + by) % 4) for i in range(4)])  43.8 us
    all_to_all x1, blocking collectives, local(): lax.all_to_all(packed, ('z', 'core', 'y', 'x'), split_axis=0, concat_axis...  20.3 us
    ppermute x2, starting transfers between devices, swap(): return lax.ppermute(value, 'core', [(0, 1), (1, 0)])  17.2 us
    pallas_call x6, Pallas kernels, lower_step(): pl.pallas_call(kernel, out_shape=(jax.ShapeDtypeStruct((128, 1024), dtype...  14.3 us
    dot_general x2, matrix products, term(): lax.dot_general(border_tiles, bound, (((0,), (0,)), ((), ())), preferred_...  11.7 us
    ppermute x6, starting transfers between devices, along_z(): return lax.ppermute(value, ('z', 'core'), pairs)  10.9 us
    ppermute x6, waiting for transfers between devices, along_z(): return lax.ppermute(value, ('z', 'core'), pairs)  5.51 us
  transfers between devices with their start and end apart: 44, of which 27 were waited for; matrix products, arithmetic and copies ran while one was open for 8% of the time, Pallas kernels for 11%

profile of v11, /device:TPU:1, one launch (start us, length us, event | category | flops | bytes accessed | tf_op | source)
XLA Modules:
  0.0 212.7 jit_solution(7334166200120012025)
XLA Ops:
  6.5 3.3 %stage.1 = (bf16[2560,256]{1,0:T(8,128)(2,1)}, bf16[2064,256]{1,0:T(8,128)(2,1)}) custom-call(bf16[6,512,256]{2,1,0:T(8,128)(2,1)} %lower_ref.1, bf16[4,256,512]{2,1,0:T(8,128)(2,1)} %diag_ref.1, s32[1,128]{1,0:T(1,128)} %bitcast.56), custom_call_target="tpu_custom_call" | custom-call | bytes 6291456 | tf_op jit(solution)/shard_map/stage/pallas_call | solution.py:323
  10.6 5.9 %fusion.6 = bf16[4,256,512]{2,1,0:T(8,128)(2,1)S(1)} fusion(f32[4,256,1024]{2,1,0:T(8,128)} %param.6, s32[]{:T(128)S(6)} %select_n.30, bf16[2048,4,256]{2,1,0:T(4,128)(2,1)} %param.8, bf16[2048,1024]{1,0:T(8,128)(2,1)} %param.7, f32[]{:T(128)S(6)} %select_n.28), kind=kOutput, calls=%fused_computation.7 | convolution fusion | flops 2149056512 | bytes 9438720 | tf_op jit(solution)/shard_map/dot_general | solution.py:449
  18.0 5.8 %fusion.7 = bf16[4,256,512]{2,1,0:T(8,128)(2,1)S(1)} fusion(f32[4,256,1024]{2,1,0:T(8,128)} %param.6, s32[]{:T(128)S(6)} %select_n.29, bf16[2048,4,256]{2,1,0:T(4,128)(2,1)} %param.8, bf16[2048,1024]{1,0:T(8,128)(2,1)} %param.7, f32[]{:T(128)S(6)} %select_n.28), kind=kOutput, calls=%fused_computation.9 | convolution fusion | flops 2149056512 | bytes 9438720 | tf_op jit(solution)/shard_map/dot_general | solution.py:449
  29.4 15.7 %collective-permute-start.8 = (bf16[256,512]{1,0:T(8,128)(2,1)S(1)}, bf16[256,512]{1,0:T(8,128)(2,1)S(1)}, u32[]{:S(2)}, u32[]{:S(2)}) collective-permute-start(bf16[256,512]{1,0:T(8,128)(2,1)S(1)} %slice_bitcast_fusion.3.refs_6_), channel_id=1, source_target_pairs={{0,16},{16,0},{1,17},{17,1},{2,18},{18,2},{3,19},{19,3},{4,20},{20... | collective-permute-start | bytes 786440 | tf_op jit(solution)/shard_map/ppermute | solution.py:22
  45.2 2.4 %collective-permute-start.5 = (bf16[256,512]{1,0:T(8,128)(2,1)S(1)}, bf16[256,512]{1,0:T(8,128)(2,1)S(1)}, u32[]{:S(2)}, u32[]{:S(2)}) collective-permute-start(bf16[256,512]{1,0:T(8,128)(2,1)S(1)} %gate.2), channel_id=1, source_target_pairs={{16,48},{48,80},{80,112},{112,16},{17,49},{49,81},{81,113},{113,17... | collective-permute-start | bytes 786440 | tf_op jit(solution)/shard_map/ppermute | solution.py:27
  47.5 4.6 %collective-permute-start.6 = (bf16[256,512]{1,0:T(8,128)(2,1)S(1)}, bf16[256,512]{1,0:T(8,128)(2,1)S(1)}, u32[]{:S(2)}, u32[]{:S(2)}) collective-permute-start(bf16[256,512]{1,0:T(8,128)(2,1)S(1)} %gate.2), channel_id=1, source_target_pairs={{16,80},{48,112},{80,16},{112,48},{17,81},{49,113},{81,17},{113,49... | collective-permute-start | bytes 786440 | tf_op jit(solution)/shard_map/ppermute | solution.py:27
  54.1 2.7 %collective-permute-done.6.refs_4_ = bf16[256,512]{1,0:T(8,128)(2,1)S(1)} collective-permute-done((bf16[256,512]{1,0:T(8,128)(2,1)S(1)}, bf16[256,512]{1,0:T(8,128)(2,1)S(1)}, u32[]{:S(2)}, u32[]{:S(2)}) %collective-permute-start.6) | collective-permute-done | bytes 262176 | tf_op jit(solution)/shard_map/ppermute | solution.py:27
  56.8 2.8 %collective-permute-done.7.refs_5_ = bf16[256,512]{1,0:T(8,128)(2,1)S(1)} collective-permute-done((bf16[256,512]{1,0:T(8,128)(2,1)S(1)}, bf16[256,512]{1,0:T(8,128)(2,1)S(1)}, u32[]{:S(2)}, u32[]{:S(2)}) %collective-permute-start.7) | collective-permute-done | bytes 262176 | tf_op jit(solution)/shard_map/ppermute | solution.py:27
  61.1 3.0 %collective-permute-start.10 = (bf16[512,256]{1,0:T(8,128)(2,1)S(1)}, bf16[512,256]{1,0:T(8,128)(2,1)S(1)}, u32[]{:S(2)}, u32[]{:S(2)}) collective-permute-start(bf16[512,256]{1,0:T(8,128)(2,1)S(1)} %get-tuple-element.37), channel_id=1, source_target_pairs={{0,8},{4,12},{8,0},{12,4},{1,9},{5,13},{9,1},{13,5},{2,10},{6,14},... | collective-permute-start | bytes 786440 | tf_op jit(solution)/shard_map/ppermute | solution.py:18
  67.8 2.4 %collective-permute-start.13 = (bf16[1,256,128]{2,1,0:T(8,128)(2,1)S(1)}, bf16[1,256,128]{2,1,0:T(8,128)(2,1)S(1)}, u32[]{:S(2)}, u32[]{:S(2)}) collective-permute-start(bf16[1,256,128]{2,1,0:T(8,128)(2,1)S(1)} %get-tuple-element.73), channel_id=1, source_target_pairs={{0,2},{1,3},{2,0},{3,1},{4,6},{5,7},{6,4},{7,5},{8,10},{9,11},{10,... | collective-permute-start | bytes 196616 | tf_op jit(solution)/shard_map/ppermute | solution.py:18
  72.9 2.5 %collective-permute-done.14.refs_2_.v3 = bf16[1,256,128]{2,1,0:T(8,128)(2,1)S(1)} collective-permute-done((bf16[1,256,128]{2,1,0:T(8,128)(2,1)S(1)}, bf16[1,256,128]{2,1,0:T(8,128)(2,1)S(1)}, u32[]{:S(2)}, u32[]{:S(2)}) %collective-permute-start.14) | collective-permute-done | bytes 65568 | tf_op jit(solution)/shard_map/ppermute | solution.py:18
  76.2 3.7 %collective-permute-start.16 = (bf16[128,256]{1,0:T(8,128)(2,1)S(1)}, bf16[128,256]{1,0:T(8,128)(2,1)S(1)}, u32[]{:S(2)}, u32[]{:S(2)}) collective-permute-start(bf16[128,256]{1,0:T(8,128)(2,1)S(1)} %get-tuple-element.41), channel_id=1, source_target_pairs={{0,2},{1,3},{2,0},{3,1},{4,6},{5,7},{6,4},{7,5},{8,10},{9,11},{10,... | collective-permute-start | bytes 196616 | tf_op jit(solution)/shard_map/ppermute | solution.py:18
  83.8 3.1 %collective-permute-start.19 = (bf16[128,256]{1,0:T(8,128)(2,1)S(1)}, bf16[128,256]{1,0:T(8,128)(2,1)S(1)}, u32[]{:S(2)}, u32[]{:S(2)}) collective-permute-start(bf16[128,256]{1,0:T(8,128)(2,1)S(1)} %add_convert_fusion.1._.refs_1_), channel_id=1, source_target_pairs={{0,8},{4,12},{8,0},{12,4},{1,9},{5,13},{9,1},{13,5},{2,10},{6,14},... | collective-permute-start | bytes 196616 | tf_op jit(solution)/shard_map/ppermute | solution.py:18
  90.0 2.6 %lower_step.6 = (bf16[128,1024]{1,0:T(8,128)(2,1)S(1)}, bf16[128,1024]{1,0:T(8,128)(2,1)S(1)}) custom-call(s32[4]{0:T(128)S(1)} %pad_add_fusion.place_ref.refs_0_, bf16[128,256]{1,0:T(8,128)(2,1)S(1)} %add_convert_fusion.1._.refs_1_, bf16[128,256]{1,0:T(8,128)(2,1)S(1)} %collective-permute-done.18.refs_2_, ...), custom_call_target="tpu_custom_call" | custom-call | flops 268435456 | bytes 4194304 | tf_op jit(solution)/shard_map/lower_step/pallas_call | solution.py:191
  97.0 3.0 %collective-permute-start.28 = (bf16[2,256,128]{2,1,0:T(8,128)(2,1)S(1)}, bf16[2,256,128]{2,1,0:T(8,128)(2,1)S(1)}, u32[]{:S(2)}, u32[]{:S(2)}) collective-permute-start(bf16[2,256,128]{2,1,0:T(8,128)(2,1)S(1)} %get-tuple-element.48), channel_id=1, source_target_pairs={{0,2},{1,3},{2,0},{3,1},{4,6},{5,7},{6,4},{7,5},{8,10},{9,11},{10,... | collective-permute-start | bytes 393224 | tf_op jit(solution)/shard_map/ppermute | solution.py:18
  106.0 2.4 %collective-permute-start.25 = (bf16[128,1024]{1,0:T(8,128)(2,1)S(1)}, bf16[128,1024]{1,0:T(8,128)(2,1)S(1)}, u32[]{:S(2)}, u32[]{:S(2)}) collective-permute-start(bf16[128,1024]{1,0:T(8,128)(2,1)S(1)} %diag_step.2.refs_0_), channel_id=1, source_target_pairs={{0,8},{4,12},{8,0},{12,4},{1,9},{5,13},{9,1},{13,5},{2,10},{6,14},... | collective-permute-start | bytes 786440 | tf_op jit(solution)/shard_map/ppermute | solution.py:18
  112.1 2.5 %lower_step.7 = (f32[128,1024]{1,0:T(8,128)S(1)}, bf16[128,1024]{1,0:T(8,128)(2,1)}) custom-call(bf16[128,1024]{1,0:T(8,128)(2,1)S(1)} %get-tuple-element.45.refs_0_.x3, f32[128,1024]{1,0:T(8,128)S(1)} %get-tuple-element.64.refs_1_, bf16[2,4,2560,256]{3,2,1,0:T(8,128)(2,1)} %bitcast.46), custom_call_target="tpu_custom_call" | custom-call | flops 268435456 | bytes 4194304 | tf_op jit(solution)/shard_map/lower_step/pallas_call | solution.py:191
  114.6 5.4 %collective-permute-done.24.refs_1_ = bf16[128,1024]{1,0:T(8,128)(2,1)S(1)} collective-permute-done((bf16[128,1024]{1,0:T(8,128)(2,1)S(1)}, bf16[128,1024]{1,0:T(8,128)(2,1)S(1)}, u32[]{:S(2)}, u32[]{:S(2)}) %collective-permute-start.24) | collective-permute-done | bytes 262176 | tf_op jit(solution)/shard_map/ppermute | solution.py:18
  120.9 2.1 lower_step.8
  123.1 3.1 %collective-permute-start.31 = (bf16[128,1024]{1,0:T(8,128)(2,1)S(1)}, bf16[128,1024]{1,0:T(8,128)(2,1)S(1)}, u32[]{:S(2)}, u32[]{:S(2)}) collective-permute-start(bf16[128,1024]{1,0:T(8,128)(2,1)S(1)} %get-tuple-element.51.v0), channel_id=1, source_target_pairs={{0,64},{32,96},{64,0},{96,32},{1,65},{33,97},{65,1},{97,33},{2,66}... | collective-permute-start | bytes 786440 | tf_op jit(solution)/shard_map/ppermute | solution.py:18
  126.7 5.6 %collective-permute-done.30.v1 = bf16[128,1024]{1,0:T(8,128)(2,1)S(1)} collective-permute-done((bf16[128,1024]{1,0:T(8,128)(2,1)S(1)}, bf16[128,1024]{1,0:T(8,128)(2,1)S(1)}, u32[]{:S(2)}, u32[]{:S(2)}) %collective-permute-start.30) | collective-permute-done | bytes 262176 | tf_op jit(solution)/shard_map/ppermute | solution.py:18
  132.3 5.9 %collective-permute-done.31.v2 = bf16[128,1024]{1,0:T(8,128)(2,1)S(1)} collective-permute-done((bf16[128,1024]{1,0:T(8,128)(2,1)S(1)}, bf16[128,1024]{1,0:T(8,128)(2,1)S(1)}, u32[]{:S(2)}, u32[]{:S(2)}) %collective-permute-start.31) | collective-permute-done | bytes 262176 | tf_op jit(solution)/shard_map/ppermute | solution.py:18
  140.7 2.8 %collective-permute-start.34 = (bf16[128,1024]{1,0:T(8,128)(2,1)S(1)}, bf16[128,1024]{1,0:T(8,128)(2,1)S(1)}, u32[]{:S(2)}, u32[]{:S(2)}) collective-permute-start(bf16[128,1024]{1,0:T(8,128)(2,1)S(1)} %diag_step.3.refs_0_), channel_id=1, source_target_pairs={{0,8},{4,12},{8,0},{12,4},{1,9},{5,13},{9,1},{13,5},{2,10},{6,14},... | collective-permute-start | bytes 786440 | tf_op jit(solution)/shard_map/ppermute | solution.py:18
  143.6 2.5 %lower_step.9 = (f32[128,1024]{1,0:T(8,128)S(1)}, bf16[128,1024]{1,0:T(8,128)(2,1)}) custom-call(bf16[128,1024]{1,0:T(8,128)(2,1)S(1)} %get-tuple-element.45.refs_0_.x3, f32[128,1024]{1,0:T(8,128)S(1)} %get-tuple-element.63.refs_1_, bf16[2,4,2064,256]{3,2,1,0:T(8,128)(2,1)} %bitcast.49), custom_call_target="tpu_custom_call" | custom-call | flops 268435456 | bytes 4194304 | tf_op jit(solution)/shard_map/lower_step/pallas_call | solution.py:191
  146.1 2.5 %lower_step.10 = (f32[128,1024]{1,0:T(8,128)S(1)}, bf16[128,1024]{1,0:T(8,128)(2,1)}) custom-call(bf16[128,1024]{1,0:T(8,128)(2,1)S(1)} %get-tuple-element.52.refs_0_.x2, f32[128,1024]{1,0:T(8,128)S(1)} %get-tuple-element.53.refs_1_, bf16[2,4,2064,256]{3,2,1,0:T(8,128)(2,1)} %bitcast.50), custom_call_target="tpu_custom_call" | custom-call | flops 268435456 | bytes 4194304 | tf_op jit(solution)/shard_map/lower_step/pallas_call | solution.py:191
  149.8 4.4 %collective-permute-done.34.refs_2_ = bf16[128,1024]{1,0:T(8,128)(2,1)S(1)} collective-permute-done((bf16[128,1024]{1,0:T(8,128)(2,1)S(1)}, bf16[128,1024]{1,0:T(8,128)(2,1)S(1)}, u32[]{:S(2)}, u32[]{:S(2)}) %collective-permute-start.34) | collective-permute-done | bytes 262176 | tf_op jit(solution)/shard_map/ppermute | solution.py:18
  158.8 2.7 %collective-permute-start.37 = (bf16[128,1024]{1,0:T(8,128)(2,1)S(1)}, bf16[128,1024]{1,0:T(8,128)(2,1)S(1)}, u32[]{:S(2)}, u32[]{:S(2)}) collective-permute-start(bf16[128,1024]{1,0:T(8,128)(2,1)S(1)} %get-tuple-element.57.v0), channel_id=1, source_target_pairs={{0,64},{32,96},{64,0},{96,32},{1,65},{33,97},{65,1},{97,33},{2,66}... | collective-permute-start | bytes 786440 | tf_op jit(solution)/shard_map/ppermute | solution.py:18
  165.4 6.8 %collective-permute-done.37.v2 = bf16[128,1024]{1,0:T(8,128)(2,1)S(1)} collective-permute-done((bf16[128,1024]{1,0:T(8,128)(2,1)S(1)}, bf16[128,1024]{1,0:T(8,128)(2,1)S(1)}, u32[]{:S(2)}, u32[]{:S(2)}) %collective-permute-start.37) | collective-permute-done | bytes 262176 | tf_op jit(solution)/shard_map/ppermute | solution.py:18
  172.4 2.5 %last_step.1 = (bf16[128,256]{1,0:T(8,128)(2,1)S(1)}, bf16[128,256]{1,0:T(8,128)(2,1)S(1)}, bf16[128,256]{1,0:T(8,128)(2,1)S(1)}, bf16[128,256]{1,0:T(8,128)(2,1)S(1)}) custom-call(s32[4]{0:T(128)S(1)} %pad_add_fusion.place_ref.refs_0_, bf16[128,1024]{1,0:T(8,128)(2,1)S(1)} %get-tuple-element.57.v0, bf16[128,1024]{1,0:T(8,128)(2,1)S(1)} %collective-permute-done.36.v1, ...), custom_call_target="tpu_custom_call" | custom-call | flops 268435456 | bytes 4194304 | tf_op jit(solution)/shard_map/last_step/pallas_call | solution.py:270
  176.3 3.3 %collective-permute-start.40 = (bf16[128,256]{1,0:T(8,128)(2,1)S(1)}, bf16[128,256]{1,0:T(8,128)(2,1)S(1)}, u32[]{:S(2)}, u32[]{:S(2)}) collective-permute-start(bf16[128,256]{1,0:T(8,128)(2,1)S(1)} %get-tuple-element.60), channel_id=1, source_target_pairs={{0,8},{4,12},{8,0},{12,4},{1,9},{5,13},{9,1},{13,5},{2,10},{6,14},... | collective-permute-start | bytes 196616 | tf_op jit(solution)/shard_map/ppermute | solution.py:18
  179.9 3.0 %pack_known.1 = (bf16[2048,128]{1,0:T(8,128)(2,1)S(1)}, bf16[2048,256]{1,0:T(8,128)(2,1)S(1)}) custom-call(s32[4]{0:T(128)S(1)} %pad_add_fusion.place_ref.refs_0_, s32[4,1,256]{2,1,0:T(1,128)S(1)} %reshape.61.target_ref, bf16[128,1024]{1,0:T(8,128)(2,1)S(1)} %get-tuple-element.55.x1, bf16[128,1024]{1,0:T(8,128)(2,1)S(1)} %get-tuple-element.52.refs_0_.x2, ...), custom_call_target="tpu_custom_call" | custom-call | flops 402653184 | bytes 2097152 | tf_op jit(solution)/shard_map/pack_known/pallas_call | solution.py:359
  184.1 20.3 %all_to_all.5 = bf16[128,16,128]{2,1,0:T(8,128)(2,1)S(1)} all-to-all(bf16[128,16,128]{2,1,0:T(8,128)(2,1)S(1)} %bitcast.43), channel_id=1, replica_groups=mesh['z'=4,'core'=2,'y'=4,'x'=4] {'z','core','y','x'}, dimensions={0} | all-to-all | bytes 1048576 | tf_op jit(solution)/shard_map/all_to_all | solution.py:489
  (104 shorter events, 57.6 us)
Async XLA Ops:
  6.5 83.5 %all-gather.7.cloned.1.call-start = ((), (), s32[]{:S(2)}) async-start(), calls=%async_computation.2 | async-start | bytes 11796480 | tf_op jit(solution)/shard_map/all_gather | solution.py:425
  9.9 133.8 %all-gather.5.cloned.1.call-start = ((), (), s32[]{:S(2)}) async-start(), calls=%async_computation.1 | async-start | bytes 9510912 | tf_op jit(solution)/shard_map/all_gather | solution.py:425
  16.5 7.4 %collective-permute-start = (bf16[4,256,512]{2,1,0:T(8,128)(2,1)S(1)}, bf16[4,256,512]{2,1,0:T(8,128)(2,1)S(1)}, u32[]{:S(2)}, u32[]{:S(2)}) collective-permute-start(bf16[4,256,512]{2,1,0:T(8,128)(2,1)S(1)} %fusion.6), channel_id=1, source_target_pairs={{0,16},{16,0},{1,17},{17,1},{2,18},{18,2},{3,19},{19,3},{4,20},{20... | collective-permute-start | bytes 3145736 | tf_op jit(solution)/shard_map/ppermute | solution.py:22
  27.1 18.0 %collective-permute-start.4 = (bf16[8,512]{1,0:T(8,128)(2,1)S(1)}, bf16[8,512]{1,0:T(8,128)(2,1)S(1)}, u32[]{:S(2)}, u32[]{:S(2)}) collective-permute-start(bf16[8,512]{1,0:T(8,128)(2,1)S(1)} %slice_add_fusion), channel_id=1, source_target_pairs={{0,16},{1,17},{2,18},{3,19},{4,20},{5,21},{6,22},{7,23},{8,24},{9,... | collective-permute-start | bytes 24584 | tf_op jit(solution)/shard_map/ppermute | solution.py:466
  29.4 24.7 %collective-permute-start.8 = (bf16[256,512]{1,0:T(8,128)(2,1)S(1)}, bf16[256,512]{1,0:T(8,128)(2,1)S(1)}, u32[]{:S(2)}, u32[]{:S(2)}) collective-permute-start(bf16[256,512]{1,0:T(8,128)(2,1)S(1)} %slice_bitcast_fusion.3.refs_6_), channel_id=1, source_target_pairs={{0,16},{16,0},{1,17},{17,1},{2,18},{18,2},{3,19},{19,3},{4,20},{20... | collective-permute-start | bytes 786440 | tf_op jit(solution)/shard_map/ppermute | solution.py:22
  45.2 9.0 %collective-permute-start.5 = (bf16[256,512]{1,0:T(8,128)(2,1)S(1)}, bf16[256,512]{1,0:T(8,128)(2,1)S(1)}, u32[]{:S(2)}, u32[]{:S(2)}) collective-permute-start(bf16[256,512]{1,0:T(8,128)(2,1)S(1)} %gate.2), channel_id=1, source_target_pairs={{16,48},{48,80},{80,112},{112,16},{17,49},{49,81},{81,113},{113,17... | collective-permute-start | bytes 786440 | tf_op jit(solution)/shard_map/ppermute | solution.py:27
  47.5 9.2 %collective-permute-start.6 = (bf16[256,512]{1,0:T(8,128)(2,1)S(1)}, bf16[256,512]{1,0:T(8,128)(2,1)S(1)}, u32[]{:S(2)}, u32[]{:S(2)}) collective-permute-start(bf16[256,512]{1,0:T(8,128)(2,1)S(1)} %gate.2), channel_id=1, source_target_pairs={{16,80},{48,112},{80,16},{112,48},{17,81},{49,113},{81,17},{113,49... | collective-permute-start | bytes 786440 | tf_op jit(solution)/shard_map/ppermute | solution.py:27
  52.1 7.5 %collective-permute-start.7 = (bf16[256,512]{1,0:T(8,128)(2,1)S(1)}, bf16[256,512]{1,0:T(8,128)(2,1)S(1)}, u32[]{:S(2)}, u32[]{:S(2)}) collective-permute-start(bf16[256,512]{1,0:T(8,128)(2,1)S(1)} %gate.2), channel_id=1, source_target_pairs={{16,112},{48,16},{80,48},{112,80},{17,113},{49,17},{81,49},{113,81... | collective-permute-start | bytes 786440 | tf_op jit(solution)/shard_map/ppermute | solution.py:27
  61.1 14.3 %collective-permute-start.10 = (bf16[512,256]{1,0:T(8,128)(2,1)S(1)}, bf16[512,256]{1,0:T(8,128)(2,1)S(1)}, u32[]{:S(2)}, u32[]{:S(2)}) collective-permute-start(bf16[512,256]{1,0:T(8,128)(2,1)S(1)} %get-tuple-element.37), channel_id=1, source_target_pairs={{0,8},{4,12},{8,0},{12,4},{1,9},{5,13},{9,1},{13,5},{2,10},{6,14},... | collective-permute-start | bytes 786440 | tf_op jit(solution)/shard_map/ppermute | solution.py:18
  64.1 11.3 %collective-permute-start.11 = (bf16[512,256]{1,0:T(8,128)(2,1)S(1)}, bf16[512,256]{1,0:T(8,128)(2,1)S(1)}, u32[]{:S(2)}, u32[]{:S(2)}) collective-permute-start(bf16[512,256]{1,0:T(8,128)(2,1)S(1)} %get-tuple-element.38), channel_id=1, source_target_pairs={{0,12},{4,0},{8,4},{12,8},{1,13},{5,1},{9,5},{13,9},{2,14},{6,2},{... | collective-permute-start | bytes 786440 | tf_op jit(solution)/shard_map/ppermute | solution.py:18
  64.8 10.5 %collective-permute-start.9 = (bf16[512,256]{1,0:T(8,128)(2,1)S(1)}, bf16[512,256]{1,0:T(8,128)(2,1)S(1)}, u32[]{:S(2)}, u32[]{:S(2)}) collective-permute-start(bf16[512,256]{1,0:T(8,128)(2,1)S(1)} %get-tuple-element.36), channel_id=1, source_target_pairs={{0,4},{4,8},{8,12},{12,0},{1,5},{5,9},{9,13},{13,1},{2,6},{6,10},{... | collective-permute-start | bytes 786440 | tf_op jit(solution)/shard_map/ppermute | solution.py:18
  76.2 6.1 %collective-permute-start.16 = (bf16[128,256]{1,0:T(8,128)(2,1)S(1)}, bf16[128,256]{1,0:T(8,128)(2,1)S(1)}, u32[]{:S(2)}, u32[]{:S(2)}) collective-permute-start(bf16[128,256]{1,0:T(8,128)(2,1)S(1)} %get-tuple-element.41), channel_id=1, source_target_pairs={{0,2},{1,3},{2,0},{3,1},{4,6},{5,7},{6,4},{7,5},{8,10},{9,11},{10,... | collective-permute-start | bytes 196616 | tf_op jit(solution)/shard_map/ppermute | solution.py:18
  92.7 8.2 %collective-permute-start.22 = (bf16[128,1024]{1,0:T(8,128)(2,1)S(1)}, bf16[128,1024]{1,0:T(8,128)(2,1)S(1)}, u32[]{:S(2)}, u32[]{:S(2)}) collective-permute-start(bf16[128,1024]{1,0:T(8,128)(2,1)S(1)} %get-tuple-element.44.v0), channel_id=1, source_target_pairs={{0,64},{32,96},{64,0},{96,32},{1,65},{33,97},{65,1},{97,33},{2,66}... | collective-permute-start | bytes 786440 | tf_op jit(solution)/shard_map/ppermute | solution.py:18
  93.5 10.4 %collective-permute-start.21 = (bf16[128,1024]{1,0:T(8,128)(2,1)S(1)}, bf16[128,1024]{1,0:T(8,128)(2,1)S(1)}, u32[]{:S(2)}, u32[]{:S(2)}) collective-permute-start(bf16[128,1024]{1,0:T(8,128)(2,1)S(1)} %get-tuple-element.44.v0), channel_id=1, source_target_pairs={{0,32},{32,64},{64,96},{96,0},{1,33},{33,65},{65,97},{97,1},{2,34}... | collective-permute-start | bytes 786440 | tf_op jit(solution)/shard_map/ppermute | solution.py:18
  95.3 8.7 %collective-permute-start.23 = (bf16[128,1024]{1,0:T(8,128)(2,1)S(1)}, bf16[128,1024]{1,0:T(8,128)(2,1)S(1)}, u32[]{:S(2)}, u32[]{:S(2)}) collective-permute-start(bf16[128,1024]{1,0:T(8,128)(2,1)S(1)} %get-tuple-element.44.v0), channel_id=1, source_target_pairs={{0,96},{32,0},{64,32},{96,64},{1,97},{33,1},{65,33},{97,65},{2,98}... | collective-permute-start | bytes 786440 | tf_op jit(solution)/shard_map/ppermute | solution.py:18
  96.3 12.0 %collective-permute-start.27 = (bf16[2,256,128]{2,1,0:T(8,128)(2,1)S(1)}, bf16[2,256,128]{2,1,0:T(8,128)(2,1)S(1)}, u32[]{:S(2)}, u32[]{:S(2)}) collective-permute-start(bf16[2,256,128]{2,1,0:T(8,128)(2,1)S(1)} %get-tuple-element.47), channel_id=1, source_target_pairs={{0,1},{1,2},{2,3},{3,0},{4,5},{5,6},{6,7},{7,4},{8,9},{9,10},{10,1... | collective-permute-start | bytes 393224 | tf_op jit(solution)/shard_map/ppermute | solution.py:18
  97.0 13.8 %collective-permute-start.28 = (bf16[2,256,128]{2,1,0:T(8,128)(2,1)S(1)}, bf16[2,256,128]{2,1,0:T(8,128)(2,1)S(1)}, u32[]{:S(2)}, u32[]{:S(2)}) collective-permute-start(bf16[2,256,128]{2,1,0:T(8,128)(2,1)S(1)} %get-tuple-element.48), channel_id=1, source_target_pairs={{0,2},{1,3},{2,0},{3,1},{4,6},{5,7},{6,4},{7,5},{8,10},{9,11},{10,... | collective-permute-start | bytes 393224 | tf_op jit(solution)/shard_map/ppermute | solution.py:18
  100.9 10.4 %collective-permute-start.29 = (bf16[2,256,128]{2,1,0:T(8,128)(2,1)S(1)}, bf16[2,256,128]{2,1,0:T(8,128)(2,1)S(1)}, u32[]{:S(2)}, u32[]{:S(2)}) collective-permute-start(bf16[2,256,128]{2,1,0:T(8,128)(2,1)S(1)} %get-tuple-element.49), channel_id=1, source_target_pairs={{0,3},{1,0},{2,1},{3,2},{4,7},{5,4},{6,5},{7,6},{8,11},{9,8},{10,9... | collective-permute-start | bytes 393224 | tf_op jit(solution)/shard_map/ppermute | solution.py:18
  105.9 14.2 %collective-permute-start.24 = (bf16[128,1024]{1,0:T(8,128)(2,1)S(1)}, bf16[128,1024]{1,0:T(8,128)(2,1)S(1)}, u32[]{:S(2)}, u32[]{:S(2)}) collective-permute-start(bf16[128,1024]{1,0:T(8,128)(2,1)S(1)} %diag_step.2.refs_0_), channel_id=1, source_target_pairs={{0,4},{4,8},{8,12},{12,0},{1,5},{5,9},{9,13},{13,1},{2,6},{6,10},{... | collective-permute-start | bytes 786440 | tf_op jit(solution)/shard_map/ppermute | solution.py:18
  106.0 14.1 %collective-permute-start.25 = (bf16[128,1024]{1,0:T(8,128)(2,1)S(1)}, bf16[128,1024]{1,0:T(8,128)(2,1)S(1)}, u32[]{:S(2)}, u32[]{:S(2)}) collective-permute-start(bf16[128,1024]{1,0:T(8,128)(2,1)S(1)} %diag_step.2.refs_0_), channel_id=1, source_target_pairs={{0,8},{4,12},{8,0},{12,4},{1,9},{5,13},{9,1},{13,5},{2,10},{6,14},... | collective-permute-start | bytes 786440 | tf_op jit(solution)/shard_map/ppermute | solution.py:18
  108.4 12.6 %collective-permute-start.26 = (bf16[128,1024]{1,0:T(8,128)(2,1)S(1)}, bf16[128,1024]{1,0:T(8,128)(2,1)S(1)}, u32[]{:S(2)}, u32[]{:S(2)}) collective-permute-start(bf16[128,1024]{1,0:T(8,128)(2,1)S(1)} %diag_step.2.refs_0_), channel_id=1, source_target_pairs={{0,12},{4,0},{8,4},{12,8},{1,13},{5,1},{9,5},{13,9},{2,14},{6,2},{... | collective-permute-start | bytes 786440 | tf_op jit(solution)/shard_map/ppermute | solution.py:18
  123.0 9.3 %collective-permute-start.30 = (bf16[128,1024]{1,0:T(8,128)(2,1)S(1)}, bf16[128,1024]{1,0:T(8,128)(2,1)S(1)}, u32[]{:S(2)}, u32[]{:S(2)}) collective-permute-start(bf16[128,1024]{1,0:T(8,128)(2,1)S(1)} %get-tuple-element.51.v0), channel_id=1, source_target_pairs={{0,32},{32,64},{64,96},{96,0},{1,33},{33,65},{65,97},{97,1},{2,34}... | collective-permute-start | bytes 786440 | tf_op jit(solution)/shard_map/ppermute | solution.py:18
  123.1 15.1 %collective-permute-start.31 = (bf16[128,1024]{1,0:T(8,128)(2,1)S(1)}, bf16[128,1024]{1,0:T(8,128)(2,1)S(1)}, u32[]{:S(2)}, u32[]{:S(2)}) collective-permute-start(bf16[128,1024]{1,0:T(8,128)(2,1)S(1)} %get-tuple-element.51.v0), channel_id=1, source_target_pairs={{0,64},{32,96},{64,0},{96,32},{1,65},{33,97},{65,1},{97,33},{2,66}... | collective-permute-start | bytes 786440 | tf_op jit(solution)/shard_map/ppermute | solution.py:18
  126.2 12.6 %collective-permute-start.32 = (bf16[128,1024]{1,0:T(8,128)(2,1)S(1)}, bf16[128,1024]{1,0:T(8,128)(2,1)S(1)}, u32[]{:S(2)}, u32[]{:S(2)}) collective-permute-start(bf16[128,1024]{1,0:T(8,128)(2,1)S(1)} %get-tuple-element.51.v0), channel_id=1, source_target_pairs={{0,96},{32,0},{64,32},{96,64},{1,97},{33,1},{65,33},{97,65},{2,98}... | collective-permute-start | bytes 786440 | tf_op jit(solution)/shard_map/ppermute | solution.py:18
  140.6 9.2 %collective-permute-start.33 = (bf16[128,1024]{1,0:T(8,128)(2,1)S(1)}, bf16[128,1024]{1,0:T(8,128)(2,1)S(1)}, u32[]{:S(2)}, u32[]{:S(2)}) collective-permute-start(bf16[128,1024]{1,0:T(8,128)(2,1)S(1)} %diag_step.3.refs_0_), channel_id=1, source_target_pairs={{0,4},{4,8},{8,12},{12,0},{1,5},{5,9},{9,13},{13,1},{2,6},{6,10},{... | collective-permute-start | bytes 786440 | tf_op jit(solution)/shard_map/ppermute | solution.py:18
  140.7 13.5 %collective-permute-start.34 = (bf16[128,1024]{1,0:T(8,128)(2,1)S(1)}, bf16[128,1024]{1,0:T(8,128)(2,1)S(1)}, u32[]{:S(2)}, u32[]{:S(2)}) collective-permute-start(bf16[128,1024]{1,0:T(8,128)(2,1)S(1)} %diag_step.3.refs_0_), channel_id=1, source_target_pairs={{0,8},{4,12},{8,0},{12,4},{1,9},{5,13},{9,1},{13,5},{2,10},{6,14},... | collective-permute-start | bytes 786440 | tf_op jit(solution)/shard_map/ppermute | solution.py:18
  143.5 11.6 %collective-permute-start.35 = (bf16[128,1024]{1,0:T(8,128)(2,1)S(1)}, bf16[128,1024]{1,0:T(8,128)(2,1)S(1)}, u32[]{:S(2)}, u32[]{:S(2)}) collective-permute-start(bf16[128,1024]{1,0:T(8,128)(2,1)S(1)} %diag_step.3.refs_0_), channel_id=1, source_target_pairs={{0,12},{4,0},{8,4},{12,8},{1,13},{5,1},{9,5},{13,9},{2,14},{6,2},{... | collective-permute-start | bytes 786440 | tf_op jit(solution)/shard_map/ppermute | solution.py:18
  157.3 8.1 %collective-permute-start.36 = (bf16[128,1024]{1,0:T(8,128)(2,1)S(1)}, bf16[128,1024]{1,0:T(8,128)(2,1)S(1)}, u32[]{:S(2)}, u32[]{:S(2)}) collective-permute-start(bf16[128,1024]{1,0:T(8,128)(2,1)S(1)} %get-tuple-element.57.v0), channel_id=1, source_target_pairs={{0,32},{32,64},{64,96},{96,0},{1,33},{33,65},{65,97},{97,1},{2,34}... | collective-permute-start | bytes 786440 | tf_op jit(solution)/shard_map/ppermute | solution.py:18
  158.8 13.3 %collective-permute-start.37 = (bf16[128,1024]{1,0:T(8,128)(2,1)S(1)}, bf16[128,1024]{1,0:T(8,128)(2,1)S(1)}, u32[]{:S(2)}, u32[]{:S(2)}) collective-permute-start(bf16[128,1024]{1,0:T(8,128)(2,1)S(1)} %get-tuple-element.57.v0), channel_id=1, source_target_pairs={{0,64},{32,96},{64,0},{96,32},{1,65},{33,97},{65,1},{97,33},{2,66}... | collective-permute-start | bytes 786440 | tf_op jit(solution)/shard_map/ppermute | solution.py:18
  161.5 10.8 %collective-permute-start.38 = (bf16[128,1024]{1,0:T(8,128)(2,1)S(1)}, bf16[128,1024]{1,0:T(8,128)(2,1)S(1)}, u32[]{:S(2)}, u32[]{:S(2)}) collective-permute-start(bf16[128,1024]{1,0:T(8,128)(2,1)S(1)} %get-tuple-element.57.v0), channel_id=1, source_target_pairs={{0,96},{32,0},{64,32},{96,64},{1,97},{33,1},{65,33},{97,65},{2,98}... | collective-permute-start | bytes 786440 | tf_op jit(solution)/shard_map/ppermute | solution.py:18
  174.8 8.0 %collective-permute-start.39 = (bf16[128,256]{1,0:T(8,128)(2,1)S(1)}, bf16[128,256]{1,0:T(8,128)(2,1)S(1)}, u32[]{:S(2)}, u32[]{:S(2)}) collective-permute-start(bf16[128,256]{1,0:T(8,128)(2,1)S(1)} %get-tuple-element.59), channel_id=1, source_target_pairs={{0,4},{4,8},{8,12},{12,0},{1,5},{5,9},{9,13},{13,1},{2,6},{6,10},{... | collective-permute-start | bytes 196616 | tf_op jit(solution)/shard_map/ppermute | solution.py:18
  176.3 6.5 %collective-permute-start.40 = (bf16[128,256]{1,0:T(8,128)(2,1)S(1)}, bf16[128,256]{1,0:T(8,128)(2,1)S(1)}, u32[]{:S(2)}, u32[]{:S(2)}) collective-permute-start(bf16[128,256]{1,0:T(8,128)(2,1)S(1)} %get-tuple-element.60), channel_id=1, source_target_pairs={{0,8},{4,12},{8,0},{12,4},{1,9},{5,13},{9,1},{13,5},{2,10},{6,14},... | collective-permute-start | bytes 196616 | tf_op jit(solution)/shard_map/ppermute | solution.py:18
  (14 other events, 70.0 us)
Sparse Core Ops, SparseCore 0:
  10.0 64.1 all-gather.6
  75.9 58.0 all-gather.4

commit v12 on v11

--- a/solution.py
+++ b/solution.py
@@ -66,10 +66,10 @@
 HBM = pl.BlockSpec(memory_space=pltpu.HBM)
 
 
-def first_product(place, own, zero, one, mine, other):
+def first_product(place, own, zero, one, mine, other, sent):
     def kernel(place_ref, own_ref, *refs):
         mine_ref, other_ref = refs[6:8]
-        outs, full, turned = refs[8:12], refs[12], refs[13]
+        outs, full, turned = refs[-6:-2], refs[-2], refs[-1]
         core, y = place_ref[0], place_ref[1]
 
         @pl.when(core == 0)
@@ -91,18 +91,18 @@
     return pl.pallas_call(
         kernel,
         out_shape=(jax.ShapeDtypeStruct((512, 256), BF16),) * 4,
-        in_specs=[SCALARS] + [VMEM] * 9,
+        in_specs=[SCALARS] + [VMEM] * 9 + [ANY] * len(sent),
         out_specs=(VMEM,) * 4,
         scratch_shapes=[pltpu.VMEM((512, 1024), BF16), pltpu.VMEM((512, 256), BF16)],
         compiler_params=params(),
         cost_estimate=cost(2 * 512 * 256 * 1024, 3 << 20),
         name="first_product",
-    )(place, own, *zero, *one, mine, other)
-
-
-def first_sum(place, pieces, sent):
-    def kernel(place_ref, v0, v1, v2, v3, *refs):
-        for step, out in enumerate(refs[len(sent) :]):
+    )(place, own, *zero, *one, mine, other, *sent)
+
+
+def first_sum(place, pieces):
+    def kernel(place_ref, v0, v1, v2, v3, *outs):
+        for step, out in enumerate(outs):
             start = lax.rem(place_ref[2] + step, 4) * 128
             rows = pl.ds(pl.multiple_of(start, 128), 128)
             out[...] = add_up([part.at[rows] for part in (v0, v1, v2, v3)]).astype(BF16)
@@ -110,12 +110,12 @@
     return pl.pallas_call(
         kernel,
         out_shape=(jax.ShapeDtypeStruct((128, 256), BF16),) * 4,
-        in_specs=[SCALARS] + [VMEM] * 4 + [ANY] * len(sent),
+        in_specs=[SCALARS] + [VMEM] * 4,
         out_specs=(VMEM,) * 4,
         compiler_params=params(),
         cost_estimate=cost(4 * 512 * 256, 1 << 20),
         name="first_sum",
-    )(place, *pieces, *sent)
+    )(place, *pieces)
 
 
 def gate(events, arrays):
@@ -464,10 +464,10 @@
     own = both[3]
     zero = [along_z(own, 0, by) for by in (1, 2, 3)]
     token = lax.ppermute(sum(piece[:8] for piece in zero), "core", [(0, 1)])
-    (held,) = gate((token,), (own,))
+    (held,) = gate((token, *near[1:]), (own,))
     one = [along_z(held, 1, by) for by in (1, 2, 3)]
-    over_y = deal(first_product(place, own, zero, one, inverse_diag[3], other), "y")
-    over_x = deal(first_sum(place, over_y, near[1:]), "x")
+    products = first_product(place, own, zero, one, inverse_diag[3], other, near[1:])
+    over_x = deal(first_sum(place, deal(products, "y")), "x")
     quarter = sum(piece.astype(F32) for piece in over_x).astype(BF16)
     base2 = turn(place, near, quarter)[0]
     quarters = spread(quarter, "y")

time: 213 us -> 211 us (level)
  blocking collectives: 20.3 us -> 23.1 us
    ppermute x2, starting transfers between devices: 17.2 us -> 12.4 us  [swap(): return lax.ppermute(value, 'core', [(0, 1), (1, 0)])]
    ppermute x33, starting transfers between devices: 43.8 us -> 47.7 us  [shift(): return lax.ppermute(value, axis, [(i, (i + by) % 4) for i in range(4)])]
    all_to_all x1, blocking collectives: 20.3 us -> 23.1 us  [local(): lax.all_to_all(packed, ('z', 'core', 'y', 'x'), split_axis=0, concat_axis...]
    ppermute x33, waiting for transfers between devices: 49.4 us -> 46.7 us  [shift(): return lax.ppermute(value, axis, [(i, (i + by) % 4) for i in range(4)])]
  transfers between devices with their start and end apart: 44 -> 44, of which waited for: 27 -> 22; matrix products, arithmetic and copies ran while one was open for 8% -> 7% of each run, Pallas kernels for 11% -> 11%
where the time goes in v12:
time: 211 us
  starting transfers between devices  71.9 us (34%)
  waiting for transfers between devices  53.8 us (25%)
  Pallas kernels  32.2 us (15%)
  blocking collectives  23.1 us (11%)
  between operations  13.8 us (7%)
  matrix products  11.7 us (6%)
  other arithmetic  2.35 us (1%)
    ppermute x33, starting transfers between devices, shift(): return lax.ppermute(value, axis, [(i, (i + by) % 4) for i in range(4)])  47.7 us
    ppermute x33, waiting for transfers between devices, shift(): return lax.ppermute(value, axis, [(i, (i + by) % 4) for i in range(4)])  46.7 us
    all_to_all x1, blocking collectives, local(): lax.all_to_all(packed, ('z', 'core', 'y', 'x'), split_axis=0, concat_axis...  23.1 us
    pallas_call x6, Pallas kernels, lower_step(): pl.pallas_call(kernel, out_shape=(jax.ShapeDtypeStruct((128, 1024), dtype...  14.2 us
    ppermute x2, starting transfers between devices, swap(): return lax.ppermute(value, 'core', [(0, 1), (1, 0)])  12.4 us
    dot_general x2, matrix products, term(): lax.dot_general(border_tiles, bound, (((0,), (0,)), ((), ())), preferred_...  11.7 us
    ppermute x6, starting transfers between devices, along_z(): return lax.ppermute(value, ('z', 'core'), pairs)  10.4 us
    ppermute x6, waiting for transfers between devices, along_z(): return lax.ppermute(value, ('z', 'core'), pairs)  6.43 us
  transfers between devices with their start and end apart: 44, of which 22 were waited for; matrix products, arithmetic and copies ran while one was open for 7% of the time, Pallas kernels for 11%

profile of v12, /device:TPU:1, one launch (start us, length us, event | category | flops | bytes accessed | tf_op | source)
XLA Modules:
  0.0 210.7 jit_solution(8964642584273373930)
XLA Ops:
  6.5 3.3 %stage.1 = (bf16[2560,256]{1,0:T(8,128)(2,1)}, bf16[2064,256]{1,0:T(8,128)(2,1)}) custom-call(bf16[6,512,256]{2,1,0:T(8,128)(2,1)} %lower_ref.1, bf16[4,256,512]{2,1,0:T(8,128)(2,1)} %diag_ref.1, s32[1,128]{1,0:T(1,128)} %bitcast.56), custom_call_target="tpu_custom_call" | custom-call | bytes 6291456 | tf_op jit(solution)/shard_map/stage/pallas_call | solution.py:323
  10.6 5.9 %fusion.6 = bf16[4,256,512]{2,1,0:T(8,128)(2,1)S(1)} fusion(f32[4,256,1024]{2,1,0:T(8,128)} %param.6, s32[]{:T(128)S(6)} %select_n.30, bf16[2048,4,256]{2,1,0:T(4,128)(2,1)} %param.8, bf16[2048,1024]{1,0:T(8,128)(2,1)} %param.7, f32[]{:T(128)S(6)} %select_n.28), kind=kOutput, calls=%fused_computation.7 | convolution fusion | flops 2149056512 | bytes 9438720 | tf_op jit(solution)/shard_map/dot_general | solution.py:449
  18.0 5.8 %fusion.7 = bf16[4,256,512]{2,1,0:T(8,128)(2,1)S(1)} fusion(f32[4,256,1024]{2,1,0:T(8,128)} %param.6, s32[]{:T(128)S(6)} %select_n.29, bf16[2048,4,256]{2,1,0:T(4,128)(2,1)} %param.8, bf16[2048,1024]{1,0:T(8,128)(2,1)} %param.7, f32[]{:T(128)S(6)} %select_n.28), kind=kOutput, calls=%fused_computation.9 | convolution fusion | flops 2149056512 | bytes 9438720 | tf_op jit(solution)/shard_map/dot_general | solution.py:449
  27.9 2.5 %collective-permute-start.6 = (bf16[1,256,128]{2,1,0:T(8,128)(2,1)S(1)}, bf16[1,256,128]{2,1,0:T(8,128)(2,1)S(1)}, u32[]{:S(2)}, u32[]{:S(2)}) collective-permute-start(bf16[1,256,128]{2,1,0:T(8,128)(2,1)S(1)} %get-tuple-element.73), channel_id=1, source_target_pairs={{0,2},{1,3},{2,0},{3,1},{4,6},{5,7},{6,4},{7,5},{8,10},{9,11},{10,... | collective-permute-start | bytes 196616 | tf_op jit(solution)/shard_map/ppermute | solution.py:18
  33.8 10.9 %collective-permute-start.11 = (bf16[256,512]{1,0:T(8,128)(2,1)S(1)}, bf16[256,512]{1,0:T(8,128)(2,1)S(1)}, u32[]{:S(2)}, u32[]{:S(2)}) collective-permute-start(bf16[256,512]{1,0:T(8,128)(2,1)S(1)} %slice_bitcast_fusion.3.refs_6_), channel_id=1, source_target_pairs={{0,16},{16,0},{1,17},{17,1},{2,18},{18,2},{3,19},{19,3},{4,20},{20... | collective-permute-start | bytes 786440 | tf_op jit(solution)/shard_map/ppermute | solution.py:22
  44.8 3.4 %collective-permute-start.10 = (bf16[256,512]{1,0:T(8,128)(2,1)S(1)}, bf16[256,512]{1,0:T(8,128)(2,1)S(1)}, u32[]{:S(2)}, u32[]{:S(2)}) collective-permute-start(bf16[256,512]{1,0:T(8,128)(2,1)S(1)} %gate.2), channel_id=1, source_target_pairs={{16,112},{48,16},{80,48},{112,80},{17,113},{49,17},{81,49},{113,81... | collective-permute-start | bytes 786440 | tf_op jit(solution)/shard_map/ppermute | solution.py:27
  50.1 3.1 %collective-permute-start.9 = (bf16[256,512]{1,0:T(8,128)(2,1)S(1)}, bf16[256,512]{1,0:T(8,128)(2,1)S(1)}, u32[]{:S(2)}, u32[]{:S(2)}) collective-permute-start(bf16[256,512]{1,0:T(8,128)(2,1)S(1)} %gate.2), channel_id=1, source_target_pairs={{16,80},{48,112},{80,16},{112,48},{17,81},{49,113},{81,17},{113,49... | collective-permute-start | bytes 786440 | tf_op jit(solution)/shard_map/ppermute | solution.py:27
  53.3 6.4 %collective-permute-done.8.refs_3_ = bf16[256,512]{1,0:T(8,128)(2,1)S(1)} collective-permute-done((bf16[256,512]{1,0:T(8,128)(2,1)S(1)}, bf16[256,512]{1,0:T(8,128)(2,1)S(1)}, u32[]{:S(2)}, u32[]{:S(2)}) %collective-permute-start.8) | collective-permute-done | bytes 262176 | tf_op jit(solution)/shard_map/ppermute | solution.py:27
  62.6 2.6 %collective-permute-start.13 = (bf16[512,256]{1,0:T(8,128)(2,1)S(1)}, bf16[512,256]{1,0:T(8,128)(2,1)S(1)}, u32[]{:S(2)}, u32[]{:S(2)}) collective-permute-start(bf16[512,256]{1,0:T(8,128)(2,1)S(1)} %get-tuple-element.37), channel_id=1, source_target_pairs={{0,8},{4,12},{8,0},{12,4},{1,9},{5,13},{9,1},{13,5},{2,10},{6,14},... | collective-permute-start | bytes 786440 | tf_op jit(solution)/shard_map/ppermute | solution.py:18
  68.2 3.9 %collective-permute-done.13.v2 = bf16[512,256]{1,0:T(8,128)(2,1)S(1)} collective-permute-done((bf16[512,256]{1,0:T(8,128)(2,1)S(1)}, bf16[512,256]{1,0:T(8,128)(2,1)S(1)}, u32[]{:S(2)}, u32[]{:S(2)}) %collective-permute-start.13) | collective-permute-done | bytes 262176 | tf_op jit(solution)/shard_map/ppermute | solution.py:18
  73.6 2.6 %collective-permute-start.16 = (bf16[128,256]{1,0:T(8,128)(2,1)S(1)}, bf16[128,256]{1,0:T(8,128)(2,1)S(1)}, u32[]{:S(2)}, u32[]{:S(2)}) collective-permute-start(bf16[128,256]{1,0:T(8,128)(2,1)S(1)} %get-tuple-element.41), channel_id=1, source_target_pairs={{0,2},{1,3},{2,0},{3,1},{4,6},{5,7},{6,4},{7,5},{8,10},{9,11},{10,... | collective-permute-start | bytes 196616 | tf_op jit(solution)/shard_map/ppermute | solution.py:18
  86.0 2.6 %lower_step.6 = (bf16[128,1024]{1,0:T(8,128)(2,1)S(1)}, bf16[128,1024]{1,0:T(8,128)(2,1)S(1)}) custom-call(s32[4]{0:T(128)S(1)} %pad_add_fusion.place_ref.refs_0_, bf16[128,256]{1,0:T(8,128)(2,1)S(1)} %add_convert_fusion.1._.refs_1_, bf16[128,256]{1,0:T(8,128)(2,1)S(1)} %collective-permute-done.18.refs_2_, ...), custom_call_target="tpu_custom_call" | custom-call | flops 268435456 | bytes 4194304 | tf_op jit(solution)/shard_map/lower_step/pallas_call | solution.py:191
  92.4 2.7 %collective-permute-start.28 = (bf16[2,256,128]{2,1,0:T(8,128)(2,1)S(1)}, bf16[2,256,128]{2,1,0:T(8,128)(2,1)S(1)}, u32[]{:S(2)}, u32[]{:S(2)}) collective-permute-start(bf16[2,256,128]{2,1,0:T(8,128)(2,1)S(1)} %get-tuple-element.48), channel_id=1, source_target_pairs={{0,2},{1,3},{2,0},{3,1},{4,6},{5,7},{6,4},{7,5},{8,10},{9,11},{10,... | collective-permute-start | bytes 393224 | tf_op jit(solution)/shard_map/ppermute | solution.py:18
  96.6 2.2 %collective-permute-start.29 = (bf16[2,256,128]{2,1,0:T(8,128)(2,1)S(1)}, bf16[2,256,128]{2,1,0:T(8,128)(2,1)S(1)}, u32[]{:S(2)}, u32[]{:S(2)}) collective-permute-start(bf16[2,256,128]{2,1,0:T(8,128)(2,1)S(1)} %get-tuple-element.49), channel_id=1, source_target_pairs={{0,3},{1,0},{2,1},{3,2},{4,7},{5,4},{6,5},{7,6},{8,11},{9,8},{10,9... | collective-permute-start | bytes 393224 | tf_op jit(solution)/shard_map/ppermute | solution.py:18
  102.2 3.1 %collective-permute-start.25 = (bf16[128,1024]{1,0:T(8,128)(2,1)S(1)}, bf16[128,1024]{1,0:T(8,128)(2,1)S(1)}, u32[]{:S(2)}, u32[]{:S(2)}) collective-permute-start(bf16[128,1024]{1,0:T(8,128)(2,1)S(1)} %diag_step.2.refs_0_), channel_id=1, source_target_pairs={{0,8},{4,12},{8,0},{12,4},{1,9},{5,13},{9,1},{13,5},{2,10},{6,14},... | collective-permute-start | bytes 786440 | tf_op jit(solution)/shard_map/ppermute | solution.py:18
  107.3 2.5 %lower_step.7 = (f32[128,1024]{1,0:T(8,128)S(1)}, bf16[128,1024]{1,0:T(8,128)(2,1)}) custom-call(bf16[128,1024]{1,0:T(8,128)(2,1)S(1)} %get-tuple-element.45.refs_0_.x3, f32[128,1024]{1,0:T(8,128)S(1)} %get-tuple-element.64.refs_1_, bf16[2,4,2560,256]{3,2,1,0:T(8,128)(2,1)} %bitcast.46), custom_call_target="tpu_custom_call" | custom-call | flops 268435456 | bytes 4194304 | tf_op jit(solution)/shard_map/lower_step/pallas_call | solution.py:191
  109.8 6.3 %collective-permute-done.25.refs_2_ = bf16[128,1024]{1,0:T(8,128)(2,1)S(1)} collective-permute-done((bf16[128,1024]{1,0:T(8,128)(2,1)S(1)}, bf16[128,1024]{1,0:T(8,128)(2,1)S(1)}, u32[]{:S(2)}, u32[]{:S(2)}) %collective-permute-start.25) | collective-permute-done | bytes 262176 | tf_op jit(solution)/shard_map/ppermute | solution.py:18
  116.1 2.0 lower_step.8
  119.6 2.5 %collective-permute-start.32 = (bf16[128,1024]{1,0:T(8,128)(2,1)S(1)}, bf16[128,1024]{1,0:T(8,128)(2,1)S(1)}, u32[]{:S(2)}, u32[]{:S(2)}) collective-permute-start(bf16[128,1024]{1,0:T(8,128)(2,1)S(1)} %get-tuple-element.51.v0), channel_id=1, source_target_pairs={{0,96},{32,0},{64,32},{96,64},{1,97},{33,1},{65,33},{97,65},{2,98}... | collective-permute-start | bytes 786440 | tf_op jit(solution)/shard_map/ppermute | solution.py:18
  122.1 10.9 %collective-permute-done.30.v1 = bf16[128,1024]{1,0:T(8,128)(2,1)S(1)} collective-permute-done((bf16[128,1024]{1,0:T(8,128)(2,1)S(1)}, bf16[128,1024]{1,0:T(8,128)(2,1)S(1)}, u32[]{:S(2)}, u32[]{:S(2)}) %collective-permute-start.30) | collective-permute-done | bytes 262176 | tf_op jit(solution)/shard_map/ppermute | solution.py:18
  135.9 2.6 %collective-permute-start.34 = (bf16[128,1024]{1,0:T(8,128)(2,1)S(1)}, bf16[128,1024]{1,0:T(8,128)(2,1)S(1)}, u32[]{:S(2)}, u32[]{:S(2)}) collective-permute-start(bf16[128,1024]{1,0:T(8,128)(2,1)S(1)} %diag_step.3.refs_0_), channel_id=1, source_target_pairs={{0,8},{4,12},{8,0},{12,4},{1,9},{5,13},{9,1},{13,5},{2,10},{6,14},... | collective-permute-start | bytes 786440 | tf_op jit(solution)/shard_map/ppermute | solution.py:18
  139.2 2.5 %lower_step.9 = (f32[128,1024]{1,0:T(8,128)S(1)}, bf16[128,1024]{1,0:T(8,128)(2,1)}) custom-call(bf16[128,1024]{1,0:T(8,128)(2,1)S(1)} %get-tuple-element.45.refs_0_.x3, f32[128,1024]{1,0:T(8,128)S(1)} %get-tuple-element.63.refs_1_, bf16[2,4,2064,256]{3,2,1,0:T(8,128)(2,1)} %bitcast.49), custom_call_target="tpu_custom_call" | custom-call | flops 268435456 | bytes 4194304 | tf_op jit(solution)/shard_map/lower_step/pallas_call | solution.py:191
  141.7 2.5 %lower_step.10 = (f32[128,1024]{1,0:T(8,128)S(1)}, bf16[128,1024]{1,0:T(8,128)(2,1)}) custom-call(bf16[128,1024]{1,0:T(8,128)(2,1)S(1)} %get-tuple-element.52.refs_0_.x2, f32[128,1024]{1,0:T(8,128)S(1)} %get-tuple-element.53.refs_1_, bf16[2,4,2064,256]{3,2,1,0:T(8,128)(2,1)} %bitcast.50), custom_call_target="tpu_custom_call" | custom-call | flops 268435456 | bytes 4194304 | tf_op jit(solution)/shard_map/lower_step/pallas_call | solution.py:191
  145.5 3.7 %collective-permute-done.34.refs_2_ = bf16[128,1024]{1,0:T(8,128)(2,1)S(1)} collective-permute-done((bf16[128,1024]{1,0:T(8,128)(2,1)S(1)}, bf16[128,1024]{1,0:T(8,128)(2,1)S(1)}, u32[]{:S(2)}, u32[]{:S(2)}) %collective-permute-start.34) | collective-permute-done | bytes 262176 | tf_op jit(solution)/shard_map/ppermute | solution.py:18
  150.5 2.0 lower_step.11
  154.0 2.5 %collective-permute-start.37 = (bf16[128,1024]{1,0:T(8,128)(2,1)S(1)}, bf16[128,1024]{1,0:T(8,128)(2,1)S(1)}, u32[]{:S(2)}, u32[]{:S(2)}) collective-permute-start(bf16[128,1024]{1,0:T(8,128)(2,1)S(1)} %get-tuple-element.57.v0), channel_id=1, source_target_pairs={{0,64},{32,96},{64,0},{96,32},{1,65},{33,97},{65,1},{97,33},{2,66}... | collective-permute-start | bytes 786440 | tf_op jit(solution)/shard_map/ppermute | solution.py:18
  160.1 7.0 %collective-permute-done.37.v2 = bf16[128,1024]{1,0:T(8,128)(2,1)S(1)} collective-permute-done((bf16[128,1024]{1,0:T(8,128)(2,1)S(1)}, bf16[128,1024]{1,0:T(8,128)(2,1)S(1)}, u32[]{:S(2)}, u32[]{:S(2)}) %collective-permute-start.37) | collective-permute-done | bytes 262176 | tf_op jit(solution)/shard_map/ppermute | solution.py:18
  167.4 2.5 %last_step.1 = (bf16[128,256]{1,0:T(8,128)(2,1)S(1)}, bf16[128,256]{1,0:T(8,128)(2,1)S(1)}, bf16[128,256]{1,0:T(8,128)(2,1)S(1)}, bf16[128,256]{1,0:T(8,128)(2,1)S(1)}) custom-call(s32[4]{0:T(128)S(1)} %pad_add_fusion.place_ref.refs_0_, bf16[128,1024]{1,0:T(8,128)(2,1)S(1)} %get-tuple-element.57.v0, bf16[128,1024]{1,0:T(8,128)(2,1)S(1)} %collective-permute-done.36.v1, ...), custom_call_target="tpu_custom_call" | custom-call | flops 268435456 | bytes 4194304 | tf_op jit(solution)/shard_map/last_step/pallas_call | solution.py:270
  169.8 2.1 collective-permute-start.39
  171.9 2.9 %collective-permute-start.40 = (bf16[128,256]{1,0:T(8,128)(2,1)S(1)}, bf16[128,256]{1,0:T(8,128)(2,1)S(1)}, u32[]{:S(2)}, u32[]{:S(2)}) collective-permute-start(bf16[128,256]{1,0:T(8,128)(2,1)S(1)} %get-tuple-element.60), channel_id=1, source_target_pairs={{0,8},{4,12},{8,0},{12,4},{1,9},{5,13},{9,1},{13,5},{2,10},{6,14},... | collective-permute-start | bytes 196616 | tf_op jit(solution)/shard_map/ppermute | solution.py:18
  175.0 3.0 %pack_known.1 = (bf16[2048,128]{1,0:T(8,128)(2,1)S(1)}, bf16[2048,256]{1,0:T(8,128)(2,1)S(1)}) custom-call(s32[4]{0:T(128)S(1)} %pad_add_fusion.place_ref.refs_0_, s32[4,1,256]{2,1,0:T(1,128)S(1)} %reshape.61.target_ref, bf16[128,1024]{1,0:T(8,128)(2,1)S(1)} %get-tuple-element.55.x1, bf16[128,1024]{1,0:T(8,128)(2,1)S(1)} %get-tuple-element.52.refs_0_.x2, ...), custom_call_target="tpu_custom_call" | custom-call | flops 402653184 | bytes 2097152 | tf_op jit(solution)/shard_map/pack_known/pallas_call | solution.py:359
  179.2 23.1 %all_to_all.5 = bf16[128,16,128]{2,1,0:T(8,128)(2,1)S(1)} all-to-all(bf16[128,16,128]{2,1,0:T(8,128)(2,1)S(1)} %bitcast.43), channel_id=1, replica_groups=mesh['z'=4,'core'=2,'y'=4,'x'=4] {'z','core','y','x'}, dimensions={0} | all-to-all | bytes 1048576 | tf_op jit(solution)/shard_map/all_to_all | solution.py:489
  (104 shorter events, 55.3 us)
Async XLA Ops:
  6.5 79.5 %all-gather.7.cloned.1.call-start = ((), (), s32[]{:S(2)}) async-start(), calls=%async_computation.2 | async-start | bytes 11796480 | tf_op jit(solution)/shard_map/all_gather | solution.py:425
  9.9 129.3 %all-gather.5.cloned.1.call-start = ((), (), s32[]{:S(2)}) async-start(), calls=%async_computation.1 | async-start | bytes 9510912 | tf_op jit(solution)/shard_map/all_gather | solution.py:425
  16.5 7.4 %collective-permute-start = (bf16[4,256,512]{2,1,0:T(8,128)(2,1)S(1)}, bf16[4,256,512]{2,1,0:T(8,128)(2,1)S(1)}, u32[]{:S(2)}, u32[]{:S(2)}) collective-permute-start(bf16[4,256,512]{2,1,0:T(8,128)(2,1)S(1)} %fusion.6), channel_id=1, source_target_pairs={{0,16},{16,0},{1,17},{17,1},{2,18},{18,2},{3,19},{19,3},{4,20},{20... | collective-permute-start | bytes 3145736 | tf_op jit(solution)/shard_map/ppermute | solution.py:22
  26.6 18.2 %collective-permute-start.5 = (bf16[1,256,128]{2,1,0:T(8,128)(2,1)S(1)}, bf16[1,256,128]{2,1,0:T(8,128)(2,1)S(1)}, u32[]{:S(2)}, u32[]{:S(2)}) collective-permute-start(bf16[1,256,128]{2,1,0:T(8,128)(2,1)S(1)} %get-tuple-element.74), channel_id=1, source_target_pairs={{0,1},{1,2},{2,3},{3,0},{4,5},{5,6},{6,7},{7,4},{8,9},{9,10},{10,1... | collective-permute-start | bytes 196616 | tf_op jit(solution)/shard_map/ppermute | solution.py:18
  27.9 16.9 %collective-permute-start.6 = (bf16[1,256,128]{2,1,0:T(8,128)(2,1)S(1)}, bf16[1,256,128]{2,1,0:T(8,128)(2,1)S(1)}, u32[]{:S(2)}, u32[]{:S(2)}) collective-permute-start(bf16[1,256,128]{2,1,0:T(8,128)(2,1)S(1)} %get-tuple-element.73), channel_id=1, source_target_pairs={{0,2},{1,3},{2,0},{3,1},{4,6},{5,7},{6,4},{7,5},{8,10},{9,11},{10,... | collective-permute-start | bytes 196616 | tf_op jit(solution)/shard_map/ppermute | solution.py:18
  30.4 14.4 %collective-permute-start.7 = (bf16[1,256,128]{2,1,0:T(8,128)(2,1)S(1)}, bf16[1,256,128]{2,1,0:T(8,128)(2,1)S(1)}, u32[]{:S(2)}, u32[]{:S(2)}) collective-permute-start(bf16[1,256,128]{2,1,0:T(8,128)(2,1)S(1)} %get-tuple-element.72), channel_id=1, source_target_pairs={{0,3},{1,0},{2,1},{3,2},{4,7},{5,4},{6,5},{7,6},{8,11},{9,8},{10,9... | collective-permute-start | bytes 196616 | tf_op jit(solution)/shard_map/ppermute | solution.py:18
  31.6 13.3 %collective-permute-start.4 = (bf16[8,512]{1,0:T(8,128)(2,1)S(1)}, bf16[8,512]{1,0:T(8,128)(2,1)S(1)}, u32[]{:S(2)}, u32[]{:S(2)}) collective-permute-start(bf16[8,512]{1,0:T(8,128)(2,1)S(1)} %slice_add_fusion), channel_id=1, source_target_pairs={{0,16},{1,17},{2,18},{3,19},{4,20},{5,21},{6,22},{7,23},{8,24},{9,... | collective-permute-start | bytes 24584 | tf_op jit(solution)/shard_map/ppermute | solution.py:466
  33.8 19.5 %collective-permute-start.11 = (bf16[256,512]{1,0:T(8,128)(2,1)S(1)}, bf16[256,512]{1,0:T(8,128)(2,1)S(1)}, u32[]{:S(2)}, u32[]{:S(2)}) collective-permute-start(bf16[256,512]{1,0:T(8,128)(2,1)S(1)} %slice_bitcast_fusion.3.refs_6_), channel_id=1, source_target_pairs={{0,16},{16,0},{1,17},{17,1},{2,18},{18,2},{3,19},{19,3},{4,20},{20... | collective-permute-start | bytes 786440 | tf_op jit(solution)/shard_map/ppermute | solution.py:22
  44.8 8.5 %collective-permute-start.10 = (bf16[256,512]{1,0:T(8,128)(2,1)S(1)}, bf16[256,512]{1,0:T(8,128)(2,1)S(1)}, u32[]{:S(2)}, u32[]{:S(2)}) collective-permute-start(bf16[256,512]{1,0:T(8,128)(2,1)S(1)} %gate.2), channel_id=1, source_target_pairs={{16,112},{48,16},{80,48},{112,80},{17,113},{49,17},{81,49},{113,81... | collective-permute-start | bytes 786440 | tf_op jit(solution)/shard_map/ppermute | solution.py:27
  48.2 11.5 %collective-permute-start.8 = (bf16[256,512]{1,0:T(8,128)(2,1)S(1)}, bf16[256,512]{1,0:T(8,128)(2,1)S(1)}, u32[]{:S(2)}, u32[]{:S(2)}) collective-permute-start(bf16[256,512]{1,0:T(8,128)(2,1)S(1)} %gate.2), channel_id=1, source_target_pairs={{16,48},{48,80},{80,112},{112,16},{17,49},{49,81},{81,113},{113,17... | collective-permute-start | bytes 786440 | tf_op jit(solution)/shard_map/ppermute | solution.py:27
  50.1 9.6 %collective-permute-start.9 = (bf16[256,512]{1,0:T(8,128)(2,1)S(1)}, bf16[256,512]{1,0:T(8,128)(2,1)S(1)}, u32[]{:S(2)}, u32[]{:S(2)}) collective-permute-start(bf16[256,512]{1,0:T(8,128)(2,1)S(1)} %gate.2), channel_id=1, source_target_pairs={{16,80},{48,112},{80,16},{112,48},{17,81},{49,113},{81,17},{113,49... | collective-permute-start | bytes 786440 | tf_op jit(solution)/shard_map/ppermute | solution.py:27
  61.2 7.0 %collective-permute-start.12 = (bf16[512,256]{1,0:T(8,128)(2,1)S(1)}, bf16[512,256]{1,0:T(8,128)(2,1)S(1)}, u32[]{:S(2)}, u32[]{:S(2)}) collective-permute-start(bf16[512,256]{1,0:T(8,128)(2,1)S(1)} %get-tuple-element.36), channel_id=1, source_target_pairs={{0,4},{4,8},{8,12},{12,0},{1,5},{5,9},{9,13},{13,1},{2,6},{6,10},{... | collective-permute-start | bytes 786440 | tf_op jit(solution)/shard_map/ppermute | solution.py:18
  62.6 9.5 %collective-permute-start.13 = (bf16[512,256]{1,0:T(8,128)(2,1)S(1)}, bf16[512,256]{1,0:T(8,128)(2,1)S(1)}, u32[]{:S(2)}, u32[]{:S(2)}) collective-permute-start(bf16[512,256]{1,0:T(8,128)(2,1)S(1)} %get-tuple-element.37), channel_id=1, source_target_pairs={{0,8},{4,12},{8,0},{12,4},{1,9},{5,13},{9,1},{13,5},{2,10},{6,14},... | collective-permute-start | bytes 786440 | tf_op jit(solution)/shard_map/ppermute | solution.py:18
  88.6 8.0 %collective-permute-start.22 = (bf16[128,1024]{1,0:T(8,128)(2,1)S(1)}, bf16[128,1024]{1,0:T(8,128)(2,1)S(1)}, u32[]{:S(2)}, u32[]{:S(2)}) collective-permute-start(bf16[128,1024]{1,0:T(8,128)(2,1)S(1)} %get-tuple-element.44.v0), channel_id=1, source_target_pairs={{0,64},{32,96},{64,0},{96,32},{1,65},{33,97},{65,1},{97,33},{2,66}... | collective-permute-start | bytes 786440 | tf_op jit(solution)/shard_map/ppermute | solution.py:18
  89.3 10.2 %collective-permute-start.21 = (bf16[128,1024]{1,0:T(8,128)(2,1)S(1)}, bf16[128,1024]{1,0:T(8,128)(2,1)S(1)}, u32[]{:S(2)}, u32[]{:S(2)}) collective-permute-start(bf16[128,1024]{1,0:T(8,128)(2,1)S(1)} %get-tuple-element.44.v0), channel_id=1, source_target_pairs={{0,32},{32,64},{64,96},{96,0},{1,33},{33,65},{65,97},{97,1},{2,34}... | collective-permute-start | bytes 786440 | tf_op jit(solution)/shard_map/ppermute | solution.py:18
  91.0 8.5 %collective-permute-start.23 = (bf16[128,1024]{1,0:T(8,128)(2,1)S(1)}, bf16[128,1024]{1,0:T(8,128)(2,1)S(1)}, u32[]{:S(2)}, u32[]{:S(2)}) collective-permute-start(bf16[128,1024]{1,0:T(8,128)(2,1)S(1)} %get-tuple-element.44.v0), channel_id=1, source_target_pairs={{0,96},{32,0},{64,32},{96,64},{1,97},{33,1},{65,33},{97,65},{2,98}... | collective-permute-start | bytes 786440 | tf_op jit(solution)/shard_map/ppermute | solution.py:18
  92.1 13.2 %collective-permute-start.27 = (bf16[2,256,128]{2,1,0:T(8,128)(2,1)S(1)}, bf16[2,256,128]{2,1,0:T(8,128)(2,1)S(1)}, u32[]{:S(2)}, u32[]{:S(2)}) collective-permute-start(bf16[2,256,128]{2,1,0:T(8,128)(2,1)S(1)} %get-tuple-element.47), channel_id=1, source_target_pairs={{0,1},{1,2},{2,3},{3,0},{4,5},{5,6},{6,7},{7,4},{8,9},{9,10},{10,1... | collective-permute-start | bytes 393224 | tf_op jit(solution)/shard_map/ppermute | solution.py:18
  92.4 13.5 %collective-permute-start.28 = (bf16[2,256,128]{2,1,0:T(8,128)(2,1)S(1)}, bf16[2,256,128]{2,1,0:T(8,128)(2,1)S(1)}, u32[]{:S(2)}, u32[]{:S(2)}) collective-permute-start(bf16[2,256,128]{2,1,0:T(8,128)(2,1)S(1)} %get-tuple-element.48), channel_id=1, source_target_pairs={{0,2},{1,3},{2,0},{3,1},{4,6},{5,7},{6,4},{7,5},{8,10},{9,11},{10,... | collective-permute-start | bytes 393224 | tf_op jit(solution)/shard_map/ppermute | solution.py:18
  96.6 9.9 %collective-permute-start.29 = (bf16[2,256,128]{2,1,0:T(8,128)(2,1)S(1)}, bf16[2,256,128]{2,1,0:T(8,128)(2,1)S(1)}, u32[]{:S(2)}, u32[]{:S(2)}) collective-permute-start(bf16[2,256,128]{2,1,0:T(8,128)(2,1)S(1)} %get-tuple-element.49), channel_id=1, source_target_pairs={{0,3},{1,0},{2,1},{3,2},{4,7},{5,4},{6,5},{7,6},{8,11},{9,8},{10,9... | collective-permute-start | bytes 393224 | tf_op jit(solution)/shard_map/ppermute | solution.py:18
  101.3 8.5 %collective-permute-start.24 = (bf16[128,1024]{1,0:T(8,128)(2,1)S(1)}, bf16[128,1024]{1,0:T(8,128)(2,1)S(1)}, u32[]{:S(2)}, u32[]{:S(2)}) collective-permute-start(bf16[128,1024]{1,0:T(8,128)(2,1)S(1)} %diag_step.2.refs_0_), channel_id=1, source_target_pairs={{0,4},{4,8},{8,12},{12,0},{1,5},{5,9},{9,13},{13,1},{2,6},{6,10},{... | collective-permute-start | bytes 786440 | tf_op jit(solution)/shard_map/ppermute | solution.py:18
  102.2 14.0 %collective-permute-start.25 = (bf16[128,1024]{1,0:T(8,128)(2,1)S(1)}, bf16[128,1024]{1,0:T(8,128)(2,1)S(1)}, u32[]{:S(2)}, u32[]{:S(2)}) collective-permute-start(bf16[128,1024]{1,0:T(8,128)(2,1)S(1)} %diag_step.2.refs_0_), channel_id=1, source_target_pairs={{0,8},{4,12},{8,0},{12,4},{1,9},{5,13},{9,1},{13,5},{2,10},{6,14},... | collective-permute-start | bytes 786440 | tf_op jit(solution)/shard_map/ppermute | solution.py:18
  105.2 10.9 %collective-permute-start.26 = (bf16[128,1024]{1,0:T(8,128)(2,1)S(1)}, bf16[128,1024]{1,0:T(8,128)(2,1)S(1)}, u32[]{:S(2)}, u32[]{:S(2)}) collective-permute-start(bf16[128,1024]{1,0:T(8,128)(2,1)S(1)} %diag_step.2.refs_0_), channel_id=1, source_target_pairs={{0,12},{4,0},{8,4},{12,8},{1,13},{5,1},{9,5},{13,9},{2,14},{6,2},{... | collective-permute-start | bytes 786440 | tf_op jit(solution)/shard_map/ppermute | solution.py:18
  118.2 14.8 %collective-permute-start.30 = (bf16[128,1024]{1,0:T(8,128)(2,1)S(1)}, bf16[128,1024]{1,0:T(8,128)(2,1)S(1)}, u32[]{:S(2)}, u32[]{:S(2)}) collective-permute-start(bf16[128,1024]{1,0:T(8,128)(2,1)S(1)} %get-tuple-element.51.v0), channel_id=1, source_target_pairs={{0,32},{32,64},{64,96},{96,0},{1,33},{33,65},{65,97},{97,1},{2,34}... | collective-permute-start | bytes 786440 | tf_op jit(solution)/shard_map/ppermute | solution.py:18
  119.6 13.4 %collective-permute-start.31 = (bf16[128,1024]{1,0:T(8,128)(2,1)S(1)}, bf16[128,1024]{1,0:T(8,128)(2,1)S(1)}, u32[]{:S(2)}, u32[]{:S(2)}) collective-permute-start(bf16[128,1024]{1,0:T(8,128)(2,1)S(1)} %get-tuple-element.51.v0), channel_id=1, source_target_pairs={{0,64},{32,96},{64,0},{96,32},{1,65},{33,97},{65,1},{97,33},{2,66}... | collective-permute-start | bytes 786440 | tf_op jit(solution)/shard_map/ppermute | solution.py:18
  119.6 14.3 %collective-permute-start.32 = (bf16[128,1024]{1,0:T(8,128)(2,1)S(1)}, bf16[128,1024]{1,0:T(8,128)(2,1)S(1)}, u32[]{:S(2)}, u32[]{:S(2)}) collective-permute-start(bf16[128,1024]{1,0:T(8,128)(2,1)S(1)} %get-tuple-element.51.v0), channel_id=1, source_target_pairs={{0,96},{32,0},{64,32},{96,64},{1,97},{33,1},{65,33},{97,65},{2,98}... | collective-permute-start | bytes 786440 | tf_op jit(solution)/shard_map/ppermute | solution.py:18
  135.8 9.7 %collective-permute-start.33 = (bf16[128,1024]{1,0:T(8,128)(2,1)S(1)}, bf16[128,1024]{1,0:T(8,128)(2,1)S(1)}, u32[]{:S(2)}, u32[]{:S(2)}) collective-permute-start(bf16[128,1024]{1,0:T(8,128)(2,1)S(1)} %diag_step.3.refs_0_), channel_id=1, source_target_pairs={{0,4},{4,8},{8,12},{12,0},{1,5},{5,9},{9,13},{13,1},{2,6},{6,10},{... | collective-permute-start | bytes 786440 | tf_op jit(solution)/shard_map/ppermute | solution.py:18
  135.9 13.2 %collective-permute-start.34 = (bf16[128,1024]{1,0:T(8,128)(2,1)S(1)}, bf16[128,1024]{1,0:T(8,128)(2,1)S(1)}, u32[]{:S(2)}, u32[]{:S(2)}) collective-permute-start(bf16[128,1024]{1,0:T(8,128)(2,1)S(1)} %diag_step.3.refs_0_), channel_id=1, source_target_pairs={{0,8},{4,12},{8,0},{12,4},{1,9},{5,13},{9,1},{13,5},{2,10},{6,14},... | collective-permute-start | bytes 786440 | tf_op jit(solution)/shard_map/ppermute | solution.py:18
  138.5 12.0 %collective-permute-start.35 = (bf16[128,1024]{1,0:T(8,128)(2,1)S(1)}, bf16[128,1024]{1,0:T(8,128)(2,1)S(1)}, u32[]{:S(2)}, u32[]{:S(2)}) collective-permute-start(bf16[128,1024]{1,0:T(8,128)(2,1)S(1)} %diag_step.3.refs_0_), channel_id=1, source_target_pairs={{0,12},{4,0},{8,4},{12,8},{1,13},{5,1},{9,5},{13,9},{2,14},{6,2},{... | collective-permute-start | bytes 786440 | tf_op jit(solution)/shard_map/ppermute | solution.py:18
  152.5 7.6 %collective-permute-start.36 = (bf16[128,1024]{1,0:T(8,128)(2,1)S(1)}, bf16[128,1024]{1,0:T(8,128)(2,1)S(1)}, u32[]{:S(2)}, u32[]{:S(2)}) collective-permute-start(bf16[128,1024]{1,0:T(8,128)(2,1)S(1)} %get-tuple-element.57.v0), channel_id=1, source_target_pairs={{0,32},{32,64},{64,96},{96,0},{1,33},{33,65},{65,97},{97,1},{2,34}... | collective-permute-start | bytes 786440 | tf_op jit(solution)/shard_map/ppermute | solution.py:18
  154.0 13.1 %collective-permute-start.37 = (bf16[128,1024]{1,0:T(8,128)(2,1)S(1)}, bf16[128,1024]{1,0:T(8,128)(2,1)S(1)}, u32[]{:S(2)}, u32[]{:S(2)}) collective-permute-start(bf16[128,1024]{1,0:T(8,128)(2,1)S(1)} %get-tuple-element.57.v0), channel_id=1, source_target_pairs={{0,64},{32,96},{64,0},{96,32},{1,65},{33,97},{65,1},{97,33},{2,66}... | collective-permute-start | bytes 786440 | tf_op jit(solution)/shard_map/ppermute | solution.py:18
  156.5 10.8 %collective-permute-start.38 = (bf16[128,1024]{1,0:T(8,128)(2,1)S(1)}, bf16[128,1024]{1,0:T(8,128)(2,1)S(1)}, u32[]{:S(2)}, u32[]{:S(2)}) collective-permute-start(bf16[128,1024]{1,0:T(8,128)(2,1)S(1)} %get-tuple-element.57.v0), channel_id=1, source_target_pairs={{0,96},{32,0},{64,32},{96,64},{1,97},{33,1},{65,33},{97,65},{2,98}... | collective-permute-start | bytes 786440 | tf_op jit(solution)/shard_map/ppermute | solution.py:18
  169.8 8.2 %collective-permute-start.39 = (bf16[128,256]{1,0:T(8,128)(2,1)S(1)}, bf16[128,256]{1,0:T(8,128)(2,1)S(1)}, u32[]{:S(2)}, u32[]{:S(2)}) collective-permute-start(bf16[128,256]{1,0:T(8,128)(2,1)S(1)} %get-tuple-element.59), channel_id=1, source_target_pairs={{0,4},{4,8},{8,12},{12,0},{1,5},{5,9},{9,13},{13,1},{2,6},{6,10},{... | collective-permute-start | bytes 196616 | tf_op jit(solution)/shard_map/ppermute | solution.py:18
  (14 other events, 68.2 us)
Sparse Core Ops, SparseCore 0:
  10.0 66.3 all-gather.6
  78.1 55.1 all-gather.4

commit v13 on v12

--- a/solution.py
+++ b/solution.py
@@ -133,6 +133,14 @@
         cost_estimate=cost(0, 1024),
         name="gate",
     )(*events, *arrays)
+
+
+def in_turn(value, events):
+    zero = [along_z(value, 0, by) for by in (1, 2, 3)]
+    token = lax.ppermute(sum(piece[:8] for piece in zero), "core", [(0, 1)])
+    (held,) = gate((token, *events), (value,))
+    one = [along_z(held, 1, by) for by in (1, 2, 3)]
+    return (value, *zero, *one)
 
 
 def turn(place, pieces, event):
@@ -239,22 +247,39 @@
 ]
 
 
-def diag_step(pieces, tiles, at):
-    def kernel(v0, v1, v2, v3, tiles_ref, out, vec, tile, sems):
+def diag_step(pieces, tiles, at, place=None):
+    count = len(pieces)
+    where = [] if place is None else [place]
+
+    def kernel(*refs):
+        place_ref = refs[0]
+        refs = refs[len(where) :]
+        tiles_ref, out, vec, tile, sems = refs[count:]
         copies = fetch_diag(tiles_ref, at, tile, sems)
-        vec[...] = add_up((v0, v1, v2, v3)).astype(BF16)
+        if where:
+
+            @pl.when(place_ref[0] == 0)
+            def _():
+                vec[...] = add_up(refs[:4]).astype(BF16)
+
+            @pl.when(place_ref[0] == 1)
+            def _():
+                vec[...] = add_up((refs[0], *refs[4:7])).astype(BF16)
+
+        else:
+            vec[...] = add_up(refs[:4]).astype(BF16)
         times_fetched(copies, vec, tile, out)
 
     return pl.pallas_call(
         kernel,
         out_shape=jax.ShapeDtypeStruct((128, 1024), BF16),
-        in_specs=[VMEM] * 4 + [HBM],
+        in_specs=[SCALARS] * len(where) + [VMEM] * count + [HBM],
         out_specs=VMEM,
         scratch_shapes=DIAG_SCRATCH,
         compiler_params=params(),
         cost_estimate=cost(2 * 128 * 1024 * 1024, 4 << 20),
         name="diag_step",
-    )(*pieces, tiles)
+    )(*where, *pieces, tiles)
 
 
 def last_step(place, pieces, tiles, at):
@@ -462,19 +487,17 @@
 
     near = deal(cut(both[2:3]), "x")
     own = both[3]
-    zero = [along_z(own, 0, by) for by in (1, 2, 3)]
-    token = lax.ppermute(sum(piece[:8] for piece in zero), "core", [(0, 1)])
-    (held,) = gate((token, *near[1:]), (own,))
-    one = [along_z(held, 1, by) for by in (1, 2, 3)]
+    over_z = in_turn(own, near[1:])
+    zero, one = over_z[1:4], over_z[4:]
     products = first_product(place, own, zero, one, inverse_diag[3], other, near[1:])
     over_x = deal(first_sum(place, deal(products, "y")), "x")
     quarter = sum(piece.astype(F32) for piece in over_x).astype(BF16)
     base2 = turn(place, near, quarter)[0]
     quarters = spread(quarter, "y")
     residual, x3 = lower_step(base2, quarters, early, 0, BF16, place)
-    over_z = spread(residual, "z")
-    base = turn(place, deal(gate((x3,), cut(both[:2])), "x"), over_z[2])
-    pieces = spread(diag_step(over_z, early, 1), "y")
+    over_z = in_turn(residual, ())
+    pieces = spread(diag_step(over_z, early, 1, place), "y")
+    base = turn(place, deal(gate((x3,), cut(both[:2])), "x"), pieces[0])
     base1, _ = lower_step(base[1], (x3,), early, 2, F32)
     residual, x2 = lower_step(base1, pieces, early, 3, BF16)
     over_z = spread(residual, "z")

time: 211 us -> 217 us (1.028)
  starting transfers between devices: 71.9 us -> 80.7 us
  waiting for transfers between devices: 53.8 us -> 50.3 us
    ppermute x33 -> x30, waiting for transfers between devices: 46.7 us -> 34.1 us  [shift(): return lax.ppermute(value, axis, [(i, (i + by) % 4) for i in range(4)])]
    ppermute x6 -> x12, starting transfers between devices: 10.4 us -> 21.7 us  [along_z(): return lax.ppermute(value, ('z', 'core'), pairs)]
    ppermute x1 -> x2, waiting for transfers between devices: 0.01 us -> 8.27 us  [in_turn(): token = lax.ppermute(sum((piece[:8] for piece in zero)), 'core', [(0, 1)])]
    ppermute x33 -> x30, starting transfers between devices: 47.7 us -> 43.9 us  [shift(): return lax.ppermute(value, axis, [(i, (i + by) % 4) for i in range(4)])]
    ppermute x6 -> x12, waiting for transfers between devices: 6.43 us -> 7.17 us  [along_z(): return lax.ppermute(value, ('z', 'core'), pairs)]
  transfers between devices with their start and end apart: 44 -> 48, of which waited for: 22 -> 21; matrix products, arithmetic and copies ran while one was open for 7% -> 7% of each run, Pallas kernels for 11% -> 11%
where the time goes in v13:
time: 217 us
  starting transfers between devices  80.7 us (37%)
  waiting for transfers between devices  50.3 us (23%)
  Pallas kernels  32.8 us (15%)
  blocking collectives  23 us (11%)
  between operations  13.9 us (6%)
  matrix products  11.7 us (5%)
  other arithmetic  2.36 us (1%)
    ppermute x30, starting transfers between devices, shift(): return lax.ppermute(value, axis, [(i, (i + by) % 4) for i in range(4)])  43.9 us
    ppermute x30, waiting for transfers between devices, shift(): return lax.ppermute(value, axis, [(i, (i + by) % 4) for i in range(4)])  34.1 us
    all_to_all x1, blocking collectives, local(): lax.all_to_all(packed, ('z', 'core', 'y', 'x'), split_axis=0, concat_axis...  23 us
    ppermute x12, starting transfers between devices, along_z(): return lax.ppermute(value, ('z', 'core'), pairs)  21.7 us
    pallas_call x6, Pallas kernels, lower_step(): pl.pallas_call(kernel, out_shape=(jax.ShapeDtypeStruct((128, 1024), dtype...  14.2 us
    ppermute x2, starting transfers between devices, swap(): return lax.ppermute(value, 'core', [(0, 1), (1, 0)])  12.4 us
    dot_general x2, matrix products, term(): lax.dot_general(border_tiles, bound, (((0,), (0,)), ((), ())), preferred_...  11.7 us
    ppermute x2, waiting for transfers between devices, in_turn(): token = lax.ppermute(sum((piece[:8] for piece in zero)), 'core', [(0, 1)])  8.27 us
  transfers between devices with their start and end apart: 48, of which 21 were waited for; matrix products, arithmetic and copies ran while one was open for 7% of the time, Pallas kernels for 11%

profile of v13, /device:TPU:1, one launch (start us, length us, event | category | flops | bytes accessed | tf_op | source)
XLA Modules:
  0.0 216.6 jit_solution(14102226060575910907)
XLA Ops:
  6.5 3.3 %stage.1 = (bf16[2560,256]{1,0:T(8,128)(2,1)}, bf16[2064,256]{1,0:T(8,128)(2,1)}) custom-call(bf16[6,512,256]{2,1,0:T(8,128)(2,1)} %lower_ref.1, bf16[4,256,512]{2,1,0:T(8,128)(2,1)} %diag_ref.1, s32[1,128]{1,0:T(1,128)} %bitcast.56), custom_call_target="tpu_custom_call" | custom-call | bytes 6291456 | tf_op jit(solution)/shard_map/stage/pallas_call | solution.py:348
  10.6 5.9 %fusion.6 = bf16[4,256,512]{2,1,0:T(8,128)(2,1)S(1)} fusion(f32[4,256,1024]{2,1,0:T(8,128)} %param.6, s32[]{:T(128)S(6)} %select_n.30, bf16[2048,4,256]{2,1,0:T(4,128)(2,1)} %param.8, bf16[2048,1024]{1,0:T(8,128)(2,1)} %param.7, f32[]{:T(128)S(6)} %select_n.28), kind=kOutput, calls=%fused_computation.7 | convolution fusion | flops 2149056512 | bytes 9438720 | tf_op jit(solution)/shard_map/dot_general | solution.py:474
  18.0 5.8 %fusion.7 = bf16[4,256,512]{2,1,0:T(8,128)(2,1)S(1)} fusion(f32[4,256,1024]{2,1,0:T(8,128)} %param.6, s32[]{:T(128)S(6)} %select_n.29, bf16[2048,4,256]{2,1,0:T(4,128)(2,1)} %param.8, bf16[2048,1024]{1,0:T(8,128)(2,1)} %param.7, f32[]{:T(128)S(6)} %select_n.28), kind=kOutput, calls=%fused_computation.9 | convolution fusion | flops 2149056512 | bytes 9438720 | tf_op jit(solution)/shard_map/dot_general | solution.py:474
  28.0 2.5 %collective-permute-start.6 = (bf16[1,256,128]{2,1,0:T(8,128)(2,1)S(1)}, bf16[1,256,128]{2,1,0:T(8,128)(2,1)S(1)}, u32[]{:S(2)}, u32[]{:S(2)}) collective-permute-start(bf16[1,256,128]{2,1,0:T(8,128)(2,1)S(1)} %get-tuple-element.73), channel_id=1, source_target_pairs={{0,2},{1,3},{2,0},{3,1},{4,6},{5,7},{6,4},{7,5},{8,10},{9,11},{10,... | collective-permute-start | bytes 196616 | tf_op jit(solution)/shard_map/ppermute | solution.py:18
  33.9 10.9 %collective-permute-start.11 = (bf16[256,512]{1,0:T(8,128)(2,1)S(1)}, bf16[256,512]{1,0:T(8,128)(2,1)S(1)}, u32[]{:S(2)}, u32[]{:S(2)}) collective-permute-start(bf16[256,512]{1,0:T(8,128)(2,1)S(1)} %slice_bitcast_fusion.3.refs_6_), channel_id=1, source_target_pairs={{0,16},{16,0},{1,17},{17,1},{2,18},{18,2},{3,19},{19,3},{4,20},{20... | collective-permute-start | bytes 786440 | tf_op jit(solution)/shard_map/ppermute | solution.py:22
  44.9 3.4 %collective-permute-start.10 = (bf16[256,512]{1,0:T(8,128)(2,1)S(1)}, bf16[256,512]{1,0:T(8,128)(2,1)S(1)}, u32[]{:S(2)}, u32[]{:S(2)}) collective-permute-start(bf16[256,512]{1,0:T(8,128)(2,1)S(1)} %gate.3), channel_id=1, source_target_pairs={{16,112},{48,16},{80,48},{112,80},{17,113},{49,17},{81,49},{113,81... | collective-permute-start | bytes 786440 | tf_op jit(solution)/shard_map/ppermute | solution.py:27
  50.2 3.1 %collective-permute-start.9 = (bf16[256,512]{1,0:T(8,128)(2,1)S(1)}, bf16[256,512]{1,0:T(8,128)(2,1)S(1)}, u32[]{:S(2)}, u32[]{:S(2)}) collective-permute-start(bf16[256,512]{1,0:T(8,128)(2,1)S(1)} %gate.3), channel_id=1, source_target_pairs={{16,80},{48,112},{80,16},{112,48},{17,81},{49,113},{81,17},{113,49... | collective-permute-start | bytes 786440 | tf_op jit(solution)/shard_map/ppermute | solution.py:27
  53.3 6.4 %collective-permute-done.8.refs_3_ = bf16[256,512]{1,0:T(8,128)(2,1)S(1)} collective-permute-done((bf16[256,512]{1,0:T(8,128)(2,1)S(1)}, bf16[256,512]{1,0:T(8,128)(2,1)S(1)}, u32[]{:S(2)}, u32[]{:S(2)}) %collective-permute-start.8) | collective-permute-done | bytes 262176 | tf_op jit(solution)/shard_map/ppermute | solution.py:27
  62.6 2.6 %collective-permute-start.13 = (bf16[512,256]{1,0:T(8,128)(2,1)S(1)}, bf16[512,256]{1,0:T(8,128)(2,1)S(1)}, u32[]{:S(2)}, u32[]{:S(2)}) collective-permute-start(bf16[512,256]{1,0:T(8,128)(2,1)S(1)} %get-tuple-element.37), channel_id=1, source_target_pairs={{0,8},{4,12},{8,0},{12,4},{1,9},{5,13},{9,1},{13,5},{2,10},{6,14},... | collective-permute-start | bytes 786440 | tf_op jit(solution)/shard_map/ppermute | solution.py:18
  68.2 3.9 %collective-permute-done.13.v2 = bf16[512,256]{1,0:T(8,128)(2,1)S(1)} collective-permute-done((bf16[512,256]{1,0:T(8,128)(2,1)S(1)}, bf16[512,256]{1,0:T(8,128)(2,1)S(1)}, u32[]{:S(2)}, u32[]{:S(2)}) %collective-permute-start.13) | collective-permute-done | bytes 262176 | tf_op jit(solution)/shard_map/ppermute | solution.py:18
  73.6 2.6 %collective-permute-start.16 = (bf16[128,256]{1,0:T(8,128)(2,1)S(1)}, bf16[128,256]{1,0:T(8,128)(2,1)S(1)}, u32[]{:S(2)}, u32[]{:S(2)}) collective-permute-start(bf16[128,256]{1,0:T(8,128)(2,1)S(1)} %get-tuple-element.41), channel_id=1, source_target_pairs={{0,2},{1,3},{2,0},{3,1},{4,6},{5,7},{6,4},{7,5},{8,10},{9,11},{10,... | collective-permute-start | bytes 196616 | tf_op jit(solution)/shard_map/ppermute | solution.py:18
  86.0 2.6 %lower_step.6 = (bf16[128,1024]{1,0:T(8,128)(2,1)S(1)}, bf16[128,1024]{1,0:T(8,128)(2,1)S(1)}) custom-call(s32[4]{0:T(128)S(1)} %pad_add_fusion.place_ref.refs_0_, bf16[128,256]{1,0:T(8,128)(2,1)S(1)} %add_convert_fusion.1._.refs_1_, bf16[128,256]{1,0:T(8,128)(2,1)S(1)} %collective-permute-done.18.refs_2_, ...), custom_call_target="tpu_custom_call" | custom-call | flops 268435456 | bytes 4194304 | tf_op jit(solution)/shard_map/lower_step/pallas_call | solution.py:199
  92.1 8.3 %collective-permute-done.24.refs_0_ = bf16[8,1024]{1,0:T(8,128)(2,1)S(1)} collective-permute-done((bf16[8,1024]{1,0:T(8,128)(2,1)S(1)}, bf16[8,1024]{1,0:T(8,128)(2,1)S(1)}, u32[]{:S(2)}, u32[]{:S(2)}) %collective-permute-start.24) | collective-permute-done | bytes 16416 | tf_op jit(solution)/shard_map/ppermute | solution.py:140
  100.4 2.8 %collective-permute-start.25 = (bf16[128,1024]{1,0:T(8,128)(2,1)S(1)}, bf16[128,1024]{1,0:T(8,128)(2,1)S(1)}, u32[]{:S(2)}, u32[]{:S(2)}) collective-permute-start(bf16[128,1024]{1,0:T(8,128)(2,1)S(1)} %gate.4), channel_id=1, source_target_pairs={{16,48},{48,80},{80,112},{112,16},{17,49},{49,81},{81,113},{113,17... | collective-permute-start | bytes 786440 | tf_op jit(solution)/shard_map/ppermute | solution.py:27
  103.1 4.6 %collective-permute-start.26 = (bf16[128,1024]{1,0:T(8,128)(2,1)S(1)}, bf16[128,1024]{1,0:T(8,128)(2,1)S(1)}, u32[]{:S(2)}, u32[]{:S(2)}) collective-permute-start(bf16[128,1024]{1,0:T(8,128)(2,1)S(1)} %gate.4), channel_id=1, source_target_pairs={{16,80},{48,112},{80,16},{112,48},{17,81},{49,113},{81,17},{113,49... | collective-permute-start | bytes 786440 | tf_op jit(solution)/shard_map/ppermute | solution.py:27
  110.2 3.1 %collective-permute-start.32 = (bf16[2,256,128]{2,1,0:T(8,128)(2,1)S(1)}, bf16[2,256,128]{2,1,0:T(8,128)(2,1)S(1)}, u32[]{:S(2)}, u32[]{:S(2)}) collective-permute-start(bf16[2,256,128]{2,1,0:T(8,128)(2,1)S(1)} %get-tuple-element.48), channel_id=1, source_target_pairs={{0,2},{1,3},{2,0},{3,1},{4,6},{5,7},{6,4},{7,5},{8,10},{9,11},{10,... | collective-permute-start | bytes 393224 | tf_op jit(solution)/shard_map/ppermute | solution.py:18
  115.3 2.4 %diag_step.2._.refs_0_ = bf16[128,1024]{1,0:T(8,128)(2,1)S(1)} custom-call(s32[4]{0:T(128)S(1)} %pad_add_fusion.place_ref.refs_0_, bf16[128,1024]{1,0:T(8,128)(2,1)S(1)} %get-tuple-element.44.refs_1_, bf16[128,1024]{1,0:T(8,128)(2,1)S(1)} %collective-permute-done.21.refs_2_, bf16[128,1024]{1,0:T(8,128)(2,1)S(1)} %collective-permute-done.22.refs_3_, ...), custom_call_target="tpu_custom_call" | custom-call | flops 268435456 | bytes 4194304 | tf_op jit(solution)/shard_map/diag_step/pallas_call | solution.py:273
  118.6 3.0 %collective-permute-start.29 = (bf16[128,1024]{1,0:T(8,128)(2,1)S(1)}, bf16[128,1024]{1,0:T(8,128)(2,1)S(1)}, u32[]{:S(2)}, u32[]{:S(2)}) collective-permute-start(bf16[128,1024]{1,0:T(8,128)(2,1)S(1)} %diag_step.2._.refs_0_), channel_id=1, source_target_pairs={{0,8},{4,12},{8,0},{12,4},{1,9},{5,13},{9,1},{13,5},{2,10},{6,14},... | collective-permute-start | bytes 786440 | tf_op jit(solution)/shard_map/ppermute | solution.py:18
  124.4 2.5 %lower_step.7 = (f32[128,1024]{1,0:T(8,128)S(1)}, bf16[128,1024]{1,0:T(8,128)(2,1)}) custom-call(bf16[128,1024]{1,0:T(8,128)(2,1)S(1)} %get-tuple-element.45.refs_0_.x3, f32[128,1024]{1,0:T(8,128)S(1)} %get-tuple-element.64.refs_1_, bf16[2,4,2560,256]{3,2,1,0:T(8,128)(2,1)} %bitcast.46), custom_call_target="tpu_custom_call" | custom-call | flops 268435456 | bytes 4194304 | tf_op jit(solution)/shard_map/lower_step/pallas_call | solution.py:199
  133.5 4.4 %collective-permute-done.34.refs_1_ = bf16[128,1024]{1,0:T(8,128)(2,1)S(1)} collective-permute-done((bf16[128,1024]{1,0:T(8,128)(2,1)S(1)}, bf16[128,1024]{1,0:T(8,128)(2,1)S(1)}, u32[]{:S(2)}, u32[]{:S(2)}) %collective-permute-start.34) | collective-permute-done | bytes 262176 | tf_op jit(solution)/shard_map/ppermute | solution.py:18
  138.0 2.8 %collective-permute-done.35.refs_2_ = bf16[128,1024]{1,0:T(8,128)(2,1)S(1)} collective-permute-done((bf16[128,1024]{1,0:T(8,128)(2,1)S(1)}, bf16[128,1024]{1,0:T(8,128)(2,1)S(1)}, u32[]{:S(2)}, u32[]{:S(2)}) %collective-permute-start.35) | collective-permute-done | bytes 262176 | tf_op jit(solution)/shard_map/ppermute | solution.py:18
  143.5 2.4 %collective-permute-start.38 = (bf16[128,1024]{1,0:T(8,128)(2,1)S(1)}, bf16[128,1024]{1,0:T(8,128)(2,1)S(1)}, u32[]{:S(2)}, u32[]{:S(2)}) collective-permute-start(bf16[128,1024]{1,0:T(8,128)(2,1)S(1)} %diag_step.3.refs_0_), channel_id=1, source_target_pairs={{0,8},{4,12},{8,0},{12,4},{1,9},{5,13},{9,1},{13,5},{2,10},{6,14},... | collective-permute-start | bytes 786440 | tf_op jit(solution)/shard_map/ppermute | solution.py:18
  146.3 2.5 %lower_step.9 = (f32[128,1024]{1,0:T(8,128)S(1)}, bf16[128,1024]{1,0:T(8,128)(2,1)}) custom-call(bf16[128,1024]{1,0:T(8,128)(2,1)S(1)} %get-tuple-element.45.refs_0_.x3, f32[128,1024]{1,0:T(8,128)S(1)} %get-tuple-element.63.refs_1_, bf16[2,4,2064,256]{3,2,1,0:T(8,128)(2,1)} %bitcast.49), custom_call_target="tpu_custom_call" | custom-call | flops 268435456 | bytes 4194304 | tf_op jit(solution)/shard_map/lower_step/pallas_call | solution.py:199
  148.8 2.5 %lower_step.10 = (f32[128,1024]{1,0:T(8,128)S(1)}, bf16[128,1024]{1,0:T(8,128)(2,1)}) custom-call(bf16[128,1024]{1,0:T(8,128)(2,1)S(1)} %get-tuple-element.52.refs_0_.x2, f32[128,1024]{1,0:T(8,128)S(1)} %get-tuple-element.53.refs_1_, bf16[2,4,2064,256]{3,2,1,0:T(8,128)(2,1)} %bitcast.50), custom_call_target="tpu_custom_call" | custom-call | flops 268435456 | bytes 4194304 | tf_op jit(solution)/shard_map/lower_step/pallas_call | solution.py:199
  151.6 2.8 %collective-permute-done.38.refs_2_ = bf16[128,1024]{1,0:T(8,128)(2,1)S(1)} collective-permute-done((bf16[128,1024]{1,0:T(8,128)(2,1)S(1)}, bf16[128,1024]{1,0:T(8,128)(2,1)S(1)}, u32[]{:S(2)}, u32[]{:S(2)}) %collective-permute-start.38) | collective-permute-done | bytes 262176 | tf_op jit(solution)/shard_map/ppermute | solution.py:18
  157.1 3.3 %collective-permute-start.40 = (bf16[128,1024]{1,0:T(8,128)(2,1)S(1)}, bf16[128,1024]{1,0:T(8,128)(2,1)S(1)}, u32[]{:S(2)}, u32[]{:S(2)}) collective-permute-start(bf16[128,1024]{1,0:T(8,128)(2,1)S(1)} %get-tuple-element.57.v0), channel_id=1, source_target_pairs={{0,32},{32,64},{64,96},{96,0},{1,33},{33,65},{65,97},{97,1},{2,34}... | collective-permute-start | bytes 786440 | tf_op jit(solution)/shard_map/ppermute | solution.py:18
  164.9 3.1 %collective-permute-done.40.v1 = bf16[128,1024]{1,0:T(8,128)(2,1)S(1)} collective-permute-done((bf16[128,1024]{1,0:T(8,128)(2,1)S(1)}, bf16[128,1024]{1,0:T(8,128)(2,1)S(1)}, u32[]{:S(2)}, u32[]{:S(2)}) %collective-permute-start.40) | collective-permute-done | bytes 262176 | tf_op jit(solution)/shard_map/ppermute | solution.py:18
  167.9 7.2 %collective-permute-done.41.v2 = bf16[128,1024]{1,0:T(8,128)(2,1)S(1)} collective-permute-done((bf16[128,1024]{1,0:T(8,128)(2,1)S(1)}, bf16[128,1024]{1,0:T(8,128)(2,1)S(1)}, u32[]{:S(2)}, u32[]{:S(2)}) %collective-permute-start.41) | collective-permute-done | bytes 262176 | tf_op jit(solution)/shard_map/ppermute | solution.py:18
  175.1 2.5 %last_step.1 = (bf16[128,256]{1,0:T(8,128)(2,1)S(1)}, bf16[128,256]{1,0:T(8,128)(2,1)S(1)}, bf16[128,256]{1,0:T(8,128)(2,1)S(1)}, bf16[128,256]{1,0:T(8,128)(2,1)S(1)}) custom-call(s32[4]{0:T(128)S(1)} %pad_add_fusion.place_ref.refs_0_, bf16[128,1024]{1,0:T(8,128)(2,1)S(1)} %get-tuple-element.57.v0, bf16[128,1024]{1,0:T(8,128)(2,1)S(1)} %collective-permute-done.40.v1, ...), custom_call_target="tpu_custom_call" | custom-call | flops 268435456 | bytes 4194304 | tf_op jit(solution)/shard_map/last_step/pallas_call | solution.py:295
  177.9 2.7 %collective-permute-start.44 = (bf16[128,256]{1,0:T(8,128)(2,1)S(1)}, bf16[128,256]{1,0:T(8,128)(2,1)S(1)}, u32[]{:S(2)}, u32[]{:S(2)}) collective-permute-start(bf16[128,256]{1,0:T(8,128)(2,1)S(1)} %get-tuple-element.60), channel_id=1, source_target_pairs={{0,8},{4,12},{8,0},{12,4},{1,9},{5,13},{9,1},{13,5},{2,10},{6,14},... | collective-permute-start | bytes 196616 | tf_op jit(solution)/shard_map/ppermute | solution.py:18
  181.3 3.0 %pack_known.1 = (bf16[2048,128]{1,0:T(8,128)(2,1)S(1)}, bf16[2048,256]{1,0:T(8,128)(2,1)S(1)}) custom-call(s32[4]{0:T(128)S(1)} %pad_add_fusion.place_ref.refs_0_, s32[4,1,256]{2,1,0:T(1,128)S(1)} %reshape.61.target_ref, bf16[128,1024]{1,0:T(8,128)(2,1)S(1)} %get-tuple-element.55.x1, bf16[128,1024]{1,0:T(8,128)(2,1)S(1)} %get-tuple-element.52.refs_0_.x2, ...), custom_call_target="tpu_custom_call" | custom-call | flops 402653184 | bytes 2097152 | tf_op jit(solution)/shard_map/pack_known/pallas_call | solution.py:384
  185.2 23.0 %all_to_all.5 = bf16[128,16,128]{2,1,0:T(8,128)(2,1)S(1)} all-to-all(bf16[128,16,128]{2,1,0:T(8,128)(2,1)S(1)} %bitcast.43), channel_id=1, replica_groups=mesh['z'=4,'core'=2,'y'=4,'x'=4] {'z','core','y','x'}, dimensions={0} | all-to-all | bytes 1048576 | tf_op jit(solution)/shard_map/all_to_all | solution.py:512
  (115 shorter events, 60.7 us)
Async XLA Ops:
  6.5 79.5 %all-gather.7.cloned.1.call-start = ((), (), s32[]{:S(2)}) async-start(), calls=%async_computation.2 | async-start | bytes 11796480 | tf_op jit(solution)/shard_map/all_gather | solution.py:450
  9.9 136.5 %all-gather.5.cloned.1.call-start = ((), (), s32[]{:S(2)}) async-start(), calls=%async_computation.1 | async-start | bytes 9510912 | tf_op jit(solution)/shard_map/all_gather | solution.py:450
  16.5 7.4 %collective-permute-start = (bf16[4,256,512]{2,1,0:T(8,128)(2,1)S(1)}, bf16[4,256,512]{2,1,0:T(8,128)(2,1)S(1)}, u32[]{:S(2)}, u32[]{:S(2)}) collective-permute-start(bf16[4,256,512]{2,1,0:T(8,128)(2,1)S(1)} %fusion.6), channel_id=1, source_target_pairs={{0,16},{16,0},{1,17},{17,1},{2,18},{18,2},{3,19},{19,3},{4,20},{20... | collective-permute-start | bytes 3145736 | tf_op jit(solution)/shard_map/ppermute | solution.py:22
  26.6 18.2 %collective-permute-start.5 = (bf16[1,256,128]{2,1,0:T(8,128)(2,1)S(1)}, bf16[1,256,128]{2,1,0:T(8,128)(2,1)S(1)}, u32[]{:S(2)}, u32[]{:S(2)}) collective-permute-start(bf16[1,256,128]{2,1,0:T(8,128)(2,1)S(1)} %get-tuple-element.74), channel_id=1, source_target_pairs={{0,1},{1,2},{2,3},{3,0},{4,5},{5,6},{6,7},{7,4},{8,9},{9,10},{10,1... | collective-permute-start | bytes 196616 | tf_op jit(solution)/shard_map/ppermute | solution.py:18
  28.0 16.9 %collective-permute-start.6 = (bf16[1,256,128]{2,1,0:T(8,128)(2,1)S(1)}, bf16[1,256,128]{2,1,0:T(8,128)(2,1)S(1)}, u32[]{:S(2)}, u32[]{:S(2)}) collective-permute-start(bf16[1,256,128]{2,1,0:T(8,128)(2,1)S(1)} %get-tuple-element.73), channel_id=1, source_target_pairs={{0,2},{1,3},{2,0},{3,1},{4,6},{5,7},{6,4},{7,5},{8,10},{9,11},{10,... | collective-permute-start | bytes 196616 | tf_op jit(solution)/shard_map/ppermute | solution.py:18
  30.4 14.4 %collective-permute-start.7 = (bf16[1,256,128]{2,1,0:T(8,128)(2,1)S(1)}, bf16[1,256,128]{2,1,0:T(8,128)(2,1)S(1)}, u32[]{:S(2)}, u32[]{:S(2)}) collective-permute-start(bf16[1,256,128]{2,1,0:T(8,128)(2,1)S(1)} %get-tuple-element.72), channel_id=1, source_target_pairs={{0,3},{1,0},{2,1},{3,2},{4,7},{5,4},{6,5},{7,6},{8,11},{9,8},{10,9... | collective-permute-start | bytes 196616 | tf_op jit(solution)/shard_map/ppermute | solution.py:18
  31.6 13.3 %collective-permute-start.4 = (bf16[8,512]{1,0:T(8,128)(2,1)S(1)}, bf16[8,512]{1,0:T(8,128)(2,1)S(1)}, u32[]{:S(2)}, u32[]{:S(2)}) collective-permute-start(bf16[8,512]{1,0:T(8,128)(2,1)S(1)} %slice_add_fusion.2), channel_id=1, source_target_pairs={{0,16},{1,17},{2,18},{3,19},{4,20},{5,21},{6,22},{7,23},{8,24},{9,... | collective-permute-start | bytes 24584 | tf_op jit(solution)/shard_map/ppermute | solution.py:140
  33.9 19.5 %collective-permute-start.11 = (bf16[256,512]{1,0:T(8,128)(2,1)S(1)}, bf16[256,512]{1,0:T(8,128)(2,1)S(1)}, u32[]{:S(2)}, u32[]{:S(2)}) collective-permute-start(bf16[256,512]{1,0:T(8,128)(2,1)S(1)} %slice_bitcast_fusion.3.refs_6_), channel_id=1, source_target_pairs={{0,16},{16,0},{1,17},{17,1},{2,18},{18,2},{3,19},{19,3},{4,20},{20... | collective-permute-start | bytes 786440 | tf_op jit(solution)/shard_map/ppermute | solution.py:22
  44.9 8.5 %collective-permute-start.10 = (bf16[256,512]{1,0:T(8,128)(2,1)S(1)}, bf16[256,512]{1,0:T(8,128)(2,1)S(1)}, u32[]{:S(2)}, u32[]{:S(2)}) collective-permute-start(bf16[256,512]{1,0:T(8,128)(2,1)S(1)} %gate.3), channel_id=1, source_target_pairs={{16,112},{48,16},{80,48},{112,80},{17,113},{49,17},{81,49},{113,81... | collective-permute-start | bytes 786440 | tf_op jit(solution)/shard_map/ppermute | solution.py:27
  48.2 11.5 %collective-permute-start.8 = (bf16[256,512]{1,0:T(8,128)(2,1)S(1)}, bf16[256,512]{1,0:T(8,128)(2,1)S(1)}, u32[]{:S(2)}, u32[]{:S(2)}) collective-permute-start(bf16[256,512]{1,0:T(8,128)(2,1)S(1)} %gate.3), channel_id=1, source_target_pairs={{16,48},{48,80},{80,112},{112,16},{17,49},{49,81},{81,113},{113,17... | collective-permute-start | bytes 786440 | tf_op jit(solution)/shard_map/ppermute | solution.py:27
  50.2 9.6 %collective-permute-start.9 = (bf16[256,512]{1,0:T(8,128)(2,1)S(1)}, bf16[256,512]{1,0:T(8,128)(2,1)S(1)}, u32[]{:S(2)}, u32[]{:S(2)}) collective-permute-start(bf16[256,512]{1,0:T(8,128)(2,1)S(1)} %gate.3), channel_id=1, source_target_pairs={{16,80},{48,112},{80,16},{112,48},{17,81},{49,113},{81,17},{113,49... | collective-permute-start | bytes 786440 | tf_op jit(solution)/shard_map/ppermute | solution.py:27
  61.2 7.0 %collective-permute-start.12 = (bf16[512,256]{1,0:T(8,128)(2,1)S(1)}, bf16[512,256]{1,0:T(8,128)(2,1)S(1)}, u32[]{:S(2)}, u32[]{:S(2)}) collective-permute-start(bf16[512,256]{1,0:T(8,128)(2,1)S(1)} %get-tuple-element.36), channel_id=1, source_target_pairs={{0,4},{4,8},{8,12},{12,0},{1,5},{5,9},{9,13},{13,1},{2,6},{6,10},{... | collective-permute-start | bytes 786440 | tf_op jit(solution)/shard_map/ppermute | solution.py:18
  62.6 9.5 %collective-permute-start.13 = (bf16[512,256]{1,0:T(8,128)(2,1)S(1)}, bf16[512,256]{1,0:T(8,128)(2,1)S(1)}, u32[]{:S(2)}, u32[]{:S(2)}) collective-permute-start(bf16[512,256]{1,0:T(8,128)(2,1)S(1)} %get-tuple-element.37), channel_id=1, source_target_pairs={{0,8},{4,12},{8,0},{12,4},{1,9},{5,13},{9,1},{13,5},{2,10},{6,14},... | collective-permute-start | bytes 786440 | tf_op jit(solution)/shard_map/ppermute | solution.py:18
  65.2 6.9 %collective-permute-start.14 = (bf16[512,256]{1,0:T(8,128)(2,1)S(1)}, bf16[512,256]{1,0:T(8,128)(2,1)S(1)}, u32[]{:S(2)}, u32[]{:S(2)}) collective-permute-start(bf16[512,256]{1,0:T(8,128)(2,1)S(1)} %get-tuple-element.38), channel_id=1, source_target_pairs={{0,12},{4,0},{8,4},{12,8},{1,13},{5,1},{9,5},{13,9},{2,14},{6,2},{... | collective-permute-start | bytes 786440 | tf_op jit(solution)/shard_map/ppermute | solution.py:18
  90.8 9.6 %collective-permute-start.24 = (bf16[8,1024]{1,0:T(8,128)(2,1)S(1)}, bf16[8,1024]{1,0:T(8,128)(2,1)S(1)}, u32[]{:S(2)}, u32[]{:S(2)}) collective-permute-start(bf16[8,1024]{1,0:T(8,128)(2,1)S(1)} %slice_add_fusion), channel_id=1, source_target_pairs={{0,16},{1,17},{2,18},{3,19},{4,20},{5,21},{6,22},{7,23},{8,24},{9,... | collective-permute-start | bytes 49160 | tf_op jit(solution)/shard_map/ppermute | solution.py:140
  100.4 13.0 %collective-permute-start.25 = (bf16[128,1024]{1,0:T(8,128)(2,1)S(1)}, bf16[128,1024]{1,0:T(8,128)(2,1)S(1)}, u32[]{:S(2)}, u32[]{:S(2)}) collective-permute-start(bf16[128,1024]{1,0:T(8,128)(2,1)S(1)} %gate.4), channel_id=1, source_target_pairs={{16,48},{48,80},{80,112},{112,16},{17,49},{49,81},{81,113},{113,17... | collective-permute-start | bytes 786440 | tf_op jit(solution)/shard_map/ppermute | solution.py:27
  103.1 11.4 %collective-permute-start.26 = (bf16[128,1024]{1,0:T(8,128)(2,1)S(1)}, bf16[128,1024]{1,0:T(8,128)(2,1)S(1)}, u32[]{:S(2)}, u32[]{:S(2)}) collective-permute-start(bf16[128,1024]{1,0:T(8,128)(2,1)S(1)} %gate.4), channel_id=1, source_target_pairs={{16,80},{48,112},{80,16},{112,48},{17,81},{49,113},{81,17},{113,49... | collective-permute-start | bytes 786440 | tf_op jit(solution)/shard_map/ppermute | solution.py:27
  107.8 7.5 %collective-permute-start.27 = (bf16[128,1024]{1,0:T(8,128)(2,1)S(1)}, bf16[128,1024]{1,0:T(8,128)(2,1)S(1)}, u32[]{:S(2)}, u32[]{:S(2)}) collective-permute-start(bf16[128,1024]{1,0:T(8,128)(2,1)S(1)} %gate.4), channel_id=1, source_target_pairs={{16,112},{48,16},{80,48},{112,80},{17,113},{49,17},{81,49},{113,81... | collective-permute-start | bytes 786440 | tf_op jit(solution)/shard_map/ppermute | solution.py:27
  109.8 11.8 %collective-permute-start.31 = (bf16[2,256,128]{2,1,0:T(8,128)(2,1)S(1)}, bf16[2,256,128]{2,1,0:T(8,128)(2,1)S(1)}, u32[]{:S(2)}, u32[]{:S(2)}) collective-permute-start(bf16[2,256,128]{2,1,0:T(8,128)(2,1)S(1)} %get-tuple-element.47), channel_id=1, source_target_pairs={{0,1},{1,2},{2,3},{3,0},{4,5},{5,6},{6,7},{7,4},{8,9},{9,10},{10,1... | collective-permute-start | bytes 393224 | tf_op jit(solution)/shard_map/ppermute | solution.py:18
  110.2 13.1 %collective-permute-start.32 = (bf16[2,256,128]{2,1,0:T(8,128)(2,1)S(1)}, bf16[2,256,128]{2,1,0:T(8,128)(2,1)S(1)}, u32[]{:S(2)}, u32[]{:S(2)}) collective-permute-start(bf16[2,256,128]{2,1,0:T(8,128)(2,1)S(1)} %get-tuple-element.48), channel_id=1, source_target_pairs={{0,2},{1,3},{2,0},{3,1},{4,6},{5,7},{6,4},{7,5},{8,10},{9,11},{10,... | collective-permute-start | bytes 393224 | tf_op jit(solution)/shard_map/ppermute | solution.py:18
  113.4 10.2 %collective-permute-start.33 = (bf16[2,256,128]{2,1,0:T(8,128)(2,1)S(1)}, bf16[2,256,128]{2,1,0:T(8,128)(2,1)S(1)}, u32[]{:S(2)}, u32[]{:S(2)}) collective-permute-start(bf16[2,256,128]{2,1,0:T(8,128)(2,1)S(1)} %get-tuple-element.49), channel_id=1, source_target_pairs={{0,3},{1,0},{2,1},{3,2},{4,7},{5,4},{6,5},{7,6},{8,11},{9,8},{10,9... | collective-permute-start | bytes 393224 | tf_op jit(solution)/shard_map/ppermute | solution.py:18
  117.7 9.2 %collective-permute-start.28 = (bf16[128,1024]{1,0:T(8,128)(2,1)S(1)}, bf16[128,1024]{1,0:T(8,128)(2,1)S(1)}, u32[]{:S(2)}, u32[]{:S(2)}) collective-permute-start(bf16[128,1024]{1,0:T(8,128)(2,1)S(1)} %diag_step.2._.refs_0_), channel_id=1, source_target_pairs={{0,4},{4,8},{8,12},{12,0},{1,5},{5,9},{9,13},{13,1},{2,6},{6,10},{... | collective-permute-start | bytes 786440 | tf_op jit(solution)/shard_map/ppermute | solution.py:18
  118.6 9.6 %collective-permute-start.29 = (bf16[128,1024]{1,0:T(8,128)(2,1)S(1)}, bf16[128,1024]{1,0:T(8,128)(2,1)S(1)}, u32[]{:S(2)}, u32[]{:S(2)}) collective-permute-start(bf16[128,1024]{1,0:T(8,128)(2,1)S(1)} %diag_step.2._.refs_0_), channel_id=1, source_target_pairs={{0,8},{4,12},{8,0},{12,4},{1,9},{5,13},{9,1},{13,5},{2,10},{6,14},... | collective-permute-start | bytes 786440 | tf_op jit(solution)/shard_map/ppermute | solution.py:18
  130.2 7.8 %collective-permute-start.34 = (bf16[128,1024]{1,0:T(8,128)(2,1)S(1)}, bf16[128,1024]{1,0:T(8,128)(2,1)S(1)}, u32[]{:S(2)}, u32[]{:S(2)}) collective-permute-start(bf16[128,1024]{1,0:T(8,128)(2,1)S(1)} %get-tuple-element.51.refs_0_), channel_id=1, source_target_pairs={{0,32},{32,64},{64,96},{96,0},{1,33},{33,65},{65,97},{97,1},{2,34}... | collective-permute-start | bytes 786440 | tf_op jit(solution)/shard_map/ppermute | solution.py:18
  131.1 9.7 %collective-permute-start.35 = (bf16[128,1024]{1,0:T(8,128)(2,1)S(1)}, bf16[128,1024]{1,0:T(8,128)(2,1)S(1)}, u32[]{:S(2)}, u32[]{:S(2)}) collective-permute-start(bf16[128,1024]{1,0:T(8,128)(2,1)S(1)} %get-tuple-element.51.refs_0_), channel_id=1, source_target_pairs={{0,64},{32,96},{64,0},{96,32},{1,65},{33,97},{65,1},{97,33},{2,66}... | collective-permute-start | bytes 786440 | tf_op jit(solution)/shard_map/ppermute | solution.py:18
  133.1 7.7 %collective-permute-start.36 = (bf16[128,1024]{1,0:T(8,128)(2,1)S(1)}, bf16[128,1024]{1,0:T(8,128)(2,1)S(1)}, u32[]{:S(2)}, u32[]{:S(2)}) collective-permute-start(bf16[128,1024]{1,0:T(8,128)(2,1)S(1)} %get-tuple-element.51.refs_0_), channel_id=1, source_target_pairs={{0,96},{32,0},{64,32},{96,64},{1,97},{33,1},{65,33},{97,65},{2,98}... | collective-permute-start | bytes 786440 | tf_op jit(solution)/shard_map/ppermute | solution.py:18
  142.7 8.9 %collective-permute-start.37 = (bf16[128,1024]{1,0:T(8,128)(2,1)S(1)}, bf16[128,1024]{1,0:T(8,128)(2,1)S(1)}, u32[]{:S(2)}, u32[]{:S(2)}) collective-permute-start(bf16[128,1024]{1,0:T(8,128)(2,1)S(1)} %diag_step.3.refs_0_), channel_id=1, source_target_pairs={{0,4},{4,8},{8,12},{12,0},{1,5},{5,9},{9,13},{13,1},{2,6},{6,10},{... | collective-permute-start | bytes 786440 | tf_op jit(solution)/shard_map/ppermute | solution.py:18
  143.5 10.8 %collective-permute-start.38 = (bf16[128,1024]{1,0:T(8,128)(2,1)S(1)}, bf16[128,1024]{1,0:T(8,128)(2,1)S(1)}, u32[]{:S(2)}, u32[]{:S(2)}) collective-permute-start(bf16[128,1024]{1,0:T(8,128)(2,1)S(1)} %diag_step.3.refs_0_), channel_id=1, source_target_pairs={{0,8},{4,12},{8,0},{12,4},{1,9},{5,13},{9,1},{13,5},{2,10},{6,14},... | collective-permute-start | bytes 786440 | tf_op jit(solution)/shard_map/ppermute | solution.py:18
  146.0 9.1 %collective-permute-start.39 = (bf16[128,1024]{1,0:T(8,128)(2,1)S(1)}, bf16[128,1024]{1,0:T(8,128)(2,1)S(1)}, u32[]{:S(2)}, u32[]{:S(2)}) collective-permute-start(bf16[128,1024]{1,0:T(8,128)(2,1)S(1)} %diag_step.3.refs_0_), channel_id=1, source_target_pairs={{0,12},{4,0},{8,4},{12,8},{1,13},{5,1},{9,5},{13,9},{2,14},{6,2},{... | collective-permute-start | bytes 786440 | tf_op jit(solution)/shard_map/ppermute | solution.py:18
  157.1 10.8 %collective-permute-start.40 = (bf16[128,1024]{1,0:T(8,128)(2,1)S(1)}, bf16[128,1024]{1,0:T(8,128)(2,1)S(1)}, u32[]{:S(2)}, u32[]{:S(2)}) collective-permute-start(bf16[128,1024]{1,0:T(8,128)(2,1)S(1)} %get-tuple-element.57.v0), channel_id=1, source_target_pairs={{0,32},{32,64},{64,96},{96,0},{1,33},{33,65},{65,97},{97,1},{2,34}... | collective-permute-start | bytes 786440 | tf_op jit(solution)/shard_map/ppermute | solution.py:18
  160.4 14.7 %collective-permute-start.41 = (bf16[128,1024]{1,0:T(8,128)(2,1)S(1)}, bf16[128,1024]{1,0:T(8,128)(2,1)S(1)}, u32[]{:S(2)}, u32[]{:S(2)}) collective-permute-start(bf16[128,1024]{1,0:T(8,128)(2,1)S(1)} %get-tuple-element.57.v0), channel_id=1, source_target_pairs={{0,64},{32,96},{64,0},{96,32},{1,65},{33,97},{65,1},{97,33},{2,66}... | collective-permute-start | bytes 786440 | tf_op jit(solution)/shard_map/ppermute | solution.py:18
  162.7 12.4 %collective-permute-start.42 = (bf16[128,1024]{1,0:T(8,128)(2,1)S(1)}, bf16[128,1024]{1,0:T(8,128)(2,1)S(1)}, u32[]{:S(2)}, u32[]{:S(2)}) collective-permute-start(bf16[128,1024]{1,0:T(8,128)(2,1)S(1)} %get-tuple-element.57.v0), channel_id=1, source_target_pairs={{0,96},{32,0},{64,32},{96,64},{1,97},{33,1},{65,33},{97,65},{2,98}... | collective-permute-start | bytes 786440 | tf_op jit(solution)/shard_map/ppermute | solution.py:18
  (18 other events, 97.0 us)
Sparse Core Ops, SparseCore 0:
  10.0 66.3 all-gather.6
  78.1 55.8 all-gather.4

commit v14 on v10

--- a/solution.py
+++ b/solution.py
@@ -464,10 +464,10 @@
         ]
 
     near = deal(cut(both[2:3]), "x")
-    own, *others = first_product(place, over_z, inverse_diag[3], other, near[1:])
+    own, *others = first_product(place, over_z, inverse_diag[3], other, near[1:2])
     zero = [along_y(others[by - 1], 0, by) for by in (1, 2, 3)]
     token = lax.ppermute(sum(piece[:8] for piece in zero), "core", [(0, 1)])
-    others = gate((token,), others)
+    others = gate((token, *near[2:]), others)
     one = [along_y(others[by - 1], 1, by) for by in (1, 2, 3)]
     over_x = deal(first_sum(place, own, zero, one), "x")
     quarter = sum(piece.astype(F32) for piece in over_x).astype(BF16)

time: 200 us -> 205 us (1.025)
  starting transfers between devices: 57.4 us -> 62.3 us
  blocking collectives: 20.2 us -> 22.3 us
    ppermute x33, waiting for transfers between devices: 32.4 us -> 42.7 us  [shift(): return lax.ppermute(value, axis, [(i, (i + by) % 4) for i in range(4)])]
    ppermute x1, waiting for transfers between devices: 19 us -> 9.28 us  [local(): token = lax.ppermute(sum((piece[:8] for piece in zero)), 'core', [(0, 1)])]
    ppermute x33, starting transfers between devices: 43.2 us -> 48.2 us  [shift(): return lax.ppermute(value, axis, [(i, (i + by) % 4) for i in range(4)])]
    all_to_all x1, blocking collectives: 20.2 us -> 22.3 us  [local(): lax.all_to_all(packed, ('z', 'core', 'y', 'x'), split_axis=0, concat_axis...]
  transfers between devices with their start and end apart: 44 -> 44, of which waited for: 21 -> 24; matrix products, arithmetic and copies ran while one was open for 9% -> 8% of each run, Pallas kernels for 11% -> 11%
where the time goes in v14:
time: 205 us; the launch traced here: 204 us
  starting transfers between devices  62.3 us (30%)
  waiting for transfers between devices  57.9 us (28%)
  Pallas kernels  32.2 us (16%)
  blocking collectives  22.3 us (11%)
  between operations  13.8 us (7%)
  matrix products  11.9 us (6%)
  other arithmetic  2.35 us (1%)
    ppermute x33, starting transfers between devices, shift(): return lax.ppermute(value, axis, [(i, (i + by) % 4) for i in range(4)])  48.2 us
    ppermute x33, waiting for transfers between devices, shift(): return lax.ppermute(value, axis, [(i, (i + by) % 4) for i in range(4)])  42.7 us
    all_to_all x1, blocking collectives, local(): lax.all_to_all(packed, ('z', 'core', 'y', 'x'), split_axis=0, concat_axis...  22.3 us
    pallas_call x6, Pallas kernels, lower_step(): pl.pallas_call(kernel, out_shape=(jax.ShapeDtypeStruct((128, 1024), dtype...  14.3 us
    dot_general x2, matrix products, term(): lax.dot_general(border_tiles, bound, (((0,), (0,)), ((), ())), preferred_...  11.9 us
    ppermute x6, starting transfers between devices, along_y(): return lax.ppermute(value, ('core', 'y'), pairs)  11.2 us
    ppermute x1, waiting for transfers between devices, local(): token = lax.ppermute(sum((piece[:8] for piece in zero)), 'core', [(0, 1)])  9.28 us
    ppermute x6, waiting for transfers between devices, along_y(): return lax.ppermute(value, ('core', 'y'), pairs)  5.19 us
  transfers between devices with their start and end apart: 44, of which 24 were waited for; matrix products, arithmetic and copies ran while one was open for 8% of the time, Pallas kernels for 11%

profile of v14, /device:TPU:1, one launch (start us, length us, event | category | flops | bytes accessed | tf_op | source)
XLA Modules:
  0.0 204.2 jit_solution(14954694639181189640)
XLA Ops:
  6.5 3.3 %stage.1 = (bf16[2560,256]{1,0:T(8,128)(2,1)}, bf16[2064,256]{1,0:T(8,128)(2,1)}) custom-call(bf16[6,512,256]{2,1,0:T(8,128)(2,1)} %lower_ref.1, bf16[4,256,512]{2,1,0:T(8,128)(2,1)} %diag_ref.1, s32[1,128]{1,0:T(1,128)} %bitcast.56), custom_call_target="tpu_custom_call" | custom-call | bytes 6291456 | tf_op jit(solution)/shard_map/stage/pallas_call | solution.py:325
  10.6 5.9 %fusion.6 = bf16[4,256,512]{2,1,0:T(8,128)(2,1)S(1)} fusion(f32[4,256,1024]{2,1,0:T(8,128)} %param.6, s32[]{:T(128)S(6)} %select_n.30, bf16[2048,4,256]{2,1,0:T(4,128)(2,1)} %param.8, bf16[2048,1024]{1,0:T(8,128)(2,1)} %param.7, f32[]{:T(128)S(6)} %select_n.28), kind=kOutput, calls=%fused_computation.7 | convolution fusion | flops 2149056512 | bytes 9438720 | tf_op jit(solution)/shard_map/dot_general | solution.py:451
  19.1 6.0 %fusion.7 = bf16[4,256,512]{2,1,0:T(8,128)(2,1)S(1)} fusion(f32[4,256,1024]{2,1,0:T(8,128)} %param.6, s32[]{:T(128)S(6)} %select_n.29, bf16[2048,4,256]{2,1,0:T(4,128)(2,1)} %param.8, bf16[2048,1024]{1,0:T(8,128)(2,1)} %param.7, f32[]{:T(128)S(6)} %select_n.28), kind=kOutput, calls=%fused_computation.9 | convolution fusion | flops 2149056512 | bytes 9438720 | tf_op jit(solution)/shard_map/dot_general | solution.py:451
  27.3 3.6 %collective-permute-start.2 = (bf16[256,512]{1,0:T(8,128)(2,1)S(1)}, bf16[256,512]{1,0:T(8,128)(2,1)S(1)}, u32[]{:S(2)}, u32[]{:S(2)}) collective-permute-start(bf16[256,512]{1,0:T(8,128)(2,1)S(1)} %get-tuple-element.72.v0), channel_id=1, source_target_pairs={{0,64},{32,96},{64,0},{96,32},{1,65},{33,97},{65,1},{97,33},{2,66}... | collective-permute-start | bytes 786440 | tf_op jit(solution)/shard_map/ppermute | solution.py:18
  32.9 4.9 %collective-permute-done.5.refs_0_.v1 = bf16[1,256,128]{2,1,0:T(8,128)(2,1)S(1)} collective-permute-done((bf16[1,256,128]{2,1,0:T(8,128)(2,1)S(1)}, bf16[1,256,128]{2,1,0:T(8,128)(2,1)S(1)}, u32[]{:S(2)}, u32[]{:S(2)}) %collective-permute-start.5) | collective-permute-done | bytes 65568 | tf_op jit(solution)/shard_map/ppermute | solution.py:18
  37.8 4.6 %collective-permute-done.2.v2 = bf16[256,512]{1,0:T(8,128)(2,1)S(1)} collective-permute-done((bf16[256,512]{1,0:T(8,128)(2,1)S(1)}, bf16[256,512]{1,0:T(8,128)(2,1)S(1)}, u32[]{:S(2)}, u32[]{:S(2)}) %collective-permute-start.2) | collective-permute-done | bytes 262176 | tf_op jit(solution)/shard_map/ppermute | solution.py:18
  45.7 2.8 %collective-permute-start.10 = (bf16[1,256,128]{2,1,0:T(8,128)(2,1)S(1)}, bf16[1,256,128]{2,1,0:T(8,128)(2,1)S(1)}, u32[]{:S(2)}, u32[]{:S(2)}) collective-permute-start(bf16[1,256,128]{2,1,0:T(8,128)(2,1)S(1)} %get-tuple-element.79), channel_id=1, source_target_pairs={{0,2},{1,3},{2,0},{3,1},{4,6},{5,7},{6,4},{7,5},{8,10},{9,11},{10,... | collective-permute-start | bytes 196616 | tf_op jit(solution)/shard_map/ppermute | solution.py:18
  51.8 2.6 %collective-permute-done.11.refs_2_.v3 = bf16[1,256,128]{2,1,0:T(8,128)(2,1)S(1)} collective-permute-done((bf16[1,256,128]{2,1,0:T(8,128)(2,1)S(1)}, bf16[1,256,128]{2,1,0:T(8,128)(2,1)S(1)}, u32[]{:S(2)}, u32[]{:S(2)}) %collective-permute-start.11) | collective-permute-done | bytes 65568 | tf_op jit(solution)/shard_map/ppermute | solution.py:18
  54.4 9.3 %collective-permute-done.9.refs_0_ = bf16[8,256]{1,0:T(8,128)(2,1)S(1)} collective-permute-done((bf16[8,256]{1,0:T(8,128)(2,1)S(1)}, bf16[8,256]{1,0:T(8,128)(2,1)S(1)}, u32[]{:S(2)}, u32[]{:S(2)}) %collective-permute-start.9) | collective-permute-done | bytes 4128 | tf_op jit(solution)/shard_map/ppermute | solution.py:469
  63.7 2.6 %collective-permute-start.12 = (bf16[512,256]{1,0:T(8,128)(2,1)S(1)}, bf16[512,256]{1,0:T(8,128)(2,1)S(1)}, u32[]{:S(2)}, u32[]{:S(2)}) collective-permute-start(bf16[512,256]{1,0:T(8,128)(2,1)S(1)} %get-tuple-element.42), channel_id=1, source_target_pairs={{16,20},{20,24},{24,28},{28,16},{17,21},{21,25},{25,29},{29,17},{1... | collective-permute-start | bytes 786440 | tf_op jit(solution)/shard_map/ppermute | solution.py:27
  66.3 4.6 %collective-permute-start.13 = (bf16[512,256]{1,0:T(8,128)(2,1)S(1)}, bf16[512,256]{1,0:T(8,128)(2,1)S(1)}, u32[]{:S(2)}, u32[]{:S(2)}) collective-permute-start(bf16[512,256]{1,0:T(8,128)(2,1)S(1)} %get-tuple-element.43), channel_id=1, source_target_pairs={{16,24},{20,28},{24,16},{28,20},{17,25},{21,29},{25,17},{29,21},{1... | collective-permute-start | bytes 786440 | tf_op jit(solution)/shard_map/ppermute | solution.py:27
  72.9 2.7 %collective-permute-done.13.refs_4_ = bf16[512,256]{1,0:T(8,128)(2,1)S(1)} collective-permute-done((bf16[512,256]{1,0:T(8,128)(2,1)S(1)}, bf16[512,256]{1,0:T(8,128)(2,1)S(1)}, u32[]{:S(2)}, u32[]{:S(2)}) %collective-permute-start.13) | collective-permute-done | bytes 262176 | tf_op jit(solution)/shard_map/ppermute | solution.py:27
  75.6 2.5 %collective-permute-done.14.refs_5_ = bf16[512,256]{1,0:T(8,128)(2,1)S(1)} collective-permute-done((bf16[512,256]{1,0:T(8,128)(2,1)S(1)}, bf16[512,256]{1,0:T(8,128)(2,1)S(1)}, u32[]{:S(2)}, u32[]{:S(2)}) %collective-permute-start.14) | collective-permute-done | bytes 262176 | tf_op jit(solution)/shard_map/ppermute | solution.py:27
  80.0 2.5 %collective-permute-start.16 = (bf16[128,256]{1,0:T(8,128)(2,1)S(1)}, bf16[128,256]{1,0:T(8,128)(2,1)S(1)}, u32[]{:S(2)}, u32[]{:S(2)}) collective-permute-start(bf16[128,256]{1,0:T(8,128)(2,1)S(1)} %get-tuple-element.47), channel_id=1, source_target_pairs={{0,2},{1,3},{2,0},{3,1},{4,6},{5,7},{6,4},{7,5},{8,10},{9,11},{10,... | collective-permute-start | bytes 196616 | tf_op jit(solution)/shard_map/ppermute | solution.py:18
  85.8 2.8 %collective-permute-start.19 = (bf16[128,256]{1,0:T(8,128)(2,1)S(1)}, bf16[128,256]{1,0:T(8,128)(2,1)S(1)}, u32[]{:S(2)}, u32[]{:S(2)}) collective-permute-start(bf16[128,256]{1,0:T(8,128)(2,1)S(1)} %add_convert_fusion.1._.refs_1_), channel_id=1, source_target_pairs={{0,8},{4,12},{8,0},{12,4},{1,9},{5,13},{9,1},{13,5},{2,10},{6,14},... | collective-permute-start | bytes 196616 | tf_op jit(solution)/shard_map/ppermute | solution.py:18
  92.0 2.6 %lower_step.6 = (bf16[128,1024]{1,0:T(8,128)(2,1)S(1)}, bf16[128,1024]{1,0:T(8,128)(2,1)S(1)}) custom-call(s32[4]{0:T(128)S(1)} %pad_add_fusion.place_ref.refs_0_, bf16[128,256]{1,0:T(8,128)(2,1)S(1)} %add_convert_fusion.1._.refs_1_, bf16[128,256]{1,0:T(8,128)(2,1)S(1)} %collective-permute-done.18.refs_2_, ...), custom_call_target="tpu_custom_call" | custom-call | flops 268435456 | bytes 4194304 | tf_op jit(solution)/shard_map/lower_step/pallas_call | solution.py:193
  99.7 3.2 %collective-permute-start.28 = (bf16[2,256,128]{2,1,0:T(8,128)(2,1)S(1)}, bf16[2,256,128]{2,1,0:T(8,128)(2,1)S(1)}, u32[]{:S(2)}, u32[]{:S(2)}) collective-permute-start(bf16[2,256,128]{2,1,0:T(8,128)(2,1)S(1)} %get-tuple-element.54), channel_id=1, source_target_pairs={{0,2},{1,3},{2,0},{3,1},{4,6},{5,7},{6,4},{7,5},{8,10},{9,11},{10,... | collective-permute-start | bytes 393224 | tf_op jit(solution)/shard_map/ppermute | solution.py:18
  107.0 2.7 %collective-permute-start.25 = (bf16[128,1024]{1,0:T(8,128)(2,1)S(1)}, bf16[128,1024]{1,0:T(8,128)(2,1)S(1)}, u32[]{:S(2)}, u32[]{:S(2)}) collective-permute-start(bf16[128,1024]{1,0:T(8,128)(2,1)S(1)} %diag_step.2.refs_0_), channel_id=1, source_target_pairs={{0,8},{4,12},{8,0},{12,4},{1,9},{5,13},{9,1},{13,5},{2,10},{6,14},... | collective-permute-start | bytes 786440 | tf_op jit(solution)/shard_map/ppermute | solution.py:18
  110.3 2.5 %collective-permute-done.28.v2 = bf16[2,256,128]{2,1,0:T(8,128)(2,1)S(1)} collective-permute-done((bf16[2,256,128]{2,1,0:T(8,128)(2,1)S(1)}, bf16[2,256,128]{2,1,0:T(8,128)(2,1)S(1)}, u32[]{:S(2)}, u32[]{:S(2)}) %collective-permute-start.28) | collective-permute-done | bytes 131104 | tf_op jit(solution)/shard_map/ppermute | solution.py:18
  114.1 2.5 %lower_step.7 = (f32[128,1024]{1,0:T(8,128)S(1)}, bf16[128,1024]{1,0:T(8,128)(2,1)}) custom-call(bf16[128,1024]{1,0:T(8,128)(2,1)S(1)} %get-tuple-element.51.refs_0_.x3, f32[128,1024]{1,0:T(8,128)S(1)} %get-tuple-element.70.refs_1_, bf16[2,4,2560,256]{3,2,1,0:T(8,128)(2,1)} %bitcast.46), custom_call_target="tpu_custom_call" | custom-call | flops 268435456 | bytes 4194304 | tf_op jit(solution)/shard_map/lower_step/pallas_call | solution.py:193
  122.7 4.1 %collective-permute-done.30.v1 = bf16[128,1024]{1,0:T(8,128)(2,1)S(1)} collective-permute-done((bf16[128,1024]{1,0:T(8,128)(2,1)S(1)}, bf16[128,1024]{1,0:T(8,128)(2,1)S(1)}, u32[]{:S(2)}, u32[]{:S(2)}) %collective-permute-start.30) | collective-permute-done | bytes 262176 | tf_op jit(solution)/shard_map/ppermute | solution.py:18
  132.3 2.7 %collective-permute-start.34 = (bf16[128,1024]{1,0:T(8,128)(2,1)S(1)}, bf16[128,1024]{1,0:T(8,128)(2,1)S(1)}, u32[]{:S(2)}, u32[]{:S(2)}) collective-permute-start(bf16[128,1024]{1,0:T(8,128)(2,1)S(1)} %diag_step.3.refs_0_), channel_id=1, source_target_pairs={{0,8},{4,12},{8,0},{12,4},{1,9},{5,13},{9,1},{13,5},{2,10},{6,14},... | collective-permute-start | bytes 786440 | tf_op jit(solution)/shard_map/ppermute | solution.py:18
  135.2 2.5 %lower_step.9 = (f32[128,1024]{1,0:T(8,128)S(1)}, bf16[128,1024]{1,0:T(8,128)(2,1)}) custom-call(bf16[128,1024]{1,0:T(8,128)(2,1)S(1)} %get-tuple-element.51.refs_0_.x3, f32[128,1024]{1,0:T(8,128)S(1)} %get-tuple-element.69.refs_1_, bf16[2,4,2064,256]{3,2,1,0:T(8,128)(2,1)} %bitcast.49), custom_call_target="tpu_custom_call" | custom-call | flops 268435456 | bytes 4194304 | tf_op jit(solution)/shard_map/lower_step/pallas_call | solution.py:193
  137.7 2.5 %lower_step.10 = (f32[128,1024]{1,0:T(8,128)S(1)}, bf16[128,1024]{1,0:T(8,128)(2,1)}) custom-call(bf16[128,1024]{1,0:T(8,128)(2,1)S(1)} %get-tuple-element.58.refs_0_.x2, f32[128,1024]{1,0:T(8,128)S(1)} %get-tuple-element.59.refs_1_, bf16[2,4,2064,256]{3,2,1,0:T(8,128)(2,1)} %bitcast.50), custom_call_target="tpu_custom_call" | custom-call | flops 268435456 | bytes 4194304 | tf_op jit(solution)/shard_map/lower_step/pallas_call | solution.py:193
  140.3 2.7 %collective-permute-done.34.refs_2_ = bf16[128,1024]{1,0:T(8,128)(2,1)S(1)} collective-permute-done((bf16[128,1024]{1,0:T(8,128)(2,1)S(1)}, bf16[128,1024]{1,0:T(8,128)(2,1)S(1)}, u32[]{:S(2)}, u32[]{:S(2)}) %collective-permute-start.34) | collective-permute-done | bytes 262176 | tf_op jit(solution)/shard_map/ppermute | solution.py:18
  145.7 5.9 %collective-permute-start.37 = (bf16[128,1024]{1,0:T(8,128)(2,1)S(1)}, bf16[128,1024]{1,0:T(8,128)(2,1)S(1)}, u32[]{:S(2)}, u32[]{:S(2)}) collective-permute-start(bf16[128,1024]{1,0:T(8,128)(2,1)S(1)} %get-tuple-element.63.v0), channel_id=1, source_target_pairs={{0,64},{32,96},{64,0},{96,32},{1,65},{33,97},{65,1},{97,33},{2,66}... | collective-permute-start | bytes 786440 | tf_op jit(solution)/shard_map/ppermute | solution.py:18
  153.6 2.8 %collective-permute-done.36.v1 = bf16[128,1024]{1,0:T(8,128)(2,1)S(1)} collective-permute-done((bf16[128,1024]{1,0:T(8,128)(2,1)S(1)}, bf16[128,1024]{1,0:T(8,128)(2,1)S(1)}, u32[]{:S(2)}, u32[]{:S(2)}) %collective-permute-start.36) | collective-permute-done | bytes 262176 | tf_op jit(solution)/shard_map/ppermute | solution.py:18
  156.4 7.1 %collective-permute-done.37.v2 = bf16[128,1024]{1,0:T(8,128)(2,1)S(1)} collective-permute-done((bf16[128,1024]{1,0:T(8,128)(2,1)S(1)}, bf16[128,1024]{1,0:T(8,128)(2,1)S(1)}, u32[]{:S(2)}, u32[]{:S(2)}) %collective-permute-start.37) | collective-permute-done | bytes 262176 | tf_op jit(solution)/shard_map/ppermute | solution.py:18
  163.5 2.5 %last_step.1 = (bf16[128,256]{1,0:T(8,128)(2,1)S(1)}, bf16[128,256]{1,0:T(8,128)(2,1)S(1)}, bf16[128,256]{1,0:T(8,128)(2,1)S(1)}, bf16[128,256]{1,0:T(8,128)(2,1)S(1)}) custom-call(s32[4]{0:T(128)S(1)} %pad_add_fusion.place_ref.refs_0_, bf16[128,1024]{1,0:T(8,128)(2,1)S(1)} %get-tuple-element.63.v0, bf16[128,1024]{1,0:T(8,128)(2,1)S(1)} %collective-permute-done.36.v1, ...), custom_call_target="tpu_custom_call" | custom-call | flops 268435456 | bytes 4194304 | tf_op jit(solution)/shard_map/last_step/pallas_call | solution.py:272
  166.1 3.2 %collective-permute-start.40 = (bf16[128,256]{1,0:T(8,128)(2,1)S(1)}, bf16[128,256]{1,0:T(8,128)(2,1)S(1)}, u32[]{:S(2)}, u32[]{:S(2)}) collective-permute-start(bf16[128,256]{1,0:T(8,128)(2,1)S(1)} %get-tuple-element.66), channel_id=1, source_target_pairs={{0,8},{4,12},{8,0},{12,4},{1,9},{5,13},{9,1},{13,5},{2,10},{6,14},... | collective-permute-start | bytes 196616 | tf_op jit(solution)/shard_map/ppermute | solution.py:18
  169.4 3.0 %pack_known.1 = (bf16[2048,128]{1,0:T(8,128)(2,1)S(1)}, bf16[2048,256]{1,0:T(8,128)(2,1)S(1)}) custom-call(s32[4]{0:T(128)S(1)} %pad_add_fusion.place_ref.refs_0_, s32[4,1,256]{2,1,0:T(1,128)S(1)} %reshape.61.target_ref, bf16[128,1024]{1,0:T(8,128)(2,1)S(1)} %get-tuple-element.61.x1, bf16[128,1024]{1,0:T(8,128)(2,1)S(1)} %get-tuple-element.58.refs_0_.x2, ...), custom_call_target="tpu_custom_call" | custom-call | flops 402653184 | bytes 2097152 | tf_op jit(solution)/shard_map/pack_known/pallas_call | solution.py:361
  173.5 22.3 %all_to_all.5 = bf16[128,16,128]{2,1,0:T(8,128)(2,1)S(1)} all-to-all(bf16[128,16,128]{2,1,0:T(8,128)(2,1)S(1)} %bitcast.43), channel_id=1, replica_groups=mesh['z'=4,'core'=2,'y'=4,'x'=4] {'z','core','y','x'}, dimensions={0} | all-to-all | bytes 1048576 | tf_op jit(solution)/shard_map/all_to_all | solution.py:491
  (100 shorter events, 55.0 us)
Async XLA Ops:
  6.5 85.5 %all-gather.7.cloned.1.call-start = ((), (), s32[]{:S(2)}) async-start(), calls=%async_computation.2 | async-start | bytes 11796480 | tf_op jit(solution)/shard_map/all_gather | solution.py:427
  9.9 125.3 %all-gather.5.cloned.1.call-start = ((), (), s32[]{:S(2)}) async-start(), calls=%async_computation.1 | async-start | bytes 9510912 | tf_op jit(solution)/shard_map/all_gather | solution.py:427
  16.5 8.6 %collective-permute-start = (bf16[4,256,512]{2,1,0:T(8,128)(2,1)S(1)}, bf16[4,256,512]{2,1,0:T(8,128)(2,1)S(1)}, u32[]{:S(2)}, u32[]{:S(2)}) collective-permute-start(bf16[4,256,512]{2,1,0:T(8,128)(2,1)S(1)} %fusion.6), channel_id=1, source_target_pairs={{0,16},{16,0},{1,17},{17,1},{2,18},{18,2},{3,19},{19,3},{4,20},{20... | collective-permute-start | bytes 3145736 | tf_op jit(solution)/shard_map/ppermute | solution.py:22
  19.0 13.9 %collective-permute-start.4 = (bf16[256,512]{1,0:T(8,128)(2,1)S(1)}, bf16[256,512]{1,0:T(8,128)(2,1)S(1)}, u32[]{:S(2)}, u32[]{:S(2)}) collective-permute-start(bf16[256,512]{1,0:T(8,128)(2,1)S(1)} %slice_bitcast_fusion.3.mine_ref), channel_id=1, source_target_pairs={{0,16},{16,0},{1,17},{17,1},{2,18},{18,2},{3,19},{19,3},{4,20},{20... | collective-permute-start | bytes 786440 | tf_op jit(solution)/shard_map/ppermute | solution.py:22
  25.4 12.3 %collective-permute-start.1 = (bf16[256,512]{1,0:T(8,128)(2,1)S(1)}, bf16[256,512]{1,0:T(8,128)(2,1)S(1)}, u32[]{:S(2)}, u32[]{:S(2)}) collective-permute-start(bf16[256,512]{1,0:T(8,128)(2,1)S(1)} %get-tuple-element.72.v0), channel_id=1, source_target_pairs={{0,32},{32,64},{64,96},{96,0},{1,33},{33,65},{65,97},{97,1},{2,34}... | collective-permute-start | bytes 786440 | tf_op jit(solution)/shard_map/ppermute | solution.py:18
  27.3 15.0 %collective-permute-start.2 = (bf16[256,512]{1,0:T(8,128)(2,1)S(1)}, bf16[256,512]{1,0:T(8,128)(2,1)S(1)}, u32[]{:S(2)}, u32[]{:S(2)}) collective-permute-start(bf16[256,512]{1,0:T(8,128)(2,1)S(1)} %get-tuple-element.72.v0), channel_id=1, source_target_pairs={{0,64},{32,96},{64,0},{96,32},{1,65},{33,97},{65,1},{97,33},{2,66}... | collective-permute-start | bytes 786440 | tf_op jit(solution)/shard_map/ppermute | solution.py:18
  30.9 11.5 %collective-permute-start.3 = (bf16[256,512]{1,0:T(8,128)(2,1)S(1)}, bf16[256,512]{1,0:T(8,128)(2,1)S(1)}, u32[]{:S(2)}, u32[]{:S(2)}) collective-permute-start(bf16[256,512]{1,0:T(8,128)(2,1)S(1)} %get-tuple-element.72.v0), channel_id=1, source_target_pairs={{0,96},{32,0},{64,32},{96,64},{1,97},{33,1},{65,33},{97,65},{2,98}... | collective-permute-start | bytes 786440 | tf_op jit(solution)/shard_map/ppermute | solution.py:18
  31.5 6.3 %collective-permute-start.5 = (bf16[1,256,128]{2,1,0:T(8,128)(2,1)S(1)}, bf16[1,256,128]{2,1,0:T(8,128)(2,1)S(1)}, u32[]{:S(2)}, u32[]{:S(2)}) collective-permute-start(bf16[1,256,128]{2,1,0:T(8,128)(2,1)S(1)} %get-tuple-element.80), channel_id=1, source_target_pairs={{0,1},{1,2},{2,3},{3,0},{4,5},{5,6},{6,7},{7,4},{8,9},{9,10},{10,1... | collective-permute-start | bytes 196616 | tf_op jit(solution)/shard_map/ppermute | solution.py:18
  49.4 14.3 %collective-permute-start.9 = (bf16[8,256]{1,0:T(8,128)(2,1)S(1)}, bf16[8,256]{1,0:T(8,128)(2,1)S(1)}, u32[]{:S(2)}, u32[]{:S(2)}) collective-permute-start(bf16[8,256]{1,0:T(8,128)(2,1)S(1)} %slice_add_fusion), channel_id=1, source_target_pairs={{0,16},{1,17},{2,18},{3,19},{4,20},{5,21},{6,22},{7,23},{8,24},{9,... | collective-permute-start | bytes 12296 | tf_op jit(solution)/shard_map/ppermute | solution.py:469
  63.7 9.2 %collective-permute-start.12 = (bf16[512,256]{1,0:T(8,128)(2,1)S(1)}, bf16[512,256]{1,0:T(8,128)(2,1)S(1)}, u32[]{:S(2)}, u32[]{:S(2)}) collective-permute-start(bf16[512,256]{1,0:T(8,128)(2,1)S(1)} %get-tuple-element.42), channel_id=1, source_target_pairs={{16,20},{20,24},{24,28},{28,16},{17,21},{21,25},{25,29},{29,17},{1... | collective-permute-start | bytes 786440 | tf_op jit(solution)/shard_map/ppermute | solution.py:27
  66.3 9.2 %collective-permute-start.13 = (bf16[512,256]{1,0:T(8,128)(2,1)S(1)}, bf16[512,256]{1,0:T(8,128)(2,1)S(1)}, u32[]{:S(2)}, u32[]{:S(2)}) collective-permute-start(bf16[512,256]{1,0:T(8,128)(2,1)S(1)} %get-tuple-element.43), channel_id=1, source_target_pairs={{16,24},{20,28},{24,16},{28,20},{17,25},{21,29},{25,17},{29,21},{1... | collective-permute-start | bytes 786440 | tf_op jit(solution)/shard_map/ppermute | solution.py:27
  70.9 7.1 %collective-permute-start.14 = (bf16[512,256]{1,0:T(8,128)(2,1)S(1)}, bf16[512,256]{1,0:T(8,128)(2,1)S(1)}, u32[]{:S(2)}, u32[]{:S(2)}) collective-permute-start(bf16[512,256]{1,0:T(8,128)(2,1)S(1)} %get-tuple-element.44), channel_id=1, source_target_pairs={{16,28},{20,16},{24,20},{28,24},{17,29},{21,17},{25,21},{29,25},{1... | collective-permute-start | bytes 786440 | tf_op jit(solution)/shard_map/ppermute | solution.py:27
  94.6 8.3 %collective-permute-start.22 = (bf16[128,1024]{1,0:T(8,128)(2,1)S(1)}, bf16[128,1024]{1,0:T(8,128)(2,1)S(1)}, u32[]{:S(2)}, u32[]{:S(2)}) collective-permute-start(bf16[128,1024]{1,0:T(8,128)(2,1)S(1)} %get-tuple-element.50.v0), channel_id=1, source_target_pairs={{0,64},{32,96},{64,0},{96,32},{1,65},{33,97},{65,1},{97,33},{2,66}... | collective-permute-start | bytes 786440 | tf_op jit(solution)/shard_map/ppermute | solution.py:18
  96.5 8.1 %collective-permute-start.21 = (bf16[128,1024]{1,0:T(8,128)(2,1)S(1)}, bf16[128,1024]{1,0:T(8,128)(2,1)S(1)}, u32[]{:S(2)}, u32[]{:S(2)}) collective-permute-start(bf16[128,1024]{1,0:T(8,128)(2,1)S(1)} %get-tuple-element.50.v0), channel_id=1, source_target_pairs={{0,32},{32,64},{64,96},{96,0},{1,33},{33,65},{65,97},{97,1},{2,34}... | collective-permute-start | bytes 786440 | tf_op jit(solution)/shard_map/ppermute | solution.py:18
  97.2 7.5 %collective-permute-start.23 = (bf16[128,1024]{1,0:T(8,128)(2,1)S(1)}, bf16[128,1024]{1,0:T(8,128)(2,1)S(1)}, u32[]{:S(2)}, u32[]{:S(2)}) collective-permute-start(bf16[128,1024]{1,0:T(8,128)(2,1)S(1)} %get-tuple-element.50.v0), channel_id=1, source_target_pairs={{0,96},{32,0},{64,32},{96,64},{1,97},{33,1},{65,33},{97,65},{2,98}... | collective-permute-start | bytes 786440 | tf_op jit(solution)/shard_map/ppermute | solution.py:18
  99.3 10.4 %collective-permute-start.27 = (bf16[2,256,128]{2,1,0:T(8,128)(2,1)S(1)}, bf16[2,256,128]{2,1,0:T(8,128)(2,1)S(1)}, u32[]{:S(2)}, u32[]{:S(2)}) collective-permute-start(bf16[2,256,128]{2,1,0:T(8,128)(2,1)S(1)} %get-tuple-element.53), channel_id=1, source_target_pairs={{0,1},{1,2},{2,3},{3,0},{4,5},{5,6},{6,7},{7,4},{8,9},{9,10},{10,1... | collective-permute-start | bytes 393224 | tf_op jit(solution)/shard_map/ppermute | solution.py:18
  99.7 13.1 %collective-permute-start.28 = (bf16[2,256,128]{2,1,0:T(8,128)(2,1)S(1)}, bf16[2,256,128]{2,1,0:T(8,128)(2,1)S(1)}, u32[]{:S(2)}, u32[]{:S(2)}) collective-permute-start(bf16[2,256,128]{2,1,0:T(8,128)(2,1)S(1)} %get-tuple-element.54), channel_id=1, source_target_pairs={{0,2},{1,3},{2,0},{3,1},{4,6},{5,7},{6,4},{7,5},{8,10},{9,11},{10,... | collective-permute-start | bytes 393224 | tf_op jit(solution)/shard_map/ppermute | solution.py:18
  103.0 10.3 %collective-permute-start.29 = (bf16[2,256,128]{2,1,0:T(8,128)(2,1)S(1)}, bf16[2,256,128]{2,1,0:T(8,128)(2,1)S(1)}, u32[]{:S(2)}, u32[]{:S(2)}) collective-permute-start(bf16[2,256,128]{2,1,0:T(8,128)(2,1)S(1)} %get-tuple-element.55), channel_id=1, source_target_pairs={{0,3},{1,0},{2,1},{3,2},{4,7},{5,4},{6,5},{7,6},{8,11},{9,8},{10,9... | collective-permute-start | bytes 393224 | tf_op jit(solution)/shard_map/ppermute | solution.py:18
  106.5 10.1 %collective-permute-start.24 = (bf16[128,1024]{1,0:T(8,128)(2,1)S(1)}, bf16[128,1024]{1,0:T(8,128)(2,1)S(1)}, u32[]{:S(2)}, u32[]{:S(2)}) collective-permute-start(bf16[128,1024]{1,0:T(8,128)(2,1)S(1)} %diag_step.2.refs_0_), channel_id=1, source_target_pairs={{0,4},{4,8},{8,12},{12,0},{1,5},{5,9},{9,13},{13,1},{2,6},{6,10},{... | collective-permute-start | bytes 786440 | tf_op jit(solution)/shard_map/ppermute | solution.py:18
  107.0 9.6 %collective-permute-start.25 = (bf16[128,1024]{1,0:T(8,128)(2,1)S(1)}, bf16[128,1024]{1,0:T(8,128)(2,1)S(1)}, u32[]{:S(2)}, u32[]{:S(2)}) collective-permute-start(bf16[128,1024]{1,0:T(8,128)(2,1)S(1)} %diag_step.2.refs_0_), channel_id=1, source_target_pairs={{0,8},{4,12},{8,0},{12,4},{1,9},{5,13},{9,1},{13,5},{2,10},{6,14},... | collective-permute-start | bytes 786440 | tf_op jit(solution)/shard_map/ppermute | solution.py:18
  109.7 7.2 %collective-permute-start.26 = (bf16[128,1024]{1,0:T(8,128)(2,1)S(1)}, bf16[128,1024]{1,0:T(8,128)(2,1)S(1)}, u32[]{:S(2)}, u32[]{:S(2)}) collective-permute-start(bf16[128,1024]{1,0:T(8,128)(2,1)S(1)} %diag_step.2.refs_0_), channel_id=1, source_target_pairs={{0,12},{4,0},{8,4},{12,8},{1,13},{5,1},{9,5},{13,9},{2,14},{6,2},{... | collective-permute-start | bytes 786440 | tf_op jit(solution)/shard_map/ppermute | solution.py:18
  118.9 7.9 %collective-permute-start.30 = (bf16[128,1024]{1,0:T(8,128)(2,1)S(1)}, bf16[128,1024]{1,0:T(8,128)(2,1)S(1)}, u32[]{:S(2)}, u32[]{:S(2)}) collective-permute-start(bf16[128,1024]{1,0:T(8,128)(2,1)S(1)} %get-tuple-element.57.v0), channel_id=1, source_target_pairs={{0,32},{32,64},{64,96},{96,0},{1,33},{33,65},{65,97},{97,1},{2,34}... | collective-permute-start | bytes 786440 | tf_op jit(solution)/shard_map/ppermute | solution.py:18
  120.1 9.2 %collective-permute-start.31 = (bf16[128,1024]{1,0:T(8,128)(2,1)S(1)}, bf16[128,1024]{1,0:T(8,128)(2,1)S(1)}, u32[]{:S(2)}, u32[]{:S(2)}) collective-permute-start(bf16[128,1024]{1,0:T(8,128)(2,1)S(1)} %get-tuple-element.57.v0), channel_id=1, source_target_pairs={{0,64},{32,96},{64,0},{96,32},{1,65},{33,97},{65,1},{97,33},{2,66}... | collective-permute-start | bytes 786440 | tf_op jit(solution)/shard_map/ppermute | solution.py:18
  122.1 8.0 %collective-permute-start.32 = (bf16[128,1024]{1,0:T(8,128)(2,1)S(1)}, bf16[128,1024]{1,0:T(8,128)(2,1)S(1)}, u32[]{:S(2)}, u32[]{:S(2)}) collective-permute-start(bf16[128,1024]{1,0:T(8,128)(2,1)S(1)} %get-tuple-element.57.v0), channel_id=1, source_target_pairs={{0,96},{32,0},{64,32},{96,64},{1,97},{33,1},{65,33},{97,65},{2,98}... | collective-permute-start | bytes 786440 | tf_op jit(solution)/shard_map/ppermute | solution.py:18
  131.9 8.4 %collective-permute-start.33 = (bf16[128,1024]{1,0:T(8,128)(2,1)S(1)}, bf16[128,1024]{1,0:T(8,128)(2,1)S(1)}, u32[]{:S(2)}, u32[]{:S(2)}) collective-permute-start(bf16[128,1024]{1,0:T(8,128)(2,1)S(1)} %diag_step.3.refs_0_), channel_id=1, source_target_pairs={{0,4},{4,8},{8,12},{12,0},{1,5},{5,9},{9,13},{13,1},{2,6},{6,10},{... | collective-permute-start | bytes 786440 | tf_op jit(solution)/shard_map/ppermute | solution.py:18
  132.3 10.6 %collective-permute-start.34 = (bf16[128,1024]{1,0:T(8,128)(2,1)S(1)}, bf16[128,1024]{1,0:T(8,128)(2,1)S(1)}, u32[]{:S(2)}, u32[]{:S(2)}) collective-permute-start(bf16[128,1024]{1,0:T(8,128)(2,1)S(1)} %diag_step.3.refs_0_), channel_id=1, source_target_pairs={{0,8},{4,12},{8,0},{12,4},{1,9},{5,13},{9,1},{13,5},{2,10},{6,14},... | collective-permute-start | bytes 786440 | tf_op jit(solution)/shard_map/ppermute | solution.py:18
  135.0 8.5 %collective-permute-start.35 = (bf16[128,1024]{1,0:T(8,128)(2,1)S(1)}, bf16[128,1024]{1,0:T(8,128)(2,1)S(1)}, u32[]{:S(2)}, u32[]{:S(2)}) collective-permute-start(bf16[128,1024]{1,0:T(8,128)(2,1)S(1)} %diag_step.3.refs_0_), channel_id=1, source_target_pairs={{0,12},{4,0},{8,4},{12,8},{1,13},{5,1},{9,5},{13,9},{2,14},{6,2},{... | collective-permute-start | bytes 786440 | tf_op jit(solution)/shard_map/ppermute | solution.py:18
  145.6 10.8 %collective-permute-start.36 = (bf16[128,1024]{1,0:T(8,128)(2,1)S(1)}, bf16[128,1024]{1,0:T(8,128)(2,1)S(1)}, u32[]{:S(2)}, u32[]{:S(2)}) collective-permute-start(bf16[128,1024]{1,0:T(8,128)(2,1)S(1)} %get-tuple-element.63.v0), channel_id=1, source_target_pairs={{0,32},{32,64},{64,96},{96,0},{1,33},{33,65},{65,97},{97,1},{2,34}... | collective-permute-start | bytes 786440 | tf_op jit(solution)/shard_map/ppermute | solution.py:18
  145.7 17.8 %collective-permute-start.37 = (bf16[128,1024]{1,0:T(8,128)(2,1)S(1)}, bf16[128,1024]{1,0:T(8,128)(2,1)S(1)}, u32[]{:S(2)}, u32[]{:S(2)}) collective-permute-start(bf16[128,1024]{1,0:T(8,128)(2,1)S(1)} %get-tuple-element.63.v0), channel_id=1, source_target_pairs={{0,64},{32,96},{64,0},{96,32},{1,65},{33,97},{65,1},{97,33},{2,66}... | collective-permute-start | bytes 786440 | tf_op jit(solution)/shard_map/ppermute | solution.py:18
  151.6 11.9 %collective-permute-start.38 = (bf16[128,1024]{1,0:T(8,128)(2,1)S(1)}, bf16[128,1024]{1,0:T(8,128)(2,1)S(1)}, u32[]{:S(2)}, u32[]{:S(2)}) collective-permute-start(bf16[128,1024]{1,0:T(8,128)(2,1)S(1)} %get-tuple-element.63.v0), channel_id=1, source_target_pairs={{0,96},{32,0},{64,32},{96,64},{1,97},{33,1},{65,33},{97,65},{2,98}... | collective-permute-start | bytes 786440 | tf_op jit(solution)/shard_map/ppermute | solution.py:18
  166.0 6.4 %collective-permute-start.39 = (bf16[128,256]{1,0:T(8,128)(2,1)S(1)}, bf16[128,256]{1,0:T(8,128)(2,1)S(1)}, u32[]{:S(2)}, u32[]{:S(2)}) collective-permute-start(bf16[128,256]{1,0:T(8,128)(2,1)S(1)} %get-tuple-element.65), channel_id=1, source_target_pairs={{0,4},{4,8},{8,12},{12,0},{1,5},{5,9},{9,13},{13,1},{2,6},{6,10},{... | collective-permute-start | bytes 196616 | tf_op jit(solution)/shard_map/ppermute | solution.py:18
  166.1 6.3 %collective-permute-start.40 = (bf16[128,256]{1,0:T(8,128)(2,1)S(1)}, bf16[128,256]{1,0:T(8,128)(2,1)S(1)}, u32[]{:S(2)}, u32[]{:S(2)}) collective-permute-start(bf16[128,256]{1,0:T(8,128)(2,1)S(1)} %get-tuple-element.66), channel_id=1, source_target_pairs={{0,8},{4,12},{8,0},{12,4},{1,9},{5,13},{9,1},{13,5},{2,10},{6,14},... | collective-permute-start | bytes 196616 | tf_op jit(solution)/shard_map/ppermute | solution.py:18
  (12 other events, 56.8 us)
Sparse Core Ops, SparseCore 0:
  10.0 64.9 all-gather.6
  76.7 57.2 all-gather.4
